TPU v7x, 128 devices: a whole 4x4x4 slice. The times are simulated.
128 devices in a mesh: section: 4 (over z_hi, core), ep: 32 (over y, x, z_lo).
Axes of the slice: x: 4, y: 4, z: 4 (z_hi: 2, z_lo: 2; z = z_hi * 2 + z_lo), core: 2. Of those that a mesh axis runs over, the one named last changes fastest.
Arguments:
- states: bfloat16 [4, 4096, 6144], P('section', 'ep'), may hold values from -6 to 6
- expert_ids: int32 [4, 4096, 2], P('section', 'ep'), may hold values from 0 to 7, all different within a row; in each aligned block of 128 rows (0 to 127, 128 to 255, ..., all dimensions but the last counted through in order) at most 48 rows name the same one
- gate_values: float32 [4, 4096, 2], P('section', 'ep'), may hold values from 0.1 to 1
- keep_mask: int32 [4, 4096, 2], P('section', 'ep'), may hold values 0 or 1
- w_gate: bfloat16 [4, 6144, 16384], P('section', None, 'ep'), may hold values from -0.078125 to 0.078125
- w_up: bfloat16 [4, 6144, 16384], P('section', None, 'ep'), may hold values from -0.078125 to 0.078125
- w_down: bfloat16 [4, 16384, 6144], P('section', 'ep'), may hold values from -0.0625 to 0.0625
Outputs:
- next_states: bfloat16 [4, 4096, 6144], P('section', 'ep')
Inputs may be any that keep to these rules, and one draw needn't show every extreme that they name: `expert_ids`: in every section and every aligned block of 128 tokens (the rows of one index of ep), no expert is named by more than 48 tokens, a bound that some block reaches; the 2 experts of a token differ.
All inputs are finite; a program needn't handle non-finite values. No bound on the sum of `keep_mask` on one device may be relied on, other than what follows from the above.
Results may differ from a plain program's by a relative error of at most 0.0057.
Values may be sent and summed in bfloat16 or wider, within the bound.
No kernel may reach another device: no remote copies, remote signals or barrier semaphores. Data moves between devices by JAX's collectives and lax.ppermute only.
A program may use at most 128 MiB of HBM per device.

v0:
```python
import jax
import jax.numpy as jnp
from jax import lax
from jax.sharding import PartitionSpec as P

EXP_WIN = 2
CAP = 48


def from_behind(value, axis, by):
    devices = lax.axis_size(axis)
    return lax.ppermute(value, axis, [(i, (i + by) % devices) for i in range(devices)])


def expert_mlp(row_block, gate_matrix, up_matrix, down_matrix):
    count_a, count_b, row_width = row_block.shape
    flat_rows = row_block.reshape(count_a * count_b, row_width)
    gate_proj = jnp.dot(flat_rows, gate_matrix, preferred_element_type=jnp.float32)
    up_proj = jnp.dot(flat_rows, up_matrix, preferred_element_type=jnp.float32)
    hidden = (jax.nn.silu(gate_proj) * up_proj).astype(jnp.bfloat16)
    partial_out = jnp.dot(hidden, down_matrix, preferred_element_type=jnp.float32).astype(
        jnp.bfloat16
    )
    return partial_out.reshape(count_a, count_b, row_width)


def send_back(partial_out):
    return lax.all_to_all(partial_out, "ep", split_axis=0, concat_axis=0, tiled=True)


def dispatch_rows(outgoing, worker):
    return worker(lax.all_to_all(outgoing, "ep", split_axis=0, concat_axis=0, tiled=True))


def body(states, expert_ids, gate_values, keep_mask, w_gate, w_up, w_down):
    tokens_here = states[0]
    ids_here = expert_ids[0]
    gates_here = gate_values[0]
    keep_here = keep_mask[0]
    gate_matrix = w_gate[0]
    up_matrix = w_up[0]
    down_matrix = w_down[0]
    slices = lax.axis_size("ep") // EXP_WIN
    model_width = tokens_here.shape[1]
    expert_range = jnp.arange(EXP_WIN, dtype=jnp.int32)
    chosen = ((ids_here[None] == expert_range[:, None, None]) & (keep_here[None] == 1)).astype(
        jnp.int32
    )
    picked = jnp.sum(chosen, axis=2)
    weights_tok = jnp.sum(chosen.astype(jnp.float32) * gates_here[None], axis=2)
    slot_index = jnp.cumsum(picked, axis=1) - 1
    positions = jnp.arange(CAP, dtype=jnp.int32)
    dispatch_table = (
        (slot_index[:, None, :] == positions[None, :, None]) & (picked[:, None, :] == 1)
    ).astype(jnp.float32)
    compact = jnp.einsum(
        "ect,td->ecd",
        dispatch_table.astype(jnp.bfloat16),
        tokens_here,
        preferred_element_type=jnp.float32,
    ).astype(jnp.bfloat16)

    def local_expert(row_block):
        return expert_mlp(row_block, gate_matrix, up_matrix, down_matrix)

    outgoing = jnp.repeat(compact, slices, axis=0)
    partials = dispatch_rows(outgoing, local_expert)
    returned = send_back(partials)
    expert_out = jnp.sum(
        returned.reshape(EXP_WIN, slices, CAP, model_width).astype(jnp.float32), axis=1
    )
    combine = dispatch_table * weights_tok[:, None, :]
    mixed = jnp.einsum("ect,ecd->td", combine, expert_out, precision=lax.Precision.HIGHEST).astype(
        jnp.bfloat16
    )
    return from_behind(mixed[None], "section", 1)


def solution(mesh):
    return jax.shard_map(
        body,
        mesh=mesh,
        in_specs=(
            P("section", "ep", None),
            P("section", "ep", None),
            P("section", "ep", None),
            P("section", "ep", None),
            P("section", None, "ep"),
            P("section", None, "ep"),
            P("section", "ep", None),
        ),
        out_specs=P("section", "ep", None),
        check_vma=False,
    )
```

profile of v0, /device:TPU:2, one launch (start us, length us, event | category | flops | bytes accessed | tf_op | source)
XLA Modules:
  0.0 645.6 jit_solution(4621060272002016661)
XLA Ops:
  0.0 0.0 copy-start
  0.0 0.8 compare_bitcast_fusion
  0.8 0.7 fusion.23
  1.5 0.3 reduce_window_sum.11
  1.8 0.0 copy-done
  1.8 0.5 convolution_convert_fusion.1
  2.3 2.4 broadcast_in_dim.4
  4.7 216.4 %all_to_all.10 = bf16[32,48,6144]{2,1,0:T(8,128)(2,1)S(1)} all-to-all(bf16[32,48,6144]{2,1,0:T(8,128)(2,1)S(1)} %bitcast.39), channel_id=1, replica_groups=mesh['section'=4,'ep'=32] {'ep'}, dimensions={0} | all-to-all | bytes 37748736 | tf_op jit(solution)/shard_map/all_to_all | solution.py:32
  221.1 14.1 %fusion.5 = f32[1536,512]{1,0:T(8,128)} fusion(bf16[1536,6144]{1,0:T(8,128)(2,1)S(1)} %bitcast.41, bf16[1,6144,512]{2,1,0:T(8,128)(2,1)} %param.11), kind=kOutput, calls=%fused_computation.9 | convolution fusion | flops 9663676416 | bytes 28311552 | tf_op jit(solution)/shard_map/dot_general | solution.py:18
  235.2 13.8 %fusion.10 = bf16[1536,512]{1,0:T(8,128)(2,1)S(1)} fusion(bf16[1536,6144]{1,0:T(8,128)(2,1)S(1)} %bitcast.42, bf16[1,6144,512]{2,1,0:T(8,128)(2,1)} %param.12, f32[1536,512]{1,0:T(8,128)} %fusion.5), kind=kOutput, calls=%fused_computation.12 | convolution fusion | flops 9668395008 | bytes 29884416 | tf_op jit(solution)/shard_map/dot_general | solution.py:19
  249.0 16.0 %convolution_convert_fusion = bf16[1536,6144]{1,0:T(8,128)(2,1)} fusion(bf16[1536,512]{1,0:T(8,128)(2,1)S(1)} %fusion.10, bf16[1,512,6144]{2,1,0:T(8,128)(2,1)} %param.13), kind=kOutput, calls=%fused_computation.1 | convolution fusion | flops 9673113600 | bytes 26738688 | tf_op jit(solution)/shard_map/dot_general | solution.py:21
  265.1 0.0 copy-start.2
  265.1 0.0 copy-start.3
  265.1 8.6 %all-to-all-start.1 = ((bf16[32,48,6144]{2,1,0:T(8,128)(2,1)}), bf16[32,48,6144]{2,1,0:T(8,128)(2,1)}, u32[]{:S(2)}, u32[]{:S(2)}) async-start(bf16[32,48,6144]{2,1,0:T(8,128)(2,1)} %bitcast.40), calls=%async_computation.1 | async-start | bytes 37748736 | tf_op jit(solution)/shard_map/all_to_all | solution.py:28
  273.6 0.0 copy-done.2
  273.6 0.0 copy-done.3
  273.7 336.2 %all-to-all-done.1 = bf16[32,48,6144]{2,1,0:T(8,128)(2,1)} async-done(((bf16[32,48,6144]{2,1,0:T(8,128)(2,1)}), bf16[32,48,6144]{2,1,0:T(8,128)(2,1)}, u32[]{:S(2)}, u32[]{:S(2)}) %all-to-all-start.1) | async-done | bytes 18874400 | tf_op jit(solution)/shard_map/all_to_all | solution.py:28
  609.9 0.0 copy-start.1
  609.9 10.4 %convert_reduce_fusion = f32[2,48,6144]{2,1,0:T(8,128)S(1)} fusion(bf16[32,48,6144]{2,1,0:T(8,128)(2,1)} %all-to-all-done.1), kind=kLoop, calls=%fused_computation | loop fusion | flops 18284544 | bytes 21233664 | tf_op jit(solution)/shard_map/reduce_sum | solution.py:69
  620.3 2.7 fusion.1
  623.0 0.1 collective-permute-start
  623.1 21.3 %collective-permute-done = bf16[1,128,6144]{2,1,0:T(8,128)(2,1)S(1)} collective-permute-done((bf16[1,128,6144]{2,1,0:T(8,128)(2,1)S(1)}, bf16[1,128,6144]{2,1,0:T(8,128)(2,1)S(1)}, u32[]{:S(2)}, u32[]{:S(2)}) %collective-permute-start) | collective-permute-done | bytes 1572896 | tf_op jit(solution)/shard_map/ppermute | solution.py:12
  644.5 1.1 copy.12
  645.6 0.0 copy-done.1
  (3 shorter events, 0.0 us)
Async XLA Ops:
  0.0 1.8 copy-start
  265.1 8.6 %copy-start.2 = (s32[1,128,2]{1,2,0:T(2,128)S(1)}, s32[1,128,2]{1,2,0:T(2,128)}, u32[]{:S(2)}) copy-start(s32[1,128,2]{1,2,0:T(2,128)} %param.8) | copy-start | bytes 3076
  265.1 8.6 %copy-start.3 = (f32[1,128,2]{1,2,0:T(2,128)S(1)}, f32[1,128,2]{1,2,0:T(2,128)}, u32[]{:S(2)}) copy-start(f32[1,128,2]{1,2,0:T(2,128)} %param.9) | copy-start | bytes 3076
  265.1 344.8 %all-to-all-start.1 = ((bf16[32,48,6144]{2,1,0:T(8,128)(2,1)}), bf16[32,48,6144]{2,1,0:T(8,128)(2,1)}, u32[]{:S(2)}, u32[]{:S(2)}) async-start(bf16[32,48,6144]{2,1,0:T(8,128)(2,1)} %bitcast.40), calls=%async_computation.1 | async-start | bytes 37748736 | tf_op jit(solution)/shard_map/all_to_all | solution.py:28
  609.9 35.7 %copy-start.1 = (bf16[1,128,6144]{2,1,0:T(8,128)(2,1)S(1)}, bf16[1,128,6144]{2,1,0:T(8,128)(2,1)}, u32[]{:S(2)}) copy-start(bf16[1,128,6144]{2,1,0:T(8,128)(2,1)} %param.7) | copy-start | bytes 4718596
  623.0 21.4 %collective-permute-start = (bf16[1,128,6144]{2,1,0:T(8,128)(2,1)S(1)}, bf16[1,128,6144]{2,1,0:T(8,128)(2,1)S(1)}, u32[]{:S(2)}, u32[]{:S(2)}) collective-permute-start(bf16[1,128,6144]{2,1,0:T(8,128)(2,1)S(1)} %fusion.1), channel_id=1, source_target_pairs={{0,32},{32,64},{64,96},{96,0},{1,33},{33,65},{65,97},{97,1},{2,34}... | collective-permute-start | bytes 4718600 | tf_op jit(solution)/shard_map/ppermute | solution.py:12
where the time goes:
time: 646 us
  waiting for transfers between devices  358 us (55%)
  blocking collectives  216 us (33%)
  matrix products  47.1 us (7%)
  other arithmetic  12.3 us (2%)
  starting transfers between devices  8.64 us (1%)
    all_to_all x1, waiting for transfers between devices, send_back(): lax.all_to_all(partial_out, 'ep', split_axis=0, concat_axis=0, tiled=True)  336 us
    all_to_all x1, blocking collectives, dispatch_rows(): lax.all_to_all(outgoing, 'ep', split_axis=0, concat_axis=0, tiled=True)  216 us
    ppermute x1, waiting for transfers between devices, from_behind(): lax.ppermute(value, axis, [(i, (i + by) % devices) for i in range(devices)])  21.3 us
    dot_general x1, matrix products, expert_mlp(): jnp.dot(hidden, down_matrix, preferred_element_type=jnp.float32)  16 us
    dot_general x1, matrix products, expert_mlp(): jnp.dot(flat_rows, gate_matrix, preferred_element_type=jnp.float32)  14.1 us
    dot_general x1, matrix products, expert_mlp(): up_proj = jnp.dot(flat_rows, up_matrix, preferred_element_type=jnp.float32)  13.8 us
  transfers between devices with their start and end apart: 2, of which 2 were waited for; matrix products, arithmetic and copies ran while one was open for 0% of the time, Pallas kernels for 0%

commit v1 on v0

v1 whole, which is shorter than its diff:
```python
import jax
import jax.numpy as jnp
from jax import lax
from jax.sharding import Mesh, PartitionSpec as P

EXP_WIN = 2
CAP = 48
PIECE = 24
F32 = jnp.float32
BF16 = jnp.bfloat16


def shift(value, axis, by):
    n = lax.axis_size(axis)
    return lax.ppermute(value, axis, [(i, (i + by) % n) for i in range(n)])


def to_partner(value):
    return lax.ppermute(value, ("yh", "yl"), [(y, 3 - y) for y in range(4)])


def to_next_section(value):
    return lax.ppermute(value, ("zh", "core"), [(s, (s + 1) % 4) for s in range(4)])


def to_next_section_partner(value):
    pairs = [(s * 4 + y, (s + 1) % 4 * 4 + 3 - y) for s in range(4) for y in range(4)]
    return lax.ppermute(value, ("zh", "core", "yh", "yl"), pairs)


def add(*terms):
    total = terms[0].astype(F32)
    for term in terms[1:]:
        total = total + term.astype(F32)
    return total.astype(BF16)


def split(rows, sizes):
    out, start = [], 0
    for size in sizes:
        out.append(rows[start : start + size])
        start += size
    return out


def spread_across(piece, first, second):
    near = jnp.concatenate([piece, shift(piece, first, 1)])
    far = shift(near, second, 1)
    near_left, near_right = shift(near, "x", 1), shift(near, "x", -1)
    far_left, far_right = shift(far, "x", 1), shift(far, "x", -1)
    near_opposite = shift(near_left, "x", 1)
    far_opposite = shift(far_right, "x", -1)
    return [near, far, near_left, near_right, far_left, far_right, near_opposite, far_opposite]


def reduce_across(parts, first, second):
    near, far, near_left, near_right, far_left, far_right, near_opposite, far_opposite = parts
    near_right_sent = shift(near_right, "x", 1)
    far_left_sent = shift(far_left, "x", -1)
    near_left = add(near_left, shift(near_opposite, "x", -1))
    far_right = add(far_right, shift(far_opposite, "x", 1))
    near_left_sent = shift(near_left, "x", -1)
    far_right_sent = shift(far_right, "x", 1)
    far = add(far, far_left_sent, far_right_sent)
    far_sent = shift(far, second, 1)
    near = add(near, near_left_sent, near_right_sent, far_sent)
    half = near.shape[0] // 2
    return add(near[:half], shift(near[half:], first, 1))


def spread_along(piece, way, first, second):
    behind, ahead = shift(piece, "x", way), shift(piece, "x", -way)
    opposite = shift(behind, "x", way)
    ring = jnp.concatenate([piece, behind, ahead, opposite])
    across = shift(ring, first, 1)
    return [ring, across, shift(ring, second, 1), shift(across, second, 1)]


def reduce_along(parts, way, first, second):
    ring, across, ring_second, across_second = parts
    ring_sent = shift(ring_second, second, 1)
    across = add(across, shift(across_second, second, 1))
    ring = add(ring, ring_sent, shift(across, first, 1))
    size = ring.shape[0] // 4
    piece, behind, ahead, opposite = split(ring, [size] * 4)
    ahead_sent = shift(ahead, "x", way)
    behind = add(behind, shift(opposite, "x", -way))
    return add(piece, ahead_sent, shift(behind, "x", -way))


def experts(pieces, gate_matrix, up_matrix, down_matrix):
    rows = jnp.concatenate(pieces)
    gate = jnp.dot(rows, gate_matrix, preferred_element_type=F32)
    up = jnp.dot(rows, up_matrix, preferred_element_type=F32)
    hidden = (jax.nn.silu(gate) * up).astype(BF16)
    out = jnp.dot(hidden, down_matrix, preferred_element_type=F32).astype(BF16)
    return split(out, [p.shape[0] for p in pieces])


def slots(ids, keep, expert):
    chosen = (ids == expert) & (keep == 1)
    picked = jnp.any(chosen, axis=1)
    position = jnp.cumsum(picked.astype(jnp.int32)) - 1
    return chosen, picked, position


def body(states, expert_ids, gate_values, keep_mask, w_gate, w_up, w_down):
    tokens = states[0]
    ids, gates, keep = expert_ids[0], gate_values[0], keep_mask[0]
    matrices = (w_gate[0], w_up[0], w_down[0])
    mine = lax.axis_index("yh")
    other = 1 - mine

    def compact(expert):
        _, picked, position = slots(ids, keep, expert)
        table = (position[None] == jnp.arange(CAP, dtype=jnp.int32)[:, None]) & picked[None]
        return jnp.dot(table.astype(BF16), tokens, preferred_element_type=F32).astype(BF16)

    partner_rows = to_partner(compact(other))
    own_rows = compact(mine)

    own_a, own_b = split(own_rows, [PIECE] * 2)
    partner_a, partner_b = split(partner_rows, [PIECE] * 2)

    b_parts = spread_along(own_b, 1, "zl", "yl")
    a_parts = spread_across(own_a, "yl", "zl")
    d_parts = spread_along(partner_b, -1, "yl", "zl")
    c_parts = spread_across(partner_a, "zl", "yl")

    a_out = experts(a_parts, *matrices)
    bd_out = experts(b_parts[:2] + d_parts[:2], *matrices)
    b2d2_out = experts(b_parts[2:] + d_parts[2:], *matrices)
    c_out = experts(c_parts, *matrices)

    a_sum = reduce_across(a_out, "yl", "zl")
    c_sum = reduce_across(c_out, "zl", "yl")
    b_sum = reduce_along(bd_out[:2] + b2d2_out[:2], 1, "zl", "yl")
    d_sum = reduce_along(bd_out[2:] + b2d2_out[2:], -1, "yl", "zl")

    own_done = jnp.concatenate([to_next_section(a_sum), to_next_section(b_sum)])
    other_done = jnp.concatenate(
        [to_next_section_partner(c_sum), to_next_section_partner(d_sum)]
    )

    ids, gates, keep = (to_next_section(v) for v in (ids, gates, keep))

    def contribution(expert, done):
        chosen, picked, position = slots(ids, keep, expert)
        weight = jnp.sum(jnp.where(chosen, gates, 0.0), axis=1)
        table = (position[:, None] == jnp.arange(CAP, dtype=jnp.int32)[None]) & picked[:, None]
        rows = jnp.dot(table.astype(BF16), done, preferred_element_type=F32)
        return weight[:, None] * rows

    mixed = contribution(mine, own_done) + contribution(other, other_done)
    return mixed.astype(BF16)[None]


def solution(mesh):
    shape = (2, 2, 2, 2, 4, 2)
    fine = Mesh(mesh.devices.reshape(shape), ("zh", "core", "yh", "yl", "x", "zl"))
    section, ep = ("zh", "core"), ("yh", "yl", "x", "zl")
    rows = P(section, ep, None)
    columns = P(section, None, ep)
    return jax.shard_map(
        body,
        mesh=fine,
        in_specs=(rows, rows, rows, rows, columns, columns, rows),
        out_specs=rows,
        check_vma=False,
    )
```

time: 646 us -> 480 us (0.74)
  the two profiles are of different devices: /device:TPU:2 before, /device:TPU:0 now
where the time goes in v1:
time: 480 us; the launch traced here: 472 us
  waiting for transfers between devices  319 us (66%)
  starting transfers between devices  68.3 us (14%)
  matrix products  56.1 us (12%)
  local copies, waits for them, and re-layouts  20.9 us (4%)
  other arithmetic  6.02 us (1%)
    ppermute x56, waiting for transfers between devices, shift(): return lax.ppermute(value, axis, [(i, (i + by) % n) for i in range(n)])  309 us
    ppermute x56, starting transfers between devices, shift(): return lax.ppermute(value, axis, [(i, (i + by) % n) for i in range(n)])  61 us
    dot_general x4, matrix products, experts(): out = jnp.dot(hidden, down_matrix, preferred_element_type=F32).astype(BF16)  22.8 us
    unnamed x54, local copies, waits for them, and re-layouts  17.3 us
    dot_general x4, matrix products, experts(): up = jnp.dot(rows, up_matrix, preferred_element_type=F32)  15.2 us
    dot_general x4, matrix products, experts(): gate = jnp.dot(rows, gate_matrix, preferred_element_type=F32)  15 us
  transfers between devices with their start and end apart: 64, of which 30 were waited for; matrix products, arithmetic and copies ran while one was open for 17% of the time, Pallas kernels for 0%

profile of v1, /device:TPU:0, one launch (start us, length us, event | category | flops | bytes accessed | tf_op | source)
XLA Modules:
  0.0 471.7 jit_solution(3280868588119509361)
XLA Ops:
  2.7 2.8 collective-permute-start.21
  5.6 4.0 collective-permute-start.1
  10.6 3.0 collective-permute-start.24
  16.7 5.8 %collective-permute-done.3 = bf16[24,6144]{1,0:T(8,128)(2,1)S(1)} collective-permute-done((bf16[24,6144]{1,0:T(8,128)(2,1)S(1)}, bf16[24,6144]{1,0:T(8,128)(2,1)S(1)}, u32[]{:S(2)}, u32[]{:S(2)}) %collective-permute-start.3) | collective-permute-done | bytes 294944 | tf_op jit(solution)/shard_map/ppermute | solution.py:15
  22.6 3.3 collective-permute-start.6
  29.4 17.5 %collective-permute-done.22 = bf16[24,6144]{1,0:T(8,128)(2,1)S(1)} collective-permute-done((bf16[24,6144]{1,0:T(8,128)(2,1)S(1)}, bf16[24,6144]{1,0:T(8,128)(2,1)S(1)}, u32[]{:S(2)}, u32[]{:S(2)}) %collective-permute-start.22) | collective-permute-done | bytes 294944 | tf_op jit(solution)/shard_map/ppermute | solution.py:15
  53.8 8.7 %collective-permute-done.8 = bf16[48,6144]{1,0:T(8,128)(2,1)S(1)} collective-permute-done((bf16[48,6144]{1,0:T(8,128)(2,1)S(1)}, bf16[48,6144]{1,0:T(8,128)(2,1)S(1)}, u32[]{:S(2)}, u32[]{:S(2)}) %collective-permute-start.8) | collective-permute-done | bytes 589856 | tf_op jit(solution)/shard_map/ppermute | solution.py:15
  62.4 4.0 collective-permute-done.7
  68.2 8.9 %collective-permute-done.9 = bf16[48,6144]{1,0:T(8,128)(2,1)S(1)} collective-permute-done((bf16[48,6144]{1,0:T(8,128)(2,1)S(1)}, bf16[48,6144]{1,0:T(8,128)(2,1)S(1)}, u32[]{:S(2)}, u32[]{:S(2)}) %collective-permute-start.9) | collective-permute-done | bytes 589856 | tf_op jit(solution)/shard_map/ppermute | solution.py:15
  80.5 2.7 collective-permute-start.25
  85.6 4.4 collective-permute-done.40
  97.5 5.0 %fusion.10 = f32[384,512]{1,0:T(8,128)S(1)} fusion(bf16[384,6144]{1,0:T(8,128)(2,1)S(1)} %constant_dynamic-update-slice_fusion, bf16[1,6144,512]{2,1,0:T(8,128)(2,1)} %param.12), kind=kOutput, calls=%fused_computation.16 | convolution fusion | flops 2415919104 | bytes 11796480 | tf_op jit(solution)/shard_map/dot_general | solution.py:94
  102.6 2.7 fusion.18
  105.3 5.7 %convolution_convert_fusion.3 = bf16[384,6144]{1,0:T(8,128)(2,1)S(1)} fusion(bf16[1,512,6144]{2,1,0:T(8,128)(2,1)} %param.13, f32[384,512]{1,0:T(8,128)S(1)} %fusion.10, f32[384,512]{1,0:T(8,128)S(1)} %fusion.18), kind=kOutput, calls=%fused_computation.3 | convolution fusion | flops 2419458048 | bytes 12582912 | tf_op jit(solution)/shard_map/dot_general | solution.py:96
  111.5 9.2 %collective-permute-done.41 = bf16[48,6144]{1,0:T(8,128)(2,1)S(1)} collective-permute-done((bf16[48,6144]{1,0:T(8,128)(2,1)S(1)}, bf16[48,6144]{1,0:T(8,128)(2,1)S(1)}, u32[]{:S(2)}, u32[]{:S(2)}) %collective-permute-start.41) | collective-permute-done | bytes 589856 | tf_op jit(solution)/shard_map/ppermute | solution.py:15
  121.6 3.2 collective-permute-start.14
  128.1 10.1 %collective-permute-done.15 = bf16[48,6144]{1,0:T(8,128)(2,1)S(1)} collective-permute-done((bf16[48,6144]{1,0:T(8,128)(2,1)S(1)}, bf16[48,6144]{1,0:T(8,128)(2,1)S(1)}, u32[]{:S(2)}, u32[]{:S(2)}) %collective-permute-start.15) | collective-permute-done | bytes 589856 | tf_op jit(solution)/shard_map/ppermute | solution.py:15
  140.4 17.6 %collective-permute-done.44 = bf16[48,6144]{1,0:T(8,128)(2,1)S(1)} collective-permute-done((bf16[48,6144]{1,0:T(8,128)(2,1)S(1)}, bf16[48,6144]{1,0:T(8,128)(2,1)S(1)}, u32[]{:S(2)}, u32[]{:S(2)}) %collective-permute-start.44) | collective-permute-done | bytes 589856 | tf_op jit(solution)/shard_map/ppermute | solution.py:15
  159.0 9.0 %collective-permute-done.45 = bf16[48,6144]{1,0:T(8,128)(2,1)S(1)} collective-permute-done((bf16[48,6144]{1,0:T(8,128)(2,1)S(1)}, bf16[48,6144]{1,0:T(8,128)(2,1)S(1)}, u32[]{:S(2)}, u32[]{:S(2)}) %collective-permute-start.45) | collective-permute-done | bytes 589856 | tf_op jit(solution)/shard_map/ppermute | solution.py:15
  168.9 13.9 %collective-permute-done.46 = bf16[48,6144]{1,0:T(8,128)(2,1)S(1)} collective-permute-done((bf16[48,6144]{1,0:T(8,128)(2,1)S(1)}, bf16[48,6144]{1,0:T(8,128)(2,1)S(1)}, u32[]{:S(2)}, u32[]{:S(2)}) %collective-permute-start.46) | collective-permute-done | bytes 589856 | tf_op jit(solution)/shard_map/ppermute | solution.py:15
  183.7 3.2 collective-permute-start.12
  186.9 7.0 %collective-permute-done.16 = bf16[48,6144]{1,0:T(8,128)(2,1)S(1)} collective-permute-done((bf16[48,6144]{1,0:T(8,128)(2,1)S(1)}, bf16[48,6144]{1,0:T(8,128)(2,1)S(1)}, u32[]{:S(2)}, u32[]{:S(2)}) %collective-permute-start.16) | collective-permute-done | bytes 589856 | tf_op jit(solution)/shard_map/ppermute | solution.py:15
  196.3 2.7 fusion.8
  198.9 4.8 %fusion.16 = f32[384,512]{1,0:T(8,128)S(1)} fusion(bf16[384,6144]{1,0:T(8,128)(2,1)S(1)} %constant_dynamic-update-slice_fusion.9, bf16[1,6144,512]{2,1,0:T(8,128)(2,1)} %param.11), kind=kOutput, calls=%fused_computation.22 | convolution fusion | flops 2415919104 | bytes 11796480 | tf_op jit(solution)/shard_map/dot_general | solution.py:93
  204.5 5.8 %convolution_convert_fusion.2 = bf16[384,6144]{1,0:T(8,128)(2,1)S(1)} fusion(bf16[1,512,6144]{2,1,0:T(8,128)(2,1)} %param.13, f32[384,512]{1,0:T(8,128)S(1)} %fusion.8, f32[384,512]{1,0:T(8,128)S(1)} %fusion.16), kind=kOutput, calls=%fused_computation.2 | convolution fusion | flops 2419458048 | bytes 12582912 | tf_op jit(solution)/shard_map/dot_general | solution.py:96
  210.4 4.9 %fusion.4 = f32[384,512]{1,0:T(8,128)S(1)} fusion(bf16[384,6144]{1,0:T(8,128)(2,1)S(1)} %constant_dynamic-update-slice_fusion.23, bf16[1,6144,512]{2,1,0:T(8,128)(2,1)} %param.12), kind=kOutput, calls=%fused_computation.10 | convolution fusion | flops 2415919104 | bytes 11796480 | tf_op jit(solution)/shard_map/dot_general | solution.py:94
  215.2 4.9 %fusion.12 = f32[384,512]{1,0:T(8,128)S(1)} fusion(bf16[384,6144]{1,0:T(8,128)(2,1)S(1)} %constant_dynamic-update-slice_fusion.23, bf16[1,6144,512]{2,1,0:T(8,128)(2,1)} %param.11), kind=kOutput, calls=%fused_computation.18 | convolution fusion | flops 2415919104 | bytes 11796480 | tf_op jit(solution)/shard_map/dot_general | solution.py:93
  220.1 5.7 %convolution_convert_fusion = bf16[384,6144]{1,0:T(8,128)(2,1)S(1)} fusion(bf16[1,512,6144]{2,1,0:T(8,128)(2,1)} %param.13, f32[384,512]{1,0:T(8,128)S(1)} %fusion.4, f32[384,512]{1,0:T(8,128)S(1)} %fusion.12), kind=kOutput, calls=%fused_computation | convolution fusion | flops 2419458048 | bytes 12582912 | tf_op jit(solution)/shard_map/dot_general | solution.py:96
  228.3 2.1 collective-permute-start.52
  235.1 5.2 %collective-permute-done.48 = bf16[48,6144]{1,0:T(8,128)(2,1)S(1)} collective-permute-done((bf16[48,6144]{1,0:T(8,128)(2,1)S(1)}, bf16[48,6144]{1,0:T(8,128)(2,1)S(1)}, u32[]{:S(2)}, u32[]{:S(2)}) %collective-permute-start.48) | collective-permute-done | bytes 589856 | tf_op jit(solution)/shard_map/ppermute | solution.py:15
  244.2 2.7 fusion.6
  246.9 2.7 fusion.14
  249.6 5.7 %convolution_convert_fusion.1 = bf16[384,6144]{1,0:T(8,128)(2,1)S(1)} fusion(bf16[1,512,6144]{2,1,0:T(8,128)(2,1)} %param.13, f32[384,512]{1,0:T(8,128)S(1)} %fusion.6, f32[384,512]{1,0:T(8,128)S(1)} %fusion.14), kind=kOutput, calls=%fused_computation.1 | convolution fusion | flops 2419458048 | bytes 12582912 | tf_op jit(solution)/shard_map/dot_general | solution.py:96
  258.9 2.2 collective-permute-start.58
  261.3 47.8 %collective-permute-done.58 = bf16[96,6144]{1,0:T(8,128)(2,1)S(1)} collective-permute-done((bf16[96,6144]{1,0:T(8,128)(2,1)S(1)}, bf16[96,6144]{1,0:T(8,128)(2,1)S(1)}, u32[]{:S(2)}, u32[]{:S(2)}) %collective-permute-start.58) | collective-permute-done | bytes 1179680 | tf_op jit(solution)/shard_map/ppermute | solution.py:15
  309.4 2.1 collective-permute-start.34
  311.6 13.7 %collective-permute-done.54 = bf16[48,6144]{1,0:T(8,128)(2,1)S(1)} collective-permute-done((bf16[48,6144]{1,0:T(8,128)(2,1)S(1)}, bf16[48,6144]{1,0:T(8,128)(2,1)S(1)}, u32[]{:S(2)}, u32[]{:S(2)}) %collective-permute-start.54) | collective-permute-done | bytes 589856 | tf_op jit(solution)/shard_map/ppermute | solution.py:15
  325.6 2.2 collective-permute-start.55
  327.9 22.7 %collective-permute-done.34 = bf16[96,6144]{1,0:T(8,128)(2,1)S(1)} collective-permute-done((bf16[96,6144]{1,0:T(8,128)(2,1)S(1)}, bf16[96,6144]{1,0:T(8,128)(2,1)S(1)}, u32[]{:S(2)}, u32[]{:S(2)}) %collective-permute-start.34) | collective-permute-done | bytes 1179680 | tf_op jit(solution)/shard_map/ppermute | solution.py:15
  350.6 50.3 %collective-permute-done.59 = bf16[96,6144]{1,0:T(8,128)(2,1)S(1)} collective-permute-done((bf16[96,6144]{1,0:T(8,128)(2,1)S(1)}, bf16[96,6144]{1,0:T(8,128)(2,1)S(1)}, u32[]{:S(2)}, u32[]{:S(2)}) %collective-permute-start.59) | collective-permute-done | bytes 1179680 | tf_op jit(solution)/shard_map/ppermute | solution.py:15
  403.6 29.1 %collective-permute-done.35 = bf16[96,6144]{1,0:T(8,128)(2,1)S(1)} collective-permute-done((bf16[96,6144]{1,0:T(8,128)(2,1)S(1)}, bf16[96,6144]{1,0:T(8,128)(2,1)S(1)}, u32[]{:S(2)}, u32[]{:S(2)}) %collective-permute-start.35) | collective-permute-done | bytes 1179680 | tf_op jit(solution)/shard_map/ppermute | solution.py:15
  433.3 2.4 collective-permute-start.37
  437.8 5.5 %collective-permute-done.37 = bf16[24,6144]{1,0:T(8,128)(2,1)S(1)} collective-permute-done((bf16[24,6144]{1,0:T(8,128)(2,1)S(1)}, bf16[24,6144]{1,0:T(8,128)(2,1)S(1)}, u32[]{:S(2)}, u32[]{:S(2)}) %collective-permute-start.37) | collective-permute-done | bytes 294944 | tf_op jit(solution)/shard_map/ppermute | solution.py:15
  443.4 2.2 collective-permute-done.61
  447.0 4.5 collective-permute-done.36
  451.7 2.3 collective-permute-done.38
  454.2 5.6 %collective-permute-done.62 = bf16[24,6144]{1,0:T(8,128)(2,1)S(1)} collective-permute-done((bf16[24,6144]{1,0:T(8,128)(2,1)S(1)}, bf16[24,6144]{1,0:T(8,128)(2,1)S(1)}, u32[]{:S(2)}, u32[]{:S(2)}) %collective-permute-start.62) | collective-permute-done | bytes 294944 | tf_op jit(solution)/shard_map/ppermute | solution.py:15
  462.4 7.3 %collective-permute-done.63 = bf16[24,6144]{1,0:T(8,128)(2,1)S(1)} collective-permute-done((bf16[24,6144]{1,0:T(8,128)(2,1)S(1)}, bf16[24,6144]{1,0:T(8,128)(2,1)S(1)}, u32[]{:S(2)}, u32[]{:S(2)}) %collective-permute-start.63) | collective-permute-done | bytes 294944 | tf_op jit(solution)/shard_map/ppermute | solution.py:28
  (208 shorter events, 72.1 us)
Async XLA Ops:
  2.7 25.9 %collective-permute-start.21 = (bf16[24,6144]{1,0:T(8,128)(2,1)S(1)}, bf16[24,6144]{1,0:T(8,128)(2,1)S(1)}, u32[]{:S(2)}, u32[]{:S(2)}) collective-permute-start(bf16[24,6144]{1,0:T(8,128)(2,1)S(1)} %get-tuple-element.41), channel_id=1, source_target_pairs={{0,6},{2,0},{4,2},{6,4},{1,7},{3,1},{5,3},{7,5},{8,14},{10,8},{12,... | collective-permute-start | bytes 884744 | tf_op jit(solution)/shard_map/ppermute | solution.py:15
  5.6 21.1 %collective-permute-start.20 = (bf16[24,6144]{1,0:T(8,128)(2,1)S(1)}, bf16[24,6144]{1,0:T(8,128)(2,1)S(1)}, u32[]{:S(2)}, u32[]{:S(2)}) collective-permute-start(bf16[24,6144]{1,0:T(8,128)(2,1)S(1)} %get-tuple-element.41), channel_id=1, source_target_pairs={{0,2},{2,4},{4,6},{6,0},{1,3},{3,5},{5,7},{7,1},{8,10},{10,12},{12... | collective-permute-start | bytes 884744 | tf_op jit(solution)/shard_map/ppermute | solution.py:15
  10.6 68.5 %collective-permute-start.24 = (bf16[48,6144]{1,0:T(8,128)(2,1)S(1)}, bf16[48,6144]{1,0:T(8,128)(2,1)S(1)}, u32[]{:S(2)}, u32[]{:S(2)}) collective-permute-start(bf16[48,6144]{1,0:T(8,128)(2,1)S(1)} %convolution_convert_fusion.4), channel_id=1, source_target_pairs={{0,24},{8,16},{16,8},{24,0},{1,25},{9,17},{17,9},{25,1},{2,26},{10... | collective-permute-start | bytes 1769480 | tf_op jit(solution)/shard_map/ppermute | solution.py:19
  22.6 28.3 %collective-permute-start.6 = (bf16[48,6144]{1,0:T(8,128)(2,1)S(1)}, bf16[48,6144]{1,0:T(8,128)(2,1)S(1)}, u32[]{:S(2)}, u32[]{:S(2)}) collective-permute-start(bf16[48,6144]{1,0:T(8,128)(2,1)S(1)} %pad_maximum_fusion.2), channel_id=1, source_target_pairs={{0,6},{2,0},{4,2},{6,4},{1,7},{3,1},{5,3},{7,5},{8,14},{10,8},{12,... | collective-permute-start | bytes 1769480 | tf_op jit(solution)/shard_map/ppermute | solution.py:15
  25.9 24.1 %collective-permute-start.5 = (bf16[48,6144]{1,0:T(8,128)(2,1)S(1)}, bf16[48,6144]{1,0:T(8,128)(2,1)S(1)}, u32[]{:S(2)}, u32[]{:S(2)}) collective-permute-start(bf16[48,6144]{1,0:T(8,128)(2,1)S(1)} %pad_maximum_fusion.2), channel_id=1, source_target_pairs={{0,2},{2,4},{4,6},{6,0},{1,3},{3,5},{5,7},{7,1},{8,10},{10,12},{12... | collective-permute-start | bytes 1769480 | tf_op jit(solution)/shard_map/ppermute | solution.py:15
  26.7 21.1 %collective-permute-start.4 = (bf16[48,6144]{1,0:T(8,128)(2,1)S(1)}, bf16[48,6144]{1,0:T(8,128)(2,1)S(1)}, u32[]{:S(2)}, u32[]{:S(2)}) collective-permute-start(bf16[48,6144]{1,0:T(8,128)(2,1)S(1)} %pad_maximum_fusion.2), channel_id=1, source_target_pairs={{0,1},{1,0},{2,3},{3,2},{4,5},{5,4},{6,7},{7,6},{8,9},{9,8},{10,11... | collective-permute-start | bytes 1769480 | tf_op jit(solution)/shard_map/ppermute | solution.py:15
  28.6 18.2 %collective-permute-start.22 = (bf16[24,6144]{1,0:T(8,128)(2,1)S(1)}, bf16[24,6144]{1,0:T(8,128)(2,1)S(1)}, u32[]{:S(2)}, u32[]{:S(2)}) collective-permute-start(bf16[24,6144]{1,0:T(8,128)(2,1)S(1)} %collective-permute-done.20), channel_id=1, source_target_pairs={{0,2},{2,4},{4,6},{6,0},{1,3},{3,5},{5,7},{7,1},{8,10},{10,12},{12... | collective-permute-start | bytes 884744 | tf_op jit(solution)/shard_map/ppermute | solution.py:15
  47.0 36.8 %collective-permute-start.29 = (bf16[96,6144]{1,0:T(8,128)(2,1)S(1)}, bf16[96,6144]{1,0:T(8,128)(2,1)S(1)}, u32[]{:S(2)}, u32[]{:S(2)}) collective-permute-start(bf16[96,6144]{1,0:T(8,128)(2,1)S(1)} %pad_maximum_fusion), channel_id=1, source_target_pairs={{0,8},{8,0},{1,9},{9,1},{2,10},{10,2},{3,11},{11,3},{4,12},{12,4},... | collective-permute-start | bytes 3538952 | tf_op jit(solution)/shard_map/ppermute | solution.py:15
  47.8 30.2 %collective-permute-start.23 = (bf16[96,6144]{1,0:T(8,128)(2,1)S(1)}, bf16[96,6144]{1,0:T(8,128)(2,1)S(1)}, u32[]{:S(2)}, u32[]{:S(2)}) collective-permute-start(bf16[96,6144]{1,0:T(8,128)(2,1)S(1)} %pad_maximum_fusion), channel_id=1, source_target_pairs={{0,1},{1,0},{2,3},{3,2},{4,5},{5,4},{6,7},{7,6},{8,9},{9,8},{10,11... | collective-permute-start | bytes 3538952 | tf_op jit(solution)/shard_map/ppermute | solution.py:15
  50.0 12.4 %collective-permute-start.8 = (bf16[48,6144]{1,0:T(8,128)(2,1)S(1)}, bf16[48,6144]{1,0:T(8,128)(2,1)S(1)}, u32[]{:S(2)}, u32[]{:S(2)}) collective-permute-start(bf16[48,6144]{1,0:T(8,128)(2,1)S(1)} %collective-permute-done.4), channel_id=1, source_target_pairs={{0,6},{2,0},{4,2},{6,4},{1,7},{3,1},{5,3},{7,5},{8,14},{10,8},{12,... | collective-permute-start | bytes 1769480 | tf_op jit(solution)/shard_map/ppermute | solution.py:15
  50.9 15.6 %collective-permute-start.7 = (bf16[48,6144]{1,0:T(8,128)(2,1)S(1)}, bf16[48,6144]{1,0:T(8,128)(2,1)S(1)}, u32[]{:S(2)}, u32[]{:S(2)}) collective-permute-start(bf16[48,6144]{1,0:T(8,128)(2,1)S(1)} %collective-permute-done.4), channel_id=1, source_target_pairs={{0,2},{2,4},{4,6},{6,0},{1,3},{3,5},{5,7},{7,1},{8,10},{10,12},{12... | collective-permute-start | bytes 1769480 | tf_op jit(solution)/shard_map/ppermute | solution.py:15
  62.4 14.7 %collective-permute-start.9 = (bf16[48,6144]{1,0:T(8,128)(2,1)S(1)}, bf16[48,6144]{1,0:T(8,128)(2,1)S(1)}, u32[]{:S(2)}, u32[]{:S(2)}) collective-permute-start(bf16[48,6144]{1,0:T(8,128)(2,1)S(1)} %collective-permute-done.5), channel_id=1, source_target_pairs={{0,2},{2,4},{4,6},{6,0},{1,3},{3,5},{5,7},{7,1},{8,10},{10,12},{12... | collective-permute-start | bytes 1769480 | tf_op jit(solution)/shard_map/ppermute | solution.py:15
  66.5 29.6 %collective-permute-start.10 = (bf16[48,6144]{1,0:T(8,128)(2,1)S(1)}, bf16[48,6144]{1,0:T(8,128)(2,1)S(1)}, u32[]{:S(2)}, u32[]{:S(2)}) collective-permute-start(bf16[48,6144]{1,0:T(8,128)(2,1)S(1)} %collective-permute-done.8), channel_id=1, source_target_pairs={{0,6},{2,0},{4,2},{6,4},{1,7},{3,1},{5,3},{7,5},{8,14},{10,8},{12,... | collective-permute-start | bytes 1769480 | tf_op jit(solution)/shard_map/ppermute | solution.py:15
  80.0 13.6 %collective-permute-start.26 = (bf16[24,6144]{1,0:T(8,128)(2,1)S(1)}, bf16[24,6144]{1,0:T(8,128)(2,1)S(1)}, u32[]{:S(2)}, u32[]{:S(2)}) collective-permute-start(bf16[24,6144]{1,0:T(8,128)(2,1)S(1)} %get-tuple-element.37), channel_id=1, source_target_pairs={{0,2},{2,4},{4,6},{6,0},{1,3},{3,5},{5,7},{7,1},{8,10},{10,12},{12... | collective-permute-start | bytes 884744 | tf_op jit(solution)/shard_map/ppermute | solution.py:15
  83.7 56.5 %collective-permute-start.30 = (bf16[96,6144]{1,0:T(8,128)(2,1)S(1)}, bf16[96,6144]{1,0:T(8,128)(2,1)S(1)}, u32[]{:S(2)}, u32[]{:S(2)}) collective-permute-start(bf16[96,6144]{1,0:T(8,128)(2,1)S(1)} %collective-permute-done.23), channel_id=1, source_target_pairs={{0,8},{8,0},{1,9},{9,1},{2,10},{10,2},{3,11},{11,3},{4,12},{12,4},... | collective-permute-start | bytes 3538952 | tf_op jit(solution)/shard_map/ppermute | solution.py:15
  90.0 35.7 %collective-permute-start.43 = (bf16[48,6144]{1,0:T(8,128)(2,1)S(1)}, bf16[48,6144]{1,0:T(8,128)(2,1)S(1)}, u32[]{:S(2)}, u32[]{:S(2)}) collective-permute-start(bf16[48,6144]{1,0:T(8,128)(2,1)S(1)} %pad_maximum_fusion.3), channel_id=1, source_target_pairs={{0,6},{2,0},{4,2},{6,4},{1,7},{3,1},{5,3},{7,5},{8,14},{10,8},{12,... | collective-permute-start | bytes 1769480 | tf_op jit(solution)/shard_map/ppermute | solution.py:15
  90.9 30.8 %collective-permute-start.42 = (bf16[48,6144]{1,0:T(8,128)(2,1)S(1)}, bf16[48,6144]{1,0:T(8,128)(2,1)S(1)}, u32[]{:S(2)}, u32[]{:S(2)}) collective-permute-start(bf16[48,6144]{1,0:T(8,128)(2,1)S(1)} %pad_maximum_fusion.3), channel_id=1, source_target_pairs={{0,2},{2,4},{4,6},{6,0},{1,3},{3,5},{5,7},{7,1},{8,10},{10,12},{12... | collective-permute-start | bytes 1769480 | tf_op jit(solution)/shard_map/ppermute | solution.py:15
  93.6 27.2 %collective-permute-start.41 = (bf16[48,6144]{1,0:T(8,128)(2,1)S(1)}, bf16[48,6144]{1,0:T(8,128)(2,1)S(1)}, u32[]{:S(2)}, u32[]{:S(2)}) collective-permute-start(bf16[48,6144]{1,0:T(8,128)(2,1)S(1)} %pad_maximum_fusion.3), channel_id=1, source_target_pairs={{0,8},{8,0},{1,9},{9,1},{2,10},{10,2},{3,11},{11,3},{4,12},{12,4},... | collective-permute-start | bytes 1769480 | tf_op jit(solution)/shard_map/ppermute | solution.py:15
  96.1 15.1 %collective-permute-start.27 = (bf16[24,6144]{1,0:T(8,128)(2,1)S(1)}, bf16[24,6144]{1,0:T(8,128)(2,1)S(1)}, u32[]{:S(2)}, u32[]{:S(2)}) collective-permute-start(bf16[24,6144]{1,0:T(8,128)(2,1)S(1)} %collective-permute-done.25), channel_id=1, source_target_pairs={{0,6},{2,0},{4,2},{6,4},{1,7},{3,1},{5,3},{7,5},{8,14},{10,8},{12,... | collective-permute-start | bytes 884744 | tf_op jit(solution)/shard_map/ppermute | solution.py:15
  111.2 15.4 %collective-permute-start.11 = (bf16[48,6144]{1,0:T(8,128)(2,1)S(1)}, bf16[48,6144]{1,0:T(8,128)(2,1)S(1)}, u32[]{:S(2)}, u32[]{:S(2)}) collective-permute-start(bf16[48,6144]{1,0:T(8,128)(2,1)S(1)} %get-tuple-element.26), channel_id=1, source_target_pairs={{0,6},{2,0},{4,2},{6,4},{1,7},{3,1},{5,3},{7,5},{8,14},{10,8},{12,... | collective-permute-start | bytes 1769480 | tf_op jit(solution)/shard_map/ppermute | solution.py:15
  120.8 17.5 %collective-permute-start.15 = (bf16[48,6144]{1,0:T(8,128)(2,1)S(1)}, bf16[48,6144]{1,0:T(8,128)(2,1)S(1)}, u32[]{:S(2)}, u32[]{:S(2)}) collective-permute-start(bf16[48,6144]{1,0:T(8,128)(2,1)S(1)} %get-tuple-element.27), channel_id=1, source_target_pairs={{0,2},{2,4},{4,6},{6,0},{1,3},{3,5},{5,7},{7,1},{8,10},{10,12},{12... | collective-permute-start | bytes 1769480 | tf_op jit(solution)/shard_map/ppermute | solution.py:15
  121.6 62.0 %collective-permute-start.14 = (bf16[48,6144]{1,0:T(8,128)(2,1)S(1)}, bf16[48,6144]{1,0:T(8,128)(2,1)S(1)}, u32[]{:S(2)}, u32[]{:S(2)}) collective-permute-start(bf16[48,6144]{1,0:T(8,128)(2,1)S(1)} %get-tuple-element.28), channel_id=1, source_target_pairs={{0,6},{2,0},{4,2},{6,4},{1,7},{3,1},{5,3},{7,5},{8,14},{10,8},{12,... | collective-permute-start | bytes 1769480 | tf_op jit(solution)/shard_map/ppermute | solution.py:15
  125.7 100.1 %collective-permute-start.13 = (bf16[48,6144]{1,0:T(8,128)(2,1)S(1)}, bf16[48,6144]{1,0:T(8,128)(2,1)S(1)}, u32[]{:S(2)}, u32[]{:S(2)}) collective-permute-start(bf16[48,6144]{1,0:T(8,128)(2,1)S(1)} %get-tuple-element.29), channel_id=1, source_target_pairs={{0,2},{2,4},{4,6},{6,0},{1,3},{3,5},{5,7},{7,1},{8,10},{10,12},{12... | collective-permute-start | bytes 1769480 | tf_op jit(solution)/shard_map/ppermute | solution.py:15
  126.6 77.2 %collective-permute-start.31 = (bf16[96,6144]{1,0:T(8,128)(2,1)S(1)}, bf16[96,6144]{1,0:T(8,128)(2,1)S(1)}, u32[]{:S(2)}, u32[]{:S(2)}) collective-permute-start(bf16[96,6144]{1,0:T(8,128)(2,1)S(1)} %pad_maximum_fusion.1), channel_id=1, source_target_pairs={{0,1},{1,0},{2,3},{3,2},{4,5},{5,4},{6,7},{7,6},{8,9},{9,8},{10,11... | collective-permute-start | bytes 3538952 | tf_op jit(solution)/shard_map/ppermute | solution.py:15
  138.2 55.9 %collective-permute-start.28 = (bf16[96,6144]{1,0:T(8,128)(2,1)S(1)}, bf16[96,6144]{1,0:T(8,128)(2,1)S(1)}, u32[]{:S(2)}, u32[]{:S(2)}) collective-permute-start(bf16[96,6144]{1,0:T(8,128)(2,1)S(1)} %pad_maximum_fusion.1), channel_id=1, source_target_pairs={{0,8},{8,0},{1,9},{9,1},{2,10},{10,2},{3,11},{11,3},{4,12},{12,4},... | collective-permute-start | bytes 3538952 | tf_op jit(solution)/shard_map/ppermute | solution.py:15
  140.3 17.8 %collective-permute-start.44 = (bf16[48,6144]{1,0:T(8,128)(2,1)S(1)}, bf16[48,6144]{1,0:T(8,128)(2,1)S(1)}, u32[]{:S(2)}, u32[]{:S(2)}) collective-permute-start(bf16[48,6144]{1,0:T(8,128)(2,1)S(1)} %collective-permute-done.41), channel_id=1, source_target_pairs={{0,2},{2,4},{4,6},{6,0},{1,3},{3,5},{5,7},{7,1},{8,10},{10,12},{12... | collective-permute-start | bytes 1769480 | tf_op jit(solution)/shard_map/ppermute | solution.py:15
  167.9 14.9 %collective-permute-start.46 = (bf16[48,6144]{1,0:T(8,128)(2,1)S(1)}, bf16[48,6144]{1,0:T(8,128)(2,1)S(1)}, u32[]{:S(2)}, u32[]{:S(2)}) collective-permute-start(bf16[48,6144]{1,0:T(8,128)(2,1)S(1)} %collective-permute-done.42), channel_id=1, source_target_pairs={{0,2},{2,4},{4,6},{6,0},{1,3},{3,5},{5,7},{7,1},{8,10},{10,12},{12... | collective-permute-start | bytes 1769480 | tf_op jit(solution)/shard_map/ppermute | solution.py:15
  183.7 42.1 %collective-permute-start.12 = (bf16[48,6144]{1,0:T(8,128)(2,1)S(1)}, bf16[48,6144]{1,0:T(8,128)(2,1)S(1)}, u32[]{:S(2)}, u32[]{:S(2)}) collective-permute-start(bf16[48,6144]{1,0:T(8,128)(2,1)S(1)} %get-tuple-element.24), channel_id=1, source_target_pairs={{0,6},{2,0},{4,2},{6,4},{1,7},{3,1},{5,3},{7,5},{8,14},{10,8},{12,... | collective-permute-start | bytes 1769480 | tf_op jit(solution)/shard_map/ppermute | solution.py:15
  193.9 16.4 %collective-permute-start.47 = (bf16[48,6144]{1,0:T(8,128)(2,1)S(1)}, bf16[48,6144]{1,0:T(8,128)(2,1)S(1)}, u32[]{:S(2)}, u32[]{:S(2)}) collective-permute-start(bf16[48,6144]{1,0:T(8,128)(2,1)S(1)} %collective-permute-done.45), channel_id=1, source_target_pairs={{0,6},{2,0},{4,2},{6,4},{1,7},{3,1},{5,3},{7,5},{8,14},{10,8},{12,... | collective-permute-start | bytes 1769480 | tf_op jit(solution)/shard_map/ppermute | solution.py:15
  194.1 31.7 %collective-permute-start.17 = (bf16[48,6144]{1,0:T(8,128)(2,1)S(1)}, bf16[48,6144]{1,0:T(8,128)(2,1)S(1)}, u32[]{:S(2)}, u32[]{:S(2)}) collective-permute-start(bf16[48,6144]{1,0:T(8,128)(2,1)S(1)} %add_convert_fusion.10), channel_id=1, source_target_pairs={{0,1},{1,0},{2,3},{3,2},{4,5},{5,4},{6,7},{7,6},{8,9},{9,8},{10,11... | collective-permute-start | bytes 1769480 | tf_op jit(solution)/shard_map/ppermute | solution.py:15
  203.8 39.2 %collective-permute-start.32 = (bf16[96,6144]{1,0:T(8,128)(2,1)S(1)}, bf16[96,6144]{1,0:T(8,128)(2,1)S(1)}, u32[]{:S(2)}, u32[]{:S(2)}) collective-permute-start(bf16[96,6144]{1,0:T(8,128)(2,1)S(1)} %collective-permute-done.28), channel_id=1, source_target_pairs={{0,1},{1,0},{2,3},{3,2},{4,5},{5,4},{6,7},{7,6},{8,9},{9,8},{10,11... | collective-permute-start | bytes 3538952 | tf_op jit(solution)/shard_map/ppermute | solution.py:15
  228.2 12.1 %collective-permute-start.48 = (bf16[48,6144]{1,0:T(8,128)(2,1)S(1)}, bf16[48,6144]{1,0:T(8,128)(2,1)S(1)}, u32[]{:S(2)}, u32[]{:S(2)}) collective-permute-start(bf16[48,6144]{1,0:T(8,128)(2,1)S(1)} %get-tuple-element.14), channel_id=1, source_target_pairs={{0,6},{2,0},{4,2},{6,4},{1,7},{3,1},{5,3},{7,5},{8,14},{10,8},{12,... | collective-permute-start | bytes 1769480 | tf_op jit(solution)/shard_map/ppermute | solution.py:15
  228.3 13.3 %collective-permute-start.52 = (bf16[48,6144]{1,0:T(8,128)(2,1)S(1)}, bf16[48,6144]{1,0:T(8,128)(2,1)S(1)}, u32[]{:S(2)}, u32[]{:S(2)}) collective-permute-start(bf16[48,6144]{1,0:T(8,128)(2,1)S(1)} %get-tuple-element.15), channel_id=1, source_target_pairs={{0,2},{2,4},{4,6},{6,0},{1,3},{3,5},{5,7},{7,1},{8,10},{10,12},{12... | collective-permute-start | bytes 1769480 | tf_op jit(solution)/shard_map/ppermute | solution.py:15
  230.4 25.4 %collective-permute-start.51 = (bf16[48,6144]{1,0:T(8,128)(2,1)S(1)}, bf16[48,6144]{1,0:T(8,128)(2,1)S(1)}, u32[]{:S(2)}, u32[]{:S(2)}) collective-permute-start(bf16[48,6144]{1,0:T(8,128)(2,1)S(1)} %get-tuple-element.16), channel_id=1, source_target_pairs={{0,6},{2,0},{4,2},{6,4},{1,7},{3,1},{5,3},{7,5},{8,14},{10,8},{12,... | collective-permute-start | bytes 1769480 | tf_op jit(solution)/shard_map/ppermute | solution.py:15
  233.0 76.4 %collective-permute-start.50 = (bf16[48,6144]{1,0:T(8,128)(2,1)S(1)}, bf16[48,6144]{1,0:T(8,128)(2,1)S(1)}, u32[]{:S(2)}, u32[]{:S(2)}) collective-permute-start(bf16[48,6144]{1,0:T(8,128)(2,1)S(1)} %get-tuple-element.17), channel_id=1, source_target_pairs={{0,2},{2,4},{4,6},{6,0},{1,3},{3,5},{5,7},{7,1},{8,10},{10,12},{12... | collective-permute-start | bytes 1769480 | tf_op jit(solution)/shard_map/ppermute | solution.py:15
  240.2 219.8 %collective-permute-start.19 = (bf16[24,6144]{1,0:T(8,128)(2,1)S(1)}, bf16[24,6144]{1,0:T(8,128)(2,1)S(1)}, u32[]{:S(2)}, u32[]{:S(2)}) collective-permute-start(bf16[24,6144]{1,0:T(8,128)(2,1)S(1)} %add_convert_fusion.18), channel_id=1, source_target_pairs={{0,32},{32,64},{64,96},{96,0},{1,33},{33,65},{65,97},{97,1},{2,34}... | collective-permute-start | bytes 884744 | tf_op jit(solution)/shard_map/ppermute | solution.py:23
  241.8 69.7 %collective-permute-start.49 = (bf16[48,6144]{1,0:T(8,128)(2,1)S(1)}, bf16[48,6144]{1,0:T(8,128)(2,1)S(1)}, u32[]{:S(2)}, u32[]{:S(2)}) collective-permute-start(bf16[48,6144]{1,0:T(8,128)(2,1)S(1)} %get-tuple-element.12), channel_id=1, source_target_pairs={{0,6},{2,0},{4,2},{6,4},{1,7},{3,1},{5,3},{7,5},{8,14},{10,8},{12,... | collective-permute-start | bytes 1769480 | tf_op jit(solution)/shard_map/ppermute | solution.py:15
  243.0 16.0 %collective-permute-start.53 = (bf16[48,6144]{1,0:T(8,128)(2,1)S(1)}, bf16[48,6144]{1,0:T(8,128)(2,1)S(1)}, u32[]{:S(2)}, u32[]{:S(2)}) collective-permute-start(bf16[48,6144]{1,0:T(8,128)(2,1)S(1)} %get-tuple-element.13), channel_id=1, source_target_pairs={{0,2},{2,4},{4,6},{6,0},{1,3},{3,5},{5,7},{7,1},{8,10},{10,12},{12... | collective-permute-start | bytes 1769480 | tf_op jit(solution)/shard_map/ppermute | solution.py:15
  255.8 69.8 %collective-permute-start.57 = (bf16[96,6144]{1,0:T(8,128)(2,1)S(1)}, bf16[96,6144]{1,0:T(8,128)(2,1)S(1)}, u32[]{:S(2)}, u32[]{:S(2)}) collective-permute-start(bf16[96,6144]{1,0:T(8,128)(2,1)S(1)} %get-tuple-element.20), channel_id=1, source_target_pairs={{0,1},{1,0},{2,3},{3,2},{4,5},{5,4},{6,7},{7,6},{8,9},{9,8},{10,11... | collective-permute-start | bytes 3538952 | tf_op jit(solution)/shard_map/ppermute | solution.py:15
  258.9 50.1 %collective-permute-start.58 = (bf16[96,6144]{1,0:T(8,128)(2,1)S(1)}, bf16[96,6144]{1,0:T(8,128)(2,1)S(1)}, u32[]{:S(2)}, u32[]{:S(2)}) collective-permute-start(bf16[96,6144]{1,0:T(8,128)(2,1)S(1)} %get-tuple-element.21), channel_id=1, source_target_pairs={{0,1},{1,0},{2,3},{3,2},{4,5},{5,4},{6,7},{7,6},{8,9},{9,8},{10,11... | collective-permute-start | bytes 3538952 | tf_op jit(solution)/shard_map/ppermute | solution.py:15
  309.1 16.2 %collective-permute-start.54 = (bf16[48,6144]{1,0:T(8,128)(2,1)S(1)}, bf16[48,6144]{1,0:T(8,128)(2,1)S(1)}, u32[]{:S(2)}, u32[]{:S(2)}) collective-permute-start(bf16[48,6144]{1,0:T(8,128)(2,1)S(1)} %add_convert_fusion.6), channel_id=1, source_target_pairs={{0,8},{8,0},{1,9},{9,1},{2,10},{10,2},{3,11},{11,3},{4,12},{12,4},... | collective-permute-start | bytes 1769480 | tf_op jit(solution)/shard_map/ppermute | solution.py:15
  309.4 41.2 %collective-permute-start.34 = (bf16[96,6144]{1,0:T(8,128)(2,1)S(1)}, bf16[96,6144]{1,0:T(8,128)(2,1)S(1)}, u32[]{:S(2)}, u32[]{:S(2)}) collective-permute-start(bf16[96,6144]{1,0:T(8,128)(2,1)S(1)} %get-tuple-element.22), channel_id=1, source_target_pairs={{0,8},{8,0},{1,9},{9,1},{2,10},{10,2},{3,11},{11,3},{4,12},{12,4},... | collective-permute-start | bytes 3538952 | tf_op jit(solution)/shard_map/ppermute | solution.py:15
  311.5 92.1 %collective-permute-start.33 = (bf16[96,6144]{1,0:T(8,128)(2,1)S(1)}, bf16[96,6144]{1,0:T(8,128)(2,1)S(1)}, u32[]{:S(2)}, u32[]{:S(2)}) collective-permute-start(bf16[96,6144]{1,0:T(8,128)(2,1)S(1)} %get-tuple-element.23), channel_id=1, source_target_pairs={{0,8},{8,0},{1,9},{9,1},{2,10},{10,2},{3,11},{11,3},{4,12},{12,4},... | collective-permute-start | bytes 3538952 | tf_op jit(solution)/shard_map/ppermute | solution.py:15
  325.3 75.6 %collective-permute-start.59 = (bf16[96,6144]{1,0:T(8,128)(2,1)S(1)}, bf16[96,6144]{1,0:T(8,128)(2,1)S(1)}, u32[]{:S(2)}, u32[]{:S(2)}) collective-permute-start(bf16[96,6144]{1,0:T(8,128)(2,1)S(1)} %add_convert_fusion.2), channel_id=1, source_target_pairs={{0,8},{8,0},{1,9},{9,1},{2,10},{10,2},{3,11},{11,3},{4,12},{12,4},... | collective-permute-start | bytes 3538952 | tf_op jit(solution)/shard_map/ppermute | solution.py:15
  325.6 77.9 %collective-permute-start.55 = (bf16[24,6144]{1,0:T(8,128)(2,1)S(1)}, bf16[24,6144]{1,0:T(8,128)(2,1)S(1)}, u32[]{:S(2)}, u32[]{:S(2)}) collective-permute-start(bf16[24,6144]{1,0:T(8,128)(2,1)S(1)} %slice.191), channel_id=1, source_target_pairs={{0,1},{1,0},{2,3},{3,2},{4,5},{5,4},{6,7},{7,6},{8,9},{9,8},{10,11... | collective-permute-start | bytes 884744 | tf_op jit(solution)/shard_map/ppermute | solution.py:15
  401.8 31.0 %collective-permute-start.35 = (bf16[96,6144]{1,0:T(8,128)(2,1)S(1)}, bf16[96,6144]{1,0:T(8,128)(2,1)S(1)}, u32[]{:S(2)}, u32[]{:S(2)}) collective-permute-start(bf16[96,6144]{1,0:T(8,128)(2,1)S(1)} %get-tuple-element.19), channel_id=1, source_target_pairs={{0,1},{1,0},{2,3},{3,2},{4,5},{5,4},{6,7},{7,6},{8,9},{9,8},{10,11... | collective-permute-start | bytes 3538952 | tf_op jit(solution)/shard_map/ppermute | solution.py:15
  403.6 58.9 %collective-permute-start.56 = (bf16[24,6144]{1,0:T(8,128)(2,1)S(1)}, bf16[24,6144]{1,0:T(8,128)(2,1)S(1)}, u32[]{:S(2)}, u32[]{:S(2)}) collective-permute-start(bf16[24,6144]{1,0:T(8,128)(2,1)S(1)} %add_convert_fusion.15), channel_id=1, source_target_pairs={{0,56},{8,48},{16,40},{24,32},{32,88},{40,80},{48,72},{56,64},{64,... | collective-permute-start | bytes 884744 | tf_op jit(solution)/shard_map/ppermute | solution.py:28
  435.7 18.5 %collective-permute-start.60 = (bf16[24,6144]{1,0:T(8,128)(2,1)S(1)}, bf16[24,6144]{1,0:T(8,128)(2,1)S(1)}, u32[]{:S(2)}, u32[]{:S(2)}) collective-permute-start(bf16[24,6144]{1,0:T(8,128)(2,1)S(1)} %get-tuple-element.30), channel_id=1, source_target_pairs={{0,6},{2,0},{4,2},{6,4},{1,7},{3,1},{5,3},{7,5},{8,14},{10,8},{12,... | collective-permute-start | bytes 884744 | tf_op jit(solution)/shard_map/ppermute | solution.py:15
  (31 other events, 383.3 us)

commit v2 on v1

v2 whole, which is shorter than its diff:
```python
import jax
import jax.numpy as jnp
from jax import lax
from jax.sharding import Mesh, PartitionSpec as P

CAP = 48
PIECE = 24
F32 = jnp.float32
BF16 = jnp.bfloat16


def shift(value, axis, by):
    n = lax.axis_size(axis)
    return lax.ppermute(value, axis, [(i, (i + by) % n) for i in range(n)])


def right(value):
    return shift(value, "x", 1)


def left(value):
    return shift(value, "x", -1)


def over_y(value):
    return shift(value, "yl", 1)


def over_z(value):
    return shift(value, "zl", 1)


def to_partner(value):
    return lax.ppermute(value, ("yh", "yl"), [(y, 3 - y) for y in range(4)])


def to_next_section(value):
    return lax.ppermute(value, ("zh", "core"), [(s, (s + 1) % 4) for s in range(4)])


def to_next_section_partner(value):
    pairs = [(s * 4 + y, (s + 1) % 4 * 4 + 3 - y) for s in range(4) for y in range(4)]
    return lax.ppermute(value, ("zh", "core", "yh", "yl"), pairs)


def together(*values):
    return lax.optimization_barrier(values)


def join(*pieces):
    return jnp.concatenate(pieces)


def add(*terms):
    total = terms[0].astype(F32)
    for term in terms[1:]:
        total = total + term.astype(F32)
    return total.astype(BF16)


def split(rows, count):
    size = rows.shape[0] // count
    return [rows[i * size : (i + 1) * size] for i in range(count)]


def experts(pieces, gate_matrix, up_matrix, down_matrix):
    rows = jnp.concatenate(pieces)
    gate = jnp.dot(rows, gate_matrix, preferred_element_type=F32)
    up = jnp.dot(rows, up_matrix, preferred_element_type=F32)
    hidden = (jax.nn.silu(gate) * up).astype(BF16)
    out = jnp.dot(hidden, down_matrix, preferred_element_type=F32).astype(BF16)
    return split(out, len(pieces))


def slots(ids, keep, expert):
    chosen = (ids == expert) & (keep == 1)
    picked = jnp.any(chosen, axis=1)
    position = jnp.cumsum(picked.astype(jnp.int32)) - 1
    return chosen, picked, position


def body(states, expert_ids, gate_values, keep_mask, w_gate, w_up, w_down):
    tokens = states[0]
    ids, gates, keep = expert_ids[0], gate_values[0], keep_mask[0]
    matrices = (w_gate[0], w_up[0], w_down[0])
    mine = lax.axis_index("yh")
    other = 1 - mine

    def compact(expert):
        _, picked, position = slots(ids, keep, expert)
        table = (position[None] == jnp.arange(CAP, dtype=jnp.int32)[:, None]) & picked[None]
        return jnp.dot(table.astype(BF16), tokens, preferred_element_type=F32).astype(BF16)

    partner = to_partner(compact(other))
    own = compact(mine)
    next_ids, next_gates, next_keep = (to_next_section(v) for v in (ids, gates, keep))
    own, partner, ids, gates, keep = together(own, partner, next_ids, next_gates, next_keep)
    (a1, b), (a2, g) = split(own, 2), split(partner, 2)

    b_behind, g_behind, a1_y, a2_z = together(right(b), left(g), over_y(a1), over_z(a2))
    a1_near, a2_near = join(a1, a1_y), join(a2, a2_z)
    from_left, from_right, a1_far, a2_far = together(
        right(join(b_behind, g)), left(join(g_behind, b)), over_z(a1_near), over_y(a2_near)
    )
    b_opposite, g_ahead = split(from_left, 2)
    g_opposite, b_ahead = split(from_right, 2)
    near, far = join(a1_near, a2_near), join(a1_far, a2_far)
    b_ring = join(b, b_behind, b_ahead, b_opposite)
    g_ring = join(g, g_behind, g_ahead, g_opposite)

    near, far, b_ring, g_ring = together(near, far, b_ring, g_ring)
    near_left, far_right, g_y, b_z = right(near), left(far), over_y(g_ring), over_z(b_ring)
    out0 = experts([near, far, b_ring, g_ring], *matrices)
    near_left, far_right, g_y, b_z, b_ring, g_ring, *out0 = together(
        near_left, far_right, g_y, b_z, b_ring, g_ring, *out0
    )

    near_opposite, far_opposite, b_y, g_z = (
        right(near_left), left(far_right), over_y(b_ring), over_z(g_ring)
    )
    out1 = experts([near_left, far_right, g_y, b_z], *matrices)
    near_opposite, far_opposite, b_y, g_z, near, far, b_z, g_y, *out1 = together(
        near_opposite, far_opposite, b_y, g_z, near, far, b_z, g_y, *out1
    )

    near_right, far_left, b_yz, g_zy = left(near), right(far), over_y(b_z), over_z(g_y)
    out2 = experts([near_opposite, far_opposite, b_y, g_z], *matrices)
    near_right, far_left, b_yz, g_zy, *out2 = together(near_right, far_left, b_yz, g_zy, *out2)

    near, far, b_ring, g_ring = out0
    near_left, far_right, g_y, b_z = out1
    near_opposite, far_opposite, b_y, g_z = out2
    got = left(near_opposite), right(far_opposite), over_y(b_y), over_z(g_z)
    out3 = experts([near_right, far_left, b_yz, g_zy], *matrices)
    *got, near_right, far_left, b_yz, g_zy = together(*got, *out3)
    near_left, far_right = add(near_left, got[0]), add(far_right, got[1])
    b_back, g_back = got[2:]

    got = together(left(near_left), right(far_right), over_y(b_yz), over_z(g_zy))
    near_back, far_back = got[:2]
    b_z, g_y = add(b_z, got[2]), add(g_y, got[3])

    got = together(right(near_right), left(far_left), over_y(g_y), over_z(b_z))
    near, far = add(near, near_back, got[0]), add(far, far_back, got[1])
    g_ring, b_ring = add(g_ring, g_back, got[2]), add(b_ring, b_back, got[3])

    (a1_near, a2_near), (a1_far, a2_far) = split(near, 2), split(far, 2)
    b, b_behind, b_ahead, b_opposite = split(b_ring, 4)
    g, g_behind, g_ahead, g_opposite = split(g_ring, 4)
    got = together(
        left(join(b_opposite, g_ahead)), right(join(g_opposite, b_ahead)), over_z(a1_far), over_y(a2_far)
    )
    (b_behind_back, g_back), (g_behind_back, b_back) = split(got[0], 2), split(got[1], 2)
    a1_near, a2_near = add(a1_near, got[2]), add(a2_near, got[3])
    (a1, a1_y), (a2, a2_z) = split(a1_near, 2), split(a2_near, 2)
    got = together(
        left(add(b_behind, b_behind_back)), right(add(g_behind, g_behind_back)), over_y(a1_y), over_z(a2_z)
    )
    own = join(add(a1, got[2]), add(b, b_back, got[0]))
    partner = join(add(a2, got[3]), add(g, g_back, got[1]))

    own_done, other_done = to_next_section(own), to_next_section_partner(partner)

    def contribution(expert, done):
        chosen, picked, position = slots(ids, keep, expert)
        weight = jnp.sum(jnp.where(chosen, gates, 0.0), axis=1)
        table = (position[:, None] == jnp.arange(CAP, dtype=jnp.int32)[None]) & picked[:, None]
        rows = jnp.dot(table.astype(BF16), done, preferred_element_type=F32)
        return weight[:, None] * rows

    mixed = contribution(mine, own_done) + contribution(other, other_done)
    return mixed.astype(BF16)[None]


def solution(mesh):
    shape = (2, 2, 2, 2, 4, 2)
    fine = Mesh(mesh.devices.reshape(shape), ("zh", "core", "yh", "yl", "x", "zl"))
    section, ep = ("zh", "core"), ("yh", "yl", "x", "zl")
    rows = P(section, ep, None)
    columns = P(section, None, ep)
    return jax.shard_map(
        body,
        mesh=fine,
        in_specs=(rows, rows, rows, rows, columns, columns, rows),
        out_specs=rows,
        check_vma=False,
    )
```

time: 480 us -> 283 us (0.59)
  the two profiles are of different devices: /device:TPU:0 before, /device:TPU:112 now
where the time goes in v2:
time: 283 us; the launch traced here: 278 us
  waiting for transfers between devices  160 us (57%)
  matrix products  55.2 us (20%)
  starting transfers between devices  51.2 us (18%)
  other arithmetic  6.3 us (2%)
  local copies, waits for them, and re-layouts  4.19 us (1%)
    ppermute x40, waiting for transfers between devices, shift(): return lax.ppermute(value, axis, [(i, (i + by) % n) for i in range(n)])  132 us
    ppermute x40, starting transfers between devices, shift(): return lax.ppermute(value, axis, [(i, (i + by) % n) for i in range(n)])  49.7 us
    dot_general x4, matrix products, experts(): out = jnp.dot(hidden, down_matrix, preferred_element_type=F32).astype(BF16)  22.5 us
    dot_general x4, matrix products, experts(): up = jnp.dot(rows, up_matrix, preferred_element_type=F32)  18.9 us
    ppermute x1, waiting for transfers between devices, to_partner(): return lax.ppermute(value, ('yh', 'yl'), [(y, 3 - y) for y in range(4)])  11 us
    ppermute x1, waiting for transfers between devices, to_next_section_partner(): return lax.ppermute(value, ('zh', 'core', 'yh', 'yl'), pairs)  10.9 us
    dot_general x4, matrix products, experts(): gate = jnp.dot(rows, gate_matrix, preferred_element_type=F32)  10.6 us
    ppermute x4, waiting for transfers between devices, to_next_section(): lax.ppermute(value, ('zh', 'core'), [(s, (s + 1) % 4) for s in range(4)])  6.69 us
  transfers between devices with their start and end apart: 46, of which 32 were waited for; matrix products, arithmetic and copies ran while one was open for 22% of the time, Pallas kernels for 0%

profile of v2, /device:TPU:112, one launch (start us, length us, event | category | flops | bytes accessed | tf_op | source)
XLA Modules:
  0.0 278.0 jit_solution(1188305989548123639)
XLA Ops:
  5.4 11.0 %collective-permute-done = bf16[48,6144]{1,0:T(8,128)(2,1)S(1)} collective-permute-done((bf16[48,6144]{1,0:T(8,128)(2,1)S(1)}, bf16[48,6144]{1,0:T(8,128)(2,1)S(1)}, u32[]{:S(2)}, u32[]{:S(2)}) %collective-permute-start) | collective-permute-done | bytes 589856 | tf_op jit(solution)/shard_map/ppermute | solution.py:34
  16.4 2.6 collective-permute-start.6
  20.6 1.8 collective-permute-start.5
  22.4 3.1 %collective-permute-done.6 = bf16[24,6144]{1,0:T(8,128)(2,1)S(1)} collective-permute-done((bf16[24,6144]{1,0:T(8,128)(2,1)S(1)}, bf16[24,6144]{1,0:T(8,128)(2,1)S(1)}, u32[]{:S(2)}, u32[]{:S(2)}) %collective-permute-start.6) | collective-permute-done | bytes 294944 | tf_op jit(solution)/shard_map/ppermute | solution.py:14
  25.6 3.9 %collective-permute-done.4 = bf16[24,6144]{1,0:T(8,128)(2,1)S(1)} collective-permute-done((bf16[24,6144]{1,0:T(8,128)(2,1)S(1)}, bf16[24,6144]{1,0:T(8,128)(2,1)S(1)}, u32[]{:S(2)}, u32[]{:S(2)}) %collective-permute-start.4) | collective-permute-done | bytes 294944 | tf_op jit(solution)/shard_map/ppermute | solution.py:14
  30.4 3.0 %collective-permute-start.9 = (bf16[48,6144]{1,0:T(8,128)(2,1)S(1)}, bf16[48,6144]{1,0:T(8,128)(2,1)S(1)}, u32[]{:S(2)}, u32[]{:S(2)}) collective-permute-start(bf16[48,6144]{1,0:T(8,128)(2,1)S(1)} %pad_maximum_fusion.5), channel_id=1, source_target_pairs={{0,6},{2,0},{4,2},{6,4},{1,7},{3,1},{5,3},{7,5},{8,14},{10,8},{12,... | collective-permute-start | bytes 1769480 | tf_op jit(solution)/shard_map/ppermute | solution.py:14
  33.5 2.1 collective-permute-start.10
  35.7 10.7 %collective-permute-done.9 = bf16[48,6144]{1,0:T(8,128)(2,1)S(1)} collective-permute-done((bf16[48,6144]{1,0:T(8,128)(2,1)S(1)}, bf16[48,6144]{1,0:T(8,128)(2,1)S(1)}, u32[]{:S(2)}, u32[]{:S(2)}) %collective-permute-start.9) | collective-permute-done | bytes 589856 | tf_op jit(solution)/shard_map/ppermute | solution.py:14
  46.4 3.4 %collective-permute-done.8 = bf16[48,6144]{1,0:T(8,128)(2,1)S(1)} collective-permute-done((bf16[48,6144]{1,0:T(8,128)(2,1)S(1)}, bf16[48,6144]{1,0:T(8,128)(2,1)S(1)}, u32[]{:S(2)}, u32[]{:S(2)}) %collective-permute-start.8) | collective-permute-done | bytes 589856 | tf_op jit(solution)/shard_map/ppermute | solution.py:14
  50.4 3.3 %collective-permute-start.13 = (bf16[96,6144]{1,0:T(8,128)(2,1)S(1)}, bf16[96,6144]{1,0:T(8,128)(2,1)S(1)}, u32[]{:S(2)}, u32[]{:S(2)}) collective-permute-start(bf16[96,6144]{1,0:T(8,128)(2,1)S(1)} %pad_maximum_fusion.1), channel_id=1, source_target_pairs={{0,6},{2,0},{4,2},{6,4},{1,7},{3,1},{5,3},{7,5},{8,14},{10,8},{12,... | collective-permute-start | bytes 3538952 | tf_op jit(solution)/shard_map/ppermute | solution.py:14
  54.5 1.9 collective-permute-start.15
  56.8 2.7 fusion.21
  59.5 2.6 fusion.46
  62.2 5.6 %convolution_convert_fusion.3 = bf16[384,6144]{1,0:T(8,128)(2,1)S(1)} fusion(bf16[384,512]{1,0:T(8,128)(2,1)S(1)} %fusion.46, bf16[1,512,6144]{2,1,0:T(8,128)(2,1)} %param.13), kind=kOutput, calls=%fused_computation.3 | convolution fusion | flops 2418278400 | bytes 11403264 | tf_op jit(solution)/shard_map/dot_general | solution.py:71
  68.3 10.0 %collective-permute-done.12 = bf16[96,6144]{1,0:T(8,128)(2,1)S(1)} collective-permute-done((bf16[96,6144]{1,0:T(8,128)(2,1)S(1)}, bf16[96,6144]{1,0:T(8,128)(2,1)S(1)}, u32[]{:S(2)}, u32[]{:S(2)}) %collective-permute-start.12) | collective-permute-done | bytes 1179680 | tf_op jit(solution)/shard_map/ppermute | solution.py:14
  84.1 3.2 %collective-permute-start.17 = (bf16[96,6144]{1,0:T(8,128)(2,1)S(1)}, bf16[96,6144]{1,0:T(8,128)(2,1)S(1)}, u32[]{:S(2)}, u32[]{:S(2)}) collective-permute-start(bf16[96,6144]{1,0:T(8,128)(2,1)S(1)} %collective-permute-done.13), channel_id=1, source_target_pairs={{0,6},{2,0},{4,2},{6,4},{1,7},{3,1},{5,3},{7,5},{8,14},{10,8},{12,... | collective-permute-start | bytes 3538952 | tf_op jit(solution)/shard_map/ppermute | solution.py:14
  87.6 2.7 fusion.19
  90.3 5.4 %fusion.43 = bf16[384,512]{1,0:T(8,128)(2,1)S(1)} fusion(bf16[384,6144]{1,0:T(8,128)(2,1)S(1)} %constant_dynamic-update-slice_fusion.4, bf16[1,6144,512]{2,1,0:T(8,128)(2,1)} %param.12, f32[384,512]{1,0:T(8,128)S(1)} %fusion.19), kind=kOutput, calls=%fused_computation.47 | convolution fusion | flops 2417098752 | bytes 12189696 | tf_op jit(solution)/shard_map/dot_general | solution.py:69
  95.7 5.6 %convolution_convert_fusion.2 = bf16[384,6144]{1,0:T(8,128)(2,1)S(1)} fusion(bf16[384,512]{1,0:T(8,128)(2,1)S(1)} %fusion.43, bf16[1,512,6144]{2,1,0:T(8,128)(2,1)} %param.13), kind=kOutput, calls=%fused_computation.2 | convolution fusion | flops 2418278400 | bytes 11403264 | tf_op jit(solution)/shard_map/dot_general | solution.py:71
  101.9 4.1 %collective-permute-done.18 = bf16[96,6144]{1,0:T(8,128)(2,1)S(1)} collective-permute-done((bf16[96,6144]{1,0:T(8,128)(2,1)S(1)}, bf16[96,6144]{1,0:T(8,128)(2,1)S(1)}, u32[]{:S(2)}, u32[]{:S(2)}) %collective-permute-start.18) | collective-permute-done | bytes 1179680 | tf_op jit(solution)/shard_map/ppermute | solution.py:14
  107.5 2.6 collective-permute-done.17
  110.1 3.4 %collective-permute-start.20 = (bf16[96,6144]{1,0:T(8,128)(2,1)S(1)}, bf16[96,6144]{1,0:T(8,128)(2,1)S(1)}, u32[]{:S(2)}, u32[]{:S(2)}) collective-permute-start(bf16[96,6144]{1,0:T(8,128)(2,1)S(1)} %pad_maximum_fusion), channel_id=1, source_target_pairs={{0,6},{2,0},{4,2},{6,4},{1,7},{3,1},{5,3},{7,5},{8,14},{10,8},{12,... | collective-permute-start | bytes 3538952 | tf_op jit(solution)/shard_map/ppermute | solution.py:14
  115.1 2.7 fusion.17
  117.8 5.4 %fusion.40 = bf16[384,512]{1,0:T(8,128)(2,1)S(1)} fusion(bf16[384,6144]{1,0:T(8,128)(2,1)S(1)} %constant_dynamic-update-slice_fusion.8, bf16[1,6144,512]{2,1,0:T(8,128)(2,1)} %param.12, f32[384,512]{1,0:T(8,128)S(1)} %fusion.17), kind=kOutput, calls=%fused_computation.46 | convolution fusion | flops 2417098752 | bytes 12189696 | tf_op jit(solution)/shard_map/dot_general | solution.py:69
  123.3 5.6 %convolution_convert_fusion.1 = bf16[384,6144]{1,0:T(8,128)(2,1)S(1)} fusion(bf16[384,512]{1,0:T(8,128)(2,1)S(1)} %fusion.40, bf16[1,512,6144]{2,1,0:T(8,128)(2,1)} %param.13), kind=kOutput, calls=%fused_computation.1 | convolution fusion | flops 2418278400 | bytes 11403264 | tf_op jit(solution)/shard_map/dot_general | solution.py:71
  129.4 6.4 %collective-permute-done.20 = bf16[96,6144]{1,0:T(8,128)(2,1)S(1)} collective-permute-done((bf16[96,6144]{1,0:T(8,128)(2,1)S(1)}, bf16[96,6144]{1,0:T(8,128)(2,1)S(1)}, u32[]{:S(2)}, u32[]{:S(2)}) %collective-permute-start.20) | collective-permute-done | bytes 1179680 | tf_op jit(solution)/shard_map/ppermute | solution.py:14
  135.8 1.9 collective-permute-done.21
  137.8 2.6 collective-permute-start.24
  143.0 2.7 fusion.15
  145.7 5.4 %fusion.37 = bf16[384,512]{1,0:T(8,128)(2,1)S(1)} fusion(bf16[384,6144]{1,0:T(8,128)(2,1)S(1)} %constant_dynamic-update-slice_fusion.12, bf16[1,6144,512]{2,1,0:T(8,128)(2,1)} %param.12, f32[384,512]{1,0:T(8,128)S(1)} %fusion.15), kind=kOutput, calls=%fused_computation.45 | convolution fusion | flops 2417098752 | bytes 12189696 | tf_op jit(solution)/shard_map/dot_general | solution.py:69
  151.2 5.6 %convolution_convert_fusion = bf16[384,6144]{1,0:T(8,128)(2,1)S(1)} fusion(bf16[384,512]{1,0:T(8,128)(2,1)S(1)} %fusion.37, bf16[1,512,6144]{2,1,0:T(8,128)(2,1)} %param.13), kind=kOutput, calls=%fused_computation | convolution fusion | flops 2418278400 | bytes 11403264 | tf_op jit(solution)/shard_map/dot_general | solution.py:71
  157.3 3.9 %collective-permute-done.24 = bf16[96,6144]{1,0:T(8,128)(2,1)S(1)} collective-permute-done((bf16[96,6144]{1,0:T(8,128)(2,1)S(1)}, bf16[96,6144]{1,0:T(8,128)(2,1)S(1)}, u32[]{:S(2)}, u32[]{:S(2)}) %collective-permute-start.24) | collective-permute-done | bytes 1179680 | tf_op jit(solution)/shard_map/ppermute | solution.py:14
  161.2 5.0 %collective-permute-done.25 = bf16[96,6144]{1,0:T(8,128)(2,1)S(1)} collective-permute-done((bf16[96,6144]{1,0:T(8,128)(2,1)S(1)}, bf16[96,6144]{1,0:T(8,128)(2,1)S(1)}, u32[]{:S(2)}, u32[]{:S(2)}) %collective-permute-start.25) | collective-permute-done | bytes 1179680 | tf_op jit(solution)/shard_map/ppermute | solution.py:14
  166.9 3.3 %collective-permute-start.28 = (bf16[96,6144]{1,0:T(8,128)(2,1)S(1)}, bf16[96,6144]{1,0:T(8,128)(2,1)S(1)}, u32[]{:S(2)}, u32[]{:S(2)}) collective-permute-start(bf16[96,6144]{1,0:T(8,128)(2,1)S(1)} %add_convert_fusion.7), channel_id=1, source_target_pairs={{0,6},{2,0},{4,2},{6,4},{1,7},{3,1},{5,3},{7,5},{8,14},{10,8},{12,... | collective-permute-start | bytes 3538952 | tf_op jit(solution)/shard_map/ppermute | solution.py:14
  171.7 24.9 %collective-permute-done.29 = bf16[96,6144]{1,0:T(8,128)(2,1)S(1)} collective-permute-done((bf16[96,6144]{1,0:T(8,128)(2,1)S(1)}, bf16[96,6144]{1,0:T(8,128)(2,1)S(1)}, u32[]{:S(2)}, u32[]{:S(2)}) %collective-permute-start.29) | collective-permute-done | bytes 1179680 | tf_op jit(solution)/shard_map/ppermute | solution.py:14
  197.2 1.8 collective-permute-start.34
  199.9 16.3 %collective-permute-done.32 = bf16[96,6144]{1,0:T(8,128)(2,1)S(1)} collective-permute-done((bf16[96,6144]{1,0:T(8,128)(2,1)S(1)}, bf16[96,6144]{1,0:T(8,128)(2,1)S(1)}, u32[]{:S(2)}, u32[]{:S(2)}) %collective-permute-start.32) | collective-permute-done | bytes 1179680 | tf_op jit(solution)/shard_map/ppermute | solution.py:14
  217.5 3.0 %collective-permute-done.35 = bf16[96,6144]{1,0:T(8,128)(2,1)S(1)} collective-permute-done((bf16[96,6144]{1,0:T(8,128)(2,1)S(1)}, bf16[96,6144]{1,0:T(8,128)(2,1)S(1)}, u32[]{:S(2)}, u32[]{:S(2)}) %collective-permute-start.35) | collective-permute-done | bytes 1179680 | tf_op jit(solution)/shard_map/ppermute | solution.py:14
  222.1 2.1 collective-permute-start.37
  225.7 8.8 %collective-permute-done.36 = bf16[48,6144]{1,0:T(8,128)(2,1)S(1)} collective-permute-done((bf16[48,6144]{1,0:T(8,128)(2,1)S(1)}, bf16[48,6144]{1,0:T(8,128)(2,1)S(1)}, u32[]{:S(2)}, u32[]{:S(2)}) %collective-permute-start.36) | collective-permute-done | bytes 589856 | tf_op jit(solution)/shard_map/ppermute | solution.py:14
  238.3 2.6 collective-permute-start.40
  240.9 1.7 collective-permute-start.42
  243.2 2.4 collective-permute-done.41
  245.6 2.0 collective-permute-done.42
  247.6 10.6 %collective-permute-done.43 = bf16[24,6144]{1,0:T(8,128)(2,1)S(1)} collective-permute-done((bf16[24,6144]{1,0:T(8,128)(2,1)S(1)}, bf16[24,6144]{1,0:T(8,128)(2,1)S(1)}, u32[]{:S(2)}, u32[]{:S(2)}) %collective-permute-start.43) | collective-permute-done | bytes 294944 | tf_op jit(solution)/shard_map/ppermute | solution.py:14
  259.7 10.9 %collective-permute-done.45 = bf16[48,6144]{1,0:T(8,128)(2,1)S(1)} collective-permute-done((bf16[48,6144]{1,0:T(8,128)(2,1)S(1)}, bf16[48,6144]{1,0:T(8,128)(2,1)S(1)}, u32[]{:S(2)}, u32[]{:S(2)}) %collective-permute-start.45) | collective-permute-done | bytes 589856 | tf_op jit(solution)/shard_map/ppermute | solution.py:43
  271.2 4.8 %collective-permute-done.44 = bf16[48,6144]{1,0:T(8,128)(2,1)S(1)} collective-permute-done((bf16[48,6144]{1,0:T(8,128)(2,1)S(1)}, bf16[48,6144]{1,0:T(8,128)(2,1)S(1)}, u32[]{:S(2)}, u32[]{:S(2)}) %collective-permute-start.44) | collective-permute-done | bytes 589856 | tf_op jit(solution)/shard_map/ppermute | solution.py:38
  276.0 1.8 fusion.2
  (157 shorter events, 37.7 us)
Async XLA Ops:
  0.0 4.7 %collective-permute-start.2 = (f32[128,2]{0,1:T(2,128)}, f32[128,2]{0,1:T(2,128)S(1)}, u32[]{:S(2)}, u32[]{:S(2)}) collective-permute-start(f32[128,2]{0,1:T(2,128)} %bitcast.89), channel_id=1, source_target_pairs={{0,32},{32,64},{64,96},{96,0},{1,33},{33,65},{65,97},{97,1},{2,34}... | collective-permute-start | bytes 3080 | tf_op jit(solution)/shard_map/ppermute | solution.py:38
  0.0 4.8 %collective-permute-start.3 = (s32[128,2]{0,1:T(2,128)}, s32[128,2]{0,1:T(2,128)S(1)}, u32[]{:S(2)}, u32[]{:S(2)}) collective-permute-start(s32[128,2]{0,1:T(2,128)} %bitcast.79), channel_id=1, source_target_pairs={{0,32},{32,64},{64,96},{96,0},{1,33},{33,65},{65,97},{97,1},{2,34}... | collective-permute-start | bytes 3080 | tf_op jit(solution)/shard_map/ppermute | solution.py:38
  0.7 4.7 %collective-permute-start.1 = (s32[128,2]{0,1:T(2,128)}, s32[128,2]{0,1:T(2,128)S(1)}, u32[]{:S(2)}, u32[]{:S(2)}) collective-permute-start(s32[128,2]{0,1:T(2,128)} %bitcast.80), channel_id=1, source_target_pairs={{0,32},{32,64},{64,96},{96,0},{1,33},{33,65},{65,97},{97,1},{2,34}... | collective-permute-start | bytes 3080 | tf_op jit(solution)/shard_map/ppermute | solution.py:38
  2.2 14.1 %collective-permute-start = (bf16[48,6144]{1,0:T(8,128)(2,1)S(1)}, bf16[48,6144]{1,0:T(8,128)(2,1)S(1)}, u32[]{:S(2)}, u32[]{:S(2)}) collective-permute-start(bf16[48,6144]{1,0:T(8,128)(2,1)S(1)} %convolution_convert_fusion.4), channel_id=1, source_target_pairs={{0,24},{8,16},{16,8},{24,0},{1,25},{9,17},{17,9},{25,1},{2,26},{10... | collective-permute-start | bytes 1769480 | tf_op jit(solution)/shard_map/ppermute | solution.py:34
  16.4 9.1 %collective-permute-start.6 = (bf16[24,6144]{1,0:T(8,128)(2,1)S(1)}, bf16[24,6144]{1,0:T(8,128)(2,1)S(1)}, u32[]{:S(2)}, u32[]{:S(2)}) collective-permute-start(bf16[24,6144]{1,0:T(8,128)(2,1)S(1)} %get-tuple-element.185), channel_id=1, source_target_pairs={{0,8},{8,0},{1,9},{9,1},{2,10},{10,2},{3,11},{11,3},{4,12},{12,4},... | collective-permute-start | bytes 884744 | tf_op jit(solution)/shard_map/ppermute | solution.py:14
  19.0 10.4 %collective-permute-start.4 = (bf16[24,6144]{1,0:T(8,128)(2,1)S(1)}, bf16[24,6144]{1,0:T(8,128)(2,1)S(1)}, u32[]{:S(2)}, u32[]{:S(2)}) collective-permute-start(bf16[24,6144]{1,0:T(8,128)(2,1)S(1)} %get-tuple-element.186), channel_id=1, source_target_pairs={{0,2},{2,4},{4,6},{6,0},{1,3},{3,5},{5,7},{7,1},{8,10},{10,12},{12... | collective-permute-start | bytes 884744 | tf_op jit(solution)/shard_map/ppermute | solution.py:14
  20.5 9.6 %collective-permute-start.7 = (bf16[24,6144]{1,0:T(8,128)(2,1)S(1)}, bf16[24,6144]{1,0:T(8,128)(2,1)S(1)}, u32[]{:S(2)}, u32[]{:S(2)}) collective-permute-start(bf16[24,6144]{1,0:T(8,128)(2,1)S(1)} %get-tuple-element.183), channel_id=1, source_target_pairs={{0,1},{1,0},{2,3},{3,2},{4,5},{5,4},{6,7},{7,6},{8,9},{9,8},{10,11... | collective-permute-start | bytes 884744 | tf_op jit(solution)/shard_map/ppermute | solution.py:14
  20.6 9.6 %collective-permute-start.5 = (bf16[24,6144]{1,0:T(8,128)(2,1)S(1)}, bf16[24,6144]{1,0:T(8,128)(2,1)S(1)}, u32[]{:S(2)}, u32[]{:S(2)}) collective-permute-start(bf16[24,6144]{1,0:T(8,128)(2,1)S(1)} %get-tuple-element.184), channel_id=1, source_target_pairs={{0,6},{2,0},{4,2},{6,4},{1,7},{3,1},{5,3},{7,5},{8,14},{10,8},{12,... | collective-permute-start | bytes 884744 | tf_op jit(solution)/shard_map/ppermute | solution.py:14
  30.4 15.9 %collective-permute-start.9 = (bf16[48,6144]{1,0:T(8,128)(2,1)S(1)}, bf16[48,6144]{1,0:T(8,128)(2,1)S(1)}, u32[]{:S(2)}, u32[]{:S(2)}) collective-permute-start(bf16[48,6144]{1,0:T(8,128)(2,1)S(1)} %pad_maximum_fusion.5), channel_id=1, source_target_pairs={{0,6},{2,0},{4,2},{6,4},{1,7},{3,1},{5,3},{7,5},{8,14},{10,8},{12,... | collective-permute-start | bytes 1769480 | tf_op jit(solution)/shard_map/ppermute | solution.py:14
  33.4 16.3 %collective-permute-start.8 = (bf16[48,6144]{1,0:T(8,128)(2,1)S(1)}, bf16[48,6144]{1,0:T(8,128)(2,1)S(1)}, u32[]{:S(2)}, u32[]{:S(2)}) collective-permute-start(bf16[48,6144]{1,0:T(8,128)(2,1)S(1)} %pad_maximum_fusion.4), channel_id=1, source_target_pairs={{0,2},{2,4},{4,6},{6,0},{1,3},{3,5},{5,7},{7,1},{8,10},{10,12},{12... | collective-permute-start | bytes 1769480 | tf_op jit(solution)/shard_map/ppermute | solution.py:14
  33.4 16.3 %collective-permute-start.11 = (bf16[48,6144]{1,0:T(8,128)(2,1)S(1)}, bf16[48,6144]{1,0:T(8,128)(2,1)S(1)}, u32[]{:S(2)}, u32[]{:S(2)}) collective-permute-start(bf16[48,6144]{1,0:T(8,128)(2,1)S(1)} %pad_maximum_fusion.7), channel_id=1, source_target_pairs={{0,8},{8,0},{1,9},{9,1},{2,10},{10,2},{3,11},{11,3},{4,12},{12,4},... | collective-permute-start | bytes 1769480 | tf_op jit(solution)/shard_map/ppermute | solution.py:14
  33.5 16.3 %collective-permute-start.10 = (bf16[48,6144]{1,0:T(8,128)(2,1)S(1)}, bf16[48,6144]{1,0:T(8,128)(2,1)S(1)}, u32[]{:S(2)}, u32[]{:S(2)}) collective-permute-start(bf16[48,6144]{1,0:T(8,128)(2,1)S(1)} %pad_maximum_fusion.6), channel_id=1, source_target_pairs={{0,1},{1,0},{2,3},{3,2},{4,5},{5,4},{6,7},{7,6},{8,9},{9,8},{10,11... | collective-permute-start | bytes 1769480 | tf_op jit(solution)/shard_map/ppermute | solution.py:14
  50.2 28.2 %collective-permute-start.12 = (bf16[96,6144]{1,0:T(8,128)(2,1)S(1)}, bf16[96,6144]{1,0:T(8,128)(2,1)S(1)}, u32[]{:S(2)}, u32[]{:S(2)}) collective-permute-start(bf16[96,6144]{1,0:T(8,128)(2,1)S(1)} %pad_maximum_fusion), channel_id=1, source_target_pairs={{0,2},{2,4},{4,6},{6,0},{1,3},{3,5},{5,7},{7,1},{8,10},{10,12},{12... | collective-permute-start | bytes 3538952 | tf_op jit(solution)/shard_map/ppermute | solution.py:14
  50.4 28.0 %collective-permute-start.13 = (bf16[96,6144]{1,0:T(8,128)(2,1)S(1)}, bf16[96,6144]{1,0:T(8,128)(2,1)S(1)}, u32[]{:S(2)}, u32[]{:S(2)}) collective-permute-start(bf16[96,6144]{1,0:T(8,128)(2,1)S(1)} %pad_maximum_fusion.1), channel_id=1, source_target_pairs={{0,6},{2,0},{4,2},{6,4},{1,7},{3,1},{5,3},{7,5},{8,14},{10,8},{12,... | collective-permute-start | bytes 3538952 | tf_op jit(solution)/shard_map/ppermute | solution.py:14
  53.7 26.3 %collective-permute-start.14 = (bf16[96,6144]{1,0:T(8,128)(2,1)S(1)}, bf16[96,6144]{1,0:T(8,128)(2,1)S(1)}, u32[]{:S(2)}, u32[]{:S(2)}) collective-permute-start(bf16[96,6144]{1,0:T(8,128)(2,1)S(1)} %get-tuple-element.97), channel_id=1, source_target_pairs={{0,8},{8,0},{1,9},{9,1},{2,10},{10,2},{3,11},{11,3},{4,12},{12,4},... | collective-permute-start | bytes 3538952 | tf_op jit(solution)/shard_map/ppermute | solution.py:14
  54.5 26.2 %collective-permute-start.15 = (bf16[96,6144]{1,0:T(8,128)(2,1)S(1)}, bf16[96,6144]{1,0:T(8,128)(2,1)S(1)}, u32[]{:S(2)}, u32[]{:S(2)}) collective-permute-start(bf16[96,6144]{1,0:T(8,128)(2,1)S(1)} %get-tuple-element.96), channel_id=1, source_target_pairs={{0,1},{1,0},{2,3},{3,2},{4,5},{5,4},{6,7},{7,6},{8,9},{9,8},{10,11... | collective-permute-start | bytes 3538952 | tf_op jit(solution)/shard_map/ppermute | solution.py:14
  80.7 26.7 %collective-permute-start.16 = (bf16[96,6144]{1,0:T(8,128)(2,1)S(1)}, bf16[96,6144]{1,0:T(8,128)(2,1)S(1)}, u32[]{:S(2)}, u32[]{:S(2)}) collective-permute-start(bf16[96,6144]{1,0:T(8,128)(2,1)S(1)} %collective-permute-done.12), channel_id=1, source_target_pairs={{0,2},{2,4},{4,6},{6,0},{1,3},{3,5},{5,7},{7,1},{8,10},{10,12},{12... | collective-permute-start | bytes 3538952 | tf_op jit(solution)/shard_map/ppermute | solution.py:14
  80.8 25.2 %collective-permute-start.18 = (bf16[96,6144]{1,0:T(8,128)(2,1)S(1)}, bf16[96,6144]{1,0:T(8,128)(2,1)S(1)}, u32[]{:S(2)}, u32[]{:S(2)}) collective-permute-start(bf16[96,6144]{1,0:T(8,128)(2,1)S(1)} %get-tuple-element.96), channel_id=1, source_target_pairs={{0,8},{8,0},{1,9},{9,1},{2,10},{10,2},{3,11},{11,3},{4,12},{12,4},... | collective-permute-start | bytes 3538952 | tf_op jit(solution)/shard_map/ppermute | solution.py:14
  82.4 25.1 %collective-permute-start.19 = (bf16[96,6144]{1,0:T(8,128)(2,1)S(1)}, bf16[96,6144]{1,0:T(8,128)(2,1)S(1)}, u32[]{:S(2)}, u32[]{:S(2)}) collective-permute-start(bf16[96,6144]{1,0:T(8,128)(2,1)S(1)} %get-tuple-element.97), channel_id=1, source_target_pairs={{0,1},{1,0},{2,3},{3,2},{4,5},{5,4},{6,7},{7,6},{8,9},{9,8},{10,11... | collective-permute-start | bytes 3538952 | tf_op jit(solution)/shard_map/ppermute | solution.py:14
  84.1 25.9 %collective-permute-start.17 = (bf16[96,6144]{1,0:T(8,128)(2,1)S(1)}, bf16[96,6144]{1,0:T(8,128)(2,1)S(1)}, u32[]{:S(2)}, u32[]{:S(2)}) collective-permute-start(bf16[96,6144]{1,0:T(8,128)(2,1)S(1)} %collective-permute-done.13), channel_id=1, source_target_pairs={{0,6},{2,0},{4,2},{6,4},{1,7},{3,1},{5,3},{7,5},{8,14},{10,8},{12,... | collective-permute-start | bytes 3538952 | tf_op jit(solution)/shard_map/ppermute | solution.py:14
  101.4 13.7 %slice-start.2 = ((s8[6291456]{0:T(1024)(128)(4,1)}), s8[2097152]{0:T(1024)(128)(4,1)S(1)}, s32[]{:S(2)}) async-start(s8[6291456]{0:T(1024)(128)(4,1)} %bitcast.83), calls=%async_computation.2 | async-start | bytes 4194304
  110.1 25.8 %collective-permute-start.20 = (bf16[96,6144]{1,0:T(8,128)(2,1)S(1)}, bf16[96,6144]{1,0:T(8,128)(2,1)S(1)}, u32[]{:S(2)}, u32[]{:S(2)}) collective-permute-start(bf16[96,6144]{1,0:T(8,128)(2,1)S(1)} %pad_maximum_fusion), channel_id=1, source_target_pairs={{0,6},{2,0},{4,2},{6,4},{1,7},{3,1},{5,3},{7,5},{8,14},{10,8},{12,... | collective-permute-start | bytes 3538952 | tf_op jit(solution)/shard_map/ppermute | solution.py:14
  113.5 24.3 %collective-permute-start.21 = (bf16[96,6144]{1,0:T(8,128)(2,1)S(1)}, bf16[96,6144]{1,0:T(8,128)(2,1)S(1)}, u32[]{:S(2)}, u32[]{:S(2)}) collective-permute-start(bf16[96,6144]{1,0:T(8,128)(2,1)S(1)} %pad_maximum_fusion.1), channel_id=1, source_target_pairs={{0,2},{2,4},{4,6},{6,0},{1,3},{3,5},{5,7},{7,1},{8,10},{10,12},{12... | collective-permute-start | bytes 3538952 | tf_op jit(solution)/shard_map/ppermute | solution.py:14
  113.5 24.3 %collective-permute-start.22 = (bf16[96,6144]{1,0:T(8,128)(2,1)S(1)}, bf16[96,6144]{1,0:T(8,128)(2,1)S(1)}, u32[]{:S(2)}, u32[]{:S(2)}) collective-permute-start(bf16[96,6144]{1,0:T(8,128)(2,1)S(1)} %collective-permute-done.15), channel_id=1, source_target_pairs={{0,8},{8,0},{1,9},{9,1},{2,10},{10,2},{3,11},{11,3},{4,12},{12,4},... | collective-permute-start | bytes 3538952 | tf_op jit(solution)/shard_map/ppermute | solution.py:14
  114.2 23.5 %collective-permute-start.23 = (bf16[96,6144]{1,0:T(8,128)(2,1)S(1)}, bf16[96,6144]{1,0:T(8,128)(2,1)S(1)}, u32[]{:S(2)}, u32[]{:S(2)}) collective-permute-start(bf16[96,6144]{1,0:T(8,128)(2,1)S(1)} %collective-permute-done.14), channel_id=1, source_target_pairs={{0,1},{1,0},{2,3},{3,2},{4,5},{5,4},{6,7},{7,6},{8,9},{9,8},{10,11... | collective-permute-start | bytes 3538952 | tf_op jit(solution)/shard_map/ppermute | solution.py:14
  128.9 14.1 %slice-start.4 = ((s8[6291456]{0:T(1024)(128)(4,1)}), s8[2097152]{0:T(1024)(128)(4,1)S(1)}, s32[]{:S(2)}) async-start(s8[6291456]{0:T(1024)(128)(4,1)} %bitcast.85), calls=%async_computation.4 | async-start | bytes 4194304
  137.8 23.4 %collective-permute-start.24 = (bf16[96,6144]{1,0:T(8,128)(2,1)S(1)}, bf16[96,6144]{1,0:T(8,128)(2,1)S(1)}, u32[]{:S(2)}, u32[]{:S(2)}) collective-permute-start(bf16[96,6144]{1,0:T(8,128)(2,1)S(1)} %get-tuple-element.109), channel_id=1, source_target_pairs={{0,6},{2,0},{4,2},{6,4},{1,7},{3,1},{5,3},{7,5},{8,14},{10,8},{12,... | collective-permute-start | bytes 3538952 | tf_op jit(solution)/shard_map/ppermute | solution.py:14
  140.4 25.8 %collective-permute-start.25 = (bf16[96,6144]{1,0:T(8,128)(2,1)S(1)}, bf16[96,6144]{1,0:T(8,128)(2,1)S(1)}, u32[]{:S(2)}, u32[]{:S(2)}) collective-permute-start(bf16[96,6144]{1,0:T(8,128)(2,1)S(1)} %get-tuple-element.110), channel_id=1, source_target_pairs={{0,2},{2,4},{4,6},{6,0},{1,3},{3,5},{5,7},{7,1},{8,10},{10,12},{12... | collective-permute-start | bytes 3538952 | tf_op jit(solution)/shard_map/ppermute | solution.py:14
  140.4 25.8 %collective-permute-start.26 = (bf16[96,6144]{1,0:T(8,128)(2,1)S(1)}, bf16[96,6144]{1,0:T(8,128)(2,1)S(1)}, u32[]{:S(2)}, u32[]{:S(2)}) collective-permute-start(bf16[96,6144]{1,0:T(8,128)(2,1)S(1)} %get-tuple-element.111), channel_id=1, source_target_pairs={{0,8},{8,0},{1,9},{9,1},{2,10},{10,2},{3,11},{11,3},{4,12},{12,4},... | collective-permute-start | bytes 3538952 | tf_op jit(solution)/shard_map/ppermute | solution.py:14
  142.0 24.2 %collective-permute-start.27 = (bf16[96,6144]{1,0:T(8,128)(2,1)S(1)}, bf16[96,6144]{1,0:T(8,128)(2,1)S(1)}, u32[]{:S(2)}, u32[]{:S(2)}) collective-permute-start(bf16[96,6144]{1,0:T(8,128)(2,1)S(1)} %get-tuple-element.112), channel_id=1, source_target_pairs={{0,1},{1,0},{2,3},{3,2},{4,5},{5,4},{6,7},{7,6},{8,9},{9,8},{10,11... | collective-permute-start | bytes 3538952 | tf_op jit(solution)/shard_map/ppermute | solution.py:14
  166.5 30.2 %collective-permute-start.29 = (bf16[96,6144]{1,0:T(8,128)(2,1)S(1)}, bf16[96,6144]{1,0:T(8,128)(2,1)S(1)}, u32[]{:S(2)}, u32[]{:S(2)}) collective-permute-start(bf16[96,6144]{1,0:T(8,128)(2,1)S(1)} %add_convert_fusion.6), channel_id=1, source_target_pairs={{0,2},{2,4},{4,6},{6,0},{1,3},{3,5},{5,7},{7,1},{8,10},{10,12},{12... | collective-permute-start | bytes 3538952 | tf_op jit(solution)/shard_map/ppermute | solution.py:14
  166.9 30.0 %collective-permute-start.28 = (bf16[96,6144]{1,0:T(8,128)(2,1)S(1)}, bf16[96,6144]{1,0:T(8,128)(2,1)S(1)}, u32[]{:S(2)}, u32[]{:S(2)}) collective-permute-start(bf16[96,6144]{1,0:T(8,128)(2,1)S(1)} %add_convert_fusion.7), channel_id=1, source_target_pairs={{0,6},{2,0},{4,2},{6,4},{1,7},{3,1},{5,3},{7,5},{8,14},{10,8},{12,... | collective-permute-start | bytes 3538952 | tf_op jit(solution)/shard_map/ppermute | solution.py:14
  170.1 26.7 %collective-permute-start.30 = (bf16[96,6144]{1,0:T(8,128)(2,1)S(1)}, bf16[96,6144]{1,0:T(8,128)(2,1)S(1)}, u32[]{:S(2)}, u32[]{:S(2)}) collective-permute-start(bf16[96,6144]{1,0:T(8,128)(2,1)S(1)} %get-tuple-element.120), channel_id=1, source_target_pairs={{0,8},{8,0},{1,9},{9,1},{2,10},{10,2},{3,11},{11,3},{4,12},{12,4},... | collective-permute-start | bytes 3538952 | tf_op jit(solution)/shard_map/ppermute | solution.py:14
  170.1 26.7 %collective-permute-start.31 = (bf16[96,6144]{1,0:T(8,128)(2,1)S(1)}, bf16[96,6144]{1,0:T(8,128)(2,1)S(1)}, u32[]{:S(2)}, u32[]{:S(2)}) collective-permute-start(bf16[96,6144]{1,0:T(8,128)(2,1)S(1)} %get-tuple-element.121), channel_id=1, source_target_pairs={{0,1},{1,0},{2,3},{3,2},{4,5},{5,4},{6,7},{7,6},{8,9},{9,8},{10,11... | collective-permute-start | bytes 3538952 | tf_op jit(solution)/shard_map/ppermute | solution.py:14
  171.7 44.5 %collective-permute-start.32 = (bf16[96,6144]{1,0:T(8,128)(2,1)S(1)}, bf16[96,6144]{1,0:T(8,128)(2,1)S(1)}, u32[]{:S(2)}, u32[]{:S(2)}) collective-permute-start(bf16[96,6144]{1,0:T(8,128)(2,1)S(1)} %get-tuple-element.123), channel_id=1, source_target_pairs={{0,2},{2,4},{4,6},{6,0},{1,3},{3,5},{5,7},{7,1},{8,10},{10,12},{12... | collective-permute-start | bytes 3538952 | tf_op jit(solution)/shard_map/ppermute | solution.py:14
  196.7 20.8 %collective-permute-start.33 = (bf16[96,6144]{1,0:T(8,128)(2,1)S(1)}, bf16[96,6144]{1,0:T(8,128)(2,1)S(1)}, u32[]{:S(2)}, u32[]{:S(2)}) collective-permute-start(bf16[96,6144]{1,0:T(8,128)(2,1)S(1)} %get-tuple-element.124), channel_id=1, source_target_pairs={{0,6},{2,0},{4,2},{6,4},{1,7},{3,1},{5,3},{7,5},{8,14},{10,8},{12,... | collective-permute-start | bytes 3538952 | tf_op jit(solution)/shard_map/ppermute | solution.py:14
  197.2 20.3 %collective-permute-start.34 = (bf16[96,6144]{1,0:T(8,128)(2,1)S(1)}, bf16[96,6144]{1,0:T(8,128)(2,1)S(1)}, u32[]{:S(2)}, u32[]{:S(2)}) collective-permute-start(bf16[96,6144]{1,0:T(8,128)(2,1)S(1)} %add_convert_fusion.5), channel_id=1, source_target_pairs={{0,8},{8,0},{1,9},{9,1},{2,10},{10,2},{3,11},{11,3},{4,12},{12,4},... | collective-permute-start | bytes 3538952 | tf_op jit(solution)/shard_map/ppermute | solution.py:14
  199.3 21.1 %collective-permute-start.35 = (bf16[96,6144]{1,0:T(8,128)(2,1)S(1)}, bf16[96,6144]{1,0:T(8,128)(2,1)S(1)}, u32[]{:S(2)}, u32[]{:S(2)}) collective-permute-start(bf16[96,6144]{1,0:T(8,128)(2,1)S(1)} %add_convert_fusion.4), channel_id=1, source_target_pairs={{0,1},{1,0},{2,3},{3,2},{4,5},{5,4},{6,7},{7,6},{8,9},{9,8},{10,11... | collective-permute-start | bytes 3538952 | tf_op jit(solution)/shard_map/ppermute | solution.py:14
  222.0 12.5 %collective-permute-start.36 = (bf16[48,6144]{1,0:T(8,128)(2,1)S(1)}, bf16[48,6144]{1,0:T(8,128)(2,1)S(1)}, u32[]{:S(2)}, u32[]{:S(2)}) collective-permute-start(bf16[48,6144]{1,0:T(8,128)(2,1)S(1)} %pad_maximum_fusion.8), channel_id=1, source_target_pairs={{0,6},{2,0},{4,2},{6,4},{1,7},{3,1},{5,3},{7,5},{8,14},{10,8},{12,... | collective-permute-start | bytes 1769480 | tf_op jit(solution)/shard_map/ppermute | solution.py:14
  222.1 13.5 %collective-permute-start.37 = (bf16[48,6144]{1,0:T(8,128)(2,1)S(1)}, bf16[48,6144]{1,0:T(8,128)(2,1)S(1)}, u32[]{:S(2)}, u32[]{:S(2)}) collective-permute-start(bf16[48,6144]{1,0:T(8,128)(2,1)S(1)} %pad_maximum_fusion.9), channel_id=1, source_target_pairs={{0,2},{2,4},{4,6},{6,0},{1,3},{3,5},{5,7},{7,1},{8,10},{10,12},{12... | collective-permute-start | bytes 1769480 | tf_op jit(solution)/shard_map/ppermute | solution.py:14
  224.2 12.9 %collective-permute-start.39 = (bf16[48,6144]{1,0:T(8,128)(2,1)S(1)}, bf16[48,6144]{1,0:T(8,128)(2,1)S(1)}, u32[]{:S(2)}, u32[]{:S(2)}) collective-permute-start(bf16[48,6144]{1,0:T(8,128)(2,1)S(1)} %get-tuple-element.173), channel_id=1, source_target_pairs={{0,8},{8,0},{1,9},{9,1},{2,10},{10,2},{3,11},{11,3},{4,12},{12,4},... | collective-permute-start | bytes 1769480 | tf_op jit(solution)/shard_map/ppermute | solution.py:14
  225.0 12.0 %collective-permute-start.38 = (bf16[48,6144]{1,0:T(8,128)(2,1)S(1)}, bf16[48,6144]{1,0:T(8,128)(2,1)S(1)}, u32[]{:S(2)}, u32[]{:S(2)}) collective-permute-start(bf16[48,6144]{1,0:T(8,128)(2,1)S(1)} %get-tuple-element.174), channel_id=1, source_target_pairs={{0,1},{1,0},{2,3},{3,2},{4,5},{5,4},{6,7},{7,6},{8,9},{9,8},{10,11... | collective-permute-start | bytes 1769480 | tf_op jit(solution)/shard_map/ppermute | solution.py:14
  237.6 8.0 %collective-permute-start.41 = (bf16[24,6144]{1,0:T(8,128)(2,1)S(1)}, bf16[24,6144]{1,0:T(8,128)(2,1)S(1)}, u32[]{:S(2)}, u32[]{:S(2)}) collective-permute-start(bf16[24,6144]{1,0:T(8,128)(2,1)S(1)} %add_convert_fusion.14), channel_id=1, source_target_pairs={{0,2},{2,4},{4,6},{6,0},{1,3},{3,5},{5,7},{7,1},{8,10},{10,12},{12... | collective-permute-start | bytes 884744 | tf_op jit(solution)/shard_map/ppermute | solution.py:14
  238.3 7.3 %collective-permute-start.40 = (bf16[24,6144]{1,0:T(8,128)(2,1)S(1)}, bf16[24,6144]{1,0:T(8,128)(2,1)S(1)}, u32[]{:S(2)}, u32[]{:S(2)}) collective-permute-start(bf16[24,6144]{1,0:T(8,128)(2,1)S(1)} %add_convert_fusion.15), channel_id=1, source_target_pairs={{0,6},{2,0},{4,2},{6,4},{1,7},{3,1},{5,3},{7,5},{8,14},{10,8},{12,... | collective-permute-start | bytes 884744 | tf_op jit(solution)/shard_map/ppermute | solution.py:14
  240.9 6.7 %collective-permute-start.42 = (bf16[24,6144]{1,0:T(8,128)(2,1)S(1)}, bf16[24,6144]{1,0:T(8,128)(2,1)S(1)}, u32[]{:S(2)}, u32[]{:S(2)}) collective-permute-start(bf16[24,6144]{1,0:T(8,128)(2,1)S(1)} %slice.202), channel_id=1, source_target_pairs={{0,8},{8,0},{1,9},{9,1},{2,10},{10,2},{3,11},{11,3},{4,12},{12,4},... | collective-permute-start | bytes 884744 | tf_op jit(solution)/shard_map/ppermute | solution.py:14
  242.6 15.6 %collective-permute-start.43 = (bf16[24,6144]{1,0:T(8,128)(2,1)S(1)}, bf16[24,6144]{1,0:T(8,128)(2,1)S(1)}, u32[]{:S(2)}, u32[]{:S(2)}) collective-permute-start(bf16[24,6144]{1,0:T(8,128)(2,1)S(1)} %slice.204), channel_id=1, source_target_pairs={{0,1},{1,0},{2,3},{3,2},{4,5},{5,4},{6,7},{7,6},{8,9},{9,8},{10,11... | collective-permute-start | bytes 884744 | tf_op jit(solution)/shard_map/ppermute | solution.py:14
  258.7 11.9 %collective-permute-start.45 = (bf16[48,6144]{1,0:T(8,128)(2,1)S(1)}, bf16[48,6144]{1,0:T(8,128)(2,1)S(1)}, u32[]{:S(2)}, u32[]{:S(2)}) collective-permute-start(bf16[48,6144]{1,0:T(8,128)(2,1)S(1)} %pad_maximum_fusion.11), channel_id=1, source_target_pairs={{0,56},{8,48},{16,40},{24,32},{32,88},{40,80},{48,72},{56,64},{64,... | collective-permute-start | bytes 1769480 | tf_op jit(solution)/shard_map/ppermute | solution.py:43
  258.8 17.2 %collective-permute-start.44 = (bf16[48,6144]{1,0:T(8,128)(2,1)S(1)}, bf16[48,6144]{1,0:T(8,128)(2,1)S(1)}, u32[]{:S(2)}, u32[]{:S(2)}) collective-permute-start(bf16[48,6144]{1,0:T(8,128)(2,1)S(1)} %pad_maximum_fusion.10), channel_id=1, source_target_pairs={{0,32},{32,64},{64,96},{96,0},{1,33},{33,65},{65,97},{97,1},{2,34}... | collective-permute-start | bytes 1769480 | tf_op jit(solution)/shard_map/ppermute | solution.py:38
  (8 other events, 32.9 us)

commit v3 on v2

--- a/solution.py
+++ b/solution.py
@@ -1,6 +1,8 @@
 import jax
 import jax.numpy as jnp
 from jax import lax
+from jax.experimental import pallas as pl
+from jax.experimental.pallas import tpu as pltpu
 from jax.sharding import Mesh, PartitionSpec as P
 
 CAP = 48
@@ -63,13 +65,76 @@
     return [rows[i * size : (i + 1) * size] for i in range(count)]
 
 
+TILE = 1536
+
+
+def experts_kernel(*refs):
+    rows, (w_gate, w_up, w_down), rest = refs[:4], refs[4:7], refs[7:]
+    outs, (gate, up, hidden) = rest[:4], rest[4:]
+    step = pl.program_id(0)
+    half = pl.num_programs(0) // 2
+
+    @pl.when(step < half)
+    def _():
+        block = jnp.concatenate([r[...] for r in rows])
+        gate_part = jnp.dot(block, w_gate[...], preferred_element_type=F32)
+        up_part = jnp.dot(block, w_up[...], preferred_element_type=F32)
+
+        @pl.when(step == 0)
+        def _():
+            gate[...] = gate_part
+            up[...] = up_part
+
+        @pl.when(step > 0)
+        def _():
+            gate[...] += gate_part
+            up[...] += up_part
+
+    @pl.when(step >= half)
+    def _():
+        @pl.when(step == half)
+        def _():
+            v = gate[...]
+            hidden[...] = (v / (1.0 + jnp.exp(-v)) * up[...]).astype(BF16)
+
+        out = jnp.dot(hidden[...], w_down[...], preferred_element_type=F32).astype(BF16)
+        size = outs[0].shape[0]
+        for i, o in enumerate(outs):
+            o[...] = out[i * size : (i + 1) * size]
+
+
 def experts(pieces, gate_matrix, up_matrix, down_matrix):
-    rows = jnp.concatenate(pieces)
-    gate = jnp.dot(rows, gate_matrix, preferred_element_type=F32)
-    up = jnp.dot(rows, up_matrix, preferred_element_type=F32)
-    hidden = (jax.nn.silu(gate) * up).astype(BF16)
-    out = jnp.dot(hidden, down_matrix, preferred_element_type=F32).astype(BF16)
-    return split(out, len(pieces))
+    size, width = pieces[0].shape
+    units = gate_matrix.shape[1]
+    half = width // TILE
+    first = lambda i: jnp.minimum(i, half - 1)
+    second = lambda i: jnp.maximum(i - half, 0)
+    rows_in = pl.BlockSpec((size, TILE), lambda i: (0, first(i)))
+    rows_out = pl.BlockSpec((size, TILE), lambda i: (0, second(i)))
+    into = pl.BlockSpec((TILE, units), lambda i: (first(i), 0))
+    out_of = pl.BlockSpec((units, TILE), lambda i: (0, second(i)))
+    total = len(pieces) * size
+    return pl.pallas_call(
+        experts_kernel,
+        grid=(2 * half,),
+        in_specs=[rows_in] * 4 + [into, into, out_of],
+        out_specs=[rows_out] * 4,
+        out_shape=[jax.ShapeDtypeStruct((size, width), BF16)] * 4,
+        scratch_shapes=[
+            pltpu.VMEM((total, units), F32),
+            pltpu.VMEM((total, units), F32),
+            pltpu.VMEM((total, units), BF16),
+        ],
+        compiler_params=pltpu.CompilerParams(
+            dimension_semantics=("arbitrary",), vmem_limit_bytes=24 << 20
+        ),
+        cost_estimate=pl.CostEstimate(
+            flops=6 * total * width * units,
+            transcendentals=total * units,
+            bytes_accessed=6 * width * units + 4 * total * width,
+        ),
+        name="experts",
+    )(*pieces, gate_matrix, up_matrix, down_matrix)
 
 
 def slots(ids, keep, expert):
@@ -86,61 +151,73 @@
     mine = lax.axis_index("yh")
     other = 1 - mine
 
-    def compact(expert):
+    def compact(expert, tokens):
         _, picked, position = slots(ids, keep, expert)
         table = (position[None] == jnp.arange(CAP, dtype=jnp.int32)[:, None]) & picked[None]
         return jnp.dot(table.astype(BF16), tokens, preferred_element_type=F32).astype(BF16)
 
-    partner = to_partner(compact(other))
-    own = compact(mine)
-    next_ids, next_gates, next_keep = (to_next_section(v) for v in (ids, gates, keep))
-    own, partner, ids, gates, keep = together(own, partner, next_ids, next_gates, next_keep)
-    (a1, b), (a2, g) = split(own, 2), split(partner, 2)
-
-    b_behind, g_behind, a1_y, a2_z = together(right(b), left(g), over_y(a1), over_z(a2))
-    a1_near, a2_near = join(a1, a1_y), join(a2, a2_z)
-    from_left, from_right, a1_far, a2_far = together(
-        right(join(b_behind, g)), left(join(g_behind, b)), over_z(a1_near), over_y(a2_near)
-    )
-    b_opposite, g_ahead = split(from_left, 2)
-    g_opposite, b_ahead = split(from_right, 2)
-    near, far = join(a1_near, a2_near), join(a1_far, a2_far)
+    others, tokens = together(compact(other, tokens), tokens)
+    partner = to_partner(others)
+    own = compact(mine, tokens)
+
+    a1, b = split(own, 2)
+    a1_y, b_behind, b_ahead = over_y(a1), right(b), left(b)
+    a1_near = join(a1, a1_y)
+    a1_far, b_opposite = over_z(a1_near), right(b_behind)
     b_ring = join(b, b_behind, b_ahead, b_opposite)
-    g_ring = join(g, g_behind, g_ahead, g_opposite)
-
-    near, far, b_ring, g_ring = together(near, far, b_ring, g_ring)
-    near_left, far_right, g_y, b_z = right(near), left(far), over_y(g_ring), over_z(b_ring)
-    out0 = experts([near, far, b_ring, g_ring], *matrices)
-    near_left, far_right, g_y, b_z, b_ring, g_ring, *out0 = together(
-        near_left, far_right, g_y, b_z, b_ring, g_ring, *out0
-    )
-
-    near_opposite, far_opposite, b_y, g_z = (
-        right(near_left), left(far_right), over_y(b_ring), over_z(g_ring)
-    )
-    out1 = experts([near_left, far_right, g_y, b_z], *matrices)
-    near_opposite, far_opposite, b_y, g_z, near, far, b_z, g_y, *out1 = together(
-        near_opposite, far_opposite, b_y, g_z, near, far, b_z, g_y, *out1
-    )
-
-    near_right, far_left, b_yz, g_zy = left(near), right(far), over_y(b_z), over_z(g_y)
-    out2 = experts([near_opposite, far_opposite, b_y, g_z], *matrices)
-    near_right, far_left, b_yz, g_zy, *out2 = together(near_right, far_left, b_yz, g_zy, *out2)
-
-    near, far, b_ring, g_ring = out0
-    near_left, far_right, g_y, b_z = out1
-    near_opposite, far_opposite, b_y, g_z = out2
-    got = left(near_opposite), right(far_opposite), over_y(b_y), over_z(g_z)
-    out3 = experts([near_right, far_left, b_yz, g_zy], *matrices)
-    *got, near_right, far_left, b_yz, g_zy = together(*got, *out3)
+
+    a2, g = split(partner, 2)
+    a2_z, g_behind, g_ahead = over_z(a2), left(g), right(g)
+    b_y = over_y(b_ring)
+    g_behind, g_ahead, b_ring_z = together(g_behind, g_ahead, b_ring)
+    g_opposite = left(g_behind)
+    a2_near = join(a2, a2_z)
+    near = join(a1_near, a2_near)
+    a2_far, b_z = over_y(a2_near), over_z(b_ring_z)
+    near_late, g_opposite_done = together(near, g_opposite)
+    near_left, near_right = right(near), left(near_late)
+    g_ring = join(g, g_behind, g_ahead, g_opposite_done)
+
+    b_y, g_ring_out = together(b_y, g_ring)
+    g_y, g_z = over_y(g_ring_out), over_z(g_ring_out)
+    far = join(a1_far, a2_far)
+    near, b_ring, g_ring, b_y = experts([near, b_ring, g_ring, b_y], *matrices)
+    far_left, far_right = right(far), left(far)
+
+    near_left, near_right, far, b_z, near, b_ring, g_ring, b_y = together(
+        near_left, near_right, far, b_z, near, b_ring, g_ring, b_y
+    )
+    near_opposite, b_yz = right(near_left), over_y(b_z)
+    near_left, near_right, far, b_z = experts([near_left, near_right, far, b_z], *matrices)
+
+    far_left, far_right, g_y, g_z, near_left, near_right, far, b_z = together(
+        far_left, far_right, g_y, g_z, near_left, near_right, far, b_z
+    )
+    far_opposite, g_zy = left(far_right), over_z(g_y)
+    far_left, far_right, g_y, g_z = experts([far_left, far_right, g_y, g_z], *matrices)
+
+    near_opposite, far_opposite, b_yz, g_zy, far_left, far_right, g_y, g_z = together(
+        near_opposite, far_opposite, b_yz, g_zy, far_left, far_right, g_y, g_z
+    )
+    near_back, far_back, b_back, g_back = (
+        right(near_right), left(far_left), over_y(b_y), over_z(g_z)
+    )
+    near_opposite, far_opposite, b_yz, g_zy = experts(
+        [near_opposite, far_opposite, b_yz, g_zy], *matrices
+    )
+
+    near_opposite, far_opposite, b_yz, g_zy, near_back, far_back, b_back, g_back = together(
+        near_opposite, far_opposite, b_yz, g_zy, near_back, far_back, b_back, g_back
+    )
+    got = left(near_opposite), right(far_opposite), over_y(b_yz), over_z(g_zy)
     near_left, far_right = add(near_left, got[0]), add(far_right, got[1])
-    b_back, g_back = got[2:]
-
-    got = together(left(near_left), right(far_right), over_y(b_yz), over_z(g_zy))
-    near_back, far_back = got[:2]
     b_z, g_y = add(b_z, got[2]), add(g_y, got[3])
-
-    got = together(right(near_right), left(far_left), over_y(g_y), over_z(b_z))
+    ids, gates, keep, near_left, far_right, b_z, g_y = together(
+        ids, gates, keep, near_left, far_right, b_z, g_y
+    )
+
+    got = together(left(near_left), right(far_right), over_y(g_y), over_z(b_z))
+    ids, gates, keep = (to_next_section(v) for v in (ids, gates, keep))
     near, far = add(near, near_back, got[0]), add(far, far_back, got[1])
     g_ring, b_ring = add(g_ring, g_back, got[2]), add(b_ring, b_back, got[3])
 

time: 283 us -> 259 us (0.915)
  the two profiles are of different devices: /device:TPU:112 before, /device:TPU:0 now
where the time goes in v3:
time: 259 us; the launch traced here: 257 us
  waiting for transfers between devices  111 us (43%)
  starting transfers between devices  59.9 us (23%)
  Pallas kernels  46.4 us (18%)
  local copies, waits for them, and re-layouts  20.3 us (8%)
  other arithmetic  16 us (6%)
  matrix products  3.13 us (1%)
    ppermute x42, waiting for transfers between devices, shift(): return lax.ppermute(value, axis, [(i, (i + by) % n) for i in range(n)])  78.6 us
    ppermute x42, starting transfers between devices, shift(): return lax.ppermute(value, axis, [(i, (i + by) % n) for i in range(n)])  53.3 us
    pallas_call x4, Pallas kernels, experts(): pl.pallas_call(experts_kernel, grid=(2 * half,), in_specs=[rows_in] * 4 +...  46.4 us
    ppermute x4, waiting for transfers between devices, to_next_section(): lax.ppermute(value, ('zh', 'core'), [(s, (s + 1) % 4) for s in range(4)])  23.8 us
    unnamed x47, local copies, waits for them, and re-layouts  18.1 us
    convert_element_type x15, other arithmetic, add(): return total.astype(BF16)  11.7 us
    ppermute x1, waiting for transfers between devices, to_partner(): return lax.ppermute(value, ('yh', 'yl'), [(y, 3 - y) for y in range(4)])  6.32 us
  transfers between devices with their start and end apart: 48, of which 23 were waited for; matrix products, arithmetic and copies ran while one was open for 5% of the time, Pallas kernels for 18%

profile of v3, /device:TPU:0, one launch (start us, length us, event | category | flops | bytes accessed | tf_op | source)
XLA Modules:
  0.0 257.1 jit_solution(17881716338287255167)
XLA Ops:
  2.4 1.7 collective-permute-start
  4.2 2.8 %collective-permute-start.8 = (bf16[24,6144]{1,0:T(8,128)(2,1)S(1)}, bf16[24,6144]{1,0:T(8,128)(2,1)S(1)}, u32[]{:S(2)}, u32[]{:S(2)}) collective-permute-start(bf16[24,6144]{1,0:T(8,128)(2,1)S(1)} %get-tuple-element.172), channel_id=1, source_target_pairs={{0,6},{2,0},{4,2},{6,4},{1,7},{3,1},{5,3},{7,5},{8,14},{10,8},{12,... | collective-permute-start | bytes 884744 | tf_op jit(solution)/shard_map/ppermute | solution.py:16
  6.9 2.2 collective-permute-start.2
  9.1 2.1 collective-permute-done
  11.2 2.2 collective-permute-start.1
  13.4 2.9 %collective-permute-done.7 = bf16[24,6144]{1,0:T(8,128)(2,1)S(1)} collective-permute-done((bf16[24,6144]{1,0:T(8,128)(2,1)S(1)}, bf16[24,6144]{1,0:T(8,128)(2,1)S(1)}, u32[]{:S(2)}, u32[]{:S(2)}) %collective-permute-start.7) | collective-permute-done | bytes 294944 | tf_op jit(solution)/shard_map/ppermute | solution.py:16
  16.3 6.3 %collective-permute-done.2 = bf16[48,6144]{1,0:T(8,128)(2,1)S(1)} collective-permute-done((bf16[48,6144]{1,0:T(8,128)(2,1)S(1)}, bf16[48,6144]{1,0:T(8,128)(2,1)S(1)}, u32[]{:S(2)}, u32[]{:S(2)}) %collective-permute-start.2) | collective-permute-done | bytes 589856 | tf_op jit(solution)/shard_map/ppermute | solution.py:36
  23.2 2.8 %collective-permute-start.11 = (bf16[24,6144]{1,0:T(8,128)(2,1)S(1)}, bf16[24,6144]{1,0:T(8,128)(2,1)S(1)}, u32[]{:S(2)}, u32[]{:S(2)}) collective-permute-start(bf16[24,6144]{1,0:T(8,128)(2,1)S(1)} %get-tuple-element.174), channel_id=1, source_target_pairs={{0,6},{2,0},{4,2},{6,4},{1,7},{3,1},{5,3},{7,5},{8,14},{10,8},{12,... | collective-permute-start | bytes 884744 | tf_op jit(solution)/shard_map/ppermute | solution.py:16
  26.0 1.9 collective-permute-start.3
  28.1 3.1 %collective-permute-done.12 = bf16[24,6144]{1,0:T(8,128)(2,1)S(1)} collective-permute-done((bf16[24,6144]{1,0:T(8,128)(2,1)S(1)}, bf16[24,6144]{1,0:T(8,128)(2,1)S(1)}, u32[]{:S(2)}, u32[]{:S(2)}) %collective-permute-start.12) | collective-permute-done | bytes 294944 | tf_op jit(solution)/shard_map/ppermute | solution.py:16
  31.2 3.0 %collective-permute-start.13 = (bf16[24,6144]{1,0:T(8,128)(2,1)S(1)}, bf16[24,6144]{1,0:T(8,128)(2,1)S(1)}, u32[]{:S(2)}, u32[]{:S(2)}) collective-permute-start(bf16[24,6144]{1,0:T(8,128)(2,1)S(1)} %collective-permute-done.11), channel_id=1, source_target_pairs={{0,6},{2,0},{4,2},{6,4},{1,7},{3,1},{5,3},{7,5},{8,14},{10,8},{12,... | collective-permute-start | bytes 884744 | tf_op jit(solution)/shard_map/ppermute | solution.py:16
  35.5 1.7 collective-permute-start.18
  38.6 3.7 %collective-permute-start.17 = (bf16[96,6144]{1,0:T(8,128)(2,1)S(1)}, bf16[96,6144]{1,0:T(8,128)(2,1)S(1)}, u32[]{:S(2)}, u32[]{:S(2)}) collective-permute-start(bf16[96,6144]{1,0:T(8,128)(2,1)S(1)} %pad_maximum_fusion.1.refs_0_), channel_id=1, source_target_pairs={{0,6},{2,0},{4,2},{6,4},{1,7},{3,1},{5,3},{7,5},{8,14},{10,8},{12,... | collective-permute-start | bytes 3538952 | tf_op jit(solution)/shard_map/ppermute | solution.py:16
  42.3 23.8 %collective-permute-done.4 = bf16[48,6144]{1,0:T(8,128)(2,1)S(1)} collective-permute-done((bf16[48,6144]{1,0:T(8,128)(2,1)S(1)}, bf16[48,6144]{1,0:T(8,128)(2,1)S(1)}, u32[]{:S(2)}, u32[]{:S(2)}) %collective-permute-start.4) | collective-permute-done | bytes 589856 | tf_op jit(solution)/shard_map/ppermute | solution.py:16
  68.9 2.8 %copy-done.4 = bf16[1,512,6144]{2,1,0:T(8,128)(2,1)S(1)} copy-done((bf16[1,512,6144]{2,1,0:T(8,128)(2,1)S(1)}, bf16[1,512,6144]{2,1,0:T(8,128)(2,1)}, u32[]{:S(2)}) %copy-start.4) | copy-done | bytes 6291480
  71.7 10.9 %experts.4 = (bf16[96,6144]{1,0:T(8,128)(2,1)S(1)}, bf16[96,6144]{1,0:T(8,128)(2,1)S(1)}, bf16[96,6144]{1,0:T(8,128)(2,1)S(1)}, bf16[96,6144]{1,0:T(8,128)(2,1)S(1)}) custom-call(bf16[96,6144]{1,0:T(8,128)(2,1)S(1)} %pad_maximum_fusion.1.refs_0_, bf16[96,6144]{1,0:T(8,128)(2,1)S(1)} %pad_maximum_fusion.refs_1_, ...), custom_call_target="tpu_custom_call" | custom-call | flops 7247757312 | bytes 28311552 | tf_op jit(solution)/shard_map/experts/pallas_call | solution.py:117
  83.0 11.5 %experts.5 = (bf16[96,6144]{1,0:T(8,128)(2,1)S(1)}, bf16[96,6144]{1,0:T(8,128)(2,1)}, bf16[96,6144]{1,0:T(8,128)(2,1)S(1)}, bf16[96,6144]{1,0:T(8,128)(2,1)S(1)}) custom-call(bf16[96,6144]{1,0:T(8,128)(2,1)S(1)} %collective-permute-done.16.refs_0_, bf16[96,6144]{1,0:T(8,128)(2,1)S(1)} %collective-permute-done.17.refs_1_, ...), custom_call_target="tpu_custom_call" | custom-call | flops 7247757312 | bytes 28311552 | tf_op jit(solution)/shard_map/experts/pallas_call | solution.py:117
  94.5 1.7 collective-permute-start.21
  96.2 1.6 collective-permute-done.5.refs_0_
  98.9 1.6 collective-permute-start.20
  100.4 1.7 collective-permute-start.22
  103.7 12.3 %experts.6 = (bf16[96,6144]{1,0:T(8,128)(2,1)}, bf16[96,6144]{1,0:T(8,128)(2,1)S(1)}, bf16[96,6144]{1,0:T(8,128)(2,1)S(1)}, bf16[96,6144]{1,0:T(8,128)(2,1)}) custom-call(bf16[96,6144]{1,0:T(8,128)(2,1)S(1)} %collective-permute-done.5.refs_0_, bf16[96,6144]{1,0:T(8,128)(2,1)S(1)} %collective-permute-done.6.refs_1_, ...), custom_call_target="tpu_custom_call" | custom-call | flops 7247757312 | bytes 28311552 | tf_op jit(solution)/shard_map/experts/pallas_call | solution.py:117
  116.0 2.9 %collective-permute-done.19.refs_0_ = bf16[96,6144]{1,0:T(8,128)(2,1)} collective-permute-done((bf16[96,6144]{1,0:T(8,128)(2,1)S(1)}, bf16[96,6144]{1,0:T(8,128)(2,1)}, u32[]{:S(2)}, u32[]{:S(2)}) %collective-permute-start.19) | collective-permute-done | bytes 1179680 | tf_op jit(solution)/shard_map/ppermute | solution.py:16
  119.1 4.3 %collective-permute-done.21.refs_2_ = bf16[96,6144]{1,0:T(8,128)(2,1)S(1)} collective-permute-done((bf16[96,6144]{1,0:T(8,128)(2,1)S(1)}, bf16[96,6144]{1,0:T(8,128)(2,1)S(1)}, u32[]{:S(2)}, u32[]{:S(2)}) %collective-permute-start.21) | collective-permute-done | bytes 1179680 | tf_op jit(solution)/shard_map/ppermute | solution.py:16
  125.4 3.2 %collective-permute-start.24 = (bf16[96,6144]{1,0:T(8,128)(2,1)}, bf16[96,6144]{1,0:T(8,128)(2,1)S(1)}, u32[]{:S(2)}, u32[]{:S(2)}) collective-permute-start(bf16[96,6144]{1,0:T(8,128)(2,1)} %get-tuple-element.120), channel_id=1, source_target_pairs={{0,6},{2,0},{4,2},{6,4},{1,7},{3,1},{5,3},{7,5},{8,14},{10,8},{12,... | collective-permute-start | bytes 3538952 | tf_op jit(solution)/shard_map/ppermute | solution.py:16
  128.6 1.7 collective-permute-start.26
  130.3 2.8 %copy-done.2 = bf16[1,6144,512]{2,1,0:T(8,128)(2,1)S(1)} copy-done((bf16[1,6144,512]{2,1,0:T(8,128)(2,1)S(1)}, bf16[1,6144,512]{2,1,0:T(8,128)(2,1)}, u32[]{:S(2)}) %copy-start.2) | copy-done | bytes 6291480
  133.1 2.8 %copy-done.3 = bf16[1,6144,512]{2,1,0:T(8,128)(2,1)S(1)} copy-done((bf16[1,6144,512]{2,1,0:T(8,128)(2,1)S(1)}, bf16[1,6144,512]{2,1,0:T(8,128)(2,1)}, u32[]{:S(2)}) %copy-start.3) | copy-done | bytes 6291480
  135.9 2.8 %copy-done.5 = bf16[1,512,6144]{2,1,0:T(8,128)(2,1)S(1)} copy-done((bf16[1,512,6144]{2,1,0:T(8,128)(2,1)S(1)}, bf16[1,512,6144]{2,1,0:T(8,128)(2,1)}, u32[]{:S(2)}) %copy-start.5) | copy-done | bytes 6291480
  141.2 11.6 %experts.7 = (bf16[96,6144]{1,0:T(8,128)(2,1)S(1)}, bf16[96,6144]{1,0:T(8,128)(2,1)S(1)}, bf16[96,6144]{1,0:T(8,128)(2,1)S(1)}, bf16[96,6144]{1,0:T(8,128)(2,1)S(1)}) custom-call(bf16[96,6144]{1,0:T(8,128)(2,1)} %collective-permute-done.19.refs_0_, bf16[96,6144]{1,0:T(8,128)(2,1)S(1)} %copy-done.11, bf16[96,6144]{1,0:T(8,128)(2,1)S(1)} %copy-done.9, ...), custom_call_target="tpu_custom_call" | custom-call | flops 7247757312 | bytes 28311552 | tf_op jit(solution)/shard_map/experts/pallas_call | solution.py:117
  155.0 1.7 collective-permute-start.29
  157.0 18.5 %collective-permute-done.27 = bf16[96,6144]{1,0:T(8,128)(2,1)S(1)} collective-permute-done((bf16[96,6144]{1,0:T(8,128)(2,1)S(1)}, bf16[96,6144]{1,0:T(8,128)(2,1)S(1)}, u32[]{:S(2)}, u32[]{:S(2)}) %collective-permute-start.27) | collective-permute-done | bytes 1179680 | tf_op jit(solution)/shard_map/ppermute | solution.py:16
  177.4 3.1 %collective-permute-start.34 = (bf16[96,6144]{1,0:T(8,128)(2,1)S(1)}, bf16[96,6144]{1,0:T(8,128)(2,1)S(1)}, u32[]{:S(2)}, u32[]{:S(2)}) collective-permute-start(bf16[96,6144]{1,0:T(8,128)(2,1)S(1)} %add_convert_fusion.8), channel_id=1, source_target_pairs={{0,6},{2,0},{4,2},{6,4},{1,7},{3,1},{5,3},{7,5},{8,14},{10,8},{12,... | collective-permute-start | bytes 3538952 | tf_op jit(solution)/shard_map/ppermute | solution.py:16
  180.6 1.7 collective-permute-start.36
  182.6 8.8 %collective-permute-done.31 = s32[128,2]{0,1:T(2,128)S(1)} collective-permute-done((s32[128,2]{0,1:T(2,128)S(1)}, s32[128,2]{0,1:T(2,128)S(1)}, u32[]{:S(2)}, u32[]{:S(2)}) %collective-permute-start.31) | collective-permute-done | bytes 1056 | tf_op jit(solution)/shard_map/ppermute | solution.py:40
  191.4 4.6 %collective-permute-done.32 = s32[128,2]{0,1:T(2,128)S(1)} collective-permute-done((s32[128,2]{0,1:T(2,128)S(1)}, s32[128,2]{0,1:T(2,128)S(1)}, u32[]{:S(2)}, u32[]{:S(2)}) %collective-permute-start.32) | collective-permute-done | bytes 1056 | tf_op jit(solution)/shard_map/ppermute | solution.py:40
  199.7 1.7 add_convert_fusion.3
  202.0 2.7 %collective-permute-start.38 = (bf16[48,6144]{1,0:T(8,128)(2,1)S(1)}, bf16[48,6144]{1,0:T(8,128)(2,1)S(1)}, u32[]{:S(2)}, u32[]{:S(2)}) collective-permute-start(bf16[48,6144]{1,0:T(8,128)(2,1)S(1)} %pad_maximum_fusion.5), channel_id=1, source_target_pairs={{0,6},{2,0},{4,2},{6,4},{1,7},{3,1},{5,3},{7,5},{8,14},{10,8},{12,... | collective-permute-start | bytes 1769480 | tf_op jit(solution)/shard_map/ppermute | solution.py:16
  206.3 1.7 add_convert_fusion.4
  208.0 6.5 %collective-permute-done.38 = bf16[48,6144]{1,0:T(8,128)(2,1)S(1)} collective-permute-done((bf16[48,6144]{1,0:T(8,128)(2,1)S(1)}, bf16[48,6144]{1,0:T(8,128)(2,1)S(1)}, u32[]{:S(2)}, u32[]{:S(2)}) %collective-permute-start.38) | collective-permute-done | bytes 589856 | tf_op jit(solution)/shard_map/ppermute | solution.py:16
  214.5 3.5 %collective-permute-done.39 = bf16[48,6144]{1,0:T(8,128)(2,1)S(1)} collective-permute-done((bf16[48,6144]{1,0:T(8,128)(2,1)S(1)}, bf16[48,6144]{1,0:T(8,128)(2,1)S(1)}, u32[]{:S(2)}, u32[]{:S(2)}) %collective-permute-start.39) | collective-permute-done | bytes 589856 | tf_op jit(solution)/shard_map/ppermute | solution.py:16
  221.5 3.2 %collective-permute-start.42 = (bf16[24,6144]{1,0:T(8,128)(2,1)}, bf16[24,6144]{1,0:T(8,128)(2,1)}, u32[]{:S(2)}, u32[]{:S(2)}) collective-permute-start(bf16[24,6144]{1,0:T(8,128)(2,1)} %add_convert_fusion.16), channel_id=1, source_target_pairs={{0,6},{2,0},{4,2},{6,4},{1,7},{3,1},{5,3},{7,5},{8,14},{10,8},{12,... | collective-permute-start | bytes 884744 | tf_op jit(solution)/shard_map/ppermute | solution.py:16
  228.1 1.6 collective-permute-done.43
  229.7 2.0 collective-permute-done.44
  236.8 4.4 %collective-permute-start.47 = (bf16[48,6144]{1,0:T(8,128)(2,1)S(1)}, bf16[48,6144]{1,0:T(8,128)(2,1)S(1)}, u32[]{:S(2)}, u32[]{:S(2)}) collective-permute-start(bf16[48,6144]{1,0:T(8,128)(2,1)S(1)} %pad_maximum_fusion.8), channel_id=1, source_target_pairs={{0,56},{8,48},{16,40},{24,32},{32,88},{40,80},{48,72},{56,64},{64,... | collective-permute-start | bytes 1769480 | tf_op jit(solution)/shard_map/ppermute | solution.py:45
  242.0 10.5 %collective-permute-done.46 = bf16[48,6144]{1,0:T(8,128)(2,1)S(1)} collective-permute-done((bf16[48,6144]{1,0:T(8,128)(2,1)S(1)}, bf16[48,6144]{1,0:T(8,128)(2,1)S(1)}, u32[]{:S(2)}, u32[]{:S(2)}) %collective-permute-start.46) | collective-permute-done | bytes 589856 | tf_op jit(solution)/shard_map/ppermute | solution.py:40
  253.0 2.2 collective-permute-done.47
  255.3 1.8 fusion
  (156 shorter events, 40.0 us)
Async XLA Ops:
  2.4 8.7 %collective-permute-start = (bf16[24,6144]{1,0:T(8,128)(2,1)S(1)}, bf16[24,6144]{1,0:T(8,128)(2,1)S(1)}, u32[]{:S(2)}, u32[]{:S(2)}) collective-permute-start(bf16[24,6144]{1,0:T(8,128)(2,1)S(1)} %get-tuple-element.173), channel_id=1, source_target_pairs={{0,8},{8,0},{1,9},{9,1},{2,10},{10,2},{3,11},{11,3},{4,12},{12,4},... | collective-permute-start | bytes 884744 | tf_op jit(solution)/shard_map/ppermute | solution.py:16
  4.2 21.8 %collective-permute-start.8 = (bf16[24,6144]{1,0:T(8,128)(2,1)S(1)}, bf16[24,6144]{1,0:T(8,128)(2,1)S(1)}, u32[]{:S(2)}, u32[]{:S(2)}) collective-permute-start(bf16[24,6144]{1,0:T(8,128)(2,1)S(1)} %get-tuple-element.172), channel_id=1, source_target_pairs={{0,6},{2,0},{4,2},{6,4},{1,7},{3,1},{5,3},{7,5},{8,14},{10,8},{12,... | collective-permute-start | bytes 884744 | tf_op jit(solution)/shard_map/ppermute | solution.py:16
  6.9 9.4 %collective-permute-start.7 = (bf16[24,6144]{1,0:T(8,128)(2,1)S(1)}, bf16[24,6144]{1,0:T(8,128)(2,1)S(1)}, u32[]{:S(2)}, u32[]{:S(2)}) collective-permute-start(bf16[24,6144]{1,0:T(8,128)(2,1)S(1)} %get-tuple-element.172), channel_id=1, source_target_pairs={{0,2},{2,4},{4,6},{6,0},{1,3},{3,5},{5,7},{7,1},{8,10},{10,12},{12... | collective-permute-start | bytes 884744 | tf_op jit(solution)/shard_map/ppermute | solution.py:16
  6.9 15.7 %collective-permute-start.2 = (bf16[48,6144]{1,0:T(8,128)(2,1)S(1)}, bf16[48,6144]{1,0:T(8,128)(2,1)S(1)}, u32[]{:S(2)}, u32[]{:S(2)}) collective-permute-start(bf16[48,6144]{1,0:T(8,128)(2,1)S(1)} %convolution_convert_fusion.1), channel_id=1, source_target_pairs={{0,24},{8,16},{16,8},{24,0},{1,25},{9,17},{17,9},{25,1},{2,26},{10... | collective-permute-start | bytes 1769480 | tf_op jit(solution)/shard_map/ppermute | solution.py:36
  11.2 24.3 %collective-permute-start.1 = (bf16[48,6144]{1,0:T(8,128)(2,1)S(1)}, bf16[48,6144]{1,0:T(8,128)(2,1)S(1)}, u32[]{:S(2)}, u32[]{:S(2)}) collective-permute-start(bf16[48,6144]{1,0:T(8,128)(2,1)S(1)} %pad_maximum_fusion.3), channel_id=1, source_target_pairs={{0,1},{1,0},{2,3},{3,2},{4,5},{5,4},{6,7},{7,6},{8,9},{9,8},{10,11... | collective-permute-start | bytes 1769480 | tf_op jit(solution)/shard_map/ppermute | solution.py:16
  16.3 11.6 %collective-permute-start.9 = (bf16[24,6144]{1,0:T(8,128)(2,1)S(1)}, bf16[24,6144]{1,0:T(8,128)(2,1)S(1)}, u32[]{:S(2)}, u32[]{:S(2)}) collective-permute-start(bf16[24,6144]{1,0:T(8,128)(2,1)S(1)} %collective-permute-done.7), channel_id=1, source_target_pairs={{0,2},{2,4},{4,6},{6,0},{1,3},{3,5},{5,7},{7,1},{8,10},{10,12},{12... | collective-permute-start | bytes 884744 | tf_op jit(solution)/shard_map/ppermute | solution.py:16
  22.7 8.5 %collective-permute-start.12 = (bf16[24,6144]{1,0:T(8,128)(2,1)S(1)}, bf16[24,6144]{1,0:T(8,128)(2,1)S(1)}, u32[]{:S(2)}, u32[]{:S(2)}) collective-permute-start(bf16[24,6144]{1,0:T(8,128)(2,1)S(1)} %get-tuple-element.174), channel_id=1, source_target_pairs={{0,2},{2,4},{4,6},{6,0},{1,3},{3,5},{5,7},{7,1},{8,10},{10,12},{12... | collective-permute-start | bytes 884744 | tf_op jit(solution)/shard_map/ppermute | solution.py:16
  23.2 8.0 %collective-permute-start.11 = (bf16[24,6144]{1,0:T(8,128)(2,1)S(1)}, bf16[24,6144]{1,0:T(8,128)(2,1)S(1)}, u32[]{:S(2)}, u32[]{:S(2)}) collective-permute-start(bf16[24,6144]{1,0:T(8,128)(2,1)S(1)} %get-tuple-element.174), channel_id=1, source_target_pairs={{0,6},{2,0},{4,2},{6,4},{1,7},{3,1},{5,3},{7,5},{8,14},{10,8},{12,... | collective-permute-start | bytes 884744 | tf_op jit(solution)/shard_map/ppermute | solution.py:16
  26.0 8.2 %collective-permute-start.3 = (bf16[24,6144]{1,0:T(8,128)(2,1)S(1)}, bf16[24,6144]{1,0:T(8,128)(2,1)S(1)}, u32[]{:S(2)}, u32[]{:S(2)}) collective-permute-start(bf16[24,6144]{1,0:T(8,128)(2,1)S(1)} %get-tuple-element.175), channel_id=1, source_target_pairs={{0,1},{1,0},{2,3},{3,2},{4,5},{5,4},{6,7},{7,6},{8,9},{9,8},{10,11... | collective-permute-start | bytes 884744 | tf_op jit(solution)/shard_map/ppermute | solution.py:16
  28.0 39.7 %collective-permute-start.10 = (bf16[96,6144]{1,0:T(8,128)(2,1)S(1)}, bf16[96,6144]{1,0:T(8,128)(2,1)S(1)}, u32[]{:S(2)}, u32[]{:S(2)}) collective-permute-start(bf16[96,6144]{1,0:T(8,128)(2,1)S(1)} %pad_maximum_fusion.refs_1_), channel_id=1, source_target_pairs={{0,8},{8,0},{1,9},{9,1},{2,10},{10,2},{3,11},{11,3},{4,12},{12,4},... | collective-permute-start | bytes 3538952 | tf_op jit(solution)/shard_map/ppermute | solution.py:16
  31.2 7.3 %collective-permute-start.13 = (bf16[24,6144]{1,0:T(8,128)(2,1)S(1)}, bf16[24,6144]{1,0:T(8,128)(2,1)S(1)}, u32[]{:S(2)}, u32[]{:S(2)}) collective-permute-start(bf16[24,6144]{1,0:T(8,128)(2,1)S(1)} %collective-permute-done.11), channel_id=1, source_target_pairs={{0,6},{2,0},{4,2},{6,4},{1,7},{3,1},{5,3},{7,5},{8,14},{10,8},{12,... | collective-permute-start | bytes 884744 | tf_op jit(solution)/shard_map/ppermute | solution.py:16
  34.2 31.9 %collective-permute-start.4 = (bf16[48,6144]{1,0:T(8,128)(2,1)S(1)}, bf16[48,6144]{1,0:T(8,128)(2,1)S(1)}, u32[]{:S(2)}, u32[]{:S(2)}) collective-permute-start(bf16[48,6144]{1,0:T(8,128)(2,1)S(1)} %pad_maximum_fusion.4), channel_id=1, source_target_pairs={{0,8},{8,0},{1,9},{9,1},{2,10},{10,2},{3,11},{11,3},{4,12},{12,4},... | collective-permute-start | bytes 1769480 | tf_op jit(solution)/shard_map/ppermute | solution.py:16
  34.6 33.7 %collective-permute-start.16 = (bf16[96,6144]{1,0:T(8,128)(2,1)S(1)}, bf16[96,6144]{1,0:T(8,128)(2,1)S(1)}, u32[]{:S(2)}, u32[]{:S(2)}) collective-permute-start(bf16[96,6144]{1,0:T(8,128)(2,1)S(1)} %pad_maximum_fusion.1.refs_0_), channel_id=1, source_target_pairs={{0,2},{2,4},{4,6},{6,0},{1,3},{3,5},{5,7},{7,1},{8,10},{10,12},{12... | collective-permute-start | bytes 3538952 | tf_op jit(solution)/shard_map/ppermute | solution.py:16
  35.5 33.1 %collective-permute-start.18 = (bf16[96,6144]{1,0:T(8,128)(2,1)S(1)}, bf16[96,6144]{1,0:T(8,128)(2,1)S(1)}, u32[]{:S(2)}, u32[]{:S(2)}) collective-permute-start(bf16[96,6144]{1,0:T(8,128)(2,1)S(1)} %pad_maximum_fusion.refs_1_), channel_id=1, source_target_pairs={{0,1},{1,0},{2,3},{3,2},{4,5},{5,4},{6,7},{7,6},{8,9},{9,8},{10,11... | collective-permute-start | bytes 3538952 | tf_op jit(solution)/shard_map/ppermute | solution.py:16
  38.6 44.0 %collective-permute-start.17 = (bf16[96,6144]{1,0:T(8,128)(2,1)S(1)}, bf16[96,6144]{1,0:T(8,128)(2,1)S(1)}, u32[]{:S(2)}, u32[]{:S(2)}) collective-permute-start(bf16[96,6144]{1,0:T(8,128)(2,1)S(1)} %pad_maximum_fusion.1.refs_0_), channel_id=1, source_target_pairs={{0,6},{2,0},{4,2},{6,4},{1,7},{3,1},{5,3},{7,5},{8,14},{10,8},{12,... | collective-permute-start | bytes 3538952 | tf_op jit(solution)/shard_map/ppermute | solution.py:16
  66.2 28.3 %collective-permute-start.6 = (bf16[96,6144]{1,0:T(8,128)(2,1)S(1)}, bf16[96,6144]{1,0:T(8,128)(2,1)S(1)}, u32[]{:S(2)}, u32[]{:S(2)}) collective-permute-start(bf16[96,6144]{1,0:T(8,128)(2,1)S(1)} %constant_dynamic-update-slice_fusion.refs_2_), channel_id=1, source_target_pairs={{0,6},{2,0},{4,2},{6,4},{1,7},{3,1},{5,3},{7,5},{8,14},{10,8},{12,... | collective-permute-start | bytes 3538952 | tf_op jit(solution)/shard_map/ppermute | solution.py:16
  67.7 30.1 %collective-permute-start.5 = (bf16[96,6144]{1,0:T(8,128)(2,1)S(1)}, bf16[96,6144]{1,0:T(8,128)(2,1)S(1)}, u32[]{:S(2)}, u32[]{:S(2)}) collective-permute-start(bf16[96,6144]{1,0:T(8,128)(2,1)S(1)} %constant_dynamic-update-slice_fusion.refs_2_), channel_id=1, source_target_pairs={{0,2},{2,4},{4,6},{6,0},{1,3},{3,5},{5,7},{7,1},{8,10},{10,12},{12... | collective-permute-start | bytes 3538952 | tf_op jit(solution)/shard_map/ppermute | solution.py:16
  68.3 29.6 %collective-permute-start.15 = (bf16[96,6144]{1,0:T(8,128)(2,1)S(1)}, bf16[96,6144]{1,0:T(8,128)(2,1)S(1)}, u32[]{:S(2)}, u32[]{:S(2)}) collective-permute-start(bf16[96,6144]{1,0:T(8,128)(2,1)S(1)} %pad_maximum_fusion.2.refs_2_), channel_id=1, source_target_pairs={{0,1},{1,0},{2,3},{3,2},{4,5},{5,4},{6,7},{7,6},{8,9},{9,8},{10,11... | collective-permute-start | bytes 3538952 | tf_op jit(solution)/shard_map/ppermute | solution.py:16
  68.6 30.3 %collective-permute-start.14 = (bf16[96,6144]{1,0:T(8,128)(2,1)S(1)}, bf16[96,6144]{1,0:T(8,128)(2,1)}, u32[]{:S(2)}, u32[]{:S(2)}) collective-permute-start(bf16[96,6144]{1,0:T(8,128)(2,1)S(1)} %pad_maximum_fusion.2.refs_2_), channel_id=1, source_target_pairs={{0,8},{8,0},{1,9},{9,1},{2,10},{10,2},{3,11},{11,3},{4,12},{12,4},... | collective-permute-start | bytes 3538952 | tf_op jit(solution)/shard_map/ppermute | solution.py:16
  82.6 36.3 %collective-permute-start.19 = (bf16[96,6144]{1,0:T(8,128)(2,1)S(1)}, bf16[96,6144]{1,0:T(8,128)(2,1)}, u32[]{:S(2)}, u32[]{:S(2)}) collective-permute-start(bf16[96,6144]{1,0:T(8,128)(2,1)S(1)} %collective-permute-done.16.refs_0_), channel_id=1, source_target_pairs={{0,2},{2,4},{4,6},{6,0},{1,3},{3,5},{5,7},{7,1},{8,10},{10,12},{12... | collective-permute-start | bytes 3538952 | tf_op jit(solution)/shard_map/ppermute | solution.py:16
  94.5 28.9 %collective-permute-start.21 = (bf16[96,6144]{1,0:T(8,128)(2,1)S(1)}, bf16[96,6144]{1,0:T(8,128)(2,1)S(1)}, u32[]{:S(2)}, u32[]{:S(2)}) collective-permute-start(bf16[96,6144]{1,0:T(8,128)(2,1)S(1)} %collective-permute-done.18.refs_3_), channel_id=1, source_target_pairs={{0,8},{8,0},{1,9},{9,1},{2,10},{10,2},{3,11},{11,3},{4,12},{12,4},... | collective-permute-start | bytes 3538952 | tf_op jit(solution)/shard_map/ppermute | solution.py:16
  98.9 25.6 %collective-permute-start.20 = (bf16[96,6144]{1,0:T(8,128)(2,1)S(1)}, bf16[96,6144]{1,0:T(8,128)(2,1)S(1)}, u32[]{:S(2)}, u32[]{:S(2)}) collective-permute-start(bf16[96,6144]{1,0:T(8,128)(2,1)S(1)} %collective-permute-done.6.refs_1_), channel_id=1, source_target_pairs={{0,6},{2,0},{4,2},{6,4},{1,7},{3,1},{5,3},{7,5},{8,14},{10,8},{12,... | collective-permute-start | bytes 3538952 | tf_op jit(solution)/shard_map/ppermute | solution.py:16
  100.4 25.0 %collective-permute-start.22 = (bf16[96,6144]{1,0:T(8,128)(2,1)}, bf16[96,6144]{1,0:T(8,128)(2,1)}, u32[]{:S(2)}, u32[]{:S(2)}) collective-permute-start(bf16[96,6144]{1,0:T(8,128)(2,1)} %collective-permute-done.14.refs_2_), channel_id=1, source_target_pairs={{0,1},{1,0},{2,3},{3,2},{4,5},{5,4},{6,7},{7,6},{8,9},{9,8},{10,11... | collective-permute-start | bytes 3538952 | tf_op jit(solution)/shard_map/ppermute | solution.py:16
  102.2 50.7 %collective-permute-start.25 = (bf16[96,6144]{1,0:T(8,128)(2,1)S(1)}, bf16[96,6144]{1,0:T(8,128)(2,1)}, u32[]{:S(2)}, u32[]{:S(2)}) collective-permute-start(bf16[96,6144]{1,0:T(8,128)(2,1)S(1)} %get-tuple-element.121), channel_id=1, source_target_pairs={{0,8},{8,0},{1,9},{9,1},{2,10},{10,2},{3,11},{11,3},{4,12},{12,4},... | collective-permute-start | bytes 3538952 | tf_op jit(solution)/shard_map/ppermute | solution.py:16
  118.9 34.0 %collective-permute-start.23 = (bf16[96,6144]{1,0:T(8,128)(2,1)}, bf16[96,6144]{1,0:T(8,128)(2,1)}, u32[]{:S(2)}, u32[]{:S(2)}) collective-permute-start(bf16[96,6144]{1,0:T(8,128)(2,1)} %get-tuple-element.119), channel_id=1, source_target_pairs={{0,2},{2,4},{4,6},{6,0},{1,3},{3,5},{5,7},{7,1},{8,10},{10,12},{12... | collective-permute-start | bytes 3538952 | tf_op jit(solution)/shard_map/ppermute | solution.py:16
  125.4 27.4 %collective-permute-start.24 = (bf16[96,6144]{1,0:T(8,128)(2,1)}, bf16[96,6144]{1,0:T(8,128)(2,1)S(1)}, u32[]{:S(2)}, u32[]{:S(2)}) collective-permute-start(bf16[96,6144]{1,0:T(8,128)(2,1)} %get-tuple-element.120), channel_id=1, source_target_pairs={{0,6},{2,0},{4,2},{6,4},{1,7},{3,1},{5,3},{7,5},{8,14},{10,8},{12,... | collective-permute-start | bytes 3538952 | tf_op jit(solution)/shard_map/ppermute | solution.py:16
  128.6 24.3 %collective-permute-start.26 = (bf16[96,6144]{1,0:T(8,128)(2,1)}, bf16[96,6144]{1,0:T(8,128)(2,1)S(1)}, u32[]{:S(2)}, u32[]{:S(2)}) collective-permute-start(bf16[96,6144]{1,0:T(8,128)(2,1)} %get-tuple-element.122), channel_id=1, source_target_pairs={{0,1},{1,0},{2,3},{3,2},{4,5},{5,4},{6,7},{7,6},{8,9},{9,8},{10,11... | collective-permute-start | bytes 3538952 | tf_op jit(solution)/shard_map/ppermute | solution.py:16
  152.9 22.6 %collective-permute-start.27 = (bf16[96,6144]{1,0:T(8,128)(2,1)S(1)}, bf16[96,6144]{1,0:T(8,128)(2,1)S(1)}, u32[]{:S(2)}, u32[]{:S(2)}) collective-permute-start(bf16[96,6144]{1,0:T(8,128)(2,1)S(1)} %get-tuple-element.123), channel_id=1, source_target_pairs={{0,6},{2,0},{4,2},{6,4},{1,7},{3,1},{5,3},{7,5},{8,14},{10,8},{12,... | collective-permute-start | bytes 3538952 | tf_op jit(solution)/shard_map/ppermute | solution.py:16
  154.4 21.4 %collective-permute-start.28 = (bf16[96,6144]{1,0:T(8,128)(2,1)S(1)}, bf16[96,6144]{1,0:T(8,128)(2,1)S(1)}, u32[]{:S(2)}, u32[]{:S(2)}) collective-permute-start(bf16[96,6144]{1,0:T(8,128)(2,1)S(1)} %get-tuple-element.125), channel_id=1, source_target_pairs={{0,2},{2,4},{4,6},{6,0},{1,3},{3,5},{5,7},{7,1},{8,10},{10,12},{12... | collective-permute-start | bytes 3538952 | tf_op jit(solution)/shard_map/ppermute | solution.py:16
  155.0 21.1 %collective-permute-start.29 = (bf16[96,6144]{1,0:T(8,128)(2,1)S(1)}, bf16[96,6144]{1,0:T(8,128)(2,1)S(1)}, u32[]{:S(2)}, u32[]{:S(2)}) collective-permute-start(bf16[96,6144]{1,0:T(8,128)(2,1)S(1)} %get-tuple-element.127), channel_id=1, source_target_pairs={{0,8},{8,0},{1,9},{9,1},{2,10},{10,2},{3,11},{11,3},{4,12},{12,4},... | collective-permute-start | bytes 3538952 | tf_op jit(solution)/shard_map/ppermute | solution.py:16
  156.7 20.4 %collective-permute-start.30 = (bf16[96,6144]{1,0:T(8,128)(2,1)S(1)}, bf16[96,6144]{1,0:T(8,128)(2,1)S(1)}, u32[]{:S(2)}, u32[]{:S(2)}) collective-permute-start(bf16[96,6144]{1,0:T(8,128)(2,1)S(1)} %get-tuple-element.129), channel_id=1, source_target_pairs={{0,1},{1,0},{2,3},{3,2},{4,5},{5,4},{6,7},{7,6},{8,9},{9,8},{10,11... | collective-permute-start | bytes 3538952 | tf_op jit(solution)/shard_map/ppermute | solution.py:16
  177.4 19.3 %collective-permute-start.34 = (bf16[96,6144]{1,0:T(8,128)(2,1)S(1)}, bf16[96,6144]{1,0:T(8,128)(2,1)S(1)}, u32[]{:S(2)}, u32[]{:S(2)}) collective-permute-start(bf16[96,6144]{1,0:T(8,128)(2,1)S(1)} %add_convert_fusion.8), channel_id=1, source_target_pairs={{0,6},{2,0},{4,2},{6,4},{1,7},{3,1},{5,3},{7,5},{8,14},{10,8},{12,... | collective-permute-start | bytes 3538952 | tf_op jit(solution)/shard_map/ppermute | solution.py:16
  180.6 17.4 %collective-permute-start.35 = (bf16[96,6144]{1,0:T(8,128)(2,1)S(1)}, bf16[96,6144]{1,0:T(8,128)(2,1)S(1)}, u32[]{:S(2)}, u32[]{:S(2)}) collective-permute-start(bf16[96,6144]{1,0:T(8,128)(2,1)S(1)} %add_convert_fusion.7), channel_id=1, source_target_pairs={{0,2},{2,4},{4,6},{6,0},{1,3},{3,5},{5,7},{7,1},{8,10},{10,12},{12... | collective-permute-start | bytes 3538952 | tf_op jit(solution)/shard_map/ppermute | solution.py:16
  180.6 17.4 %collective-permute-start.36 = (bf16[96,6144]{1,0:T(8,128)(2,1)S(1)}, bf16[96,6144]{1,0:T(8,128)(2,1)S(1)}, u32[]{:S(2)}, u32[]{:S(2)}) collective-permute-start(bf16[96,6144]{1,0:T(8,128)(2,1)S(1)} %add_convert_fusion.5), channel_id=1, source_target_pairs={{0,8},{8,0},{1,9},{9,1},{2,10},{10,2},{3,11},{11,3},{4,12},{12,4},... | collective-permute-start | bytes 3538952 | tf_op jit(solution)/shard_map/ppermute | solution.py:16
  182.3 16.9 %collective-permute-start.37 = (bf16[96,6144]{1,0:T(8,128)(2,1)S(1)}, bf16[96,6144]{1,0:T(8,128)(2,1)S(1)}, u32[]{:S(2)}, u32[]{:S(2)}) collective-permute-start(bf16[96,6144]{1,0:T(8,128)(2,1)S(1)} %add_convert_fusion.6), channel_id=1, source_target_pairs={{0,1},{1,0},{2,3},{3,2},{4,5},{5,4},{6,7},{7,6},{8,9},{9,8},{10,11... | collective-permute-start | bytes 3538952 | tf_op jit(solution)/shard_map/ppermute | solution.py:16
  182.6 8.8 %collective-permute-start.31 = (s32[128,2]{0,1:T(2,128)S(1)}, s32[128,2]{0,1:T(2,128)S(1)}, u32[]{:S(2)}, u32[]{:S(2)}) collective-permute-start(s32[128,2]{0,1:T(2,128)S(1)} %bitcast.43), channel_id=1, source_target_pairs={{0,32},{32,64},{64,96},{96,0},{1,33},{33,65},{65,97},{97,1},{2,34}... | collective-permute-start | bytes 3080 | tf_op jit(solution)/shard_map/ppermute | solution.py:40
  191.4 4.6 %collective-permute-start.32 = (s32[128,2]{0,1:T(2,128)S(1)}, s32[128,2]{0,1:T(2,128)S(1)}, u32[]{:S(2)}, u32[]{:S(2)}) collective-permute-start(s32[128,2]{0,1:T(2,128)S(1)} %bitcast.44), channel_id=1, source_target_pairs={{0,32},{32,64},{64,96},{96,0},{1,33},{33,65},{65,97},{97,1},{2,34}... | collective-permute-start | bytes 3080 | tf_op jit(solution)/shard_map/ppermute | solution.py:40
  196.0 30.3 %collective-permute-start.33 = (f32[128,2]{0,1:T(2,128)S(1)}, f32[128,2]{0,1:T(2,128)S(1)}, u32[]{:S(2)}, u32[]{:S(2)}) collective-permute-start(f32[128,2]{0,1:T(2,128)S(1)} %bitcast.45), channel_id=1, source_target_pairs={{0,32},{32,64},{64,96},{96,0},{1,33},{33,65},{65,97},{97,1},{2,34}... | collective-permute-start | bytes 3080 | tf_op jit(solution)/shard_map/ppermute | solution.py:40
  202.0 12.5 %collective-permute-start.38 = (bf16[48,6144]{1,0:T(8,128)(2,1)S(1)}, bf16[48,6144]{1,0:T(8,128)(2,1)S(1)}, u32[]{:S(2)}, u32[]{:S(2)}) collective-permute-start(bf16[48,6144]{1,0:T(8,128)(2,1)S(1)} %pad_maximum_fusion.5), channel_id=1, source_target_pairs={{0,6},{2,0},{4,2},{6,4},{1,7},{3,1},{5,3},{7,5},{8,14},{10,8},{12,... | collective-permute-start | bytes 1769480 | tf_op jit(solution)/shard_map/ppermute | solution.py:16
  204.7 13.3 %collective-permute-start.39 = (bf16[48,6144]{1,0:T(8,128)(2,1)S(1)}, bf16[48,6144]{1,0:T(8,128)(2,1)S(1)}, u32[]{:S(2)}, u32[]{:S(2)}) collective-permute-start(bf16[48,6144]{1,0:T(8,128)(2,1)S(1)} %pad_maximum_fusion.6), channel_id=1, source_target_pairs={{0,2},{2,4},{4,6},{6,0},{1,3},{3,5},{5,7},{7,1},{8,10},{10,12},{12... | collective-permute-start | bytes 1769480 | tf_op jit(solution)/shard_map/ppermute | solution.py:16
  204.8 13.2 %collective-permute-start.41 = (bf16[48,6144]{1,0:T(8,128)(2,1)S(1)}, bf16[48,6144]{1,0:T(8,128)(2,1)S(1)}, u32[]{:S(2)}, u32[]{:S(2)}) collective-permute-start(bf16[48,6144]{1,0:T(8,128)(2,1)S(1)} %get-tuple-element.166), channel_id=1, source_target_pairs={{0,8},{8,0},{1,9},{9,1},{2,10},{10,2},{3,11},{11,3},{4,12},{12,4},... | collective-permute-start | bytes 1769480 | tf_op jit(solution)/shard_map/ppermute | solution.py:16
  205.1 12.9 %collective-permute-start.40 = (bf16[48,6144]{1,0:T(8,128)(2,1)S(1)}, bf16[48,6144]{1,0:T(8,128)(2,1)S(1)}, u32[]{:S(2)}, u32[]{:S(2)}) collective-permute-start(bf16[48,6144]{1,0:T(8,128)(2,1)S(1)} %get-tuple-element.167), channel_id=1, source_target_pairs={{0,1},{1,0},{2,3},{3,2},{4,5},{5,4},{6,7},{7,6},{8,9},{9,8},{10,11... | collective-permute-start | bytes 1769480 | tf_op jit(solution)/shard_map/ppermute | solution.py:16
  221.5 8.2 %collective-permute-start.43 = (bf16[24,6144]{1,0:T(8,128)(2,1)}, bf16[24,6144]{1,0:T(8,128)(2,1)}, u32[]{:S(2)}, u32[]{:S(2)}) collective-permute-start(bf16[24,6144]{1,0:T(8,128)(2,1)} %add_convert_fusion.15), channel_id=1, source_target_pairs={{0,2},{2,4},{4,6},{6,0},{1,3},{3,5},{5,7},{7,1},{8,10},{10,12},{12... | collective-permute-start | bytes 884744 | tf_op jit(solution)/shard_map/ppermute | solution.py:16
  221.5 8.2 %collective-permute-start.42 = (bf16[24,6144]{1,0:T(8,128)(2,1)}, bf16[24,6144]{1,0:T(8,128)(2,1)}, u32[]{:S(2)}, u32[]{:S(2)}) collective-permute-start(bf16[24,6144]{1,0:T(8,128)(2,1)} %add_convert_fusion.16), channel_id=1, source_target_pairs={{0,6},{2,0},{4,2},{6,4},{1,7},{3,1},{5,3},{7,5},{8,14},{10,8},{12,... | collective-permute-start | bytes 884744 | tf_op jit(solution)/shard_map/ppermute | solution.py:16
  224.7 7.0 %collective-permute-start.44 = (bf16[24,6144]{1,0:T(8,128)(2,1)}, bf16[24,6144]{1,0:T(8,128)(2,1)}, u32[]{:S(2)}, u32[]{:S(2)}) collective-permute-start(bf16[24,6144]{1,0:T(8,128)(2,1)} %slice.110), channel_id=1, source_target_pairs={{0,8},{8,0},{1,9},{9,1},{2,10},{10,2},{3,11},{11,3},{4,12},{12,4},... | collective-permute-start | bytes 884744 | tf_op jit(solution)/shard_map/ppermute | solution.py:16
  225.2 7.0 %collective-permute-start.45 = (bf16[24,6144]{1,0:T(8,128)(2,1)}, bf16[24,6144]{1,0:T(8,128)(2,1)}, u32[]{:S(2)}, u32[]{:S(2)}) collective-permute-start(bf16[24,6144]{1,0:T(8,128)(2,1)} %slice.112), channel_id=1, source_target_pairs={{0,1},{1,0},{2,3},{3,2},{4,5},{5,4},{6,7},{7,6},{8,9},{9,8},{10,11... | collective-permute-start | bytes 884744 | tf_op jit(solution)/shard_map/ppermute | solution.py:16
  236.7 15.8 %collective-permute-start.46 = (bf16[48,6144]{1,0:T(8,128)(2,1)S(1)}, bf16[48,6144]{1,0:T(8,128)(2,1)S(1)}, u32[]{:S(2)}, u32[]{:S(2)}) collective-permute-start(bf16[48,6144]{1,0:T(8,128)(2,1)S(1)} %pad_maximum_fusion.7), channel_id=1, source_target_pairs={{0,32},{32,64},{64,96},{96,0},{1,33},{33,65},{65,97},{97,1},{2,34}... | collective-permute-start | bytes 1769480 | tf_op jit(solution)/shard_map/ppermute | solution.py:40
  236.8 18.5 %collective-permute-start.47 = (bf16[48,6144]{1,0:T(8,128)(2,1)S(1)}, bf16[48,6144]{1,0:T(8,128)(2,1)S(1)}, u32[]{:S(2)}, u32[]{:S(2)}) collective-permute-start(bf16[48,6144]{1,0:T(8,128)(2,1)S(1)} %pad_maximum_fusion.8), channel_id=1, source_target_pairs={{0,56},{8,48},{16,40},{24,32},{32,88},{40,80},{48,72},{56,64},{64,... | collective-permute-start | bytes 1769480 | tf_op jit(solution)/shard_map/ppermute | solution.py:45
  (23 other events, 297.2 us)

commit v4 on v3

v4 whole, which is shorter than its diff:
```python
import jax
import jax.numpy as jnp
from jax import lax
from jax.experimental import pallas as pl
from jax.experimental.pallas import tpu as pltpu
from jax.sharding import Mesh, PartitionSpec as P

CAP = 48
PIECE = 24
F32 = jnp.float32
BF16 = jnp.bfloat16


def shift(value, axis, by):
    n = lax.axis_size(axis)
    return lax.ppermute(value, axis, [(i, (i + by) % n) for i in range(n)])


def right(value):
    return shift(value, "x", 1)


def left(value):
    return shift(value, "x", -1)


def over_y(value):
    return shift(value, "yl", 1)


def over_z(value):
    return shift(value, "zl", 1)


def to_partner(value):
    return lax.ppermute(value, ("yh", "yl"), [(y, 3 - y) for y in range(4)])


def to_next_section(value):
    return lax.ppermute(value, ("zh", "core"), [(s, (s + 1) % 4) for s in range(4)])


def to_owner(value):
    pairs = [(s * 2 + z, (s + 1) % 4 * 2 + 1 - z) for s in range(4) for z in range(2)]
    return lax.ppermute(value, ("zh", "core", "zl"), pairs)


def to_owner_across(value):
    pairs = [
        ((s * 4 + y) * 2 + z, ((s + 1) % 4 * 4 + 3 - y) * 2 + 1 - z)
        for s in range(4)
        for y in range(4)
        for z in range(2)
    ]
    return lax.ppermute(value, ("zh", "core", "yh", "yl", "zl"), pairs)


def together(*values):
    return lax.optimization_barrier(values)


def join(*pieces):
    return jnp.concatenate(pieces)


def add(*terms):
    total = terms[0].astype(F32)
    for term in terms[1:]:
        total = total + term.astype(F32)
    return total.astype(BF16)


def split(rows, count):
    size = rows.shape[0] // count
    return [rows[i * size : (i + 1) * size] for i in range(count)]


TILE = 1536


def experts_kernel(*refs):
    count = (len(refs) - 6) // 2
    rows, (w_gate, w_up, w_down), rest = refs[:count], refs[count : count + 3], refs[count + 3 :]
    outs, (gate, up, hidden) = rest[:count], rest[count:]
    step = pl.program_id(0)
    half = pl.num_programs(0) // 2

    @pl.when(step < half)
    def _():
        block = jnp.concatenate([r[...] for r in rows])
        gate_part = jnp.dot(block, w_gate[...], preferred_element_type=F32)
        up_part = jnp.dot(block, w_up[...], preferred_element_type=F32)

        @pl.when(step == 0)
        def _():
            gate[...] = gate_part
            up[...] = up_part

        @pl.when(step > 0)
        def _():
            gate[...] += gate_part
            up[...] += up_part

    @pl.when(step >= half)
    def _():
        @pl.when(step == half)
        def _():
            v = gate[...]
            hidden[...] = (v / (1.0 + jnp.exp(-v)) * up[...]).astype(BF16)

        out = jnp.dot(hidden[...], w_down[...], preferred_element_type=F32).astype(BF16)
        start = 0
        for o in outs:
            o[...] = out[start : start + o.shape[0]]
            start += o.shape[0]


def experts(pieces, gate_matrix, up_matrix, down_matrix):
    sizes, width = [p.shape[0] for p in pieces], pieces[0].shape[1]
    units = gate_matrix.shape[1]
    half = width // TILE
    first = lambda i: jnp.minimum(i, half - 1)
    second = lambda i: jnp.maximum(i - half, 0)
    rows_in = [pl.BlockSpec((n, TILE), lambda i: (0, first(i))) for n in sizes]
    rows_out = [pl.BlockSpec((n, TILE), lambda i: (0, second(i))) for n in sizes]
    into = pl.BlockSpec((TILE, units), lambda i: (first(i), 0))
    out_of = pl.BlockSpec((units, TILE), lambda i: (0, second(i)))
    total = sum(sizes)
    return pl.pallas_call(
        experts_kernel,
        grid=(2 * half,),
        in_specs=rows_in + [into, into, out_of],
        out_specs=rows_out,
        out_shape=[jax.ShapeDtypeStruct((n, width), BF16) for n in sizes],
        scratch_shapes=[
            pltpu.VMEM((total, units), F32),
            pltpu.VMEM((total, units), F32),
            pltpu.VMEM((total, units), BF16),
        ],
        compiler_params=pltpu.CompilerParams(
            dimension_semantics=("arbitrary",), vmem_limit_bytes=24 << 20
        ),
        cost_estimate=pl.CostEstimate(
            flops=6 * total * width * units,
            transcendentals=total * units,
            bytes_accessed=6 * width * units + 4 * total * width,
        ),
        name="experts",
    )(*pieces, gate_matrix, up_matrix, down_matrix)


def slots(ids, keep, expert):
    chosen = (ids == expert) & (keep == 1)
    picked = jnp.any(chosen, axis=1)
    position = jnp.cumsum(picked.astype(jnp.int32)) - 1
    return chosen, picked, position


def body(states, expert_ids, gate_values, keep_mask, w_gate, w_up, w_down):
    tokens = states[0]
    ids, gates, keep = expert_ids[0], gate_values[0], keep_mask[0]
    matrices = (w_gate[0], w_up[0], w_down[0])
    mine = lax.axis_index("yh")
    other = 1 - mine

    def compact(expert, tokens):
        _, picked, position = slots(ids, keep, expert)
        table = (position[None] == jnp.arange(CAP, dtype=jnp.int32)[:, None]) & picked[None]
        return jnp.dot(table.astype(BF16), tokens, preferred_element_type=F32).astype(BF16)

    others, tokens = together(compact(other, tokens), tokens)
    partner = to_partner(others)
    own = compact(mine, tokens)

    a1, b = split(own, 2)
    a1_y, b_behind, b_ahead = over_y(a1), right(b), left(b)
    a1_near = join(a1, a1_y)
    a1_far, b_opposite = over_z(a1_near), right(b_behind)
    a1_near_left, a1_near_right = right(a1_near), left(a1_near)
    b_ring = join(b, b_behind, b_ahead, b_opposite)
    b_y = over_y(b_ring)

    a2, g = split(partner, 2)
    a2_z, g_behind, g_ahead = over_z(a2), left(g), right(g)
    g_behind, g_ahead, b_ring_late, a1_far_late = together(g_behind, g_ahead, b_ring, a1_far)
    g_opposite = left(g_behind)
    b_z = over_z(b_ring_late)
    a1_far_left, a1_far_right = right(a1_far_late), left(a1_far_late)
    a2_near = join(a2, a2_z)
    a2_far = over_y(a2_near)
    g_opposite, a2_near_late = together(g_opposite, a2_near)
    a2_near_left, a2_near_right = right(a2_near_late), left(a2_near_late)
    g_ring = join(g, g_behind, g_ahead, g_opposite)
    b_y, g_ring = together(b_y, g_ring)
    g_y, g_z = over_y(g_ring), over_z(g_ring)

    a1_near, a1_far, b_ring, b_y, p_near_left, p_near_right = experts(
        [a1_near, a1_far, b_ring, b_y, a1_near_left, a1_near_right], *matrices
    )
    a1_near_left, a1_far_right, b_z, a2_far, a1_near = together(
        a1_near_left, a1_far_right, b_z, a2_far, a1_near
    )
    a1_near_opposite, a1_far_opposite = right(a1_near_left), left(a1_far_right)
    a2_far_left, a2_far_right = right(a2_far), left(a2_far)
    b_yz = over_y(b_z)
    a1_near_left, a1_near_right = p_near_left, p_near_right
    g_ring, a2_near, a2_far, a1_far_left, p_far_right, b_z = experts(
        [g_ring, a2_near, a2_far, a1_far_left, a1_far_right, b_z], *matrices
    )
    a1_far_right = p_far_right
    a2_near_left, a2_far_right, g_y, g_z, a1_near_opposite, a1_far_opposite, g_ring = together(
        a2_near_left, a2_far_right, g_y, g_z, a1_near_opposite, a1_far_opposite, g_ring
    )
    a2_near_opposite, a2_far_opposite = right(a2_near_left), left(a2_far_right)
    g_zy = over_z(g_y)
    a2_near_left, a2_near_right, a1_near_opposite, a1_far_opposite, g_y, g_z = experts(
        [a2_near_left, a2_near_right, a1_near_opposite, a1_far_opposite, g_y, g_z], *matrices
    )
    last = together(a2_far_left, a2_far_right, a2_near_opposite, a2_far_opposite, b_yz, g_zy, g_y)
    g_y = last[-1]

    a1_near_opposite, a1_far_opposite, a1_near_right, a1_far_left, b_y, g_own = together(
        left(a1_near_opposite), right(a1_far_opposite), right(a1_near_right), left(a1_far_left),
        over_y(b_y), over_z(g_ring),
    )
    a2_far_left, a2_far_right, a2_near_opposite, a2_far_opposite, b_yz, g_zy = experts(
        list(last[:-1]), *matrices
    )
    (
        a1_near_opposite, a1_far_opposite, a1_near_right, a1_far_left, b_y, g_own, g_y,
        a2_near_opposite, a2_far_opposite, b_yz,
    ) = together(
        a1_near_opposite, a1_far_opposite, a1_near_right, a1_far_left, b_y, g_own, g_y,
        a2_near_opposite, a2_far_opposite, b_yz,
    )
    g_y_back, b_yz_back = over_z(g_y), over_y(b_yz)
    a2_near_opposite, a2_far_opposite = left(a2_near_opposite), right(a2_far_opposite)
    a1_near_left = left(add(a1_near_left, a1_near_opposite))
    a1_far_right = right(add(a1_far_right, a1_far_opposite))
    b_ring = add(b_ring, b_y)
    g_y_back, b_yz_back, a2_near_opposite, a2_far_opposite, b_ring, ids, gates, keep = together(
        g_y_back, b_yz_back, a2_near_opposite, a2_far_opposite, b_ring, ids, gates, keep
    )

    b_own, g_zy_back = over_z(b_ring), over_y(add(g_zy, g_y_back))
    a2_near_right, a2_far_left = right(a2_near_right), left(a2_far_left)
    a2_near_left = left(add(a2_near_left, a2_near_opposite))
    a2_far_right = right(add(a2_far_right, a2_far_opposite))
    ids, gates, keep = (to_next_section(v) for v in (ids, gates, keep))
    a1_near = add(a1_near, a1_near_left, a1_near_right)
    (
        a1_near, a1_far, b_z, b_yz_back, b_own, g_z, g_own, g_zy_back,
        a2_near_left, a2_near_right, a2_far_left, a2_far_right,
    ) = together(
        a1_near, add(a1_far, a1_far_left, a1_far_right), b_z, b_yz_back, b_own, g_z, g_own, g_zy_back,
        a2_near_left, a2_near_right, a2_far_left, a2_far_right,
    )

    def part(terms, i, count):
        return [t[i * t.shape[0] // count : (i + 1) * t.shape[0] // count] for t in terms]

    b_terms, g_terms = (b_z, b_yz_back, b_own), (g_z, g_own, g_zy_back)
    a2_near_terms = (a2_near, a2_near_left, a2_near_right)
    got = together(
        left(join(add(*part(b_terms, 3, 4)), add(*part(g_terms, 2, 4)))),
        right(join(add(*part(g_terms, 3, 4)), add(*part(b_terms, 2, 4)))),
        over_z(a1_near),
        over_y(add(a2_far, a2_far_left, a2_far_right)),
    )
    (b_behind_back, g_back), (g_behind_back, b_back) = split(got[0], 2), split(got[1], 2)
    a1_terms, a2_terms = (a1_far, got[2]), (*a2_near_terms, got[3])
    ends = together(
        left(add(*part(b_terms, 1, 4), b_behind_back)),
        right(add(*part(g_terms, 1, 4), g_behind_back)),
        over_y(add(*part(a1_terms, 1, 2))),
        over_z(add(*part(a2_terms, 0, 2))),
    )

    own_done = to_owner(
        join(add(*part(a1_terms, 0, 2), ends[2]), add(*part(b_terms, 0, 4), b_back, ends[0]))
    )
    other_done = to_owner_across(
        join(add(*part(a2_terms, 1, 2), ends[3]), add(*part(g_terms, 0, 4), g_back, ends[1]))
    )

    def contribution(expert, done):
        chosen, picked, position = slots(ids, keep, expert)
        weight = jnp.sum(jnp.where(chosen, gates, 0.0), axis=1)
        table = (position[:, None] == jnp.arange(CAP, dtype=jnp.int32)[None]) & picked[:, None]
        rows = jnp.dot(table.astype(BF16), done, preferred_element_type=F32)
        return weight[:, None] * rows

    mixed = contribution(mine, own_done) + contribution(other, other_done)
    return mixed.astype(BF16)[None]


def solution(mesh):
    shape = (2, 2, 2, 2, 4, 2)
    fine = Mesh(mesh.devices.reshape(shape), ("zh", "core", "yh", "yl", "x", "zl"))
    section, ep = ("zh", "core"), ("yh", "yl", "x", "zl")
    rows = P(section, ep, None)
    columns = P(section, None, ep)
    return jax.shard_map(
        body,
        mesh=fine,
        in_specs=(rows, rows, rows, rows, columns, columns, rows),
        out_specs=rows,
        check_vma=False,
    )
```

time: 259 us -> 333 us (1.29)
  waiting for transfers between devices: 111 us -> 158 us
  starting transfers between devices: 59.9 us -> 75.1 us
  local copies, waits for them, and re-layouts: 20.3 us -> 31.9 us
    ppermute x42 -> x54, waiting for transfers between devices: 78.6 us -> 126 us  [shift(): return lax.ppermute(value, axis, [(i, (i + by) % n) for i in range(n)])]
    ppermute x42 -> x54, starting transfers between devices: 53.3 us -> 72.3 us  [shift(): return lax.ppermute(value, axis, [(i, (i + by) % n) for i in range(n)])]
    ppermute x4 -> x3, waiting for transfers between devices: 23.8 us -> 9.07 us  [to_next_section(): lax.ppermute(value, ('zh', 'core'), [(s, (s + 1) % 4) for s in range(4)])]
    ppermute x1 -> x2, waiting for transfers between devices: 2.25 us -> 16.7 us  [the longest x1 13.5 us: to_owner(): return lax.ppermute(value, ('zh', 'core', 'zl'), pairs)]
    unnamed x47 -> x94, local copies, waits for them, and re-layouts: 18.1 us -> 31.4 us
    ppermute x1 -> x2, starting transfers between devices: 4.37 us -> 0.65 us  [the longest x1 0.57 us: to_owner(): return lax.ppermute(value, ('zh', 'core', 'zl'), pairs)]
    convert_element_type x15 -> x19, other arithmetic: 11.7 us -> 14.2 us  [add(): return total.astype(BF16)]
  transfers between devices with their start and end apart: 48 -> 60, of which waited for: 23 -> 28; matrix products, arithmetic and copies ran while one was open for 5% -> 3% of each run, Pallas kernels for 18% -> 14%
where the time goes in v4:
time: 333 us; the launch traced here: 332 us
  waiting for transfers between devices  158 us (47%)
  starting transfers between devices  75.1 us (23%)
  Pallas kernels  45.6 us (14%)
  local copies, waits for them, and re-layouts  31.9 us (10%)
  other arithmetic  18.2 us (5%)
    ppermute x54, waiting for transfers between devices, shift(): return lax.ppermute(value, axis, [(i, (i + by) % n) for i in range(n)])  126 us
    ppermute x54, starting transfers between devices, shift(): return lax.ppermute(value, axis, [(i, (i + by) % n) for i in range(n)])  72.3 us
    pallas_call x4, Pallas kernels, experts(): pl.pallas_call(experts_kernel, grid=(2 * half,), in_specs=rows_in + [into...  45.6 us
    unnamed x94, local copies, waits for them, and re-layouts  31.4 us
    convert_element_type x19, other arithmetic, add(): return total.astype(BF16)  14.2 us
    ppermute x1, waiting for transfers between devices, to_owner(): return lax.ppermute(value, ('zh', 'core', 'zl'), pairs)  13.5 us
    ppermute x3, waiting for transfers between devices, to_next_section(): lax.ppermute(value, ('zh', 'core'), [(s, (s + 1) % 4) for s in range(4)])  9.07 us
  transfers between devices with their start and end apart: 60, of which 28 were waited for; matrix products, arithmetic and copies ran while one was open for 3% of the time, Pallas kernels for 14%

profile of v4, /device:TPU:0, one launch (start us, length us, event | category | flops | bytes accessed | tf_op | source)
XLA Modules:
  0.0 332.3 jit_solution(18176770556607436393)
XLA Ops:
  4.2 2.8 collective-permute-start.4
  6.9 2.2 collective-permute-start
  9.1 2.1 collective-permute-done.6
  11.2 3.0 collective-permute-start.16
  16.3 6.3 %collective-permute-done = bf16[48,6144]{1,0:T(8,128)(2,1)S(1)} collective-permute-done((bf16[48,6144]{1,0:T(8,128)(2,1)S(1)}, bf16[48,6144]{1,0:T(8,128)(2,1)S(1)}, u32[]{:S(2)}, u32[]{:S(2)}) %collective-permute-start) | collective-permute-done | bytes 589856 | tf_op jit(solution)/shard_map/ppermute | solution.py:36
  23.2 2.8 collective-permute-start.1
  30.0 2.4 collective-permute-done.2
  33.4 2.5 collective-permute-start.8
  36.0 7.4 %collective-permute-done.8 = bf16[24,6144]{1,0:T(8,128)(2,1)S(1)} collective-permute-done((bf16[24,6144]{1,0:T(8,128)(2,1)S(1)}, bf16[24,6144]{1,0:T(8,128)(2,1)S(1)}, u32[]{:S(2)}, u32[]{:S(2)}) %collective-permute-start.8) | collective-permute-done | bytes 294944 | tf_op jit(solution)/shard_map/ppermute | solution.py:16
  45.4 12.4 %collective-permute-done.15.refs_3_ = bf16[96,6144]{1,0:T(8,128)(2,1)S(1)} collective-permute-done((bf16[96,6144]{1,0:T(8,128)(2,1)S(1)}, bf16[96,6144]{1,0:T(8,128)(2,1)S(1)}, u32[]{:S(2)}, u32[]{:S(2)}) %collective-permute-start.15) | collective-permute-done | bytes 1179680 | tf_op jit(solution)/shard_map/ppermute | solution.py:16
  61.0 2.8 copy-done.8
  63.7 11.1 %experts.4 = (bf16[48,6144]{1,0:T(8,128)(2,1)S(1)}, bf16[48,6144]{1,0:T(8,128)(2,1)S(1)}, bf16[96,6144]{1,0:T(8,128)(2,1)S(1)}, bf16[96,6144]{1,0:T(8,128)(2,1)S...) custom-call(bf16[48,6144]{1,0:T(8,128)(2,1)S(1)} %pad_maximum_fusion.2.refs_0_, ...), custom_call_target="tpu_custom_call" | custom-call | flops 7247757312 | bytes 28311552 | tf_op jit(solution)/shard_map/experts/pallas_call | solution.py:129
  75.7 2.6 collective-permute-start.21
  80.2 7.7 %collective-permute-done.10.refs_0_ = bf16[48,6144]{1,0:T(8,128)(2,1)S(1)} collective-permute-done((bf16[48,6144]{1,0:T(8,128)(2,1)S(1)}, bf16[48,6144]{1,0:T(8,128)(2,1)S(1)}, u32[]{:S(2)}, u32[]{:S(2)}) %collective-permute-start.10) | collective-permute-done | bytes 589856 | tf_op jit(solution)/shard_map/ppermute | solution.py:16
  89.7 6.0 %collective-permute-done.20.refs_2_ = bf16[48,6144]{1,0:T(8,128)(2,1)S(1)} collective-permute-done((bf16[48,6144]{1,0:T(8,128)(2,1)S(1)}, bf16[48,6144]{1,0:T(8,128)(2,1)S(1)}, u32[]{:S(2)}, u32[]{:S(2)}) %collective-permute-start.20) | collective-permute-done | bytes 589856 | tf_op jit(solution)/shard_map/ppermute | solution.py:16
  95.6 2.4 collective-permute-start.33
  98.9 4.0 %collective-permute-done.17.refs_1_ = bf16[48,6144]{1,0:T(8,128)(2,1)S(1)} collective-permute-done((bf16[48,6144]{1,0:T(8,128)(2,1)S(1)}, bf16[48,6144]{1,0:T(8,128)(2,1)S(1)}, u32[]{:S(2)}, u32[]{:S(2)}) %collective-permute-start.17) | collective-permute-done | bytes 589856 | tf_op jit(solution)/shard_map/ppermute | solution.py:16
  102.9 4.0 %collective-permute-start.26 = (bf16[48,6144]{1,0:T(8,128)(2,1)S(1)}, bf16[48,6144]{1,0:T(8,128)(2,1)S(1)}, u32[]{:S(2)}, u32[]{:S(2)}) collective-permute-start(bf16[48,6144]{1,0:T(8,128)(2,1)S(1)} %get-tuple-element.125), channel_id=1, source_target_pairs={{0,2},{2,4},{4,6},{6,0},{1,3},{3,5},{5,7},{7,1},{8,10},{10,12},{12... | collective-permute-start | bytes 1769480 | tf_op jit(solution)/shard_map/ppermute | solution.py:16
  107.9 11.6 %experts.5 = (bf16[96,6144]{1,0:T(8,128)(2,1)}, bf16[48,6144]{1,0:T(8,128)(2,1)S(1)}, bf16[48,6144]{1,0:T(8,128)(2,1)S(1)}, bf16[48,6144]{1,0:T(8,128)(2,1)S(1)}...) custom-call(bf16[96,6144]{1,0:T(8,128)(2,1)S(1)} %pad_maximum_fusion.1.refs_0_, ...), custom_call_target="tpu_custom_call" | custom-call | flops 7247757312 | bytes 28311552 | tf_op jit(solution)/shard_map/experts/pallas_call | solution.py:129
  125.1 4.8 %collective-permute-done.30.refs_0_ = bf16[48,6144]{1,0:T(8,128)(2,1)S(1)} collective-permute-done((bf16[48,6144]{1,0:T(8,128)(2,1)S(1)}, bf16[48,6144]{1,0:T(8,128)(2,1)S(1)}, u32[]{:S(2)}, u32[]{:S(2)}) %collective-permute-start.30) | collective-permute-done | bytes 589856 | tf_op jit(solution)/shard_map/ppermute | solution.py:16
  131.3 10.8 %collective-permute-done.33.refs_4_ = bf16[96,6144]{1,0:T(8,128)(2,1)S(1)} collective-permute-done((bf16[96,6144]{1,0:T(8,128)(2,1)S(1)}, bf16[96,6144]{1,0:T(8,128)(2,1)S(1)}, u32[]{:S(2)}, u32[]{:S(2)}) %collective-permute-start.33) | collective-permute-done | bytes 1179680 | tf_op jit(solution)/shard_map/ppermute | solution.py:16
  142.1 2.8 copy-done.3
  144.9 2.8 copy-done.6
  147.7 2.8 copy-done.9
  152.6 11.8 %experts.6 = (bf16[48,6144]{1,0:T(8,128)(2,1)S(1)}, bf16[48,6144]{1,0:T(8,128)(2,1)S(1)}, bf16[48,6144]{1,0:T(8,128)(2,1)S(1)}, bf16[48,6144]{1,0:T(8,128)(2,1)S...) custom-call(bf16[48,6144]{1,0:T(8,128)(2,1)S(1)} %collective-permute-done.10.refs_0_, ...), custom_call_target="tpu_custom_call" | custom-call | flops 7247757312 | bytes 28311552 | tf_op jit(solution)/shard_map/experts/pallas_call | solution.py:129
  167.9 2.0 collective-permute-start.25
  169.9 5.4 %collective-permute-done.27 = bf16[48,6144]{1,0:T(8,128)(2,1)S(1)} collective-permute-done((bf16[48,6144]{1,0:T(8,128)(2,1)S(1)}, bf16[48,6144]{1,0:T(8,128)(2,1)S(1)}, u32[]{:S(2)}, u32[]{:S(2)}) %collective-permute-start.27) | collective-permute-done | bytes 589856 | tf_op jit(solution)/shard_map/ppermute | solution.py:16
  175.4 6.3 %collective-permute-done.24 = bf16[48,6144]{1,0:T(8,128)(2,1)S(1)} collective-permute-done((bf16[48,6144]{1,0:T(8,128)(2,1)S(1)}, bf16[48,6144]{1,0:T(8,128)(2,1)S(1)}, u32[]{:S(2)}, u32[]{:S(2)}) %collective-permute-start.24) | collective-permute-done | bytes 589856 | tf_op jit(solution)/shard_map/ppermute | solution.py:16
  181.7 2.8 copy-done.4
  184.4 2.8 copy-done.7
  187.2 2.8 copy-done.10
  193.4 11.1 %experts.7 = (bf16[48,6144]{1,0:T(8,128)(2,1)S(1)}, bf16[48,6144]{1,0:T(8,128)(2,1)S(1)}, bf16[48,6144]{1,0:T(8,128)(2,1)S(1)}, bf16[48,6144]{1,0:T(8,128)(2,1)S...) custom-call(bf16[48,6144]{1,0:T(8,128)(2,1)S(1)} %copy-done.16, ...), custom_call_target="tpu_custom_call" | custom-call | flops 7247757312 | bytes 28311552 | tf_op jit(solution)/shard_map/experts/pallas_call | solution.py:129
  206.8 3.0 collective-permute-start.42
  211.7 17.2 %collective-permute-done.42 = bf16[48,6144]{1,0:T(8,128)(2,1)S(1)} collective-permute-done((bf16[48,6144]{1,0:T(8,128)(2,1)S(1)}, bf16[48,6144]{1,0:T(8,128)(2,1)S(1)}, u32[]{:S(2)}, u32[]{:S(2)}) %collective-permute-start.42) | collective-permute-done | bytes 589856 | tf_op jit(solution)/shard_map/ppermute | solution.py:16
  229.1 2.7 collective-permute-start.43
  233.0 16.1 %collective-permute-done.36 = bf16[96,6144]{1,0:T(8,128)(2,1)S(1)} collective-permute-done((bf16[96,6144]{1,0:T(8,128)(2,1)S(1)}, bf16[96,6144]{1,0:T(8,128)(2,1)S(1)}, u32[]{:S(2)}, u32[]{:S(2)}) %collective-permute-start.36) | collective-permute-done | bytes 1179680 | tf_op jit(solution)/shard_map/ppermute | solution.py:16
  249.3 3.0 collective-permute-start.46
  256.5 3.2 collective-permute-done.46
  259.7 3.9 %collective-permute-done.49 = bf16[48,6144]{1,0:T(8,128)(2,1)S(1)} collective-permute-done((bf16[48,6144]{1,0:T(8,128)(2,1)S(1)}, bf16[48,6144]{1,0:T(8,128)(2,1)S(1)}, u32[]{:S(2)}, u32[]{:S(2)}) %collective-permute-start.49) | collective-permute-done | bytes 589856 | tf_op jit(solution)/shard_map/ppermute | solution.py:16
  263.6 5.5 %collective-permute-done.44 = bf16[96,6144]{1,0:T(8,128)(2,1)S(1)} collective-permute-done((bf16[96,6144]{1,0:T(8,128)(2,1)S(1)}, bf16[96,6144]{1,0:T(8,128)(2,1)S(1)}, u32[]{:S(2)}, u32[]{:S(2)}) %collective-permute-start.44) | collective-permute-done | bytes 1179680 | tf_op jit(solution)/shard_map/ppermute | solution.py:16
  272.5 3.3 collective-permute-start.50
  278.4 4.6 %collective-permute-done.39 = s32[128,2]{0,1:T(2,128)S(1)} collective-permute-done((s32[128,2]{0,1:T(2,128)S(1)}, s32[128,2]{0,1:T(2,128)S(1)}, u32[]{:S(2)}, u32[]{:S(2)}) %collective-permute-start.39) | collective-permute-done | bytes 1056 | tf_op jit(solution)/shard_map/ppermute | solution.py:40
  283.0 4.5 %collective-permute-done.40 = s32[128,2]{0,1:T(2,128)S(1)} collective-permute-done((s32[128,2]{0,1:T(2,128)S(1)}, s32[128,2]{0,1:T(2,128)S(1)}, u32[]{:S(2)}, u32[]{:S(2)}) %collective-permute-start.40) | collective-permute-done | bytes 1056 | tf_op jit(solution)/shard_map/ppermute | solution.py:40
  293.9 3.2 collective-permute-start.54
  299.9 2.6 collective-permute-done.57
  304.0 2.3 collective-permute-done.56
  313.2 13.5 %collective-permute-done.58 = bf16[48,6144]{1,0:T(8,128)(2,1)S(1)} collective-permute-done((bf16[48,6144]{1,0:T(8,128)(2,1)S(1)}, bf16[48,6144]{1,0:T(8,128)(2,1)S(1)}, u32[]{:S(2)}, u32[]{:S(2)}) %collective-permute-start.58) | collective-permute-done | bytes 589856 | tf_op jit(solution)/shard_map/ppermute | solution.py:45
  327.3 3.2 collective-permute-done.59
  (222 shorter events, 75.0 us)
Async XLA Ops:
  4.2 19.1 %collective-permute-start.4 = (bf16[24,6144]{1,0:T(8,128)(2,1)S(1)}, bf16[24,6144]{1,0:T(8,128)(2,1)S(1)}, u32[]{:S(2)}, u32[]{:S(2)}) collective-permute-start(bf16[24,6144]{1,0:T(8,128)(2,1)S(1)} %get-tuple-element.213), channel_id=1, source_target_pairs={{0,6},{2,0},{4,2},{6,4},{1,7},{3,1},{5,3},{7,5},{8,14},{10,8},{12,... | collective-permute-start | bytes 884744 | tf_op jit(solution)/shard_map/ppermute | solution.py:16
  6.9 15.7 %collective-permute-start = (bf16[48,6144]{1,0:T(8,128)(2,1)S(1)}, bf16[48,6144]{1,0:T(8,128)(2,1)S(1)}, u32[]{:S(2)}, u32[]{:S(2)}) collective-permute-start(bf16[48,6144]{1,0:T(8,128)(2,1)S(1)} %convolution_convert_fusion.1), channel_id=1, source_target_pairs={{0,24},{8,16},{16,8},{24,0},{1,25},{9,17},{17,9},{25,1},{2,26},{10... | collective-permute-start | bytes 1769480 | tf_op jit(solution)/shard_map/ppermute | solution.py:36
  11.2 46.6 %collective-permute-start.16 = (bf16[48,6144]{1,0:T(8,128)(2,1)S(1)}, bf16[48,6144]{1,0:T(8,128)(2,1)S(1)}, u32[]{:S(2)}, u32[]{:S(2)}) collective-permute-start(bf16[48,6144]{1,0:T(8,128)(2,1)S(1)} %pad_maximum_fusion.2.refs_0_), channel_id=1, source_target_pairs={{0,6},{2,0},{4,2},{6,4},{1,7},{3,1},{5,3},{7,5},{8,14},{10,8},{12,... | collective-permute-start | bytes 1769480 | tf_op jit(solution)/shard_map/ppermute | solution.py:16
  14.2 15.8 %collective-permute-start.7 = (bf16[48,6144]{1,0:T(8,128)(2,1)S(1)}, bf16[48,6144]{1,0:T(8,128)(2,1)S(1)}, u32[]{:S(2)}, u32[]{:S(2)}) collective-permute-start(bf16[48,6144]{1,0:T(8,128)(2,1)S(1)} %pad_maximum_fusion.2.refs_0_), channel_id=1, source_target_pairs={{0,1},{1,0},{2,3},{3,2},{4,5},{5,4},{6,7},{7,6},{8,9},{9,8},{10,11... | collective-permute-start | bytes 1769480 | tf_op jit(solution)/shard_map/ppermute | solution.py:16
  23.2 10.2 %collective-permute-start.1 = (bf16[24,6144]{1,0:T(8,128)(2,1)S(1)}, bf16[24,6144]{1,0:T(8,128)(2,1)S(1)}, u32[]{:S(2)}, u32[]{:S(2)}) collective-permute-start(bf16[24,6144]{1,0:T(8,128)(2,1)S(1)} %get-tuple-element.211), channel_id=1, source_target_pairs={{0,6},{2,0},{4,2},{6,4},{1,7},{3,1},{5,3},{7,5},{8,14},{10,8},{12,... | collective-permute-start | bytes 884744 | tf_op jit(solution)/shard_map/ppermute | solution.py:16
  30.0 29.6 %collective-permute-start.11 = (bf16[48,6144]{1,0:T(8,128)(2,1)S(1)}, bf16[48,6144]{1,0:T(8,128)(2,1)S(1)}, u32[]{:S(2)}, u32[]{:S(2)}) collective-permute-start(bf16[48,6144]{1,0:T(8,128)(2,1)S(1)} %pad_maximum_fusion.2.refs_0_), channel_id=1, source_target_pairs={{0,2},{2,4},{4,6},{6,0},{1,3},{3,5},{5,7},{7,1},{8,10},{10,12},{12... | collective-permute-start | bytes 1769480 | tf_op jit(solution)/shard_map/ppermute | solution.py:16
  32.4 25.4 %collective-permute-start.15 = (bf16[96,6144]{1,0:T(8,128)(2,1)S(1)}, bf16[96,6144]{1,0:T(8,128)(2,1)S(1)}, u32[]{:S(2)}, u32[]{:S(2)}) collective-permute-start(bf16[96,6144]{1,0:T(8,128)(2,1)S(1)} %pad_maximum_fusion.refs_2_), channel_id=1, source_target_pairs={{0,8},{8,0},{1,9},{9,1},{2,10},{10,2},{3,11},{11,3},{4,12},{12,4},... | collective-permute-start | bytes 3538952 | tf_op jit(solution)/shard_map/ppermute | solution.py:16
  35.9 23.6 %collective-permute-start.12 = (bf16[48,6144]{1,0:T(8,128)(2,1)S(1)}, bf16[48,6144]{1,0:T(8,128)(2,1)S(1)}, u32[]{:S(2)}, u32[]{:S(2)}) collective-permute-start(bf16[48,6144]{1,0:T(8,128)(2,1)S(1)} %collective-permute-done.7.refs_1_), channel_id=1, source_target_pairs={{0,6},{2,0},{4,2},{6,4},{1,7},{3,1},{5,3},{7,5},{8,14},{10,8},{12,... | collective-permute-start | bytes 1769480 | tf_op jit(solution)/shard_map/ppermute | solution.py:16
  43.4 31.5 %collective-permute-start.13 = (bf16[96,6144]{1,0:T(8,128)(2,1)S(1)}, bf16[96,6144]{1,0:T(8,128)(2,1)S(1)}, u32[]{:S(2)}, u32[]{:S(2)}) collective-permute-start(bf16[96,6144]{1,0:T(8,128)(2,1)S(1)} %pad_maximum_fusion.refs_2_), channel_id=1, source_target_pairs={{0,1},{1,0},{2,3},{3,2},{4,5},{5,4},{6,7},{7,6},{8,9},{9,8},{10,11... | collective-permute-start | bytes 3538952 | tf_op jit(solution)/shard_map/ppermute | solution.py:16
  57.8 20.4 %collective-permute-start.22 = (bf16[48,6144]{1,0:T(8,128)(2,1)S(1)}, bf16[48,6144]{1,0:T(8,128)(2,1)S(1)}, u32[]{:S(2)}, u32[]{:S(2)}) collective-permute-start(bf16[48,6144]{1,0:T(8,128)(2,1)S(1)} %collective-permute-done.7.refs_1_), channel_id=1, source_target_pairs={{0,2},{2,4},{4,6},{6,0},{1,3},{3,5},{5,7},{7,1},{8,10},{10,12},{12... | collective-permute-start | bytes 1769480 | tf_op jit(solution)/shard_map/ppermute | solution.py:16
  57.8 17.0 %collective-permute-start.14 = (bf16[48,6144]{1,0:T(8,128)(2,1)S(1)}, bf16[48,6144]{1,0:T(8,128)(2,1)S(1)}, u32[]{:S(2)}, u32[]{:S(2)}) collective-permute-start(bf16[48,6144]{1,0:T(8,128)(2,1)S(1)} %pad_maximum_fusion.3.refs_1_), channel_id=1, source_target_pairs={{0,8},{8,0},{1,9},{9,1},{2,10},{10,2},{3,11},{11,3},{4,12},{12,4},... | collective-permute-start | bytes 1769480 | tf_op jit(solution)/shard_map/ppermute | solution.py:16
  59.5 28.4 %collective-permute-start.10 = (bf16[48,6144]{1,0:T(8,128)(2,1)S(1)}, bf16[48,6144]{1,0:T(8,128)(2,1)S(1)}, u32[]{:S(2)}, u32[]{:S(2)}) collective-permute-start(bf16[48,6144]{1,0:T(8,128)(2,1)S(1)} %pad_maximum_fusion.3.refs_1_), channel_id=1, source_target_pairs={{0,2},{2,4},{4,6},{6,0},{1,3},{3,5},{5,7},{7,1},{8,10},{10,12},{12... | collective-permute-start | bytes 1769480 | tf_op jit(solution)/shard_map/ppermute | solution.py:16
  59.6 47.4 %collective-permute-start.19 = (bf16[96,6144]{1,0:T(8,128)(2,1)S(1)}, bf16[96,6144]{1,0:T(8,128)(2,1)S(1)}, u32[]{:S(2)}, u32[]{:S(2)}) collective-permute-start(bf16[96,6144]{1,0:T(8,128)(2,1)S(1)} %pad_maximum_fusion.1.refs_0_), channel_id=1, source_target_pairs={{0,1},{1,0},{2,3},{3,2},{4,5},{5,4},{6,7},{7,6},{8,9},{9,8},{10,11... | collective-permute-start | bytes 3538952 | tf_op jit(solution)/shard_map/ppermute | solution.py:16
  74.9 20.7 %collective-permute-start.20 = (bf16[48,6144]{1,0:T(8,128)(2,1)S(1)}, bf16[48,6144]{1,0:T(8,128)(2,1)S(1)}, u32[]{:S(2)}, u32[]{:S(2)}) collective-permute-start(bf16[48,6144]{1,0:T(8,128)(2,1)S(1)} %collective-permute-done.11.refs_4_), channel_id=1, source_target_pairs={{0,2},{2,4},{4,6},{6,0},{1,3},{3,5},{5,7},{7,1},{8,10},{10,12},{12... | collective-permute-start | bytes 1769480 | tf_op jit(solution)/shard_map/ppermute | solution.py:16
  75.7 22.4 %collective-permute-start.21 = (bf16[48,6144]{1,0:T(8,128)(2,1)S(1)}, bf16[48,6144]{1,0:T(8,128)(2,1)S(1)}, u32[]{:S(2)}, u32[]{:S(2)}) collective-permute-start(bf16[48,6144]{1,0:T(8,128)(2,1)S(1)} %collective-permute-done.12.refs_4_), channel_id=1, source_target_pairs={{0,6},{2,0},{4,2},{6,4},{1,7},{3,1},{5,3},{7,5},{8,14},{10,8},{12,... | collective-permute-start | bytes 1769480 | tf_op jit(solution)/shard_map/ppermute | solution.py:16
  78.2 24.6 %collective-permute-start.17 = (bf16[48,6144]{1,0:T(8,128)(2,1)S(1)}, bf16[48,6144]{1,0:T(8,128)(2,1)S(1)}, u32[]{:S(2)}, u32[]{:S(2)}) collective-permute-start(bf16[48,6144]{1,0:T(8,128)(2,1)S(1)} %collective-permute-done.14.refs_2_), channel_id=1, source_target_pairs={{0,6},{2,0},{4,2},{6,4},{1,7},{3,1},{5,3},{7,5},{8,14},{10,8},{12,... | collective-permute-start | bytes 1769480 | tf_op jit(solution)/shard_map/ppermute | solution.py:16
  87.9 32.5 %collective-permute-start.18 = (bf16[96,6144]{1,0:T(8,128)(2,1)S(1)}, bf16[96,6144]{1,0:T(8,128)(2,1)}, u32[]{:S(2)}, u32[]{:S(2)}) collective-permute-start(bf16[96,6144]{1,0:T(8,128)(2,1)S(1)} %pad_maximum_fusion.1.refs_0_), channel_id=1, source_target_pairs={{0,8},{8,0},{1,9},{9,1},{2,10},{10,2},{3,11},{11,3},{4,12},{12,4},... | collective-permute-start | bytes 3538952 | tf_op jit(solution)/shard_map/ppermute | solution.py:16
  95.6 46.5 %collective-permute-start.33 = (bf16[96,6144]{1,0:T(8,128)(2,1)S(1)}, bf16[96,6144]{1,0:T(8,128)(2,1)S(1)}, u32[]{:S(2)}, u32[]{:S(2)}) collective-permute-start(bf16[96,6144]{1,0:T(8,128)(2,1)S(1)} %collective-permute-done.13.refs_5_), channel_id=1, source_target_pairs={{0,8},{8,0},{1,9},{9,1},{2,10},{10,2},{3,11},{11,3},{4,12},{12,4},... | collective-permute-start | bytes 3538952 | tf_op jit(solution)/shard_map/ppermute | solution.py:16
  98.9 22.8 %collective-permute-start.23 = (bf16[48,6144]{1,0:T(8,128)(2,1)S(1)}, bf16[48,6144]{1,0:T(8,128)(2,1)S(1)}, u32[]{:S(2)}, u32[]{:S(2)}) collective-permute-start(bf16[48,6144]{1,0:T(8,128)(2,1)S(1)} %pad_maximum_fusion.3.refs_1_), channel_id=1, source_target_pairs={{0,6},{2,0},{4,2},{6,4},{1,7},{3,1},{5,3},{7,5},{8,14},{10,8},{12,... | collective-permute-start | bytes 1769480 | tf_op jit(solution)/shard_map/ppermute | solution.py:16
  102.9 20.9 %collective-permute-start.26 = (bf16[48,6144]{1,0:T(8,128)(2,1)S(1)}, bf16[48,6144]{1,0:T(8,128)(2,1)S(1)}, u32[]{:S(2)}, u32[]{:S(2)}) collective-permute-start(bf16[48,6144]{1,0:T(8,128)(2,1)S(1)} %get-tuple-element.125), channel_id=1, source_target_pairs={{0,2},{2,4},{4,6},{6,0},{1,3},{3,5},{5,7},{7,1},{8,10},{10,12},{12... | collective-permute-start | bytes 1769480 | tf_op jit(solution)/shard_map/ppermute | solution.py:16
  106.9 22.9 %collective-permute-start.30 = (bf16[48,6144]{1,0:T(8,128)(2,1)S(1)}, bf16[48,6144]{1,0:T(8,128)(2,1)S(1)}, u32[]{:S(2)}, u32[]{:S(2)}) collective-permute-start(bf16[48,6144]{1,0:T(8,128)(2,1)S(1)} %collective-permute-done.14.refs_2_), channel_id=1, source_target_pairs={{0,2},{2,4},{4,6},{6,0},{1,3},{3,5},{5,7},{7,1},{8,10},{10,12},{12... | collective-permute-start | bytes 1769480 | tf_op jit(solution)/shard_map/ppermute | solution.py:16
  120.4 46.5 %collective-permute-start.34 = (bf16[96,6144]{1,0:T(8,128)(2,1)}, bf16[96,6144]{1,0:T(8,128)(2,1)S(1)}, u32[]{:S(2)}, u32[]{:S(2)}) collective-permute-start(bf16[96,6144]{1,0:T(8,128)(2,1)} %collective-permute-done.18.refs_4_), channel_id=1, source_target_pairs={{0,1},{1,0},{2,3},{3,2},{4,5},{5,4},{6,7},{7,6},{8,9},{9,8},{10,11... | collective-permute-start | bytes 3538952 | tf_op jit(solution)/shard_map/ppermute | solution.py:16
  122.5 52.8 %collective-permute-start.28 = (bf16[96,6144]{1,0:T(8,128)(2,1)S(1)}, bf16[96,6144]{1,0:T(8,128)(2,1)S(1)}, u32[]{:S(2)}, u32[]{:S(2)}) collective-permute-start(bf16[96,6144]{1,0:T(8,128)(2,1)S(1)} %get-tuple-element.127), channel_id=1, source_target_pairs={{0,8},{8,0},{1,9},{9,1},{2,10},{10,2},{3,11},{11,3},{4,12},{12,4},... | collective-permute-start | bytes 3538952 | tf_op jit(solution)/shard_map/ppermute | solution.py:16
  123.8 41.6 %collective-permute-start.31 = (bf16[48,6144]{1,0:T(8,128)(2,1)S(1)}, bf16[48,6144]{1,0:T(8,128)(2,1)S(1)}, u32[]{:S(2)}, u32[]{:S(2)}) collective-permute-start(bf16[48,6144]{1,0:T(8,128)(2,1)S(1)} %collective-permute-done.10.refs_0_), channel_id=1, source_target_pairs={{0,2},{2,4},{4,6},{6,0},{1,3},{3,5},{5,7},{7,1},{8,10},{10,12},{12... | collective-permute-start | bytes 1769480 | tf_op jit(solution)/shard_map/ppermute | solution.py:16
  130.7 35.3 %collective-permute-start.32 = (bf16[48,6144]{1,0:T(8,128)(2,1)S(1)}, bf16[48,6144]{1,0:T(8,128)(2,1)S(1)}, u32[]{:S(2)}, u32[]{:S(2)}) collective-permute-start(bf16[48,6144]{1,0:T(8,128)(2,1)S(1)} %collective-permute-done.17.refs_1_), channel_id=1, source_target_pairs={{0,6},{2,0},{4,2},{6,4},{1,7},{3,1},{5,3},{7,5},{8,14},{10,8},{12,... | collective-permute-start | bytes 1769480 | tf_op jit(solution)/shard_map/ppermute | solution.py:16
  142.1 39.5 %collective-permute-start.29 = (bf16[96,6144]{1,0:T(8,128)(2,1)}, bf16[96,6144]{1,0:T(8,128)(2,1)}, u32[]{:S(2)}, u32[]{:S(2)}) collective-permute-start(bf16[96,6144]{1,0:T(8,128)(2,1)} %get-tuple-element.128), channel_id=1, source_target_pairs={{0,1},{1,0},{2,3},{3,2},{4,5},{5,4},{6,7},{7,6},{8,9},{9,8},{10,11... | collective-permute-start | bytes 3538952 | tf_op jit(solution)/shard_map/ppermute | solution.py:16
  166.8 14.8 %collective-permute-start.24 = (bf16[48,6144]{1,0:T(8,128)(2,1)S(1)}, bf16[48,6144]{1,0:T(8,128)(2,1)S(1)}, u32[]{:S(2)}, u32[]{:S(2)}) collective-permute-start(bf16[48,6144]{1,0:T(8,128)(2,1)S(1)} %get-tuple-element.123), channel_id=1, source_target_pairs={{0,6},{2,0},{4,2},{6,4},{1,7},{3,1},{5,3},{7,5},{8,14},{10,8},{12,... | collective-permute-start | bytes 1769480 | tf_op jit(solution)/shard_map/ppermute | solution.py:16
  167.9 13.8 %collective-permute-start.25 = (bf16[48,6144]{1,0:T(8,128)(2,1)S(1)}, bf16[48,6144]{1,0:T(8,128)(2,1)S(1)}, u32[]{:S(2)}, u32[]{:S(2)}) collective-permute-start(bf16[48,6144]{1,0:T(8,128)(2,1)S(1)} %get-tuple-element.124), channel_id=1, source_target_pairs={{0,2},{2,4},{4,6},{6,0},{1,3},{3,5},{5,7},{7,1},{8,10},{10,12},{12... | collective-permute-start | bytes 1769480 | tf_op jit(solution)/shard_map/ppermute | solution.py:16
  175.3 77.5 %collective-permute-start.47 = (bf16[48,6144]{1,0:T(8,128)(2,1)S(1)}, bf16[48,6144]{1,0:T(8,128)(2,1)}, u32[]{:S(2)}, u32[]{:S(2)}) collective-permute-start(bf16[48,6144]{1,0:T(8,128)(2,1)S(1)} %get-tuple-element.173), channel_id=1, source_target_pairs={{0,2},{2,4},{4,6},{6,0},{1,3},{3,5},{5,7},{7,1},{8,10},{10,12},{12... | collective-permute-start | bytes 1769480 | tf_op jit(solution)/shard_map/ppermute | solution.py:16
  204.5 24.6 %collective-permute-start.37 = (bf16[48,6144]{1,0:T(8,128)(2,1)S(1)}, bf16[48,6144]{1,0:T(8,128)(2,1)S(1)}, u32[]{:S(2)}, u32[]{:S(2)}) collective-permute-start(bf16[48,6144]{1,0:T(8,128)(2,1)S(1)} %get-tuple-element.149), channel_id=1, source_target_pairs={{0,6},{2,0},{4,2},{6,4},{1,7},{3,1},{5,3},{7,5},{8,14},{10,8},{12,... | collective-permute-start | bytes 1769480 | tf_op jit(solution)/shard_map/ppermute | solution.py:16
  206.3 25.5 %collective-permute-start.38 = (bf16[48,6144]{1,0:T(8,128)(2,1)S(1)}, bf16[48,6144]{1,0:T(8,128)(2,1)S(1)}, u32[]{:S(2)}, u32[]{:S(2)}) collective-permute-start(bf16[48,6144]{1,0:T(8,128)(2,1)S(1)} %get-tuple-element.150), channel_id=1, source_target_pairs={{0,2},{2,4},{4,6},{6,0},{1,3},{3,5},{5,7},{7,1},{8,10},{10,12},{12... | collective-permute-start | bytes 1769480 | tf_op jit(solution)/shard_map/ppermute | solution.py:16
  206.8 22.1 %collective-permute-start.42 = (bf16[48,6144]{1,0:T(8,128)(2,1)S(1)}, bf16[48,6144]{1,0:T(8,128)(2,1)S(1)}, u32[]{:S(2)}, u32[]{:S(2)}) collective-permute-start(bf16[48,6144]{1,0:T(8,128)(2,1)S(1)} %add_convert_fusion.9), channel_id=1, source_target_pairs={{0,6},{2,0},{4,2},{6,4},{1,7},{3,1},{5,3},{7,5},{8,14},{10,8},{12,... | collective-permute-start | bytes 1769480 | tf_op jit(solution)/shard_map/ppermute | solution.py:16
  209.8 23.2 %collective-permute-start.35 = (bf16[96,6144]{1,0:T(8,128)(2,1)S(1)}, bf16[96,6144]{1,0:T(8,128)(2,1)S(1)}, u32[]{:S(2)}, u32[]{:S(2)}) collective-permute-start(bf16[96,6144]{1,0:T(8,128)(2,1)S(1)} %copy-done.12), channel_id=1, source_target_pairs={{0,1},{1,0},{2,3},{3,2},{4,5},{5,4},{6,7},{7,6},{8,9},{9,8},{10,11... | collective-permute-start | bytes 3538952 | tf_op jit(solution)/shard_map/ppermute | solution.py:16
  228.9 20.2 %collective-permute-start.36 = (bf16[96,6144]{1,0:T(8,128)(2,1)S(1)}, bf16[96,6144]{1,0:T(8,128)(2,1)S(1)}, u32[]{:S(2)}, u32[]{:S(2)}) collective-permute-start(bf16[96,6144]{1,0:T(8,128)(2,1)S(1)} %get-tuple-element.148), channel_id=1, source_target_pairs={{0,8},{8,0},{1,9},{9,1},{2,10},{10,2},{3,11},{11,3},{4,12},{12,4},... | collective-permute-start | bytes 3538952 | tf_op jit(solution)/shard_map/ppermute | solution.py:16
  229.1 25.4 %collective-permute-start.43 = (bf16[48,6144]{1,0:T(8,128)(2,1)S(1)}, bf16[48,6144]{1,0:T(8,128)(2,1)S(1)}, u32[]{:S(2)}, u32[]{:S(2)}) collective-permute-start(bf16[48,6144]{1,0:T(8,128)(2,1)S(1)} %add_convert_fusion.7), channel_id=1, source_target_pairs={{0,2},{2,4},{4,6},{6,0},{1,3},{3,5},{5,7},{7,1},{8,10},{10,12},{12... | collective-permute-start | bytes 1769480 | tf_op jit(solution)/shard_map/ppermute | solution.py:16
  231.8 24.7 %collective-permute-start.48 = (bf16[48,6144]{1,0:T(8,128)(2,1)S(1)}, bf16[48,6144]{1,0:T(8,128)(2,1)S(1)}, u32[]{:S(2)}, u32[]{:S(2)}) collective-permute-start(bf16[48,6144]{1,0:T(8,128)(2,1)S(1)} %get-tuple-element.174), channel_id=1, source_target_pairs={{0,6},{2,0},{4,2},{6,4},{1,7},{3,1},{5,3},{7,5},{8,14},{10,8},{12,... | collective-permute-start | bytes 1769480 | tf_op jit(solution)/shard_map/ppermute | solution.py:16
  249.3 10.4 %collective-permute-start.46 = (bf16[48,6144]{1,0:T(8,128)(2,1)S(1)}, bf16[48,6144]{1,0:T(8,128)(2,1)S(1)}, u32[]{:S(2)}, u32[]{:S(2)}) collective-permute-start(bf16[48,6144]{1,0:T(8,128)(2,1)S(1)} %add_convert_fusion.5), channel_id=1, source_target_pairs={{0,6},{2,0},{4,2},{6,4},{1,7},{3,1},{5,3},{7,5},{8,14},{10,8},{12,... | collective-permute-start | bytes 1769480 | tf_op jit(solution)/shard_map/ppermute | solution.py:16
  252.4 11.2 %collective-permute-start.49 = (bf16[48,6144]{1,0:T(8,128)(2,1)S(1)}, bf16[48,6144]{1,0:T(8,128)(2,1)S(1)}, u32[]{:S(2)}, u32[]{:S(2)}) collective-permute-start(bf16[48,6144]{1,0:T(8,128)(2,1)S(1)} %add_convert_fusion.4), channel_id=1, source_target_pairs={{0,2},{2,4},{4,6},{6,0},{1,3},{3,5},{5,7},{7,1},{8,10},{10,12},{12... | collective-permute-start | bytes 1769480 | tf_op jit(solution)/shard_map/ppermute | solution.py:16
  252.8 16.3 %collective-permute-start.44 = (bf16[96,6144]{1,0:T(8,128)(2,1)S(1)}, bf16[96,6144]{1,0:T(8,128)(2,1)S(1)}, u32[]{:S(2)}, u32[]{:S(2)}) collective-permute-start(bf16[96,6144]{1,0:T(8,128)(2,1)S(1)} %add_convert_fusion.2), channel_id=1, source_target_pairs={{0,1},{1,0},{2,3},{3,2},{4,5},{5,4},{6,7},{7,6},{8,9},{9,8},{10,11... | collective-permute-start | bytes 3538952 | tf_op jit(solution)/shard_map/ppermute | solution.py:16
  254.5 16.2 %collective-permute-start.45 = (bf16[96,6144]{1,0:T(8,128)(2,1)S(1)}, bf16[96,6144]{1,0:T(8,128)(2,1)S(1)}, u32[]{:S(2)}, u32[]{:S(2)}) collective-permute-start(bf16[96,6144]{1,0:T(8,128)(2,1)S(1)} %add_convert_fusion.1), channel_id=1, source_target_pairs={{0,8},{8,0},{1,9},{9,1},{2,10},{10,2},{3,11},{11,3},{4,12},{12,4},... | collective-permute-start | bytes 3538952 | tf_op jit(solution)/shard_map/ppermute | solution.py:16
  272.5 15.0 %collective-permute-start.50 = (bf16[48,6144]{1,0:T(8,128)(2,1)S(1)}, bf16[48,6144]{1,0:T(8,128)(2,1)S(1)}, u32[]{:S(2)}, u32[]{:S(2)}) collective-permute-start(bf16[48,6144]{1,0:T(8,128)(2,1)S(1)} %pad_maximum_fusion.4), channel_id=1, source_target_pairs={{0,6},{2,0},{4,2},{6,4},{1,7},{3,1},{5,3},{7,5},{8,14},{10,8},{12,... | collective-permute-start | bytes 1769480 | tf_op jit(solution)/shard_map/ppermute | solution.py:16
  275.8 11.7 %collective-permute-start.51 = (bf16[48,6144]{1,0:T(8,128)(2,1)S(1)}, bf16[48,6144]{1,0:T(8,128)(2,1)S(1)}, u32[]{:S(2)}, u32[]{:S(2)}) collective-permute-start(bf16[48,6144]{1,0:T(8,128)(2,1)S(1)} %pad_maximum_fusion.5), channel_id=1, source_target_pairs={{0,2},{2,4},{4,6},{6,0},{1,3},{3,5},{5,7},{7,1},{8,10},{10,12},{12... | collective-permute-start | bytes 1769480 | tf_op jit(solution)/shard_map/ppermute | solution.py:16
  276.1 11.4 %collective-permute-start.53 = (bf16[48,6144]{1,0:T(8,128)(2,1)S(1)}, bf16[48,6144]{1,0:T(8,128)(2,1)S(1)}, u32[]{:S(2)}, u32[]{:S(2)}) collective-permute-start(bf16[48,6144]{1,0:T(8,128)(2,1)S(1)} %add_convert_fusion.3), channel_id=1, source_target_pairs={{0,8},{8,0},{1,9},{9,1},{2,10},{10,2},{3,11},{11,3},{4,12},{12,4},... | collective-permute-start | bytes 1769480 | tf_op jit(solution)/shard_map/ppermute | solution.py:16
  287.5 10.8 %collective-permute-start.41 = (f32[128,2]{0,1:T(2,128)S(1)}, f32[128,2]{0,1:T(2,128)S(1)}, u32[]{:S(2)}, u32[]{:S(2)}) collective-permute-start(f32[128,2]{0,1:T(2,128)S(1)} %bitcast.41), channel_id=1, source_target_pairs={{0,32},{32,64},{64,96},{96,0},{1,33},{33,65},{65,97},{97,1},{2,34}... | collective-permute-start | bytes 3080 | tf_op jit(solution)/shard_map/ppermute | solution.py:40
  293.9 10.1 %collective-permute-start.55 = (bf16[24,6144]{1,0:T(8,128)(2,1)}, bf16[24,6144]{1,0:T(8,128)(2,1)}, u32[]{:S(2)}, u32[]{:S(2)}) collective-permute-start(bf16[24,6144]{1,0:T(8,128)(2,1)} %add_convert_fusion.16), channel_id=1, source_target_pairs={{0,2},{2,4},{4,6},{6,0},{1,3},{3,5},{5,7},{7,1},{8,10},{10,12},{12... | collective-permute-start | bytes 884744 | tf_op jit(solution)/shard_map/ppermute | solution.py:16
  293.9 10.1 %collective-permute-start.54 = (bf16[24,6144]{1,0:T(8,128)(2,1)}, bf16[24,6144]{1,0:T(8,128)(2,1)}, u32[]{:S(2)}, u32[]{:S(2)}) collective-permute-start(bf16[24,6144]{1,0:T(8,128)(2,1)} %add_convert_fusion.17), channel_id=1, source_target_pairs={{0,6},{2,0},{4,2},{6,4},{1,7},{3,1},{5,3},{7,5},{8,14},{10,8},{12,... | collective-permute-start | bytes 884744 | tf_op jit(solution)/shard_map/ppermute | solution.py:16
  311.6 15.0 %collective-permute-start.58 = (bf16[48,6144]{1,0:T(8,128)(2,1)S(1)}, bf16[48,6144]{1,0:T(8,128)(2,1)S(1)}, u32[]{:S(2)}, u32[]{:S(2)}) collective-permute-start(bf16[48,6144]{1,0:T(8,128)(2,1)S(1)} %pad_maximum_fusion.6), channel_id=1, source_target_pairs={{0,33},{1,32},{32,65},{33,64},{64,97},{65,96},{96,1},{97,0},{2,35}... | collective-permute-start | bytes 1769480 | tf_op jit(solution)/shard_map/ppermute | solution.py:45
  312.3 18.2 %collective-permute-start.59 = (bf16[48,6144]{1,0:T(8,128)(2,1)S(1)}, bf16[48,6144]{1,0:T(8,128)(2,1)S(1)}, u32[]{:S(2)}, u32[]{:S(2)}) collective-permute-start(bf16[48,6144]{1,0:T(8,128)(2,1)S(1)} %pad_maximum_fusion.7), channel_id=1, source_target_pairs={{0,57},{1,56},{8,49},{9,48},{16,41},{17,40},{24,33},{25,32},{32,89... | collective-permute-start | bytes 1769480 | tf_op jit(solution)/shard_map/ppermute | solution.py:55
  (59 other events, 494.4 us)

commit v5 on v3

--- a/solution.py
+++ b/solution.py
@@ -40,9 +40,19 @@
     return lax.ppermute(value, ("zh", "core"), [(s, (s + 1) % 4) for s in range(4)])
 
 
-def to_next_section_partner(value):
-    pairs = [(s * 4 + y, (s + 1) % 4 * 4 + 3 - y) for s in range(4) for y in range(4)]
-    return lax.ppermute(value, ("zh", "core", "yh", "yl"), pairs)
+def to_owner(value):
+    pairs = [(s * 2 + z, (s + 1) % 4 * 2 + 1 - z) for s in range(4) for z in range(2)]
+    return lax.ppermute(value, ("zh", "core", "zl"), pairs)
+
+
+def to_owner_across(value):
+    pairs = [
+        ((s * 4 + y) * 2 + z, ((s + 1) % 4 * 4 + 3 - y) * 2 + 1 - z)
+        for s in range(4)
+        for y in range(4)
+        for z in range(2)
+    ]
+    return lax.ppermute(value, ("zh", "core", "yh", "yl", "zl"), pairs)
 
 
 def together(*values):
@@ -65,12 +75,45 @@
     return [rows[i * size : (i + 1) * size] for i in range(count)]
 
 
+def take(arrays, part, parts):
+    return [(array, part, array.shape[0] // parts) for array in arrays]
+
+
+def sums(*wanted):
+    width = wanted[0][0][0][0].shape[1]
+    tile = width // 2
+    blocks = [term for segments in wanted for terms in segments for term in terms]
+    heights = [sum(terms[0][2] for terms in segments) for segments in wanted]
+
+    def kernel(*refs):
+        ins, outs = iter(refs[: len(blocks)]), refs[len(blocks) :]
+        for segments, out in zip(wanted, outs):
+            start = 0
+            for terms in segments:
+                total = next(ins)[...].astype(F32)
+                for _ in terms[1:]:
+                    total = total + next(ins)[...].astype(F32)
+                out[start : start + terms[0][2]] = total.astype(BF16)
+                start += terms[0][2]
+
+    return pl.pallas_call(
+        kernel,
+        grid=(width // tile,),
+        in_specs=[pl.BlockSpec((n, tile), lambda i, part=part: (part, i)) for _, part, n in blocks],
+        out_specs=[pl.BlockSpec((n, tile), lambda i: (0, i)) for n in heights],
+        out_shape=[jax.ShapeDtypeStruct((n, width), BF16) for n in heights],
+        compiler_params=pltpu.CompilerParams(dimension_semantics=("arbitrary",)),
+        name="sums",
+    )(*[array for array, _, _ in blocks])
+
+
 TILE = 1536
 
 
 def experts_kernel(*refs):
-    rows, (w_gate, w_up, w_down), rest = refs[:4], refs[4:7], refs[7:]
-    outs, (gate, up, hidden) = rest[:4], rest[4:]
+    count = (len(refs) - 6) // 2
+    rows, (w_gate, w_up, w_down), rest = refs[:count], refs[count : count + 3], refs[count + 3 :]
+    outs, (gate, up, hidden) = rest[:count], rest[count:]
     step = pl.program_id(0)
     half = pl.num_programs(0) // 2
 
@@ -98,28 +141,29 @@
             hidden[...] = (v / (1.0 + jnp.exp(-v)) * up[...]).astype(BF16)
 
         out = jnp.dot(hidden[...], w_down[...], preferred_element_type=F32).astype(BF16)
-        size = outs[0].shape[0]
-        for i, o in enumerate(outs):
-            o[...] = out[i * size : (i + 1) * size]
+        start = 0
+        for o in outs:
+            o[...] = out[start : start + o.shape[0]]
+            start += o.shape[0]
 
 
 def experts(pieces, gate_matrix, up_matrix, down_matrix):
-    size, width = pieces[0].shape
+    sizes, width = [p.shape[0] for p in pieces], pieces[0].shape[1]
     units = gate_matrix.shape[1]
     half = width // TILE
     first = lambda i: jnp.minimum(i, half - 1)
     second = lambda i: jnp.maximum(i - half, 0)
-    rows_in = pl.BlockSpec((size, TILE), lambda i: (0, first(i)))
-    rows_out = pl.BlockSpec((size, TILE), lambda i: (0, second(i)))
+    rows_in = [pl.BlockSpec((n, TILE), lambda i: (0, first(i))) for n in sizes]
+    rows_out = [pl.BlockSpec((n, TILE), lambda i: (0, second(i))) for n in sizes]
     into = pl.BlockSpec((TILE, units), lambda i: (first(i), 0))
     out_of = pl.BlockSpec((units, TILE), lambda i: (0, second(i)))
-    total = len(pieces) * size
+    total = sum(sizes)
     return pl.pallas_call(
         experts_kernel,
         grid=(2 * half,),
-        in_specs=[rows_in] * 4 + [into, into, out_of],
-        out_specs=[rows_out] * 4,
-        out_shape=[jax.ShapeDtypeStruct((size, width), BF16)] * 4,
+        in_specs=rows_in + [into, into, out_of],
+        out_specs=rows_out,
+        out_shape=[jax.ShapeDtypeStruct((n, width), BF16) for n in sizes],
         scratch_shapes=[
             pltpu.VMEM((total, units), F32),
             pltpu.VMEM((total, units), F32),
@@ -134,14 +178,7 @@
             bytes_accessed=6 * width * units + 4 * total * width,
         ),
         name="experts",
-    )(*pieces, gate_matrix, up_matrix, down_matrix)
-
-
-def slots(ids, keep, expert):
-    chosen = (ids == expert) & (keep == 1)
-    picked = jnp.any(chosen, axis=1)
-    position = jnp.cumsum(picked.astype(jnp.int32)) - 1
-    return chosen, picked, position
+    )(*pieces, *(pltpu.with_memory_space_constraint(m, pltpu.HBM) for m in (gate_matrix, up_matrix, down_matrix)))
 
 
 def body(states, expert_ids, gate_values, keep_mask, w_gate, w_up, w_down):
@@ -151,14 +188,22 @@
     mine = lax.axis_index("yh")
     other = 1 - mine
 
-    def compact(expert, tokens):
-        _, picked, position = slots(ids, keep, expert)
-        table = (position[None] == jnp.arange(CAP, dtype=jnp.int32)[:, None]) & picked[None]
+    def slots(expert):
+        chosen = (ids == expert) & (keep == 1)
+        picked = jnp.any(chosen, axis=1)
+        position = jnp.where(picked, jnp.cumsum(picked.astype(jnp.int32)) - 1, -1)
+        return position, jnp.sum(jnp.where(chosen, gates, 0.0), axis=1)
+
+    def compact(position, tokens):
+        table = position[None] == jnp.arange(CAP, dtype=jnp.int32)[:, None]
         return jnp.dot(table.astype(BF16), tokens, preferred_element_type=F32).astype(BF16)
 
-    others, tokens = together(compact(other, tokens), tokens)
+    (mine_at, mine_weight), (other_at, other_weight) = slots(mine), slots(other)
+    info = jnp.stack([mine_at.astype(F32), other_at.astype(F32), mine_weight, other_weight])
+
+    others, tokens = together(compact(other_at, tokens), tokens)
     partner = to_partner(others)
-    own = compact(mine, tokens)
+    own = compact(mine_at, tokens)
 
     a1, b = split(own, 2)
     a1_y, b_behind, b_ahead = over_y(a1), right(b), left(b)
@@ -199,53 +244,62 @@
     near_opposite, far_opposite, b_yz, g_zy, far_left, far_right, g_y, g_z = together(
         near_opposite, far_opposite, b_yz, g_zy, far_left, far_right, g_y, g_z
     )
-    near_back, far_back, b_back, g_back = (
-        right(near_right), left(far_left), over_y(b_y), over_z(g_z)
+    near_back, far_back, b_back, g_own = (
+        right(near_right), left(far_left), over_y(b_y), over_z(g_ring)
     )
     near_opposite, far_opposite, b_yz, g_zy = experts(
         [near_opposite, far_opposite, b_yz, g_zy], *matrices
     )
-
-    near_opposite, far_opposite, b_yz, g_zy, near_back, far_back, b_back, g_back = together(
-        near_opposite, far_opposite, b_yz, g_zy, near_back, far_back, b_back, g_back
-    )
-    got = left(near_opposite), right(far_opposite), over_y(b_yz), over_z(g_zy)
+    near_opposite, far_opposite, b_yz, g_y, near_back, far_back, b_back, g_own = together(
+        near_opposite, far_opposite, b_yz, g_y, near_back, far_back, b_back, g_own
+    )
+    got = left(near_opposite), right(far_opposite), over_y(b_yz), over_z(g_y)
     near_left, far_right = add(near_left, got[0]), add(far_right, got[1])
-    b_z, g_y = add(b_z, got[2]), add(g_y, got[3])
-    ids, gates, keep, near_left, far_right, b_z, g_y = together(
-        ids, gates, keep, near_left, far_right, b_z, g_y
-    )
-
-    got = together(left(near_left), right(far_right), over_y(g_y), over_z(b_z))
-    ids, gates, keep = (to_next_section(v) for v in (ids, gates, keep))
-    near, far = add(near, near_back, got[0]), add(far, far_back, got[1])
-    g_ring, b_ring = add(g_ring, g_back, got[2]), add(b_ring, b_back, got[3])
-
-    (a1_near, a2_near), (a1_far, a2_far) = split(near, 2), split(far, 2)
-    b, b_behind, b_ahead, b_opposite = split(b_ring, 4)
-    g, g_behind, g_ahead, g_opposite = split(g_ring, 4)
-    got = together(
-        left(join(b_opposite, g_ahead)), right(join(g_opposite, b_ahead)), over_z(a1_far), over_y(a2_far)
-    )
-    (b_behind_back, g_back), (g_behind_back, b_back) = split(got[0], 2), split(got[1], 2)
-    a1_near, a2_near = add(a1_near, got[2]), add(a2_near, got[3])
-    (a1, a1_y), (a2, a2_z) = split(a1_near, 2), split(a2_near, 2)
-    got = together(
-        left(add(b_behind, b_behind_back)), right(add(g_behind, g_behind_back)), over_y(a1_y), over_z(a2_z)
-    )
-    own = join(add(a1, got[2]), add(b, b_back, got[0]))
-    partner = join(add(a2, got[3]), add(g, g_back, got[1]))
-
-    own_done, other_done = to_next_section(own), to_next_section_partner(partner)
-
-    def contribution(expert, done):
-        chosen, picked, position = slots(ids, keep, expert)
-        weight = jnp.sum(jnp.where(chosen, gates, 0.0), axis=1)
-        table = (position[:, None] == jnp.arange(CAP, dtype=jnp.int32)[None]) & picked[:, None]
+    b_ring, g_zy = add(b_ring, b_back), add(g_zy, got[3])
+    info, b_yz_back, near_left, far_right, b_ring, g_zy = together(
+        info, got[2], near_left, far_right, b_ring, g_zy
+    )
+    *got, info = together(
+        left(near_left), right(far_right), over_z(b_ring), over_y(g_zy), to_next_section(info)
+    )
+
+    near, far = (near, near_back, got[0]), (far, far_back, got[1])
+    b_terms, g_terms = (b_z, b_yz_back, got[2]), (g_z, g_own, got[3])
+    got = sums(
+        [take(b_terms, 3, 4), take(g_terms, 2, 4)],
+        [take(g_terms, 3, 4), take(b_terms, 2, 4)],
+        [take(near, 0, 2)],
+        [take(far, 1, 2)],
+    )
+    got = together(left(got[0]), right(got[1]), over_z(got[2]), over_y(got[3]))
+    a1_terms = take(far, 0, 4), take(far, 1, 4)
+    a2_terms = take(near, 2, 4), take(near, 3, 4)
+    ends = sums(
+        [take(b_terms, 1, 4) + take(got[:1], 0, 2)],
+        [take(g_terms, 1, 4) + take(got[1:2], 0, 2)],
+        [a1_terms[1] + take(got[2:3], 1, 2)],
+        [a2_terms[0] + take(got[3:], 0, 2)],
+    )
+    ends = together(left(ends[0]), right(ends[1]), over_y(ends[2]), over_z(ends[3]))
+    own, partner = sums(
+        [
+            a1_terms[0] + take(got[2:3], 0, 2) + take(ends[2:3], 0, 1),
+            take(b_terms, 0, 4) + take(got[1:2], 1, 2) + take(ends[:1], 0, 1),
+        ],
+        [
+            a2_terms[1] + take(got[3:], 1, 2) + take(ends[3:], 0, 1),
+            take(g_terms, 0, 4) + take(got[:1], 1, 2) + take(ends[1:2], 0, 1),
+        ],
+    )
+
+    own_done, other_done = to_owner(own), to_owner_across(partner)
+
+    def contribution(position, weight, done):
+        table = position[:, None] == jnp.arange(CAP, dtype=F32)[None]
         rows = jnp.dot(table.astype(BF16), done, preferred_element_type=F32)
         return weight[:, None] * rows
 
-    mixed = contribution(mine, own_done) + contribution(other, other_done)
+    mixed = contribution(info[0], info[2], own_done) + contribution(info[1], info[3], other_done)
     return mixed.astype(BF16)[None]
 
 

time: 259 us -> 268 us (1.035)
  Pallas kernels: 46.4 us -> 67.8 us
  other arithmetic: 16 us -> 2.94 us
  waiting for transfers between devices: 111 us -> 123 us
  local copies, waits for them, and re-layouts: 20.3 us -> 9.7 us
    pallas_call x4 -> x7, Pallas kernels: 46.4 us -> 67.8 us  [the longest x4 55.8 us: experts(): pl.pallas_call(experts_kernel, grid=(2 * half,), in_specs=rows_in + [into...]
    ppermute x42, waiting for transfers between devices: 78.6 us -> 90.9 us  [shift(): return lax.ppermute(value, axis, [(i, (i + by) % n) for i in range(n)])]
    ppermute x4 -> x1, waiting for transfers between devices: 23.8 us -> 11.8 us  [to_next_section(): lax.ppermute(value, ('zh', 'core'), [(s, (s + 1) % 4) for s in range(4)])]
    ppermute x1 -> x2, waiting for transfers between devices: 2.25 us -> 14.1 us  [the longest x1 14.1 us: to_owner_across(): return lax.ppermute(value, ('zh', 'core', 'yh', 'yl', 'zl'), pairs)]
    convert_element_type x15 -> x4, other arithmetic: 11.7 us -> 1.16 us  [add(): return total.astype(BF16)]
    unnamed x47 -> x45, local copies, waits for them, and re-layouts: 18.1 us -> 9.35 us
  transfers between devices with their start and end apart: 48 -> 46, of which waited for: 23 -> 21; matrix products, arithmetic and copies ran while one was open for 5% -> 1% of each run, Pallas kernels for 18% -> 21%
where the time goes in v5:
time: 268 us; the launch traced here: 267 us
  waiting for transfers between devices  123 us (46%)
  Pallas kernels  67.8 us (25%)
  starting transfers between devices  60.4 us (23%)
  local copies, waits for them, and re-layouts  9.7 us (4%)
  matrix products  3.07 us (1%)
  other arithmetic  2.94 us (1%)
    ppermute x42, waiting for transfers between devices, shift(): return lax.ppermute(value, axis, [(i, (i + by) % n) for i in range(n)])  90.9 us
    pallas_call x4, Pallas kernels, experts(): pl.pallas_call(experts_kernel, grid=(2 * half,), in_specs=rows_in + [into...  55.8 us
    ppermute x42, starting transfers between devices, shift(): return lax.ppermute(value, axis, [(i, (i + by) % n) for i in range(n)])  53.3 us
    ppermute x1, waiting for transfers between devices, to_owner_across(): return lax.ppermute(value, ('zh', 'core', 'yh', 'yl', 'zl'), pairs)  14.1 us
    pallas_call x3, Pallas kernels, sums(): pl.pallas_call(kernel, grid=(width // tile,), in_specs=[pl.BlockSpec((n,...  12 us
    ppermute x1, waiting for transfers between devices, to_next_section(): lax.ppermute(value, ('zh', 'core'), [(s, (s + 1) % 4) for s in range(4)])  11.8 us
    unnamed x45, local copies, waits for them, and re-layouts  9.35 us
    ppermute x1, waiting for transfers between devices, to_partner(): return lax.ppermute(value, ('yh', 'yl'), [(y, 3 - y) for y in range(4)])  6.32 us
  transfers between devices with their start and end apart: 46, of which 21 were waited for; matrix products, arithmetic and copies ran while one was open for 1% of the time, Pallas kernels for 21%

profile of v5, /device:TPU:0, one launch (start us, length us, event | category | flops | bytes accessed | tf_op | source)
XLA Modules:
  0.0 267.5 jit_solution(9143119952553223928)
XLA Ops:
  2.5 1.7 collective-permute-start
  4.2 2.8 %collective-permute-start.7 = (bf16[24,6144]{1,0:T(8,128)(2,1)S(1)}, bf16[24,6144]{1,0:T(8,128)(2,1)S(1)}, u32[]{:S(2)}, u32[]{:S(2)}) collective-permute-start(bf16[24,6144]{1,0:T(8,128)(2,1)S(1)} %get-tuple-element.183), channel_id=1, source_target_pairs={{0,6},{2,0},{4,2},{6,4},{1,7},{3,1},{5,3},{7,5},{8,14},{10,8},{12,... | collective-permute-start | bytes 884744 | tf_op jit(solution)/shard_map/ppermute | solution.py:16
  7.0 2.2 collective-permute-start.1
  9.2 2.1 collective-permute-done
  11.3 2.2 collective-permute-start.11
  13.4 2.9 %collective-permute-done.6 = bf16[24,6144]{1,0:T(8,128)(2,1)S(1)} collective-permute-done((bf16[24,6144]{1,0:T(8,128)(2,1)S(1)}, bf16[24,6144]{1,0:T(8,128)(2,1)S(1)}, u32[]{:S(2)}, u32[]{:S(2)}) %collective-permute-start.6) | collective-permute-done | bytes 294944 | tf_op jit(solution)/shard_map/ppermute | solution.py:16
  16.4 6.3 %collective-permute-done.1 = bf16[48,6144]{1,0:T(8,128)(2,1)S(1)} collective-permute-done((bf16[48,6144]{1,0:T(8,128)(2,1)S(1)}, bf16[48,6144]{1,0:T(8,128)(2,1)S(1)}, u32[]{:S(2)}, u32[]{:S(2)}) %collective-permute-start.1) | collective-permute-done | bytes 589856 | tf_op jit(solution)/shard_map/ppermute | solution.py:36
  23.3 2.8 %collective-permute-start.4 = (bf16[24,6144]{1,0:T(8,128)(2,1)S(1)}, bf16[24,6144]{1,0:T(8,128)(2,1)S(1)}, u32[]{:S(2)}, u32[]{:S(2)}) collective-permute-start(bf16[24,6144]{1,0:T(8,128)(2,1)S(1)} %get-tuple-element.181), channel_id=1, source_target_pairs={{0,6},{2,0},{4,2},{6,4},{1,7},{3,1},{5,3},{7,5},{8,14},{10,8},{12,... | collective-permute-start | bytes 884744 | tf_op jit(solution)/shard_map/ppermute | solution.py:16
  26.1 1.9 collective-permute-start.2
  28.2 3.1 %collective-permute-done.5 = bf16[24,6144]{1,0:T(8,128)(2,1)S(1)} collective-permute-done((bf16[24,6144]{1,0:T(8,128)(2,1)S(1)}, bf16[24,6144]{1,0:T(8,128)(2,1)S(1)}, u32[]{:S(2)}, u32[]{:S(2)}) %collective-permute-start.5) | collective-permute-done | bytes 294944 | tf_op jit(solution)/shard_map/ppermute | solution.py:16
  31.3 3.0 %collective-permute-start.9 = (bf16[24,6144]{1,0:T(8,128)(2,1)S(1)}, bf16[24,6144]{1,0:T(8,128)(2,1)S(1)}, u32[]{:S(2)}, u32[]{:S(2)}) collective-permute-start(bf16[24,6144]{1,0:T(8,128)(2,1)S(1)} %collective-permute-done.4), channel_id=1, source_target_pairs={{0,6},{2,0},{4,2},{6,4},{1,7},{3,1},{5,3},{7,5},{8,14},{10,8},{12,... | collective-permute-start | bytes 884744 | tf_op jit(solution)/shard_map/ppermute | solution.py:16
  35.6 1.7 collective-permute-start.13
  38.6 3.7 %collective-permute-start.10 = (bf16[96,6144]{1,0:T(8,128)(2,1)S(1)}, bf16[96,6144]{1,0:T(8,128)(2,1)S(1)}, u32[]{:S(2)}, u32[]{:S(2)}) collective-permute-start(bf16[96,6144]{1,0:T(8,128)(2,1)S(1)} %pad_maximum_fusion.refs_0_), channel_id=1, source_target_pairs={{0,6},{2,0},{4,2},{6,4},{1,7},{3,1},{5,3},{7,5},{8,14},{10,8},{12,... | collective-permute-start | bytes 3538952 | tf_op jit(solution)/shard_map/ppermute | solution.py:16
  42.4 23.8 %collective-permute-done.12 = bf16[48,6144]{1,0:T(8,128)(2,1)S(1)} collective-permute-done((bf16[48,6144]{1,0:T(8,128)(2,1)S(1)}, bf16[48,6144]{1,0:T(8,128)(2,1)S(1)}, u32[]{:S(2)}, u32[]{:S(2)}) %collective-permute-start.12) | collective-permute-done | bytes 589856 | tf_op jit(solution)/shard_map/ppermute | solution.py:16
  66.2 1.5 collective-permute-start.17
  68.9 13.9 %experts.4 = (bf16[96,6144]{1,0:T(8,128)(2,1)S(1)}, bf16[96,6144]{1,0:T(8,128)(2,1)S(1)}, bf16[96,6144]{1,0:T(8,128)(2,1)S(1)}, bf16[96,6144]{1,0:T(8,128)(2,1)S(1)}) custom-call(bf16[96,6144]{1,0:T(8,128)(2,1)S(1)} %pad_maximum_fusion.refs_0_, bf16[96,6144]{1,0:T(8,128)(2,1)S(1)} %pad_maximum_fusion.1.refs_1_, ...), custom_call_target="tpu_custom_call" | custom-call | flops 7247757312 | bytes 28311552 | tf_op jit(solution)/shard_map/experts/pallas_call | solution.py:161
  84.0 13.9 %experts.5 = (bf16[96,6144]{1,0:T(8,128)(2,1)S(1)}, bf16[96,6144]{1,0:T(8,128)(2,1)S(1)}, bf16[96,6144]{1,0:T(8,128)(2,1)S(1)}, bf16[96,6144]{1,0:T(8,128)(2,1)S(1)}) custom-call(bf16[96,6144]{1,0:T(8,128)(2,1)S(1)} %collective-permute-done.3.refs_0_, bf16[96,6144]{1,0:T(8,128)(2,1)S(1)} %collective-permute-done.10.refs_1_, ...), custom_call_target="tpu_custom_call" | custom-call | flops 7247757312 | bytes 28311552 | tf_op jit(solution)/shard_map/experts/pallas_call | solution.py:161
  100.0 1.7 collective-permute-start.21
  101.7 3.2 %collective-permute-start.20 = (bf16[96,6144]{1,0:T(8,128)(2,1)S(1)}, bf16[96,6144]{1,0:T(8,128)(2,1)S(1)}, u32[]{:S(2)}, u32[]{:S(2)}) collective-permute-start(bf16[96,6144]{1,0:T(8,128)(2,1)S(1)} %collective-permute-done.17.refs_1_), channel_id=1, source_target_pairs={{0,6},{2,0},{4,2},{6,4},{1,7},{3,1},{5,3},{7,5},{8,14},{10,8},{12,... | collective-permute-start | bytes 3538952 | tf_op jit(solution)/shard_map/ppermute | solution.py:16
  104.9 1.7 collective-permute-start.22
  107.0 13.9 %experts.6 = (bf16[96,6144]{1,0:T(8,128)(2,1)S(1)}, bf16[96,6144]{1,0:T(8,128)(2,1)S(1)}, bf16[96,6144]{1,0:T(8,128)(2,1)S(1)}, bf16[96,6144]{1,0:T(8,128)(2,1)S(1)}) custom-call(bf16[96,6144]{1,0:T(8,128)(2,1)S(1)} %collective-permute-done.16.refs_0_, bf16[96,6144]{1,0:T(8,128)(2,1)S(1)} %collective-permute-done.17.refs_1_, ...), custom_call_target="tpu_custom_call" | custom-call | flops 7247757312 | bytes 28311552 | tf_op jit(solution)/shard_map/experts/pallas_call | solution.py:161
  122.2 6.6 %collective-permute-done.21.refs_2_ = bf16[96,6144]{1,0:T(8,128)(2,1)S(1)} collective-permute-done((bf16[96,6144]{1,0:T(8,128)(2,1)S(1)}, bf16[96,6144]{1,0:T(8,128)(2,1)S(1)}, u32[]{:S(2)}, u32[]{:S(2)}) %collective-permute-start.21) | collective-permute-done | bytes 1179680 | tf_op jit(solution)/shard_map/ppermute | solution.py:16
  130.0 3.9 %collective-permute-done.22.refs_3_ = bf16[96,6144]{1,0:T(8,128)(2,1)S(1)} collective-permute-done((bf16[96,6144]{1,0:T(8,128)(2,1)S(1)}, bf16[96,6144]{1,0:T(8,128)(2,1)S(1)}, u32[]{:S(2)}, u32[]{:S(2)}) %collective-permute-start.22) | collective-permute-done | bytes 1179680 | tf_op jit(solution)/shard_map/ppermute | solution.py:16
  133.9 1.5 collective-permute-start.24
  135.3 14.0 %experts.7 = (bf16[96,6144]{1,0:T(8,128)(2,1)S(1)}, bf16[96,6144]{1,0:T(8,128)(2,1)S(1)}, bf16[96,6144]{1,0:T(8,128)(2,1)S(1)}, bf16[96,6144]{1,0:T(8,128)(2,1)S(1)}) custom-call(bf16[96,6144]{1,0:T(8,128)(2,1)S(1)} %collective-permute-done.15.refs_0_, bf16[96,6144]{1,0:T(8,128)(2,1)S(1)} %collective-permute-done.20.refs_1_, ...), custom_call_target="tpu_custom_call" | custom-call | flops 7247757312 | bytes 28311552 | tf_op jit(solution)/shard_map/experts/pallas_call | solution.py:161
  149.3 4.9 %collective-permute-done.26.refs_4_.refs_7_.refs_5_.refs_16_ = bf16[96,6144]{1,0:T(8,128)(2,1)S(1)} collective-permute-done((bf16[96,6144]{1,0:T(8,128)(2,1)S(1)}, bf16[96,6144]{1,0:T(8,128)(2,1)S(1)}, u32[]{:S(2)}, u32[]{:S(2)}) %collective-permute-start.26) | collective-permute-done | bytes 1179680 | tf_op jit(solution)/shard_map/ppermute | solution.py:16
  154.3 2.2 collective-permute-start.28
  156.6 1.7 collective-permute-start.30
  158.6 19.4 %collective-permute-done.28 = bf16[96,6144]{1,0:T(8,128)(2,1)S(1)} collective-permute-done((bf16[96,6144]{1,0:T(8,128)(2,1)S(1)}, bf16[96,6144]{1,0:T(8,128)(2,1)S(1)}, u32[]{:S(2)}, u32[]{:S(2)}) %collective-permute-start.28) | collective-permute-done | bytes 1179680 | tf_op jit(solution)/shard_map/ppermute | solution.py:16
  178.6 1.6 collective-permute-done.30
  180.5 2.2 collective-permute-start.31
  182.7 1.7 collective-permute-start.33
  184.4 2.0 collective-permute-start.34
  186.5 11.8 %collective-permute-done.35 = f32[4,128]{1,0:T(4,128)S(1)} collective-permute-done((f32[4,128]{1,0:T(4,128)S(1)}, f32[4,128]{1,0:T(4,128)S(1)}, u32[]{:S(2)}, u32[]{:S(2)}) %collective-permute-start.35) | collective-permute-done | bytes 2080 | tf_op jit(solution)/shard_map/ppermute | solution.py:40
  198.3 3.0 %collective-permute-done.31.refs_14_.refs_12_ = bf16[96,6144]{1,0:T(8,128)(2,1)S(1)} collective-permute-done((bf16[96,6144]{1,0:T(8,128)(2,1)S(1)}, bf16[96,6144]{1,0:T(8,128)(2,1)S(1)}, u32[]{:S(2)}, u32[]{:S(2)}) %collective-permute-start.31) | collective-permute-done | bytes 1179680 | tf_op jit(solution)/shard_map/ppermute | solution.py:16
  205.7 4.5 %sums.3 = (bf16[48,6144]{1,0:T(8,128)(2,1)}, bf16[48,6144]{1,0:T(8,128)(2,1)}, bf16[48,6144]{1,0:T(8,128)(2,1)}, bf16[48,6144]{1,0:T(8,128)(2,1)}) custom-call(bf16[96,6144]{1,0:T(8,128)(2,1)} %copy-done.2, bf16[96,6144]{1,0:T(8,128)(2,1)} %copy-done.7, bf16[96,6144]{1,0:T(8,128)(2,1)} %copy-done.8, bf16[96,6144]{1,0:T(8,128)(2,1)} %copy-done.3, ...), custom_call_target="tpu_custom_call" | custom-call | tf_op jit(solution)/shard_map/sums/pallas_call | solution.py:99
  210.2 2.9 %collective-permute-start.36 = (bf16[48,6144]{1,0:T(8,128)(2,1)}, bf16[48,6144]{1,0:T(8,128)(2,1)S(1)}, u32[]{:S(2)}, u32[]{:S(2)}) collective-permute-start(bf16[48,6144]{1,0:T(8,128)(2,1)} %get-tuple-element.159), channel_id=1, source_target_pairs={{0,6},{2,0},{4,2},{6,4},{1,7},{3,1},{5,3},{7,5},{8,14},{10,8},{12,... | collective-permute-start | bytes 1769480 | tf_op jit(solution)/shard_map/ppermute | solution.py:16
  213.1 1.6 collective-permute-start.38
  215.2 5.6 %collective-permute-done.36.refs_3_.refs_18_ = bf16[48,6144]{1,0:T(8,128)(2,1)S(1)} collective-permute-done((bf16[48,6144]{1,0:T(8,128)(2,1)}, bf16[48,6144]{1,0:T(8,128)(2,1)S(1)}, u32[]{:S(2)}, u32[]{:S(2)}) %collective-permute-start.36) | collective-permute-done | bytes 589856 | tf_op jit(solution)/shard_map/ppermute | solution.py:16
  220.8 3.6 %collective-permute-done.37.refs_7_.refs_8_ = bf16[48,6144]{1,0:T(8,128)(2,1)S(1)} collective-permute-done((bf16[48,6144]{1,0:T(8,128)(2,1)}, bf16[48,6144]{1,0:T(8,128)(2,1)S(1)}, u32[]{:S(2)}, u32[]{:S(2)}) %collective-permute-start.37) | collective-permute-done | bytes 589856 | tf_op jit(solution)/shard_map/ppermute | solution.py:16
  226.2 3.5 %sums.4 = (bf16[24,6144]{1,0:T(8,128)(2,1)}, bf16[24,6144]{1,0:T(8,128)(2,1)}, bf16[24,6144]{1,0:T(8,128)(2,1)}, bf16[24,6144]{1,0:T(8,128)(2,1)}) custom-call(bf16[96,6144]{1,0:T(8,128)(2,1)} %copy-done.2, bf16[96,6144]{1,0:T(8,128)(2,1)} %copy-done.7, bf16[96,6144]{1,0:T(8,128)(2,1)} %copy-done.8, bf16[48,6144]{1,0:T(8,128)(2,1)} %copy-done.14, ...), custom_call_target="tpu_custom_call" | custom-call | tf_op jit(solution)/shard_map/sums/pallas_call | solution.py:99
  229.7 2.7 collective-permute-start.40
  234.0 3.0 %collective-permute-done.40.refs_9_ = bf16[24,6144]{1,0:T(8,128)(2,1)S(1)} collective-permute-done((bf16[24,6144]{1,0:T(8,128)(2,1)}, bf16[24,6144]{1,0:T(8,128)(2,1)S(1)}, u32[]{:S(2)}, u32[]{:S(2)}) %collective-permute-start.40) | collective-permute-done | bytes 294944 | tf_op jit(solution)/shard_map/ppermute | solution.py:16
  236.9 3.6 %collective-permute-done.41.refs_19_ = bf16[24,6144]{1,0:T(8,128)(2,1)S(1)} collective-permute-done((bf16[24,6144]{1,0:T(8,128)(2,1)}, bf16[24,6144]{1,0:T(8,128)(2,1)S(1)}, u32[]{:S(2)}, u32[]{:S(2)}) %collective-permute-start.41) | collective-permute-done | bytes 294944 | tf_op jit(solution)/shard_map/ppermute | solution.py:16
  242.1 4.0 %sums.5 = (bf16[48,6144]{1,0:T(8,128)(2,1)}, bf16[48,6144]{1,0:T(8,128)(2,1)}) custom-call(bf16[96,6144]{1,0:T(8,128)(2,1)} %copy-done.5, bf16[96,6144]{1,0:T(8,128)(2,1)} %copy-done.11, bf16[96,6144]{1,0:T(8,128)(2,1)} %copy-done.13, bf16[48,6144]{1,0:T(8,128)(2,1)} %copy-done.16, bf16[24,6144]{1,0:T(8,128)(2,1)} %copy-done.20, bf16[96,6144]{1,0:T(8,128)(2,1)} %copy-done.2, ...), custom_call_target="tpu_custom_call" | custom-call | tf_op jit(solution)/shard_map/sums/pallas_call | solution.py:99
  246.1 4.9 %collective-permute-start.44 = (bf16[48,6144]{1,0:T(8,128)(2,1)}, bf16[48,6144]{1,0:T(8,128)(2,1)S(1)}, u32[]{:S(2)}, u32[]{:S(2)}) collective-permute-start(bf16[48,6144]{1,0:T(8,128)(2,1)} %get-tuple-element.175), channel_id=1, source_target_pairs={{0,33},{1,32},{32,65},{33,64},{64,97},{65,96},{96,1},{97,0},{2,35}... | collective-permute-start | bytes 1769480 | tf_op jit(solution)/shard_map/ppermute | solution.py:45
  251.0 14.1 %collective-permute-done.45 = bf16[48,6144]{1,0:T(8,128)(2,1)S(1)} collective-permute-done((bf16[48,6144]{1,0:T(8,128)(2,1)}, bf16[48,6144]{1,0:T(8,128)(2,1)S(1)}, u32[]{:S(2)}, u32[]{:S(2)}) %collective-permute-start.45) | collective-permute-done | bytes 589856 | tf_op jit(solution)/shard_map/ppermute | solution.py:55
  265.7 1.8 fusion.2
  (128 shorter events, 24.8 us)
Async XLA Ops:
  2.5 8.7 %collective-permute-start = (bf16[24,6144]{1,0:T(8,128)(2,1)S(1)}, bf16[24,6144]{1,0:T(8,128)(2,1)S(1)}, u32[]{:S(2)}, u32[]{:S(2)}) collective-permute-start(bf16[24,6144]{1,0:T(8,128)(2,1)S(1)} %get-tuple-element.184), channel_id=1, source_target_pairs={{0,8},{8,0},{1,9},{9,1},{2,10},{10,2},{3,11},{11,3},{4,12},{12,4},... | collective-permute-start | bytes 884744 | tf_op jit(solution)/shard_map/ppermute | solution.py:16
  4.2 21.8 %collective-permute-start.7 = (bf16[24,6144]{1,0:T(8,128)(2,1)S(1)}, bf16[24,6144]{1,0:T(8,128)(2,1)S(1)}, u32[]{:S(2)}, u32[]{:S(2)}) collective-permute-start(bf16[24,6144]{1,0:T(8,128)(2,1)S(1)} %get-tuple-element.183), channel_id=1, source_target_pairs={{0,6},{2,0},{4,2},{6,4},{1,7},{3,1},{5,3},{7,5},{8,14},{10,8},{12,... | collective-permute-start | bytes 884744 | tf_op jit(solution)/shard_map/ppermute | solution.py:16
  7.0 9.4 %collective-permute-start.6 = (bf16[24,6144]{1,0:T(8,128)(2,1)S(1)}, bf16[24,6144]{1,0:T(8,128)(2,1)S(1)}, u32[]{:S(2)}, u32[]{:S(2)}) collective-permute-start(bf16[24,6144]{1,0:T(8,128)(2,1)S(1)} %get-tuple-element.183), channel_id=1, source_target_pairs={{0,2},{2,4},{4,6},{6,0},{1,3},{3,5},{5,7},{7,1},{8,10},{10,12},{12... | collective-permute-start | bytes 884744 | tf_op jit(solution)/shard_map/ppermute | solution.py:16
  7.0 15.7 %collective-permute-start.1 = (bf16[48,6144]{1,0:T(8,128)(2,1)S(1)}, bf16[48,6144]{1,0:T(8,128)(2,1)S(1)}, u32[]{:S(2)}, u32[]{:S(2)}) collective-permute-start(bf16[48,6144]{1,0:T(8,128)(2,1)S(1)} %convolution_convert_fusion.1), channel_id=1, source_target_pairs={{0,24},{8,16},{16,8},{24,0},{1,25},{9,17},{17,9},{25,1},{2,26},{10... | collective-permute-start | bytes 1769480 | tf_op jit(solution)/shard_map/ppermute | solution.py:36
  11.3 24.3 %collective-permute-start.11 = (bf16[48,6144]{1,0:T(8,128)(2,1)S(1)}, bf16[48,6144]{1,0:T(8,128)(2,1)S(1)}, u32[]{:S(2)}, u32[]{:S(2)}) collective-permute-start(bf16[48,6144]{1,0:T(8,128)(2,1)S(1)} %pad_maximum_fusion.3), channel_id=1, source_target_pairs={{0,1},{1,0},{2,3},{3,2},{4,5},{5,4},{6,7},{7,6},{8,9},{9,8},{10,11... | collective-permute-start | bytes 1769480 | tf_op jit(solution)/shard_map/ppermute | solution.py:16
  16.4 11.6 %collective-permute-start.8 = (bf16[24,6144]{1,0:T(8,128)(2,1)S(1)}, bf16[24,6144]{1,0:T(8,128)(2,1)S(1)}, u32[]{:S(2)}, u32[]{:S(2)}) collective-permute-start(bf16[24,6144]{1,0:T(8,128)(2,1)S(1)} %collective-permute-done.6), channel_id=1, source_target_pairs={{0,2},{2,4},{4,6},{6,0},{1,3},{3,5},{5,7},{7,1},{8,10},{10,12},{12... | collective-permute-start | bytes 884744 | tf_op jit(solution)/shard_map/ppermute | solution.py:16
  22.8 8.5 %collective-permute-start.5 = (bf16[24,6144]{1,0:T(8,128)(2,1)S(1)}, bf16[24,6144]{1,0:T(8,128)(2,1)S(1)}, u32[]{:S(2)}, u32[]{:S(2)}) collective-permute-start(bf16[24,6144]{1,0:T(8,128)(2,1)S(1)} %get-tuple-element.181), channel_id=1, source_target_pairs={{0,2},{2,4},{4,6},{6,0},{1,3},{3,5},{5,7},{7,1},{8,10},{10,12},{12... | collective-permute-start | bytes 884744 | tf_op jit(solution)/shard_map/ppermute | solution.py:16
  23.3 8.0 %collective-permute-start.4 = (bf16[24,6144]{1,0:T(8,128)(2,1)S(1)}, bf16[24,6144]{1,0:T(8,128)(2,1)S(1)}, u32[]{:S(2)}, u32[]{:S(2)}) collective-permute-start(bf16[24,6144]{1,0:T(8,128)(2,1)S(1)} %get-tuple-element.181), channel_id=1, source_target_pairs={{0,6},{2,0},{4,2},{6,4},{1,7},{3,1},{5,3},{7,5},{8,14},{10,8},{12,... | collective-permute-start | bytes 884744 | tf_op jit(solution)/shard_map/ppermute | solution.py:16
  26.1 8.2 %collective-permute-start.2 = (bf16[24,6144]{1,0:T(8,128)(2,1)S(1)}, bf16[24,6144]{1,0:T(8,128)(2,1)S(1)}, u32[]{:S(2)}, u32[]{:S(2)}) collective-permute-start(bf16[24,6144]{1,0:T(8,128)(2,1)S(1)} %get-tuple-element.182), channel_id=1, source_target_pairs={{0,1},{1,0},{2,3},{3,2},{4,5},{5,4},{6,7},{7,6},{8,9},{9,8},{10,11... | collective-permute-start | bytes 884744 | tf_op jit(solution)/shard_map/ppermute | solution.py:16
  28.1 39.7 %collective-permute-start.14 = (bf16[96,6144]{1,0:T(8,128)(2,1)S(1)}, bf16[96,6144]{1,0:T(8,128)(2,1)S(1)}, u32[]{:S(2)}, u32[]{:S(2)}) collective-permute-start(bf16[96,6144]{1,0:T(8,128)(2,1)S(1)} %pad_maximum_fusion.1.refs_1_), channel_id=1, source_target_pairs={{0,8},{8,0},{1,9},{9,1},{2,10},{10,2},{3,11},{11,3},{4,12},{12,4},... | collective-permute-start | bytes 3538952 | tf_op jit(solution)/shard_map/ppermute | solution.py:16
  31.3 7.3 %collective-permute-start.9 = (bf16[24,6144]{1,0:T(8,128)(2,1)S(1)}, bf16[24,6144]{1,0:T(8,128)(2,1)S(1)}, u32[]{:S(2)}, u32[]{:S(2)}) collective-permute-start(bf16[24,6144]{1,0:T(8,128)(2,1)S(1)} %collective-permute-done.4), channel_id=1, source_target_pairs={{0,6},{2,0},{4,2},{6,4},{1,7},{3,1},{5,3},{7,5},{8,14},{10,8},{12,... | collective-permute-start | bytes 884744 | tf_op jit(solution)/shard_map/ppermute | solution.py:16
  34.3 31.9 %collective-permute-start.12 = (bf16[48,6144]{1,0:T(8,128)(2,1)S(1)}, bf16[48,6144]{1,0:T(8,128)(2,1)S(1)}, u32[]{:S(2)}, u32[]{:S(2)}) collective-permute-start(bf16[48,6144]{1,0:T(8,128)(2,1)S(1)} %pad_maximum_fusion.4), channel_id=1, source_target_pairs={{0,8},{8,0},{1,9},{9,1},{2,10},{10,2},{3,11},{11,3},{4,12},{12,4},... | collective-permute-start | bytes 1769480 | tf_op jit(solution)/shard_map/ppermute | solution.py:16
  34.7 33.7 %collective-permute-start.3 = (bf16[96,6144]{1,0:T(8,128)(2,1)S(1)}, bf16[96,6144]{1,0:T(8,128)(2,1)S(1)}, u32[]{:S(2)}, u32[]{:S(2)}) collective-permute-start(bf16[96,6144]{1,0:T(8,128)(2,1)S(1)} %pad_maximum_fusion.refs_0_), channel_id=1, source_target_pairs={{0,2},{2,4},{4,6},{6,0},{1,3},{3,5},{5,7},{7,1},{8,10},{10,12},{12... | collective-permute-start | bytes 3538952 | tf_op jit(solution)/shard_map/ppermute | solution.py:16
  35.6 33.1 %collective-permute-start.13 = (bf16[96,6144]{1,0:T(8,128)(2,1)S(1)}, bf16[96,6144]{1,0:T(8,128)(2,1)S(1)}, u32[]{:S(2)}, u32[]{:S(2)}) collective-permute-start(bf16[96,6144]{1,0:T(8,128)(2,1)S(1)} %pad_maximum_fusion.1.refs_1_), channel_id=1, source_target_pairs={{0,1},{1,0},{2,3},{3,2},{4,5},{5,4},{6,7},{7,6},{8,9},{9,8},{10,11... | collective-permute-start | bytes 3538952 | tf_op jit(solution)/shard_map/ppermute | solution.py:16
  38.6 45.2 %collective-permute-start.10 = (bf16[96,6144]{1,0:T(8,128)(2,1)S(1)}, bf16[96,6144]{1,0:T(8,128)(2,1)S(1)}, u32[]{:S(2)}, u32[]{:S(2)}) collective-permute-start(bf16[96,6144]{1,0:T(8,128)(2,1)S(1)} %pad_maximum_fusion.refs_0_), channel_id=1, source_target_pairs={{0,6},{2,0},{4,2},{6,4},{1,7},{3,1},{5,3},{7,5},{8,14},{10,8},{12,... | collective-permute-start | bytes 3538952 | tf_op jit(solution)/shard_map/ppermute | solution.py:16
  66.2 33.8 %collective-permute-start.17 = (bf16[96,6144]{1,0:T(8,128)(2,1)S(1)}, bf16[96,6144]{1,0:T(8,128)(2,1)S(1)}, u32[]{:S(2)}, u32[]{:S(2)}) collective-permute-start(bf16[96,6144]{1,0:T(8,128)(2,1)S(1)} %constant_dynamic-update-slice_fusion.refs_2_), channel_id=1, source_target_pairs={{0,6},{2,0},{4,2},{6,4},{1,7},{3,1},{5,3},{7,5},{8,14},{10,8},{12,... | collective-permute-start | bytes 3538952 | tf_op jit(solution)/shard_map/ppermute | solution.py:16
  67.8 34.0 %collective-permute-start.16 = (bf16[96,6144]{1,0:T(8,128)(2,1)S(1)}, bf16[96,6144]{1,0:T(8,128)(2,1)S(1)}, u32[]{:S(2)}, u32[]{:S(2)}) collective-permute-start(bf16[96,6144]{1,0:T(8,128)(2,1)S(1)} %constant_dynamic-update-slice_fusion.refs_2_), channel_id=1, source_target_pairs={{0,2},{2,4},{4,6},{6,0},{1,3},{3,5},{5,7},{7,1},{8,10},{10,12},{12... | collective-permute-start | bytes 3538952 | tf_op jit(solution)/shard_map/ppermute | solution.py:16
  68.3 33.4 %collective-permute-start.19 = (bf16[96,6144]{1,0:T(8,128)(2,1)S(1)}, bf16[96,6144]{1,0:T(8,128)(2,1)S(1)}, u32[]{:S(2)}, u32[]{:S(2)}) collective-permute-start(bf16[96,6144]{1,0:T(8,128)(2,1)S(1)} %pad_maximum_fusion.2.refs_2_), channel_id=1, source_target_pairs={{0,1},{1,0},{2,3},{3,2},{4,5},{5,4},{6,7},{7,6},{8,9},{9,8},{10,11... | collective-permute-start | bytes 3538952 | tf_op jit(solution)/shard_map/ppermute | solution.py:16
  68.6 33.1 %collective-permute-start.18 = (bf16[96,6144]{1,0:T(8,128)(2,1)S(1)}, bf16[96,6144]{1,0:T(8,128)(2,1)S(1)}, u32[]{:S(2)}, u32[]{:S(2)}) collective-permute-start(bf16[96,6144]{1,0:T(8,128)(2,1)S(1)} %pad_maximum_fusion.2.refs_2_), channel_id=1, source_target_pairs={{0,8},{8,0},{1,9},{9,1},{2,10},{10,2},{3,11},{11,3},{4,12},{12,4},... | collective-permute-start | bytes 3538952 | tf_op jit(solution)/shard_map/ppermute | solution.py:16
  83.9 38.1 %collective-permute-start.15 = (bf16[96,6144]{1,0:T(8,128)(2,1)S(1)}, bf16[96,6144]{1,0:T(8,128)(2,1)S(1)}, u32[]{:S(2)}, u32[]{:S(2)}) collective-permute-start(bf16[96,6144]{1,0:T(8,128)(2,1)S(1)} %collective-permute-done.3.refs_0_), channel_id=1, source_target_pairs={{0,2},{2,4},{4,6},{6,0},{1,3},{3,5},{5,7},{7,1},{8,10},{10,12},{12... | collective-permute-start | bytes 3538952 | tf_op jit(solution)/shard_map/ppermute | solution.py:16
  100.0 28.9 %collective-permute-start.21 = (bf16[96,6144]{1,0:T(8,128)(2,1)S(1)}, bf16[96,6144]{1,0:T(8,128)(2,1)S(1)}, u32[]{:S(2)}, u32[]{:S(2)}) collective-permute-start(bf16[96,6144]{1,0:T(8,128)(2,1)S(1)} %collective-permute-done.13.refs_3_), channel_id=1, source_target_pairs={{0,8},{8,0},{1,9},{9,1},{2,10},{10,2},{3,11},{11,3},{4,12},{12,4},... | collective-permute-start | bytes 3538952 | tf_op jit(solution)/shard_map/ppermute | solution.py:16
  101.7 28.2 %collective-permute-start.20 = (bf16[96,6144]{1,0:T(8,128)(2,1)S(1)}, bf16[96,6144]{1,0:T(8,128)(2,1)S(1)}, u32[]{:S(2)}, u32[]{:S(2)}) collective-permute-start(bf16[96,6144]{1,0:T(8,128)(2,1)S(1)} %collective-permute-done.17.refs_1_), channel_id=1, source_target_pairs={{0,6},{2,0},{4,2},{6,4},{1,7},{3,1},{5,3},{7,5},{8,14},{10,8},{12,... | collective-permute-start | bytes 3538952 | tf_op jit(solution)/shard_map/ppermute | solution.py:16
  104.9 28.9 %collective-permute-start.22 = (bf16[96,6144]{1,0:T(8,128)(2,1)S(1)}, bf16[96,6144]{1,0:T(8,128)(2,1)S(1)}, u32[]{:S(2)}, u32[]{:S(2)}) collective-permute-start(bf16[96,6144]{1,0:T(8,128)(2,1)S(1)} %collective-permute-done.18.refs_2_), channel_id=1, source_target_pairs={{0,1},{1,0},{2,3},{3,2},{4,5},{5,4},{6,7},{7,6},{8,9},{9,8},{10,11... | collective-permute-start | bytes 3538952 | tf_op jit(solution)/shard_map/ppermute | solution.py:16
  106.7 42.6 %collective-permute-start.25 = (bf16[96,6144]{1,0:T(8,128)(2,1)S(1)}, bf16[96,6144]{1,0:T(8,128)(2,1)S(1)}, u32[]{:S(2)}, u32[]{:S(2)}) collective-permute-start(bf16[96,6144]{1,0:T(8,128)(2,1)S(1)} %get-tuple-element.130), channel_id=1, source_target_pairs={{0,8},{8,0},{1,9},{9,1},{2,10},{10,2},{3,11},{11,3},{4,12},{12,4},... | collective-permute-start | bytes 3538952 | tf_op jit(solution)/shard_map/ppermute | solution.py:16
  121.9 32.3 %collective-permute-start.26 = (bf16[96,6144]{1,0:T(8,128)(2,1)S(1)}, bf16[96,6144]{1,0:T(8,128)(2,1)S(1)}, u32[]{:S(2)}, u32[]{:S(2)}) collective-permute-start(bf16[96,6144]{1,0:T(8,128)(2,1)S(1)} %get-tuple-element.131), channel_id=1, source_target_pairs={{0,1},{1,0},{2,3},{3,2},{4,5},{5,4},{6,7},{7,6},{8,9},{9,8},{10,11... | collective-permute-start | bytes 3538952 | tf_op jit(solution)/shard_map/ppermute | solution.py:16
  128.9 25.3 %collective-permute-start.23 = (bf16[96,6144]{1,0:T(8,128)(2,1)S(1)}, bf16[96,6144]{1,0:T(8,128)(2,1)S(1)}, u32[]{:S(2)}, u32[]{:S(2)}) collective-permute-start(bf16[96,6144]{1,0:T(8,128)(2,1)S(1)} %get-tuple-element.128), channel_id=1, source_target_pairs={{0,2},{2,4},{4,6},{6,0},{1,3},{3,5},{5,7},{7,1},{8,10},{10,12},{12... | collective-permute-start | bytes 3538952 | tf_op jit(solution)/shard_map/ppermute | solution.py:16
  133.9 20.4 %collective-permute-start.24 = (bf16[96,6144]{1,0:T(8,128)(2,1)S(1)}, bf16[96,6144]{1,0:T(8,128)(2,1)S(1)}, u32[]{:S(2)}, u32[]{:S(2)}) collective-permute-start(bf16[96,6144]{1,0:T(8,128)(2,1)S(1)} %get-tuple-element.129), channel_id=1, source_target_pairs={{0,6},{2,0},{4,2},{6,4},{1,7},{3,1},{5,3},{7,5},{8,14},{10,8},{12,... | collective-permute-start | bytes 3538952 | tf_op jit(solution)/shard_map/ppermute | solution.py:16
  154.2 4.4 %copy-start.11 = (bf16[96,6144]{1,0:T(8,128)(2,1)}, bf16[96,6144]{1,0:T(8,128)(2,1)S(1)}, u32[]{:S(2)}) copy-start(bf16[96,6144]{1,0:T(8,128)(2,1)S(1)} %collective-permute-done.24.refs_16_.refs_9_.refs_1_) | copy-start | bytes 3538948
  154.2 26.3 %collective-permute-start.27 = (bf16[96,6144]{1,0:T(8,128)(2,1)S(1)}, bf16[96,6144]{1,0:T(8,128)(2,1)S(1)}, u32[]{:S(2)}, u32[]{:S(2)}) collective-permute-start(bf16[96,6144]{1,0:T(8,128)(2,1)S(1)} %get-tuple-element.132), channel_id=1, source_target_pairs={{0,8},{8,0},{1,9},{9,1},{2,10},{10,2},{3,11},{11,3},{4,12},{12,4},... | collective-permute-start | bytes 3538952 | tf_op jit(solution)/shard_map/ppermute | solution.py:16
  154.3 23.7 %collective-permute-start.28 = (bf16[96,6144]{1,0:T(8,128)(2,1)S(1)}, bf16[96,6144]{1,0:T(8,128)(2,1)S(1)}, u32[]{:S(2)}, u32[]{:S(2)}) collective-permute-start(bf16[96,6144]{1,0:T(8,128)(2,1)S(1)} %get-tuple-element.134), channel_id=1, source_target_pairs={{0,6},{2,0},{4,2},{6,4},{1,7},{3,1},{5,3},{7,5},{8,14},{10,8},{12,... | collective-permute-start | bytes 3538952 | tf_op jit(solution)/shard_map/ppermute | solution.py:16
  156.6 21.7 %collective-permute-start.29 = (bf16[96,6144]{1,0:T(8,128)(2,1)S(1)}, bf16[96,6144]{1,0:T(8,128)(2,1)S(1)}, u32[]{:S(2)}, u32[]{:S(2)}) collective-permute-start(bf16[96,6144]{1,0:T(8,128)(2,1)S(1)} %get-tuple-element.136), channel_id=1, source_target_pairs={{0,2},{2,4},{4,6},{6,0},{1,3},{3,5},{5,7},{7,1},{8,10},{10,12},{12... | collective-permute-start | bytes 3538952 | tf_op jit(solution)/shard_map/ppermute | solution.py:16
  156.6 23.6 %collective-permute-start.30 = (bf16[96,6144]{1,0:T(8,128)(2,1)S(1)}, bf16[96,6144]{1,0:T(8,128)(2,1)S(1)}, u32[]{:S(2)}, u32[]{:S(2)}) collective-permute-start(bf16[96,6144]{1,0:T(8,128)(2,1)S(1)} %get-tuple-element.140), channel_id=1, source_target_pairs={{0,1},{1,0},{2,3},{3,2},{4,5},{5,4},{6,7},{7,6},{8,9},{9,8},{10,11... | collective-permute-start | bytes 3538952 | tf_op jit(solution)/shard_map/ppermute | solution.py:16
  180.5 23.1 %copy-start.7 = (bf16[96,6144]{1,0:T(8,128)(2,1)}, bf16[96,6144]{1,0:T(8,128)(2,1)S(1)}, u32[]{:S(2)}) copy-start(bf16[96,6144]{1,0:T(8,128)(2,1)S(1)} %collective-permute-done.27.refs_1_.refs_10_.refs_6_) | copy-start | bytes 3538948
  180.5 20.8 %collective-permute-start.31 = (bf16[96,6144]{1,0:T(8,128)(2,1)S(1)}, bf16[96,6144]{1,0:T(8,128)(2,1)S(1)}, u32[]{:S(2)}, u32[]{:S(2)}) collective-permute-start(bf16[96,6144]{1,0:T(8,128)(2,1)S(1)} %add_convert_fusion.3), channel_id=1, source_target_pairs={{0,6},{2,0},{4,2},{6,4},{1,7},{3,1},{5,3},{7,5},{8,14},{10,8},{12,... | collective-permute-start | bytes 3538952 | tf_op jit(solution)/shard_map/ppermute | solution.py:16
  182.7 19.9 %collective-permute-start.32 = (bf16[96,6144]{1,0:T(8,128)(2,1)S(1)}, bf16[96,6144]{1,0:T(8,128)(2,1)S(1)}, u32[]{:S(2)}, u32[]{:S(2)}) collective-permute-start(bf16[96,6144]{1,0:T(8,128)(2,1)S(1)} %add_convert_fusion.2), channel_id=1, source_target_pairs={{0,2},{2,4},{4,6},{6,0},{1,3},{3,5},{5,7},{7,1},{8,10},{10,12},{12... | collective-permute-start | bytes 3538952 | tf_op jit(solution)/shard_map/ppermute | solution.py:16
  182.7 20.8 %collective-permute-start.33 = (bf16[96,6144]{1,0:T(8,128)(2,1)S(1)}, bf16[96,6144]{1,0:T(8,128)(2,1)S(1)}, u32[]{:S(2)}, u32[]{:S(2)}) collective-permute-start(bf16[96,6144]{1,0:T(8,128)(2,1)S(1)} %add_convert_fusion.1), channel_id=1, source_target_pairs={{0,1},{1,0},{2,3},{3,2},{4,5},{5,4},{6,7},{7,6},{8,9},{9,8},{10,11... | collective-permute-start | bytes 3538952 | tf_op jit(solution)/shard_map/ppermute | solution.py:16
  184.4 19.2 %collective-permute-start.34 = (bf16[96,6144]{1,0:T(8,128)(2,1)S(1)}, bf16[96,6144]{1,0:T(8,128)(2,1)S(1)}, u32[]{:S(2)}, u32[]{:S(2)}) collective-permute-start(bf16[96,6144]{1,0:T(8,128)(2,1)S(1)} %add_convert_fusion), channel_id=1, source_target_pairs={{0,8},{8,0},{1,9},{9,1},{2,10},{10,2},{3,11},{11,3},{4,12},{12,4},... | collective-permute-start | bytes 3538952 | tf_op jit(solution)/shard_map/ppermute | solution.py:16
  186.5 11.8 %collective-permute-start.35 = (f32[4,128]{1,0:T(4,128)S(1)}, f32[4,128]{1,0:T(4,128)S(1)}, u32[]{:S(2)}, u32[]{:S(2)}) collective-permute-start(f32[4,128]{1,0:T(4,128)S(1)} %pad_maximum_fusion.5), channel_id=1, source_target_pairs={{0,32},{32,64},{64,96},{96,0},{1,33},{33,65},{65,97},{97,1},{2,34}... | collective-permute-start | bytes 6152 | tf_op jit(solution)/shard_map/ppermute | solution.py:40
  210.2 10.6 %collective-permute-start.36 = (bf16[48,6144]{1,0:T(8,128)(2,1)}, bf16[48,6144]{1,0:T(8,128)(2,1)S(1)}, u32[]{:S(2)}, u32[]{:S(2)}) collective-permute-start(bf16[48,6144]{1,0:T(8,128)(2,1)} %get-tuple-element.159), channel_id=1, source_target_pairs={{0,6},{2,0},{4,2},{6,4},{1,7},{3,1},{5,3},{7,5},{8,14},{10,8},{12,... | collective-permute-start | bytes 1769480 | tf_op jit(solution)/shard_map/ppermute | solution.py:16
  213.1 11.3 %collective-permute-start.37 = (bf16[48,6144]{1,0:T(8,128)(2,1)}, bf16[48,6144]{1,0:T(8,128)(2,1)S(1)}, u32[]{:S(2)}, u32[]{:S(2)}) collective-permute-start(bf16[48,6144]{1,0:T(8,128)(2,1)} %get-tuple-element.160), channel_id=1, source_target_pairs={{0,2},{2,4},{4,6},{6,0},{1,3},{3,5},{5,7},{7,1},{8,10},{10,12},{12... | collective-permute-start | bytes 1769480 | tf_op jit(solution)/shard_map/ppermute | solution.py:16
  213.1 11.3 %collective-permute-start.38 = (bf16[48,6144]{1,0:T(8,128)(2,1)}, bf16[48,6144]{1,0:T(8,128)(2,1)S(1)}, u32[]{:S(2)}, u32[]{:S(2)}) collective-permute-start(bf16[48,6144]{1,0:T(8,128)(2,1)} %get-tuple-element.161), channel_id=1, source_target_pairs={{0,1},{1,0},{2,3},{3,2},{4,5},{5,4},{6,7},{7,6},{8,9},{9,8},{10,11... | collective-permute-start | bytes 1769480 | tf_op jit(solution)/shard_map/ppermute | solution.py:16
  214.6 10.1 %collective-permute-start.39 = (bf16[48,6144]{1,0:T(8,128)(2,1)}, bf16[48,6144]{1,0:T(8,128)(2,1)S(1)}, u32[]{:S(2)}, u32[]{:S(2)}) collective-permute-start(bf16[48,6144]{1,0:T(8,128)(2,1)} %get-tuple-element.162), channel_id=1, source_target_pairs={{0,8},{8,0},{1,9},{9,1},{2,10},{10,2},{3,11},{11,3},{4,12},{12,4},... | collective-permute-start | bytes 1769480 | tf_op jit(solution)/shard_map/ppermute | solution.py:16
  229.7 7.2 %collective-permute-start.40 = (bf16[24,6144]{1,0:T(8,128)(2,1)}, bf16[24,6144]{1,0:T(8,128)(2,1)S(1)}, u32[]{:S(2)}, u32[]{:S(2)}) collective-permute-start(bf16[24,6144]{1,0:T(8,128)(2,1)} %get-tuple-element.167), channel_id=1, source_target_pairs={{0,6},{2,0},{4,2},{6,4},{1,7},{3,1},{5,3},{7,5},{8,14},{10,8},{12,... | collective-permute-start | bytes 884744 | tf_op jit(solution)/shard_map/ppermute | solution.py:16
  232.4 8.1 %collective-permute-start.41 = (bf16[24,6144]{1,0:T(8,128)(2,1)}, bf16[24,6144]{1,0:T(8,128)(2,1)S(1)}, u32[]{:S(2)}, u32[]{:S(2)}) collective-permute-start(bf16[24,6144]{1,0:T(8,128)(2,1)} %get-tuple-element.168), channel_id=1, source_target_pairs={{0,2},{2,4},{4,6},{6,0},{1,3},{3,5},{5,7},{7,1},{8,10},{10,12},{12... | collective-permute-start | bytes 884744 | tf_op jit(solution)/shard_map/ppermute | solution.py:16
  232.4 8.1 %collective-permute-start.42 = (bf16[24,6144]{1,0:T(8,128)(2,1)}, bf16[24,6144]{1,0:T(8,128)(2,1)S(1)}, u32[]{:S(2)}, u32[]{:S(2)}) collective-permute-start(bf16[24,6144]{1,0:T(8,128)(2,1)} %get-tuple-element.169), channel_id=1, source_target_pairs={{0,8},{8,0},{1,9},{9,1},{2,10},{10,2},{3,11},{11,3},{4,12},{12,4},... | collective-permute-start | bytes 884744 | tf_op jit(solution)/shard_map/ppermute | solution.py:16
  233.0 7.6 %collective-permute-start.43 = (bf16[24,6144]{1,0:T(8,128)(2,1)}, bf16[24,6144]{1,0:T(8,128)(2,1)S(1)}, u32[]{:S(2)}, u32[]{:S(2)}) collective-permute-start(bf16[24,6144]{1,0:T(8,128)(2,1)} %get-tuple-element.170), channel_id=1, source_target_pairs={{0,1},{1,0},{2,3},{3,2},{4,5},{5,4},{6,7},{7,6},{8,9},{9,8},{10,11... | collective-permute-start | bytes 884744 | tf_op jit(solution)/shard_map/ppermute | solution.py:16
  246.0 19.0 %collective-permute-start.45 = (bf16[48,6144]{1,0:T(8,128)(2,1)}, bf16[48,6144]{1,0:T(8,128)(2,1)S(1)}, u32[]{:S(2)}, u32[]{:S(2)}) collective-permute-start(bf16[48,6144]{1,0:T(8,128)(2,1)} %get-tuple-element.176), channel_id=1, source_target_pairs={{0,57},{1,56},{8,49},{9,48},{16,41},{17,40},{24,33},{25,32},{32,89... | collective-permute-start | bytes 1769480 | tf_op jit(solution)/shard_map/ppermute | solution.py:55
  246.1 19.6 %collective-permute-start.44 = (bf16[48,6144]{1,0:T(8,128)(2,1)}, bf16[48,6144]{1,0:T(8,128)(2,1)S(1)}, u32[]{:S(2)}, u32[]{:S(2)}) collective-permute-start(bf16[48,6144]{1,0:T(8,128)(2,1)} %get-tuple-element.175), channel_id=1, source_target_pairs={{0,33},{1,32},{32,65},{33,64},{64,97},{65,96},{96,1},{97,0},{2,35}... | collective-permute-start | bytes 1769480 | tf_op jit(solution)/shard_map/ppermute | solution.py:45
  (20 other events, 34.2 us)

commit v6 on v5

--- a/solution.py
+++ b/solution.py
@@ -80,31 +80,11 @@
 
 
 def sums(*wanted):
-    width = wanted[0][0][0][0].shape[1]
-    tile = width // 2
-    blocks = [term for segments in wanted for terms in segments for term in terms]
-    heights = [sum(terms[0][2] for terms in segments) for segments in wanted]
-
-    def kernel(*refs):
-        ins, outs = iter(refs[: len(blocks)]), refs[len(blocks) :]
-        for segments, out in zip(wanted, outs):
-            start = 0
-            for terms in segments:
-                total = next(ins)[...].astype(F32)
-                for _ in terms[1:]:
-                    total = total + next(ins)[...].astype(F32)
-                out[start : start + terms[0][2]] = total.astype(BF16)
-                start += terms[0][2]
-
-    return pl.pallas_call(
-        kernel,
-        grid=(width // tile,),
-        in_specs=[pl.BlockSpec((n, tile), lambda i, part=part: (part, i)) for _, part, n in blocks],
-        out_specs=[pl.BlockSpec((n, tile), lambda i: (0, i)) for n in heights],
-        out_shape=[jax.ShapeDtypeStruct((n, width), BF16) for n in heights],
-        compiler_params=pltpu.CompilerParams(dimension_semantics=("arbitrary",)),
-        name="sums",
-    )(*[array for array, _, _ in blocks])
+    pick = lambda array, part, rows: array[part * rows : (part + 1) * rows]
+    out = []
+    for segments in wanted:
+        out.append(join(*(add(*(pick(*term) for term in terms)) for terms in segments)))
+    return out
 
 
 TILE = 1536
@@ -170,7 +150,7 @@
             pltpu.VMEM((total, units), BF16),
         ],
         compiler_params=pltpu.CompilerParams(
-            dimension_semantics=("arbitrary",), vmem_limit_bytes=24 << 20
+            dimension_semantics=("arbitrary",), vmem_limit_bytes=18 << 20
         ),
         cost_estimate=pl.CostEstimate(
             flops=6 * total * width * units,
@@ -178,7 +158,7 @@
             bytes_accessed=6 * width * units + 4 * total * width,
         ),
         name="experts",
-    )(*pieces, *(pltpu.with_memory_space_constraint(m, pltpu.HBM) for m in (gate_matrix, up_matrix, down_matrix)))
+    )(*pieces, gate_matrix, up_matrix, down_matrix)
 
 
 def body(states, expert_ids, gate_values, keep_mask, w_gate, w_up, w_down):
@@ -208,20 +188,22 @@
     a1, b = split(own, 2)
     a1_y, b_behind, b_ahead = over_y(a1), right(b), left(b)
     a1_near = join(a1, a1_y)
-    a1_far, b_opposite = over_z(a1_near), right(b_behind)
+    b_opposite = right(b_behind)
     b_ring = join(b, b_behind, b_ahead, b_opposite)
+    b_y = over_y(b_ring)
 
     a2, g = split(partner, 2)
     a2_z, g_behind, g_ahead = over_z(a2), left(g), right(g)
-    b_y = over_y(b_ring)
-    g_behind, g_ahead, b_ring_z = together(g_behind, g_ahead, b_ring)
+    g_behind, g_ahead, b_ring_late, a1_near_late = together(g_behind, g_ahead, b_ring, a1_near)
     g_opposite = left(g_behind)
+    a1_far = over_z(a1_near_late)
     a2_near = join(a2, a2_z)
     near = join(a1_near, a2_near)
-    a2_far, b_z = over_y(a2_near), over_z(b_ring_z)
-    near_late, g_opposite_done = together(near, g_opposite)
+    a1_far, b_ring_late = together(a1_far, b_ring_late)
+    a2_far, b_z = over_y(a2_near), over_z(b_ring_late)
+    near_late, g_opposite = together(near, g_opposite)
     near_left, near_right = right(near), left(near_late)
-    g_ring = join(g, g_behind, g_ahead, g_opposite_done)
+    g_ring = join(g, g_behind, g_ahead, g_opposite)
 
     b_y, g_ring_out = together(b_y, g_ring)
     g_y, g_z = over_y(g_ring_out), over_z(g_ring_out)
@@ -232,20 +214,20 @@
     near_left, near_right, far, b_z, near, b_ring, g_ring, b_y = together(
         near_left, near_right, far, b_z, near, b_ring, g_ring, b_y
     )
-    near_opposite, b_yz = right(near_left), over_y(b_z)
+    near_opposite, b_yz = left(near_right), over_y(b_z)
     near_left, near_right, far, b_z = experts([near_left, near_right, far, b_z], *matrices)
 
     far_left, far_right, g_y, g_z, near_left, near_right, far, b_z = together(
         far_left, far_right, g_y, g_z, near_left, near_right, far, b_z
     )
-    far_opposite, g_zy = left(far_right), over_z(g_y)
+    far_opposite, g_zy = right(far_left), over_z(g_y)
     far_left, far_right, g_y, g_z = experts([far_left, far_right, g_y, g_z], *matrices)
 
     near_opposite, far_opposite, b_yz, g_zy, far_left, far_right, g_y, g_z = together(
         near_opposite, far_opposite, b_yz, g_zy, far_left, far_right, g_y, g_z
     )
     near_back, far_back, b_back, g_own = (
-        right(near_right), left(far_left), over_y(b_y), over_z(g_ring)
+        left(near_left), right(far_right), over_y(b_y), over_z(g_ring)
     )
     near_opposite, far_opposite, b_yz, g_zy = experts(
         [near_opposite, far_opposite, b_yz, g_zy], *matrices
@@ -253,14 +235,14 @@
     near_opposite, far_opposite, b_yz, g_y, near_back, far_back, b_back, g_own = together(
         near_opposite, far_opposite, b_yz, g_y, near_back, far_back, b_back, g_own
     )
-    got = left(near_opposite), right(far_opposite), over_y(b_yz), over_z(g_y)
-    near_left, far_right = add(near_left, got[0]), add(far_right, got[1])
+    got = right(near_opposite), left(far_opposite), over_y(b_yz), over_z(g_y)
+    near_right, far_left = add(near_right, got[0]), add(far_left, got[1])
     b_ring, g_zy = add(b_ring, b_back), add(g_zy, got[3])
-    info, b_yz_back, near_left, far_right, b_ring, g_zy = together(
-        info, got[2], near_left, far_right, b_ring, g_zy
+    info, b_yz_back, near_right, far_left, b_ring, g_zy = together(
+        info, got[2], near_right, far_left, b_ring, g_zy
     )
     *got, info = together(
-        left(near_left), right(far_right), over_z(b_ring), over_y(g_zy), to_next_section(info)
+        right(near_right), left(far_left), over_z(b_ring), over_y(g_zy), to_next_section(info)
     )
 
     near, far = (near, near_back, got[0]), (far, far_back, got[1])

time: 268 us -> 253 us (0.944)
  Pallas kernels: 67.8 us -> 43.7 us
  waiting for transfers between devices: 123 us -> 128 us
  starting transfers between devices: 60.4 us -> 65.1 us
  local copies, waits for them, and re-layouts: 9.7 us -> 5.49 us
  other arithmetic: 2.94 us -> 6.57 us
    pallas_call x4, Pallas kernels: 55.8 us -> 43.7 us  [experts(): pl.pallas_call(experts_kernel, grid=(2 * half,), in_specs=rows_in + [into...]
    pallas_call x3 -> x0, Pallas kernels: 12 us -> none  [sums(): pl.pallas_call(kernel, grid=(width // tile,), in_specs=[pl.BlockSpec((n,...]
    ppermute x42, starting transfers between devices: 53.3 us -> 57.8 us  [shift(): return lax.ppermute(value, axis, [(i, (i + by) % n) for i in range(n)])]
    unnamed x45 -> x21, local copies, waits for them, and re-layouts: 9.35 us -> 5.14 us
    ppermute x1, waiting for transfers between devices: 6.32 us -> 9.96 us  [to_partner(): return lax.ppermute(value, ('yh', 'yl'), [(y, 3 - y) for y in range(4)])]
    convert_element_type x4 -> x16, other arithmetic: 1.16 us -> 4.63 us  [add(): return total.astype(BF16)]
  transfers between devices with their start and end apart: 46 -> 46, of which waited for: 21 -> 25; matrix products, arithmetic and copies ran while one was open for 1% -> 2% of each run, Pallas kernels for 21% -> 17%
where the time goes in v6:
time: 253 us; the launch traced here: 252 us
  waiting for transfers between devices  128 us (51%)
  starting transfers between devices  65.1 us (26%)
  Pallas kernels  43.7 us (17%)
  other arithmetic  6.57 us (3%)
  local copies, waits for them, and re-layouts  5.49 us (2%)
  matrix products  3.07 us (1%)
    ppermute x42, waiting for transfers between devices, shift(): return lax.ppermute(value, axis, [(i, (i + by) % n) for i in range(n)])  93.5 us
    ppermute x42, starting transfers between devices, shift(): return lax.ppermute(value, axis, [(i, (i + by) % n) for i in range(n)])  57.8 us
    pallas_call x4, Pallas kernels, experts(): pl.pallas_call(experts_kernel, grid=(2 * half,), in_specs=rows_in + [into...  43.7 us
    ppermute x1, waiting for transfers between devices, to_owner_across(): return lax.ppermute(value, ('zh', 'core', 'yh', 'yl', 'zl'), pairs)  13.3 us
    ppermute x1, waiting for transfers between devices, to_next_section(): lax.ppermute(value, ('zh', 'core'), [(s, (s + 1) % 4) for s in range(4)])  10.8 us
    ppermute x1, waiting for transfers between devices, to_partner(): return lax.ppermute(value, ('yh', 'yl'), [(y, 3 - y) for y in range(4)])  9.96 us
    unnamed x21, local copies, waits for them, and re-layouts  5.14 us
  transfers between devices with their start and end apart: 46, of which 25 were waited for; matrix products, arithmetic and copies ran while one was open for 2% of the time, Pallas kernels for 17%

profile of v6, /device:TPU:0, one launch (start us, length us, event | category | flops | bytes accessed | tf_op | source)
XLA Modules:
  0.0 252.0 jit_solution(12707203584712526408)
XLA Ops:
  2.5 1.6 collective-permute-start.6
  5.7 1.7 collective-permute-start.7
  7.4 2.2 collective-permute-start.1
  9.6 2.8 %collective-permute-done.6 = bf16[24,6144]{1,0:T(8,128)(2,1)S(1)} collective-permute-done((bf16[24,6144]{1,0:T(8,128)(2,1)S(1)}, bf16[24,6144]{1,0:T(8,128)(2,1)S(1)}, u32[]{:S(2)}, u32[]{:S(2)}) %collective-permute-start.6) | collective-permute-done | bytes 294944 | tf_op jit(solution)/shard_map/ppermute | solution.py:16
  12.9 10.0 %collective-permute-done.1 = bf16[48,6144]{1,0:T(8,128)(2,1)S(1)} collective-permute-done((bf16[48,6144]{1,0:T(8,128)(2,1)S(1)}, bf16[48,6144]{1,0:T(8,128)(2,1)S(1)}, u32[]{:S(2)}, u32[]{:S(2)}) %collective-permute-start.1) | collective-permute-done | bytes 589856 | tf_op jit(solution)/shard_map/ppermute | solution.py:36
  23.3 3.0 %collective-permute-start.4 = (bf16[24,6144]{1,0:T(8,128)(2,1)S(1)}, bf16[24,6144]{1,0:T(8,128)(2,1)S(1)}, u32[]{:S(2)}, u32[]{:S(2)}) collective-permute-start(bf16[24,6144]{1,0:T(8,128)(2,1)S(1)} %get-tuple-element.175), channel_id=1, source_target_pairs={{0,6},{2,0},{4,2},{6,4},{1,7},{3,1},{5,3},{7,5},{8,14},{10,8},{12,... | collective-permute-start | bytes 884744 | tf_op jit(solution)/shard_map/ppermute | solution.py:16
  26.2 1.9 collective-permute-start.2
  28.4 2.8 %collective-permute-done.5 = bf16[24,6144]{1,0:T(8,128)(2,1)S(1)} collective-permute-done((bf16[24,6144]{1,0:T(8,128)(2,1)S(1)}, bf16[24,6144]{1,0:T(8,128)(2,1)S(1)}, u32[]{:S(2)}, u32[]{:S(2)}) %collective-permute-start.5) | collective-permute-done | bytes 294944 | tf_op jit(solution)/shard_map/ppermute | solution.py:16
  31.2 3.0 %collective-permute-start.9 = (bf16[24,6144]{1,0:T(8,128)(2,1)S(1)}, bf16[24,6144]{1,0:T(8,128)(2,1)S(1)}, u32[]{:S(2)}, u32[]{:S(2)}) collective-permute-start(bf16[24,6144]{1,0:T(8,128)(2,1)S(1)} %collective-permute-done.4), channel_id=1, source_target_pairs={{0,6},{2,0},{4,2},{6,4},{1,7},{3,1},{5,3},{7,5},{8,14},{10,8},{12,... | collective-permute-start | bytes 884744 | tf_op jit(solution)/shard_map/ppermute | solution.py:16
  34.4 1.9 collective-permute-start.11
  36.5 2.5 collective-permute-done.9
  39.0 3.7 %collective-permute-start.10 = (bf16[96,6144]{1,0:T(8,128)(2,1)S(1)}, bf16[96,6144]{1,0:T(8,128)(2,1)S(1)}, u32[]{:S(2)}, u32[]{:S(2)}) collective-permute-start(bf16[96,6144]{1,0:T(8,128)(2,1)S(1)} %pad_maximum_fusion.refs_0_), channel_id=1, source_target_pairs={{0,6},{2,0},{4,2},{6,4},{1,7},{3,1},{5,3},{7,5},{8,14},{10,8},{12,... | collective-permute-start | bytes 3538952 | tf_op jit(solution)/shard_map/ppermute | solution.py:16
  42.8 5.1 %collective-permute-done.11 = bf16[48,6144]{1,0:T(8,128)(2,1)S(1)} collective-permute-done((bf16[48,6144]{1,0:T(8,128)(2,1)S(1)}, bf16[48,6144]{1,0:T(8,128)(2,1)S(1)}, u32[]{:S(2)}, u32[]{:S(2)}) %collective-permute-start.11) | collective-permute-done | bytes 589856 | tf_op jit(solution)/shard_map/ppermute | solution.py:16
  47.9 1.9 collective-permute-start.13
  49.9 16.2 %collective-permute-done.12 = bf16[48,6144]{1,0:T(8,128)(2,1)S(1)} collective-permute-done((bf16[48,6144]{1,0:T(8,128)(2,1)S(1)}, bf16[48,6144]{1,0:T(8,128)(2,1)S(1)}, u32[]{:S(2)}, u32[]{:S(2)}) %collective-permute-start.12) | collective-permute-done | bytes 589856 | tf_op jit(solution)/shard_map/ppermute | solution.py:16
  66.5 1.7 collective-permute-start.16
  68.8 2.8 %copy-done.2 = bf16[1,512,6144]{2,1,0:T(8,128)(2,1)S(1)} copy-done((bf16[1,512,6144]{2,1,0:T(8,128)(2,1)S(1)}, bf16[1,512,6144]{2,1,0:T(8,128)(2,1)}, u32[]{:S(2)}) %copy-start.2) | copy-done | bytes 6291480
  71.6 10.9 %experts.4 = (bf16[96,6144]{1,0:T(8,128)(2,1)S(1)}, bf16[96,6144]{1,0:T(8,128)(2,1)S(1)}, bf16[96,6144]{1,0:T(8,128)(2,1)S(1)}, bf16[96,6144]{1,0:T(8,128)(2,1)S(1)}) custom-call(bf16[96,6144]{1,0:T(8,128)(2,1)S(1)} %pad_maximum_fusion.refs_0_, bf16[96,6144]{1,0:T(8,128)(2,1)S(1)} %pad_maximum_fusion.1.refs_1_, ...), custom_call_target="tpu_custom_call" | custom-call | flops 7247757312 | bytes 28311552 | tf_op jit(solution)/shard_map/experts/pallas_call | solution.py:141
  82.6 1.8 collective-permute-start.15
  84.4 10.9 %experts.5 = (bf16[96,6144]{1,0:T(8,128)(2,1)S(1)}, bf16[96,6144]{1,0:T(8,128)(2,1)S(1)}, bf16[96,6144]{1,0:T(8,128)(2,1)S(1)}, bf16[96,6144]{1,0:T(8,128)(2,1)S(1)}) custom-call(bf16[96,6144]{1,0:T(8,128)(2,1)S(1)} %collective-permute-done.3.refs_0_, bf16[96,6144]{1,0:T(8,128)(2,1)S(1)} %collective-permute-done.10.refs_1_, ...), custom_call_target="tpu_custom_call" | custom-call | flops 7247757312 | bytes 28311552 | tf_op jit(solution)/shard_map/experts/pallas_call | solution.py:141
  95.3 1.8 collective-permute-start.21
  99.2 2.0 collective-permute-start.22
  101.2 1.9 collective-permute-start.25
  104.4 10.9 %experts.6 = (bf16[96,6144]{1,0:T(8,128)(2,1)S(1)}, bf16[96,6144]{1,0:T(8,128)(2,1)S(1)}, bf16[96,6144]{1,0:T(8,128)(2,1)S(1)}, bf16[96,6144]{1,0:T(8,128)(2,1)S(1)}) custom-call(bf16[96,6144]{1,0:T(8,128)(2,1)S(1)} %collective-permute-done.16.refs_0_, bf16[96,6144]{1,0:T(8,128)(2,1)S(1)} %collective-permute-done.17.refs_1_, ...), custom_call_target="tpu_custom_call" | custom-call | flops 7247757312 | bytes 28311552 | tf_op jit(solution)/shard_map/experts/pallas_call | solution.py:141
  116.1 8.1 %collective-permute-done.21.refs_2_ = bf16[96,6144]{1,0:T(8,128)(2,1)S(1)} collective-permute-done((bf16[96,6144]{1,0:T(8,128)(2,1)S(1)}, bf16[96,6144]{1,0:T(8,128)(2,1)S(1)}, u32[]{:S(2)}, u32[]{:S(2)}) %collective-permute-start.21) | collective-permute-done | bytes 1179680 | tf_op jit(solution)/shard_map/ppermute | solution.py:16
  125.6 2.6 %collective-permute-done.22.refs_3_ = bf16[96,6144]{1,0:T(8,128)(2,1)S(1)} collective-permute-done((bf16[96,6144]{1,0:T(8,128)(2,1)S(1)}, bf16[96,6144]{1,0:T(8,128)(2,1)S(1)}, u32[]{:S(2)}, u32[]{:S(2)}) %collective-permute-start.22) | collective-permute-done | bytes 1179680 | tf_op jit(solution)/shard_map/ppermute | solution.py:16
  128.2 11.0 %experts.7 = (bf16[96,6144]{1,0:T(8,128)(2,1)S(1)}, bf16[96,6144]{1,0:T(8,128)(2,1)S(1)}, bf16[96,6144]{1,0:T(8,128)(2,1)S(1)}, bf16[96,6144]{1,0:T(8,128)(2,1)S(1)}) custom-call(bf16[96,6144]{1,0:T(8,128)(2,1)S(1)} %collective-permute-done.15.refs_0_, bf16[96,6144]{1,0:T(8,128)(2,1)S(1)} %collective-permute-done.20.refs_1_, ...), custom_call_target="tpu_custom_call" | custom-call | flops 7247757312 | bytes 28311552 | tf_op jit(solution)/shard_map/experts/pallas_call | solution.py:141
  139.2 4.9 %collective-permute-done.25 = bf16[96,6144]{1,0:T(8,128)(2,1)} collective-permute-done((bf16[96,6144]{1,0:T(8,128)(2,1)S(1)}, bf16[96,6144]{1,0:T(8,128)(2,1)}, u32[]{:S(2)}, u32[]{:S(2)}) %collective-permute-start.25) | collective-permute-done | bytes 1179680 | tf_op jit(solution)/shard_map/ppermute | solution.py:16
  144.1 3.5 %collective-permute-done.26 = bf16[96,6144]{1,0:T(8,128)(2,1)S(1)} collective-permute-done((bf16[96,6144]{1,0:T(8,128)(2,1)S(1)}, bf16[96,6144]{1,0:T(8,128)(2,1)S(1)}, u32[]{:S(2)}, u32[]{:S(2)}) %collective-permute-start.26) | collective-permute-done | bytes 1179680 | tf_op jit(solution)/shard_map/ppermute | solution.py:16
  148.9 3.2 %collective-permute-start.29 = (bf16[96,6144]{1,0:T(8,128)(2,1)S(1)}, bf16[96,6144]{1,0:T(8,128)(2,1)S(1)}, u32[]{:S(2)}, u32[]{:S(2)}) collective-permute-start(bf16[96,6144]{1,0:T(8,128)(2,1)S(1)} %get-tuple-element.132), channel_id=1, source_target_pairs={{0,6},{2,0},{4,2},{6,4},{1,7},{3,1},{5,3},{7,5},{8,14},{10,8},{12,... | collective-permute-start | bytes 3538952 | tf_op jit(solution)/shard_map/ppermute | solution.py:16
  152.2 1.9 collective-permute-start.30
  155.6 18.5 %collective-permute-done.28 = bf16[96,6144]{1,0:T(8,128)(2,1)S(1)} collective-permute-done((bf16[96,6144]{1,0:T(8,128)(2,1)S(1)}, bf16[96,6144]{1,0:T(8,128)(2,1)S(1)}, u32[]{:S(2)}, u32[]{:S(2)}) %collective-permute-start.28) | collective-permute-done | bytes 1179680 | tf_op jit(solution)/shard_map/ppermute | solution.py:16
  175.1 3.2 %collective-permute-start.32 = (bf16[96,6144]{1,0:T(8,128)(2,1)S(1)}, bf16[96,6144]{1,0:T(8,128)(2,1)S(1)}, u32[]{:S(2)}, u32[]{:S(2)}) collective-permute-start(bf16[96,6144]{1,0:T(8,128)(2,1)S(1)} %add_convert_fusion.2), channel_id=1, source_target_pairs={{0,6},{2,0},{4,2},{6,4},{1,7},{3,1},{5,3},{7,5},{8,14},{10,8},{12,... | collective-permute-start | bytes 3538952 | tf_op jit(solution)/shard_map/ppermute | solution.py:16
  178.3 1.9 collective-permute-start.33
  181.4 10.8 %collective-permute-done.35 = f32[4,128]{1,0:T(4,128)S(1)} collective-permute-done((f32[4,128]{1,0:T(4,128)S(1)}, f32[4,128]{1,0:T(4,128)S(1)}, u32[]{:S(2)}, u32[]{:S(2)}) %collective-permute-start.35) | collective-permute-done | bytes 2080 | tf_op jit(solution)/shard_map/ppermute | solution.py:40
  192.2 7.1 %collective-permute-done.31 = bf16[96,6144]{1,0:T(8,128)(2,1)S(1)} collective-permute-done((bf16[96,6144]{1,0:T(8,128)(2,1)S(1)}, bf16[96,6144]{1,0:T(8,128)(2,1)S(1)}, u32[]{:S(2)}, u32[]{:S(2)}) %collective-permute-start.31) | collective-permute-done | bytes 1179680 | tf_op jit(solution)/shard_map/ppermute | solution.py:16
  201.1 2.1 collective-permute-start.36
  203.5 2.1 collective-permute-start.38
  205.8 2.4 collective-permute-start.39
  208.2 4.8 %collective-permute-done.36 = bf16[48,6144]{1,0:T(8,128)(2,1)S(1)} collective-permute-done((bf16[48,6144]{1,0:T(8,128)(2,1)S(1)}, bf16[48,6144]{1,0:T(8,128)(2,1)S(1)}, u32[]{:S(2)}, u32[]{:S(2)}) %collective-permute-start.36) | collective-permute-done | bytes 589856 | tf_op jit(solution)/shard_map/ppermute | solution.py:16
  213.0 4.5 %collective-permute-done.37 = bf16[48,6144]{1,0:T(8,128)(2,1)S(1)} collective-permute-done((bf16[48,6144]{1,0:T(8,128)(2,1)S(1)}, bf16[48,6144]{1,0:T(8,128)(2,1)S(1)}, u32[]{:S(2)}, u32[]{:S(2)}) %collective-permute-start.37) | collective-permute-done | bytes 589856 | tf_op jit(solution)/shard_map/ppermute | solution.py:16
  217.5 1.7 collective-permute-done.39
  220.9 2.6 %collective-permute-start.40 = (bf16[24,6144]{1,0:T(8,128)(2,1)S(1)}, bf16[24,6144]{1,0:T(8,128)(2,1)S(1)}, u32[]{:S(2)}, u32[]{:S(2)}) collective-permute-start(bf16[24,6144]{1,0:T(8,128)(2,1)S(1)} %add_convert_fusion.13), channel_id=1, source_target_pairs={{0,6},{2,0},{4,2},{6,4},{1,7},{3,1},{5,3},{7,5},{8,14},{10,8},{12,... | collective-permute-start | bytes 884744 | tf_op jit(solution)/shard_map/ppermute | solution.py:16
  223.5 2.0 collective-permute-start.42
  228.2 2.0 collective-permute-done.42
  231.2 5.0 %collective-permute-start.44 = (bf16[48,6144]{1,0:T(8,128)(2,1)S(1)}, bf16[48,6144]{1,0:T(8,128)(2,1)S(1)}, u32[]{:S(2)}, u32[]{:S(2)}) collective-permute-start(bf16[48,6144]{1,0:T(8,128)(2,1)S(1)} %pad_maximum_fusion.7), channel_id=1, source_target_pairs={{0,33},{1,32},{32,65},{33,64},{64,97},{65,96},{96,1},{97,0},{2,35}... | collective-permute-start | bytes 1769480 | tf_op jit(solution)/shard_map/ppermute | solution.py:45
  236.3 13.3 %collective-permute-done.45 = bf16[48,6144]{1,0:T(8,128)(2,1)S(1)} collective-permute-done((bf16[48,6144]{1,0:T(8,128)(2,1)S(1)}, bf16[48,6144]{1,0:T(8,128)(2,1)S(1)}, u32[]{:S(2)}, u32[]{:S(2)}) %collective-permute-start.45) | collective-permute-done | bytes 589856 | tf_op jit(solution)/shard_map/ppermute | solution.py:55
  250.2 1.8 fusion.2
  (117 shorter events, 25.4 us)
Async XLA Ops:
  1.7 67.1 %slice-start.2 = ((s8[6291456]{0:T(1024)(128)(4,1)}), s8[4194304]{0:T(1024)(128)(4,1)S(1)}, s32[]{:S(2)}) async-start(s8[6291456]{0:T(1024)(128)(4,1)} %bitcast.44), calls=%async_computation.2 | async-start | bytes 8388608
  2.4 66.4 %slice-start = ((s8[6291456]{0:T(1024)(128)(4,1)}), s8[4194304]{0:T(1024)(128)(4,1)S(1)}, s32[]{:S(2)}) async-start(s8[6291456]{0:T(1024)(128)(4,1)} %bitcast.38), calls=%async_computation | async-start | bytes 8388608
  2.5 9.9 %collective-permute-start.6 = (bf16[24,6144]{1,0:T(8,128)(2,1)S(1)}, bf16[24,6144]{1,0:T(8,128)(2,1)S(1)}, u32[]{:S(2)}, u32[]{:S(2)}) collective-permute-start(bf16[24,6144]{1,0:T(8,128)(2,1)S(1)} %get-tuple-element.173), channel_id=1, source_target_pairs={{0,2},{2,4},{4,6},{6,0},{1,3},{3,5},{5,7},{7,1},{8,10},{10,12},{12... | collective-permute-start | bytes 884744 | tf_op jit(solution)/shard_map/ppermute | solution.py:16
  4.1 8.8 %collective-permute-start = (bf16[24,6144]{1,0:T(8,128)(2,1)S(1)}, bf16[24,6144]{1,0:T(8,128)(2,1)S(1)}, u32[]{:S(2)}, u32[]{:S(2)}) collective-permute-start(bf16[24,6144]{1,0:T(8,128)(2,1)S(1)} %get-tuple-element.174), channel_id=1, source_target_pairs={{0,8},{8,0},{1,9},{9,1},{2,10},{10,2},{3,11},{11,3},{4,12},{12,4},... | collective-permute-start | bytes 884744 | tf_op jit(solution)/shard_map/ppermute | solution.py:16
  5.7 22.5 %collective-permute-start.7 = (bf16[24,6144]{1,0:T(8,128)(2,1)S(1)}, bf16[24,6144]{1,0:T(8,128)(2,1)S(1)}, u32[]{:S(2)}, u32[]{:S(2)}) collective-permute-start(bf16[24,6144]{1,0:T(8,128)(2,1)S(1)} %get-tuple-element.173), channel_id=1, source_target_pairs={{0,6},{2,0},{4,2},{6,4},{1,7},{3,1},{5,3},{7,5},{8,14},{10,8},{12,... | collective-permute-start | bytes 884744 | tf_op jit(solution)/shard_map/ppermute | solution.py:16
  7.4 15.4 %collective-permute-start.1 = (bf16[48,6144]{1,0:T(8,128)(2,1)S(1)}, bf16[48,6144]{1,0:T(8,128)(2,1)S(1)}, u32[]{:S(2)}, u32[]{:S(2)}) collective-permute-start(bf16[48,6144]{1,0:T(8,128)(2,1)S(1)} %convolution_convert_fusion.1), channel_id=1, source_target_pairs={{0,24},{8,16},{16,8},{24,0},{1,25},{9,17},{17,9},{25,1},{2,26},{10... | collective-permute-start | bytes 1769480 | tf_op jit(solution)/shard_map/ppermute | solution.py:36
  12.4 15.8 %collective-permute-start.8 = (bf16[24,6144]{1,0:T(8,128)(2,1)S(1)}, bf16[24,6144]{1,0:T(8,128)(2,1)S(1)}, u32[]{:S(2)}, u32[]{:S(2)}) collective-permute-start(bf16[24,6144]{1,0:T(8,128)(2,1)S(1)} %collective-permute-done.6), channel_id=1, source_target_pairs={{0,2},{2,4},{4,6},{6,0},{1,3},{3,5},{5,7},{7,1},{8,10},{10,12},{12... | collective-permute-start | bytes 884744 | tf_op jit(solution)/shard_map/ppermute | solution.py:16
  22.9 8.3 %collective-permute-start.5 = (bf16[24,6144]{1,0:T(8,128)(2,1)S(1)}, bf16[24,6144]{1,0:T(8,128)(2,1)S(1)}, u32[]{:S(2)}, u32[]{:S(2)}) collective-permute-start(bf16[24,6144]{1,0:T(8,128)(2,1)S(1)} %get-tuple-element.175), channel_id=1, source_target_pairs={{0,2},{2,4},{4,6},{6,0},{1,3},{3,5},{5,7},{7,1},{8,10},{10,12},{12... | collective-permute-start | bytes 884744 | tf_op jit(solution)/shard_map/ppermute | solution.py:16
  23.3 7.9 %collective-permute-start.4 = (bf16[24,6144]{1,0:T(8,128)(2,1)S(1)}, bf16[24,6144]{1,0:T(8,128)(2,1)S(1)}, u32[]{:S(2)}, u32[]{:S(2)}) collective-permute-start(bf16[24,6144]{1,0:T(8,128)(2,1)S(1)} %get-tuple-element.175), channel_id=1, source_target_pairs={{0,6},{2,0},{4,2},{6,4},{1,7},{3,1},{5,3},{7,5},{8,14},{10,8},{12,... | collective-permute-start | bytes 884744 | tf_op jit(solution)/shard_map/ppermute | solution.py:16
  26.2 7.9 %collective-permute-start.2 = (bf16[24,6144]{1,0:T(8,128)(2,1)S(1)}, bf16[24,6144]{1,0:T(8,128)(2,1)S(1)}, u32[]{:S(2)}, u32[]{:S(2)}) collective-permute-start(bf16[24,6144]{1,0:T(8,128)(2,1)S(1)} %get-tuple-element.176), channel_id=1, source_target_pairs={{0,1},{1,0},{2,3},{3,2},{4,5},{5,4},{6,7},{7,6},{8,9},{9,8},{10,11... | collective-permute-start | bytes 884744 | tf_op jit(solution)/shard_map/ppermute | solution.py:16
  28.3 38.3 %collective-permute-start.14 = (bf16[96,6144]{1,0:T(8,128)(2,1)S(1)}, bf16[96,6144]{1,0:T(8,128)(2,1)S(1)}, u32[]{:S(2)}, u32[]{:S(2)}) collective-permute-start(bf16[96,6144]{1,0:T(8,128)(2,1)S(1)} %pad_maximum_fusion.1.refs_1_), channel_id=1, source_target_pairs={{0,8},{8,0},{1,9},{9,1},{2,10},{10,2},{3,11},{11,3},{4,12},{12,4},... | collective-permute-start | bytes 3538952 | tf_op jit(solution)/shard_map/ppermute | solution.py:16
  31.2 7.8 %collective-permute-start.9 = (bf16[24,6144]{1,0:T(8,128)(2,1)S(1)}, bf16[24,6144]{1,0:T(8,128)(2,1)S(1)}, u32[]{:S(2)}, u32[]{:S(2)}) collective-permute-start(bf16[24,6144]{1,0:T(8,128)(2,1)S(1)} %collective-permute-done.4), channel_id=1, source_target_pairs={{0,6},{2,0},{4,2},{6,4},{1,7},{3,1},{5,3},{7,5},{8,14},{10,8},{12,... | collective-permute-start | bytes 884744 | tf_op jit(solution)/shard_map/ppermute | solution.py:16
  34.2 31.9 %collective-permute-start.12 = (bf16[48,6144]{1,0:T(8,128)(2,1)S(1)}, bf16[48,6144]{1,0:T(8,128)(2,1)S(1)}, u32[]{:S(2)}, u32[]{:S(2)}) collective-permute-start(bf16[48,6144]{1,0:T(8,128)(2,1)S(1)} %pad_maximum_fusion.4), channel_id=1, source_target_pairs={{0,8},{8,0},{1,9},{9,1},{2,10},{10,2},{3,11},{11,3},{4,12},{12,4},... | collective-permute-start | bytes 1769480 | tf_op jit(solution)/shard_map/ppermute | solution.py:16
  34.4 13.5 %collective-permute-start.11 = (bf16[48,6144]{1,0:T(8,128)(2,1)S(1)}, bf16[48,6144]{1,0:T(8,128)(2,1)S(1)}, u32[]{:S(2)}, u32[]{:S(2)}) collective-permute-start(bf16[48,6144]{1,0:T(8,128)(2,1)S(1)} %pad_maximum_fusion.3), channel_id=1, source_target_pairs={{0,1},{1,0},{2,3},{3,2},{4,5},{5,4},{6,7},{7,6},{8,9},{9,8},{10,11... | collective-permute-start | bytes 1769480 | tf_op jit(solution)/shard_map/ppermute | solution.py:16
  36.4 31.8 %collective-permute-start.3 = (bf16[96,6144]{1,0:T(8,128)(2,1)S(1)}, bf16[96,6144]{1,0:T(8,128)(2,1)S(1)}, u32[]{:S(2)}, u32[]{:S(2)}) collective-permute-start(bf16[96,6144]{1,0:T(8,128)(2,1)S(1)} %pad_maximum_fusion.refs_0_), channel_id=1, source_target_pairs={{0,2},{2,4},{4,6},{6,0},{1,3},{3,5},{5,7},{7,1},{8,10},{10,12},{12... | collective-permute-start | bytes 3538952 | tf_op jit(solution)/shard_map/ppermute | solution.py:16
  39.0 29.5 %collective-permute-start.10 = (bf16[96,6144]{1,0:T(8,128)(2,1)S(1)}, bf16[96,6144]{1,0:T(8,128)(2,1)S(1)}, u32[]{:S(2)}, u32[]{:S(2)}) collective-permute-start(bf16[96,6144]{1,0:T(8,128)(2,1)S(1)} %pad_maximum_fusion.refs_0_), channel_id=1, source_target_pairs={{0,6},{2,0},{4,2},{6,4},{1,7},{3,1},{5,3},{7,5},{8,14},{10,8},{12,... | collective-permute-start | bytes 3538952 | tf_op jit(solution)/shard_map/ppermute | solution.py:16
  47.9 34.6 %collective-permute-start.13 = (bf16[96,6144]{1,0:T(8,128)(2,1)S(1)}, bf16[96,6144]{1,0:T(8,128)(2,1)S(1)}, u32[]{:S(2)}, u32[]{:S(2)}) collective-permute-start(bf16[96,6144]{1,0:T(8,128)(2,1)S(1)} %pad_maximum_fusion.1.refs_1_), channel_id=1, source_target_pairs={{0,1},{1,0},{2,3},{3,2},{4,5},{5,4},{6,7},{7,6},{8,9},{9,8},{10,11... | collective-permute-start | bytes 3538952 | tf_op jit(solution)/shard_map/ppermute | solution.py:16
  66.1 29.2 %collective-permute-start.17 = (bf16[96,6144]{1,0:T(8,128)(2,1)S(1)}, bf16[96,6144]{1,0:T(8,128)(2,1)S(1)}, u32[]{:S(2)}, u32[]{:S(2)}) collective-permute-start(bf16[96,6144]{1,0:T(8,128)(2,1)S(1)} %constant_dynamic-update-slice_fusion.refs_2_), channel_id=1, source_target_pairs={{0,6},{2,0},{4,2},{6,4},{1,7},{3,1},{5,3},{7,5},{8,14},{10,8},{12,... | collective-permute-start | bytes 3538952 | tf_op jit(solution)/shard_map/ppermute | solution.py:16
  66.5 30.6 %collective-permute-start.16 = (bf16[96,6144]{1,0:T(8,128)(2,1)S(1)}, bf16[96,6144]{1,0:T(8,128)(2,1)S(1)}, u32[]{:S(2)}, u32[]{:S(2)}) collective-permute-start(bf16[96,6144]{1,0:T(8,128)(2,1)S(1)} %constant_dynamic-update-slice_fusion.refs_2_), channel_id=1, source_target_pairs={{0,2},{2,4},{4,6},{6,0},{1,3},{3,5},{5,7},{7,1},{8,10},{10,12},{12... | collective-permute-start | bytes 3538952 | tf_op jit(solution)/shard_map/ppermute | solution.py:16
  68.2 29.9 %collective-permute-start.19 = (bf16[96,6144]{1,0:T(8,128)(2,1)S(1)}, bf16[96,6144]{1,0:T(8,128)(2,1)S(1)}, u32[]{:S(2)}, u32[]{:S(2)}) collective-permute-start(bf16[96,6144]{1,0:T(8,128)(2,1)S(1)} %pad_maximum_fusion.2.refs_2_), channel_id=1, source_target_pairs={{0,1},{1,0},{2,3},{3,2},{4,5},{5,4},{6,7},{7,6},{8,9},{9,8},{10,11... | collective-permute-start | bytes 3538952 | tf_op jit(solution)/shard_map/ppermute | solution.py:16
  68.5 30.6 %collective-permute-start.18 = (bf16[96,6144]{1,0:T(8,128)(2,1)S(1)}, bf16[96,6144]{1,0:T(8,128)(2,1)S(1)}, u32[]{:S(2)}, u32[]{:S(2)}) collective-permute-start(bf16[96,6144]{1,0:T(8,128)(2,1)S(1)} %pad_maximum_fusion.2.refs_2_), channel_id=1, source_target_pairs={{0,8},{8,0},{1,9},{9,1},{2,10},{10,2},{3,11},{11,3},{4,12},{12,4},... | collective-permute-start | bytes 3538952 | tf_op jit(solution)/shard_map/ppermute | solution.py:16
  82.6 33.1 %collective-permute-start.15 = (bf16[96,6144]{1,0:T(8,128)(2,1)S(1)}, bf16[96,6144]{1,0:T(8,128)(2,1)S(1)}, u32[]{:S(2)}, u32[]{:S(2)}) collective-permute-start(bf16[96,6144]{1,0:T(8,128)(2,1)S(1)} %collective-permute-done.10.refs_1_), channel_id=1, source_target_pairs={{0,6},{2,0},{4,2},{6,4},{1,7},{3,1},{5,3},{7,5},{8,14},{10,8},{12,... | collective-permute-start | bytes 3538952 | tf_op jit(solution)/shard_map/ppermute | solution.py:16
  95.3 29.0 %collective-permute-start.21 = (bf16[96,6144]{1,0:T(8,128)(2,1)S(1)}, bf16[96,6144]{1,0:T(8,128)(2,1)S(1)}, u32[]{:S(2)}, u32[]{:S(2)}) collective-permute-start(bf16[96,6144]{1,0:T(8,128)(2,1)S(1)} %collective-permute-done.13.refs_3_), channel_id=1, source_target_pairs={{0,8},{8,0},{1,9},{9,1},{2,10},{10,2},{3,11},{11,3},{4,12},{12,4},... | collective-permute-start | bytes 3538952 | tf_op jit(solution)/shard_map/ppermute | solution.py:16
  99.1 26.4 %collective-permute-start.20 = (bf16[96,6144]{1,0:T(8,128)(2,1)S(1)}, bf16[96,6144]{1,0:T(8,128)(2,1)S(1)}, u32[]{:S(2)}, u32[]{:S(2)}) collective-permute-start(bf16[96,6144]{1,0:T(8,128)(2,1)S(1)} %collective-permute-done.16.refs_0_), channel_id=1, source_target_pairs={{0,2},{2,4},{4,6},{6,0},{1,3},{3,5},{5,7},{7,1},{8,10},{10,12},{12... | collective-permute-start | bytes 3538952 | tf_op jit(solution)/shard_map/ppermute | solution.py:16
  99.2 29.0 %collective-permute-start.22 = (bf16[96,6144]{1,0:T(8,128)(2,1)S(1)}, bf16[96,6144]{1,0:T(8,128)(2,1)S(1)}, u32[]{:S(2)}, u32[]{:S(2)}) collective-permute-start(bf16[96,6144]{1,0:T(8,128)(2,1)S(1)} %collective-permute-done.18.refs_2_), channel_id=1, source_target_pairs={{0,1},{1,0},{2,3},{3,2},{4,5},{5,4},{6,7},{7,6},{8,9},{9,8},{10,11... | collective-permute-start | bytes 3538952 | tf_op jit(solution)/shard_map/ppermute | solution.py:16
  101.2 42.9 %collective-permute-start.25 = (bf16[96,6144]{1,0:T(8,128)(2,1)S(1)}, bf16[96,6144]{1,0:T(8,128)(2,1)}, u32[]{:S(2)}, u32[]{:S(2)}) collective-permute-start(bf16[96,6144]{1,0:T(8,128)(2,1)S(1)} %get-tuple-element.126), channel_id=1, source_target_pairs={{0,8},{8,0},{1,9},{9,1},{2,10},{10,2},{3,11},{11,3},{4,12},{12,4},... | collective-permute-start | bytes 3538952 | tf_op jit(solution)/shard_map/ppermute | solution.py:16
  115.7 31.9 %collective-permute-start.26 = (bf16[96,6144]{1,0:T(8,128)(2,1)S(1)}, bf16[96,6144]{1,0:T(8,128)(2,1)S(1)}, u32[]{:S(2)}, u32[]{:S(2)}) collective-permute-start(bf16[96,6144]{1,0:T(8,128)(2,1)S(1)} %get-tuple-element.127), channel_id=1, source_target_pairs={{0,1},{1,0},{2,3},{3,2},{4,5},{5,4},{6,7},{7,6},{8,9},{9,8},{10,11... | collective-permute-start | bytes 3538952 | tf_op jit(solution)/shard_map/ppermute | solution.py:16
  124.3 23.3 %collective-permute-start.23 = (bf16[96,6144]{1,0:T(8,128)(2,1)S(1)}, bf16[96,6144]{1,0:T(8,128)(2,1)S(1)}, u32[]{:S(2)}, u32[]{:S(2)}) collective-permute-start(bf16[96,6144]{1,0:T(8,128)(2,1)S(1)} %get-tuple-element.124), channel_id=1, source_target_pairs={{0,6},{2,0},{4,2},{6,4},{1,7},{3,1},{5,3},{7,5},{8,14},{10,8},{12,... | collective-permute-start | bytes 3538952 | tf_op jit(solution)/shard_map/ppermute | solution.py:16
  128.1 20.5 %collective-permute-start.24 = (bf16[96,6144]{1,0:T(8,128)(2,1)S(1)}, bf16[96,6144]{1,0:T(8,128)(2,1)S(1)}, u32[]{:S(2)}, u32[]{:S(2)}) collective-permute-start(bf16[96,6144]{1,0:T(8,128)(2,1)S(1)} %get-tuple-element.125), channel_id=1, source_target_pairs={{0,2},{2,4},{4,6},{6,0},{1,3},{3,5},{5,7},{7,1},{8,10},{10,12},{12... | collective-permute-start | bytes 3538952 | tf_op jit(solution)/shard_map/ppermute | solution.py:16
  148.6 26.4 %collective-permute-start.27 = (bf16[96,6144]{1,0:T(8,128)(2,1)S(1)}, bf16[96,6144]{1,0:T(8,128)(2,1)S(1)}, u32[]{:S(2)}, u32[]{:S(2)}) collective-permute-start(bf16[96,6144]{1,0:T(8,128)(2,1)S(1)} %get-tuple-element.128), channel_id=1, source_target_pairs={{0,8},{8,0},{1,9},{9,1},{2,10},{10,2},{3,11},{11,3},{4,12},{12,4},... | collective-permute-start | bytes 3538952 | tf_op jit(solution)/shard_map/ppermute | solution.py:16
  148.9 25.1 %collective-permute-start.28 = (bf16[96,6144]{1,0:T(8,128)(2,1)S(1)}, bf16[96,6144]{1,0:T(8,128)(2,1)S(1)}, u32[]{:S(2)}, u32[]{:S(2)}) collective-permute-start(bf16[96,6144]{1,0:T(8,128)(2,1)S(1)} %get-tuple-element.130), channel_id=1, source_target_pairs={{0,2},{2,4},{4,6},{6,0},{1,3},{3,5},{5,7},{7,1},{8,10},{10,12},{12... | collective-permute-start | bytes 3538952 | tf_op jit(solution)/shard_map/ppermute | solution.py:16
  148.9 25.4 %collective-permute-start.29 = (bf16[96,6144]{1,0:T(8,128)(2,1)S(1)}, bf16[96,6144]{1,0:T(8,128)(2,1)S(1)}, u32[]{:S(2)}, u32[]{:S(2)}) collective-permute-start(bf16[96,6144]{1,0:T(8,128)(2,1)S(1)} %get-tuple-element.132), channel_id=1, source_target_pairs={{0,6},{2,0},{4,2},{6,4},{1,7},{3,1},{5,3},{7,5},{8,14},{10,8},{12,... | collective-permute-start | bytes 3538952 | tf_op jit(solution)/shard_map/ppermute | solution.py:16
  152.2 22.5 %collective-permute-start.30 = (bf16[96,6144]{1,0:T(8,128)(2,1)S(1)}, bf16[96,6144]{1,0:T(8,128)(2,1)S(1)}, u32[]{:S(2)}, u32[]{:S(2)}) collective-permute-start(bf16[96,6144]{1,0:T(8,128)(2,1)S(1)} %get-tuple-element.136), channel_id=1, source_target_pairs={{0,1},{1,0},{2,3},{3,2},{4,5},{5,4},{6,7},{7,6},{8,9},{9,8},{10,11... | collective-permute-start | bytes 3538952 | tf_op jit(solution)/shard_map/ppermute | solution.py:16
  175.0 24.3 %collective-permute-start.31 = (bf16[96,6144]{1,0:T(8,128)(2,1)S(1)}, bf16[96,6144]{1,0:T(8,128)(2,1)S(1)}, u32[]{:S(2)}, u32[]{:S(2)}) collective-permute-start(bf16[96,6144]{1,0:T(8,128)(2,1)S(1)} %add_convert_fusion.3), channel_id=1, source_target_pairs={{0,2},{2,4},{4,6},{6,0},{1,3},{3,5},{5,7},{7,1},{8,10},{10,12},{12... | collective-permute-start | bytes 3538952 | tf_op jit(solution)/shard_map/ppermute | solution.py:16
  175.1 24.3 %collective-permute-start.32 = (bf16[96,6144]{1,0:T(8,128)(2,1)S(1)}, bf16[96,6144]{1,0:T(8,128)(2,1)S(1)}, u32[]{:S(2)}, u32[]{:S(2)}) collective-permute-start(bf16[96,6144]{1,0:T(8,128)(2,1)S(1)} %add_convert_fusion.2), channel_id=1, source_target_pairs={{0,6},{2,0},{4,2},{6,4},{1,7},{3,1},{5,3},{7,5},{8,14},{10,8},{12,... | collective-permute-start | bytes 3538952 | tf_op jit(solution)/shard_map/ppermute | solution.py:16
  178.3 22.1 %collective-permute-start.33 = (bf16[96,6144]{1,0:T(8,128)(2,1)S(1)}, bf16[96,6144]{1,0:T(8,128)(2,1)S(1)}, u32[]{:S(2)}, u32[]{:S(2)}) collective-permute-start(bf16[96,6144]{1,0:T(8,128)(2,1)S(1)} %add_convert_fusion.1), channel_id=1, source_target_pairs={{0,1},{1,0},{2,3},{3,2},{4,5},{5,4},{6,7},{7,6},{8,9},{9,8},{10,11... | collective-permute-start | bytes 3538952 | tf_op jit(solution)/shard_map/ppermute | solution.py:16
  180.2 20.4 %collective-permute-start.34 = (bf16[96,6144]{1,0:T(8,128)(2,1)S(1)}, bf16[96,6144]{1,0:T(8,128)(2,1)S(1)}, u32[]{:S(2)}, u32[]{:S(2)}) collective-permute-start(bf16[96,6144]{1,0:T(8,128)(2,1)S(1)} %add_convert_fusion), channel_id=1, source_target_pairs={{0,8},{8,0},{1,9},{9,1},{2,10},{10,2},{3,11},{11,3},{4,12},{12,4},... | collective-permute-start | bytes 3538952 | tf_op jit(solution)/shard_map/ppermute | solution.py:16
  181.4 10.8 %collective-permute-start.35 = (f32[4,128]{1,0:T(4,128)S(1)}, f32[4,128]{1,0:T(4,128)S(1)}, u32[]{:S(2)}, u32[]{:S(2)}) collective-permute-start(f32[4,128]{1,0:T(4,128)S(1)} %pad_maximum_fusion.9), channel_id=1, source_target_pairs={{0,32},{32,64},{64,96},{96,0},{1,33},{33,65},{65,97},{97,1},{2,34}... | collective-permute-start | bytes 6152 | tf_op jit(solution)/shard_map/ppermute | solution.py:40
  201.1 11.9 %collective-permute-start.36 = (bf16[48,6144]{1,0:T(8,128)(2,1)S(1)}, bf16[48,6144]{1,0:T(8,128)(2,1)S(1)}, u32[]{:S(2)}, u32[]{:S(2)}) collective-permute-start(bf16[48,6144]{1,0:T(8,128)(2,1)S(1)} %pad_maximum_fusion.5), channel_id=1, source_target_pairs={{0,6},{2,0},{4,2},{6,4},{1,7},{3,1},{5,3},{7,5},{8,14},{10,8},{12,... | collective-permute-start | bytes 1769480 | tf_op jit(solution)/shard_map/ppermute | solution.py:16
  203.2 14.3 %collective-permute-start.37 = (bf16[48,6144]{1,0:T(8,128)(2,1)S(1)}, bf16[48,6144]{1,0:T(8,128)(2,1)S(1)}, u32[]{:S(2)}, u32[]{:S(2)}) collective-permute-start(bf16[48,6144]{1,0:T(8,128)(2,1)S(1)} %pad_maximum_fusion.6), channel_id=1, source_target_pairs={{0,2},{2,4},{4,6},{6,0},{1,3},{3,5},{5,7},{7,1},{8,10},{10,12},{12... | collective-permute-start | bytes 1769480 | tf_op jit(solution)/shard_map/ppermute | solution.py:16
  203.5 14.0 %collective-permute-start.38 = (bf16[48,6144]{1,0:T(8,128)(2,1)S(1)}, bf16[48,6144]{1,0:T(8,128)(2,1)S(1)}, u32[]{:S(2)}, u32[]{:S(2)}) collective-permute-start(bf16[48,6144]{1,0:T(8,128)(2,1)S(1)} %add_convert_fusion.5), channel_id=1, source_target_pairs={{0,1},{1,0},{2,3},{3,2},{4,5},{5,4},{6,7},{7,6},{8,9},{9,8},{10,11... | collective-permute-start | bytes 1769480 | tf_op jit(solution)/shard_map/ppermute | solution.py:16
  205.8 13.4 %collective-permute-start.39 = (bf16[48,6144]{1,0:T(8,128)(2,1)S(1)}, bf16[48,6144]{1,0:T(8,128)(2,1)S(1)}, u32[]{:S(2)}, u32[]{:S(2)}) collective-permute-start(bf16[48,6144]{1,0:T(8,128)(2,1)S(1)} %add_convert_fusion.4), channel_id=1, source_target_pairs={{0,8},{8,0},{1,9},{9,1},{2,10},{10,2},{3,11},{11,3},{4,12},{12,4},... | collective-permute-start | bytes 1769480 | tf_op jit(solution)/shard_map/ppermute | solution.py:16
  219.8 6.8 %collective-permute-start.43 = (bf16[24,6144]{1,0:T(8,128)(2,1)S(1)}, bf16[24,6144]{1,0:T(8,128)(2,1)S(1)}, u32[]{:S(2)}, u32[]{:S(2)}) collective-permute-start(bf16[24,6144]{1,0:T(8,128)(2,1)S(1)} %add_convert_fusion.10), channel_id=1, source_target_pairs={{0,1},{1,0},{2,3},{3,2},{4,5},{5,4},{6,7},{7,6},{8,9},{9,8},{10,11... | collective-permute-start | bytes 884744 | tf_op jit(solution)/shard_map/ppermute | solution.py:16
  220.3 7.9 %collective-permute-start.41 = (bf16[24,6144]{1,0:T(8,128)(2,1)S(1)}, bf16[24,6144]{1,0:T(8,128)(2,1)S(1)}, u32[]{:S(2)}, u32[]{:S(2)}) collective-permute-start(bf16[24,6144]{1,0:T(8,128)(2,1)S(1)} %add_convert_fusion.12), channel_id=1, source_target_pairs={{0,2},{2,4},{4,6},{6,0},{1,3},{3,5},{5,7},{7,1},{8,10},{10,12},{12... | collective-permute-start | bytes 884744 | tf_op jit(solution)/shard_map/ppermute | solution.py:16
  220.9 7.3 %collective-permute-start.40 = (bf16[24,6144]{1,0:T(8,128)(2,1)S(1)}, bf16[24,6144]{1,0:T(8,128)(2,1)S(1)}, u32[]{:S(2)}, u32[]{:S(2)}) collective-permute-start(bf16[24,6144]{1,0:T(8,128)(2,1)S(1)} %add_convert_fusion.13), channel_id=1, source_target_pairs={{0,6},{2,0},{4,2},{6,4},{1,7},{3,1},{5,3},{7,5},{8,14},{10,8},{12,... | collective-permute-start | bytes 884744 | tf_op jit(solution)/shard_map/ppermute | solution.py:16
  223.5 6.7 %collective-permute-start.42 = (bf16[24,6144]{1,0:T(8,128)(2,1)S(1)}, bf16[24,6144]{1,0:T(8,128)(2,1)S(1)}, u32[]{:S(2)}, u32[]{:S(2)}) collective-permute-start(bf16[24,6144]{1,0:T(8,128)(2,1)S(1)} %add_convert_fusion.11), channel_id=1, source_target_pairs={{0,8},{8,0},{1,9},{9,1},{2,10},{10,2},{3,11},{11,3},{4,12},{12,4},... | collective-permute-start | bytes 884744 | tf_op jit(solution)/shard_map/ppermute | solution.py:16
  231.1 18.5 %collective-permute-start.45 = (bf16[48,6144]{1,0:T(8,128)(2,1)S(1)}, bf16[48,6144]{1,0:T(8,128)(2,1)S(1)}, u32[]{:S(2)}, u32[]{:S(2)}) collective-permute-start(bf16[48,6144]{1,0:T(8,128)(2,1)S(1)} %pad_maximum_fusion.8), channel_id=1, source_target_pairs={{0,57},{1,56},{8,49},{9,48},{16,41},{17,40},{24,33},{25,32},{32,89... | collective-permute-start | bytes 1769480 | tf_op jit(solution)/shard_map/ppermute | solution.py:55
  231.2 19.0 %collective-permute-start.44 = (bf16[48,6144]{1,0:T(8,128)(2,1)S(1)}, bf16[48,6144]{1,0:T(8,128)(2,1)S(1)}, u32[]{:S(2)}, u32[]{:S(2)}) collective-permute-start(bf16[48,6144]{1,0:T(8,128)(2,1)S(1)} %pad_maximum_fusion.7), channel_id=1, source_target_pairs={{0,33},{1,32},{32,65},{33,64},{64,97},{65,96},{96,1},{97,0},{2,35}... | collective-permute-start | bytes 1769480 | tf_op jit(solution)/shard_map/ppermute | solution.py:45
  (8 other events, 120.7 us)

commit v7 on v6

--- a/solution.py
+++ b/solution.py
@@ -188,39 +188,39 @@
     a1, b = split(own, 2)
     a1_y, b_behind, b_ahead = over_y(a1), right(b), left(b)
     a1_near = join(a1, a1_y)
-    b_opposite = right(b_behind)
+    a1_far, b_opposite = over_z(a1_near), right(b_behind)
+    partner, b_ahead, b_opposite = together(partner, b_ahead, b_opposite)
     b_ring = join(b, b_behind, b_ahead, b_opposite)
-    b_y = over_y(b_ring)
+    b_z = over_z(b_ring)
 
     a2, g = split(partner, 2)
-    a2_z, g_behind, g_ahead = over_z(a2), left(g), right(g)
-    g_behind, g_ahead, b_ring_late, a1_near_late = together(g_behind, g_ahead, b_ring, a1_near)
+    a2_y, g_behind, g_ahead = over_y(a2), left(g), right(g)
+    g_behind, g_ahead, b_ring_late = together(g_behind, g_ahead, b_ring)
     g_opposite = left(g_behind)
-    a1_far = over_z(a1_near_late)
-    a2_near = join(a2, a2_z)
+    b_y = over_y(b_ring_late)
+    a2_near = join(a2, a2_y)
     near = join(a1_near, a2_near)
-    a1_far, b_ring_late = together(a1_far, b_ring_late)
-    a2_far, b_z = over_y(a2_near), over_z(b_ring_late)
+    a2_far = over_z(a2_near)
     near_late, g_opposite = together(near, g_opposite)
     near_left, near_right = right(near), left(near_late)
     g_ring = join(g, g_behind, g_ahead, g_opposite)
 
-    b_y, g_ring_out = together(b_y, g_ring)
+    b_z, g_ring_out = together(b_z, g_ring)
     g_y, g_z = over_y(g_ring_out), over_z(g_ring_out)
     far = join(a1_far, a2_far)
-    near, b_ring, g_ring, b_y = experts([near, b_ring, g_ring, b_y], *matrices)
+    near, b_ring, g_ring, b_z = experts([near, b_ring, g_ring, b_z], *matrices)
     far_left, far_right = right(far), left(far)
 
-    near_left, near_right, far, b_z, near, b_ring, g_ring, b_y = together(
-        near_left, near_right, far, b_z, near, b_ring, g_ring, b_y
-    )
-    near_opposite, b_yz = left(near_right), over_y(b_z)
-    near_left, near_right, far, b_z = experts([near_left, near_right, far, b_z], *matrices)
-
-    far_left, far_right, g_y, g_z, near_left, near_right, far, b_z = together(
-        far_left, far_right, g_y, g_z, near_left, near_right, far, b_z
-    )
-    far_opposite, g_zy = right(far_left), over_z(g_y)
+    near_left, near_right, far, b_y, near, b_ring, g_ring, b_z = together(
+        near_left, near_right, far, b_y, near, b_ring, g_ring, b_z
+    )
+    near_opposite, b_yz = left(near_right), over_z(b_y)
+    near_left, near_right, far, b_y = experts([near_left, near_right, far, b_y], *matrices)
+
+    far_left, far_right, g_y, g_z, near_left, near_right, far, b_y = together(
+        far_left, far_right, g_y, g_z, near_left, near_right, far, b_y
+    )
+    far_opposite, g_zy = right(far_left), over_y(g_z)
     far_left, far_right, g_y, g_z = experts([far_left, far_right, g_y, g_z], *matrices)
 
     near_opposite, far_opposite, b_yz, g_zy, far_left, far_right, g_y, g_z = together(
@@ -251,25 +251,23 @@
         [take(b_terms, 3, 4), take(g_terms, 2, 4)],
         [take(g_terms, 3, 4), take(b_terms, 2, 4)],
         [take(near, 0, 2)],
-        [take(far, 1, 2)],
+        [take(near, 3, 4), take(far, 3, 4)],
     )
     got = together(left(got[0]), right(got[1]), over_z(got[2]), over_y(got[3]))
-    a1_terms = take(far, 0, 4), take(far, 1, 4)
-    a2_terms = take(near, 2, 4), take(near, 3, 4)
     ends = sums(
         [take(b_terms, 1, 4) + take(got[:1], 0, 2)],
         [take(g_terms, 1, 4) + take(got[1:2], 0, 2)],
-        [a1_terms[1] + take(got[2:3], 1, 2)],
-        [a2_terms[0] + take(got[3:], 0, 2)],
+        [take(far, 1, 4) + take(got[2:3], 1, 2)],
+        [take(near, 2, 4) + take(got[3:], 0, 2)],
     )
     ends = together(left(ends[0]), right(ends[1]), over_y(ends[2]), over_z(ends[3]))
     own, partner = sums(
         [
-            a1_terms[0] + take(got[2:3], 0, 2) + take(ends[2:3], 0, 1),
+            take(far, 0, 4) + take(got[2:3], 0, 2) + take(ends[2:3], 0, 1),
             take(b_terms, 0, 4) + take(got[1:2], 1, 2) + take(ends[:1], 0, 1),
         ],
         [
-            a2_terms[1] + take(got[3:], 1, 2) + take(ends[3:], 0, 1),
+            take(far, 2, 4) + take(got[3:], 1, 2) + take(ends[3:], 0, 1),
             take(g_terms, 0, 4) + take(got[:1], 1, 2) + take(ends[1:2], 0, 1),
         ],
     )

time: 253 us -> 257 us (1.016)
  starting transfers between devices: 65.1 us -> 70.4 us
    ppermute x42, waiting for transfers between devices: 93.5 us -> 103 us  [shift(): return lax.ppermute(value, axis, [(i, (i + by) % n) for i in range(n)])]
    ppermute x1, waiting for transfers between devices: 9.96 us -> 1.53 us  [to_partner(): return lax.ppermute(value, ('yh', 'yl'), [(y, 3 - y) for y in range(4)])]
    ppermute x42, starting transfers between devices: 57.8 us -> 64.1 us  [shift(): return lax.ppermute(value, axis, [(i, (i + by) % n) for i in range(n)])]
    unnamed x21 -> x29, local copies, waits for them, and re-layouts: 5.14 us -> 6.19 us
  transfers between devices with their start and end apart: 46 -> 46, of which waited for: 25 -> 23; matrix products, arithmetic and copies ran while one was open for 2% -> 1% of each run, Pallas kernels for 17% -> 17%
where the time goes in v7:
time: 257 us; the launch traced here: 256 us
  waiting for transfers between devices  127 us (49%)
  starting transfers between devices  70.4 us (27%)
  Pallas kernels  43.7 us (17%)
  local copies, waits for them, and re-layouts  6.54 us (3%)
  other arithmetic  5.37 us (2%)
  matrix products  3.07 us (1%)
    ppermute x42, waiting for transfers between devices, shift(): return lax.ppermute(value, axis, [(i, (i + by) % n) for i in range(n)])  103 us
    ppermute x42, starting transfers between devices, shift(): return lax.ppermute(value, axis, [(i, (i + by) % n) for i in range(n)])  64.1 us
    pallas_call x4, Pallas kernels, experts(): pl.pallas_call(experts_kernel, grid=(2 * half,), in_specs=rows_in + [into...  43.7 us
    ppermute x1, waiting for transfers between devices, to_owner_across(): return lax.ppermute(value, ('zh', 'core', 'yh', 'yl', 'zl'), pairs)  14.1 us
    ppermute x1, waiting for transfers between devices, to_next_section(): lax.ppermute(value, ('zh', 'core'), [(s, (s + 1) % 4) for s in range(4)])  8.5 us
    unnamed x29, local copies, waits for them, and re-layouts  6.19 us
  transfers between devices with their start and end apart: 46, of which 23 were waited for; matrix products, arithmetic and copies ran while one was open for 1% of the time, Pallas kernels for 17%

profile of v7, /device:TPU:0, one launch (start us, length us, event | category | flops | bytes accessed | tf_op | source)
XLA Modules:
  0.0 256.5 jit_solution(3178311243122702860)
XLA Ops:
  2.5 1.6 collective-permute-start.3
  4.1 1.6 collective-permute-start
  5.7 1.7 collective-permute-start.2
  7.4 2.2 collective-permute-start.1
  9.6 2.8 %collective-permute-done.3 = bf16[24,6144]{1,0:T(8,128)(2,1)S(1)} collective-permute-done((bf16[24,6144]{1,0:T(8,128)(2,1)S(1)}, bf16[24,6144]{1,0:T(8,128)(2,1)S(1)}, u32[]{:S(2)}, u32[]{:S(2)}) %collective-permute-start.3) | collective-permute-done | bytes 294944 | tf_op jit(solution)/shard_map/ppermute | solution.py:16
  12.9 2.0 collective-permute-start.11
  14.9 6.4 %collective-permute-done.4 = bf16[24,6144]{1,0:T(8,128)(2,1)S(1)} collective-permute-done((bf16[24,6144]{1,0:T(8,128)(2,1)S(1)}, bf16[24,6144]{1,0:T(8,128)(2,1)S(1)}, u32[]{:S(2)}, u32[]{:S(2)}) %collective-permute-start.4) | collective-permute-done | bytes 294944 | tf_op jit(solution)/shard_map/ppermute | solution.py:16
  23.3 3.0 %collective-permute-start.7 = (bf16[24,6144]{1,0:T(8,128)(2,1)S(1)}, bf16[24,6144]{1,0:T(8,128)(2,1)S(1)}, u32[]{:S(2)}, u32[]{:S(2)}) collective-permute-start(bf16[24,6144]{1,0:T(8,128)(2,1)S(1)} %get-tuple-element.175), channel_id=1, source_target_pairs={{0,6},{2,0},{4,2},{6,4},{1,7},{3,1},{5,3},{7,5},{8,14},{10,8},{12,... | collective-permute-start | bytes 884744 | tf_op jit(solution)/shard_map/ppermute | solution.py:16
  26.7 2.0 collective-permute-start.14
  28.7 2.5 collective-permute-done.8
  31.2 3.0 %collective-permute-start.9 = (bf16[24,6144]{1,0:T(8,128)(2,1)S(1)}, bf16[24,6144]{1,0:T(8,128)(2,1)S(1)}, u32[]{:S(2)}, u32[]{:S(2)}) collective-permute-start(bf16[24,6144]{1,0:T(8,128)(2,1)S(1)} %collective-permute-done.7), channel_id=1, source_target_pairs={{0,6},{2,0},{4,2},{6,4},{1,7},{3,1},{5,3},{7,5},{8,14},{10,8},{12,... | collective-permute-start | bytes 884744 | tf_op jit(solution)/shard_map/ppermute | solution.py:16
  34.2 2.0 collective-permute-start.12
  36.8 2.2 collective-permute-done.9
  39.0 3.7 %collective-permute-start.10 = (bf16[96,6144]{1,0:T(8,128)(2,1)S(1)}, bf16[96,6144]{1,0:T(8,128)(2,1)S(1)}, u32[]{:S(2)}, u32[]{:S(2)}) collective-permute-start(bf16[96,6144]{1,0:T(8,128)(2,1)S(1)} %pad_maximum_fusion.refs_0_), channel_id=1, source_target_pairs={{0,6},{2,0},{4,2},{6,4},{1,7},{3,1},{5,3},{7,5},{8,14},{10,8},{12,... | collective-permute-start | bytes 3538952 | tf_op jit(solution)/shard_map/ppermute | solution.py:16
  42.8 22.2 %collective-permute-done.12 = bf16[48,6144]{1,0:T(8,128)(2,1)S(1)} collective-permute-done((bf16[48,6144]{1,0:T(8,128)(2,1)S(1)}, bf16[48,6144]{1,0:T(8,128)(2,1)S(1)}, u32[]{:S(2)}, u32[]{:S(2)}) %collective-permute-start.12) | collective-permute-done | bytes 589856 | tf_op jit(solution)/shard_map/ppermute | solution.py:16
  65.0 3.0 %collective-permute-start.17 = (bf16[96,6144]{1,0:T(8,128)(2,1)S(1)}, bf16[96,6144]{1,0:T(8,128)(2,1)S(1)}, u32[]{:S(2)}, u32[]{:S(2)}) collective-permute-start(bf16[96,6144]{1,0:T(8,128)(2,1)S(1)} %constant_dynamic-update-slice_fusion.refs_2_), channel_id=1, source_target_pairs={{0,6},{2,0},{4,2},{6,4},{1,7},{3,1},{5,3},{7,5},{8,14},{10,8},{12,... | collective-permute-start | bytes 3538952 | tf_op jit(solution)/shard_map/ppermute | solution.py:16
  68.1 1.8 collective-permute-start.19
  69.9 1.6 collective-permute-start.18
  71.5 2.8 %copy-done.2 = bf16[1,512,6144]{2,1,0:T(8,128)(2,1)S(1)} copy-done((bf16[1,512,6144]{2,1,0:T(8,128)(2,1)S(1)}, bf16[1,512,6144]{2,1,0:T(8,128)(2,1)}, u32[]{:S(2)}) %copy-start.2) | copy-done | bytes 6291480
  74.3 10.9 %experts.4 = (bf16[96,6144]{1,0:T(8,128)(2,1)S(1)}, bf16[96,6144]{1,0:T(8,128)(2,1)S(1)}, bf16[96,6144]{1,0:T(8,128)(2,1)S(1)}, bf16[96,6144]{1,0:T(8,128)(2,1)S(1)}) custom-call(bf16[96,6144]{1,0:T(8,128)(2,1)S(1)} %pad_maximum_fusion.refs_0_, bf16[96,6144]{1,0:T(8,128)(2,1)S(1)} %pad_maximum_fusion.1.refs_1_, ...), custom_call_target="tpu_custom_call" | custom-call | flops 7247757312 | bytes 28311552 | tf_op jit(solution)/shard_map/experts/pallas_call | solution.py:141
  85.2 3.4 %collective-permute-start.15 = (bf16[96,6144]{1,0:T(8,128)(2,1)S(1)}, bf16[96,6144]{1,0:T(8,128)(2,1)S(1)}, u32[]{:S(2)}, u32[]{:S(2)}) collective-permute-start(bf16[96,6144]{1,0:T(8,128)(2,1)S(1)} %collective-permute-done.10.refs_1_), channel_id=1, source_target_pairs={{0,6},{2,0},{4,2},{6,4},{1,7},{3,1},{5,3},{7,5},{8,14},{10,8},{12,... | collective-permute-start | bytes 3538952 | tf_op jit(solution)/shard_map/ppermute | solution.py:16
  88.6 10.9 %experts.5 = (bf16[96,6144]{1,0:T(8,128)(2,1)S(1)}, bf16[96,6144]{1,0:T(8,128)(2,1)S(1)}, bf16[96,6144]{1,0:T(8,128)(2,1)S(1)}, bf16[96,6144]{1,0:T(8,128)(2,1)S(1)}) custom-call(bf16[96,6144]{1,0:T(8,128)(2,1)S(1)} %collective-permute-done.6.refs_0_, bf16[96,6144]{1,0:T(8,128)(2,1)S(1)} %collective-permute-done.10.refs_1_, ...), custom_call_target="tpu_custom_call" | custom-call | flops 7247757312 | bytes 28311552 | tf_op jit(solution)/shard_map/experts/pallas_call | solution.py:141
  100.6 1.7 collective-permute-start.26
  102.3 10.9 %experts.6 = (bf16[96,6144]{1,0:T(8,128)(2,1)S(1)}, bf16[96,6144]{1,0:T(8,128)(2,1)S(1)}, bf16[96,6144]{1,0:T(8,128)(2,1)S(1)}, bf16[96,6144]{1,0:T(8,128)(2,1)S(1)}) custom-call(bf16[96,6144]{1,0:T(8,128)(2,1)S(1)} %collective-permute-done.16.refs_0_, bf16[96,6144]{1,0:T(8,128)(2,1)S(1)} %collective-permute-done.17.refs_1_, ...), custom_call_target="tpu_custom_call" | custom-call | flops 7247757312 | bytes 28311552 | tf_op jit(solution)/shard_map/experts/pallas_call | solution.py:141
  113.3 3.5 %collective-permute-done.15.refs_0_ = bf16[96,6144]{1,0:T(8,128)(2,1)S(1)} collective-permute-done((bf16[96,6144]{1,0:T(8,128)(2,1)S(1)}, bf16[96,6144]{1,0:T(8,128)(2,1)S(1)}, u32[]{:S(2)}, u32[]{:S(2)}) %collective-permute-start.15) | collective-permute-done | bytes 1179680 | tf_op jit(solution)/shard_map/ppermute | solution.py:16
  116.8 3.7 %collective-permute-start.23 = (bf16[96,6144]{1,0:T(8,128)(2,1)S(1)}, bf16[96,6144]{1,0:T(8,128)(2,1)S(1)}, u32[]{:S(2)}, u32[]{:S(2)}) collective-permute-start(bf16[96,6144]{1,0:T(8,128)(2,1)S(1)} %get-tuple-element.124), channel_id=1, source_target_pairs={{0,6},{2,0},{4,2},{6,4},{1,7},{3,1},{5,3},{7,5},{8,14},{10,8},{12,... | collective-permute-start | bytes 3538952 | tf_op jit(solution)/shard_map/ppermute | solution.py:16
  120.5 8.1 %collective-permute-done.21.refs_2_ = bf16[96,6144]{1,0:T(8,128)(2,1)S(1)} collective-permute-done((bf16[96,6144]{1,0:T(8,128)(2,1)S(1)}, bf16[96,6144]{1,0:T(8,128)(2,1)S(1)}, u32[]{:S(2)}, u32[]{:S(2)}) %collective-permute-start.21) | collective-permute-done | bytes 1179680 | tf_op jit(solution)/shard_map/ppermute | solution.py:16
  131.4 10.9 %experts.7 = (bf16[96,6144]{1,0:T(8,128)(2,1)S(1)}, bf16[96,6144]{1,0:T(8,128)(2,1)S(1)}, bf16[96,6144]{1,0:T(8,128)(2,1)S(1)}, bf16[96,6144]{1,0:T(8,128)(2,1)S(1)}) custom-call(bf16[96,6144]{1,0:T(8,128)(2,1)S(1)} %collective-permute-done.15.refs_0_, bf16[96,6144]{1,0:T(8,128)(2,1)S(1)} %collective-permute-done.20.refs_1_, ...), custom_call_target="tpu_custom_call" | custom-call | flops 7247757312 | bytes 28311552 | tf_op jit(solution)/shard_map/experts/pallas_call | solution.py:141
  142.3 6.9 %collective-permute-done.26 = bf16[96,6144]{1,0:T(8,128)(2,1)S(1)} collective-permute-done((bf16[96,6144]{1,0:T(8,128)(2,1)S(1)}, bf16[96,6144]{1,0:T(8,128)(2,1)S(1)}, u32[]{:S(2)}, u32[]{:S(2)}) %collective-permute-start.26) | collective-permute-done | bytes 1179680 | tf_op jit(solution)/shard_map/ppermute | solution.py:16
  151.8 3.3 %collective-permute-start.29 = (bf16[96,6144]{1,0:T(8,128)(2,1)S(1)}, bf16[96,6144]{1,0:T(8,128)(2,1)S(1)}, u32[]{:S(2)}, u32[]{:S(2)}) collective-permute-start(bf16[96,6144]{1,0:T(8,128)(2,1)S(1)} %get-tuple-element.132), channel_id=1, source_target_pairs={{0,6},{2,0},{4,2},{6,4},{1,7},{3,1},{5,3},{7,5},{8,14},{10,8},{12,... | collective-permute-start | bytes 3538952 | tf_op jit(solution)/shard_map/ppermute | solution.py:16
  155.2 1.9 collective-permute-start.30
  157.4 19.6 %collective-permute-done.28 = bf16[96,6144]{1,0:T(8,128)(2,1)S(1)} collective-permute-done((bf16[96,6144]{1,0:T(8,128)(2,1)S(1)}, bf16[96,6144]{1,0:T(8,128)(2,1)S(1)}, u32[]{:S(2)}, u32[]{:S(2)}) %collective-permute-start.28) | collective-permute-done | bytes 1179680 | tf_op jit(solution)/shard_map/ppermute | solution.py:16
  178.1 3.2 %collective-permute-start.32 = (bf16[96,6144]{1,0:T(8,128)(2,1)S(1)}, bf16[96,6144]{1,0:T(8,128)(2,1)S(1)}, u32[]{:S(2)}, u32[]{:S(2)}) collective-permute-start(bf16[96,6144]{1,0:T(8,128)(2,1)S(1)} %add_convert_fusion.2), channel_id=1, source_target_pairs={{0,6},{2,0},{4,2},{6,4},{1,7},{3,1},{5,3},{7,5},{8,14},{10,8},{12,... | collective-permute-start | bytes 3538952 | tf_op jit(solution)/shard_map/ppermute | solution.py:16
  181.3 1.9 collective-permute-start.33
  183.3 2.0 collective-permute-start.34
  185.2 8.5 %collective-permute-done.35 = f32[4,128]{1,0:T(4,128)S(1)} collective-permute-done((f32[4,128]{1,0:T(4,128)S(1)}, f32[4,128]{1,0:T(4,128)S(1)}, u32[]{:S(2)}, u32[]{:S(2)}) %collective-permute-start.35) | collective-permute-done | bytes 2080 | tf_op jit(solution)/shard_map/ppermute | solution.py:40
  193.7 8.0 %collective-permute-done.31 = bf16[96,6144]{1,0:T(8,128)(2,1)S(1)} collective-permute-done((bf16[96,6144]{1,0:T(8,128)(2,1)S(1)}, bf16[96,6144]{1,0:T(8,128)(2,1)S(1)}, u32[]{:S(2)}, u32[]{:S(2)}) %collective-permute-start.31) | collective-permute-done | bytes 1179680 | tf_op jit(solution)/shard_map/ppermute | solution.py:16
  204.9 2.5 collective-permute-start.36
  208.5 2.8 %collective-permute-start.39 = (bf16[48,6144]{1,0:T(8,128)(2,1)S(1)}, bf16[48,6144]{1,0:T(8,128)(2,1)S(1)}, u32[]{:S(2)}, u32[]{:S(2)}) collective-permute-start(bf16[48,6144]{1,0:T(8,128)(2,1)S(1)} %pad_maximum_fusion.7), channel_id=1, source_target_pairs={{0,8},{8,0},{1,9},{9,1},{2,10},{10,2},{3,11},{11,3},{4,12},{12,4},... | collective-permute-start | bytes 1769480 | tf_op jit(solution)/shard_map/ppermute | solution.py:16
  211.3 6.2 %collective-permute-done.36 = bf16[48,6144]{1,0:T(8,128)(2,1)S(1)} collective-permute-done((bf16[48,6144]{1,0:T(8,128)(2,1)S(1)}, bf16[48,6144]{1,0:T(8,128)(2,1)S(1)}, u32[]{:S(2)}, u32[]{:S(2)}) %collective-permute-start.36) | collective-permute-done | bytes 589856 | tf_op jit(solution)/shard_map/ppermute | solution.py:16
  217.5 4.3 %collective-permute-done.37 = bf16[48,6144]{1,0:T(8,128)(2,1)S(1)} collective-permute-done((bf16[48,6144]{1,0:T(8,128)(2,1)S(1)}, bf16[48,6144]{1,0:T(8,128)(2,1)S(1)}, u32[]{:S(2)}, u32[]{:S(2)}) %collective-permute-start.37) | collective-permute-done | bytes 589856 | tf_op jit(solution)/shard_map/ppermute | solution.py:16
  223.1 3.1 %collective-permute-start.40 = (bf16[24,6144]{1,0:T(8,128)(2,1)S(1)}, bf16[24,6144]{1,0:T(8,128)(2,1)S(1)}, u32[]{:S(2)}, u32[]{:S(2)}) collective-permute-start(bf16[24,6144]{1,0:T(8,128)(2,1)S(1)} %add_convert_fusion.12), channel_id=1, source_target_pairs={{0,6},{2,0},{4,2},{6,4},{1,7},{3,1},{5,3},{7,5},{8,14},{10,8},{12,... | collective-permute-start | bytes 884744 | tf_op jit(solution)/shard_map/ppermute | solution.py:16
  226.3 2.0 collective-permute-start.42
  231.0 2.0 collective-permute-done.42
  233.0 2.0 collective-permute-done.43
  235.9 4.0 %collective-permute-start.44 = (bf16[48,6144]{1,0:T(8,128)(2,1)S(1)}, bf16[48,6144]{1,0:T(8,128)(2,1)S(1)}, u32[]{:S(2)}, u32[]{:S(2)}) collective-permute-start(bf16[48,6144]{1,0:T(8,128)(2,1)S(1)} %pad_maximum_fusion.8), channel_id=1, source_target_pairs={{0,33},{1,32},{32,65},{33,64},{64,97},{65,96},{96,1},{97,0},{2,35}... | collective-permute-start | bytes 1769480 | tf_op jit(solution)/shard_map/ppermute | solution.py:45
  239.9 14.1 %collective-permute-done.45 = bf16[48,6144]{1,0:T(8,128)(2,1)S(1)} collective-permute-done((bf16[48,6144]{1,0:T(8,128)(2,1)S(1)}, bf16[48,6144]{1,0:T(8,128)(2,1)S(1)}, u32[]{:S(2)}, u32[]{:S(2)}) %collective-permute-start.45) | collective-permute-done | bytes 589856 | tf_op jit(solution)/shard_map/ppermute | solution.py:55
  254.7 1.8 fusion.2
  (126 shorter events, 23.3 us)
Async XLA Ops:
  1.7 69.8 %slice-start.2 = ((s8[6291456]{0:T(1024)(128)(4,1)}), s8[4194304]{0:T(1024)(128)(4,1)S(1)}, s32[]{:S(2)}) async-start(s8[6291456]{0:T(1024)(128)(4,1)} %bitcast.44), calls=%async_computation.2 | async-start | bytes 8388608
  2.4 69.1 %slice-start = ((s8[6291456]{0:T(1024)(128)(4,1)}), s8[4194304]{0:T(1024)(128)(4,1)S(1)}, s32[]{:S(2)}) async-start(s8[6291456]{0:T(1024)(128)(4,1)} %bitcast.38), calls=%async_computation | async-start | bytes 8388608
  2.5 9.9 %collective-permute-start.3 = (bf16[24,6144]{1,0:T(8,128)(2,1)S(1)}, bf16[24,6144]{1,0:T(8,128)(2,1)S(1)}, u32[]{:S(2)}, u32[]{:S(2)}) collective-permute-start(bf16[24,6144]{1,0:T(8,128)(2,1)S(1)} %get-tuple-element.178), channel_id=1, source_target_pairs={{0,2},{2,4},{4,6},{6,0},{1,3},{3,5},{5,7},{7,1},{8,10},{10,12},{12... | collective-permute-start | bytes 884744 | tf_op jit(solution)/shard_map/ppermute | solution.py:16
  4.1 8.8 %collective-permute-start = (bf16[24,6144]{1,0:T(8,128)(2,1)S(1)}, bf16[24,6144]{1,0:T(8,128)(2,1)S(1)}, u32[]{:S(2)}, u32[]{:S(2)}) collective-permute-start(bf16[24,6144]{1,0:T(8,128)(2,1)S(1)} %get-tuple-element.177), channel_id=1, source_target_pairs={{0,8},{8,0},{1,9},{9,1},{2,10},{10,2},{3,11},{11,3},{4,12},{12,4},... | collective-permute-start | bytes 884744 | tf_op jit(solution)/shard_map/ppermute | solution.py:16
  5.7 9.2 %collective-permute-start.2 = (bf16[24,6144]{1,0:T(8,128)(2,1)S(1)}, bf16[24,6144]{1,0:T(8,128)(2,1)S(1)}, u32[]{:S(2)}, u32[]{:S(2)}) collective-permute-start(bf16[24,6144]{1,0:T(8,128)(2,1)S(1)} %get-tuple-element.178), channel_id=1, source_target_pairs={{0,6},{2,0},{4,2},{6,4},{1,7},{3,1},{5,3},{7,5},{8,14},{10,8},{12,... | collective-permute-start | bytes 884744 | tf_op jit(solution)/shard_map/ppermute | solution.py:16
  7.4 15.4 %collective-permute-start.1 = (bf16[48,6144]{1,0:T(8,128)(2,1)S(1)}, bf16[48,6144]{1,0:T(8,128)(2,1)S(1)}, u32[]{:S(2)}, u32[]{:S(2)}) collective-permute-start(bf16[48,6144]{1,0:T(8,128)(2,1)S(1)} %convolution_convert_fusion.1), channel_id=1, source_target_pairs={{0,24},{8,16},{16,8},{24,0},{1,25},{9,17},{17,9},{25,1},{2,26},{10... | collective-permute-start | bytes 1769480 | tf_op jit(solution)/shard_map/ppermute | solution.py:36
  12.4 9.0 %collective-permute-start.4 = (bf16[24,6144]{1,0:T(8,128)(2,1)S(1)}, bf16[24,6144]{1,0:T(8,128)(2,1)S(1)}, u32[]{:S(2)}, u32[]{:S(2)}) collective-permute-start(bf16[24,6144]{1,0:T(8,128)(2,1)S(1)} %collective-permute-done.3), channel_id=1, source_target_pairs={{0,2},{2,4},{4,6},{6,0},{1,3},{3,5},{5,7},{7,1},{8,10},{10,12},{12... | collective-permute-start | bytes 884744 | tf_op jit(solution)/shard_map/ppermute | solution.py:16
  12.9 23.8 %collective-permute-start.11 = (bf16[48,6144]{1,0:T(8,128)(2,1)S(1)}, bf16[48,6144]{1,0:T(8,128)(2,1)S(1)}, u32[]{:S(2)}, u32[]{:S(2)}) collective-permute-start(bf16[48,6144]{1,0:T(8,128)(2,1)S(1)} %pad_maximum_fusion.3), channel_id=1, source_target_pairs={{0,1},{1,0},{2,3},{3,2},{4,5},{5,4},{6,7},{7,6},{8,9},{9,8},{10,11... | collective-permute-start | bytes 1769480 | tf_op jit(solution)/shard_map/ppermute | solution.py:16
  22.9 8.3 %collective-permute-start.8 = (bf16[24,6144]{1,0:T(8,128)(2,1)S(1)}, bf16[24,6144]{1,0:T(8,128)(2,1)S(1)}, u32[]{:S(2)}, u32[]{:S(2)}) collective-permute-start(bf16[24,6144]{1,0:T(8,128)(2,1)S(1)} %get-tuple-element.175), channel_id=1, source_target_pairs={{0,2},{2,4},{4,6},{6,0},{1,3},{3,5},{5,7},{7,1},{8,10},{10,12},{12... | collective-permute-start | bytes 884744 | tf_op jit(solution)/shard_map/ppermute | solution.py:16
  23.3 7.9 %collective-permute-start.7 = (bf16[24,6144]{1,0:T(8,128)(2,1)S(1)}, bf16[24,6144]{1,0:T(8,128)(2,1)S(1)}, u32[]{:S(2)}, u32[]{:S(2)}) collective-permute-start(bf16[24,6144]{1,0:T(8,128)(2,1)S(1)} %get-tuple-element.175), channel_id=1, source_target_pairs={{0,6},{2,0},{4,2},{6,4},{1,7},{3,1},{5,3},{7,5},{8,14},{10,8},{12,... | collective-permute-start | bytes 884744 | tf_op jit(solution)/shard_map/ppermute | solution.py:16
  26.2 7.9 %collective-permute-start.5 = (bf16[24,6144]{1,0:T(8,128)(2,1)S(1)}, bf16[24,6144]{1,0:T(8,128)(2,1)S(1)}, u32[]{:S(2)}, u32[]{:S(2)}) collective-permute-start(bf16[24,6144]{1,0:T(8,128)(2,1)S(1)} %get-tuple-element.176), channel_id=1, source_target_pairs={{0,8},{8,0},{1,9},{9,1},{2,10},{10,2},{3,11},{11,3},{4,12},{12,4},... | collective-permute-start | bytes 884744 | tf_op jit(solution)/shard_map/ppermute | solution.py:16
  26.7 41.4 %collective-permute-start.14 = (bf16[96,6144]{1,0:T(8,128)(2,1)S(1)}, bf16[96,6144]{1,0:T(8,128)(2,1)S(1)}, u32[]{:S(2)}, u32[]{:S(2)}) collective-permute-start(bf16[96,6144]{1,0:T(8,128)(2,1)S(1)} %pad_maximum_fusion.1.refs_1_), channel_id=1, source_target_pairs={{0,1},{1,0},{2,3},{3,2},{4,5},{5,4},{6,7},{7,6},{8,9},{9,8},{10,11... | collective-permute-start | bytes 3538952 | tf_op jit(solution)/shard_map/ppermute | solution.py:16
  31.2 7.8 %collective-permute-start.9 = (bf16[24,6144]{1,0:T(8,128)(2,1)S(1)}, bf16[24,6144]{1,0:T(8,128)(2,1)S(1)}, u32[]{:S(2)}, u32[]{:S(2)}) collective-permute-start(bf16[24,6144]{1,0:T(8,128)(2,1)S(1)} %collective-permute-done.7), channel_id=1, source_target_pairs={{0,6},{2,0},{4,2},{6,4},{1,7},{3,1},{5,3},{7,5},{8,14},{10,8},{12,... | collective-permute-start | bytes 884744 | tf_op jit(solution)/shard_map/ppermute | solution.py:16
  34.2 30.8 %collective-permute-start.12 = (bf16[48,6144]{1,0:T(8,128)(2,1)S(1)}, bf16[48,6144]{1,0:T(8,128)(2,1)S(1)}, u32[]{:S(2)}, u32[]{:S(2)}) collective-permute-start(bf16[48,6144]{1,0:T(8,128)(2,1)S(1)} %pad_maximum_fusion.4), channel_id=1, source_target_pairs={{0,1},{1,0},{2,3},{3,2},{4,5},{5,4},{6,7},{7,6},{8,9},{9,8},{10,11... | collective-permute-start | bytes 1769480 | tf_op jit(solution)/shard_map/ppermute | solution.py:16
  36.2 31.9 %collective-permute-start.13 = (bf16[96,6144]{1,0:T(8,128)(2,1)S(1)}, bf16[96,6144]{1,0:T(8,128)(2,1)S(1)}, u32[]{:S(2)}, u32[]{:S(2)}) collective-permute-start(bf16[96,6144]{1,0:T(8,128)(2,1)S(1)} %pad_maximum_fusion.1.refs_1_), channel_id=1, source_target_pairs={{0,8},{8,0},{1,9},{9,1},{2,10},{10,2},{3,11},{11,3},{4,12},{12,4},... | collective-permute-start | bytes 3538952 | tf_op jit(solution)/shard_map/ppermute | solution.py:16
  36.7 33.2 %collective-permute-start.6 = (bf16[96,6144]{1,0:T(8,128)(2,1)S(1)}, bf16[96,6144]{1,0:T(8,128)(2,1)S(1)}, u32[]{:S(2)}, u32[]{:S(2)}) collective-permute-start(bf16[96,6144]{1,0:T(8,128)(2,1)S(1)} %pad_maximum_fusion.refs_0_), channel_id=1, source_target_pairs={{0,2},{2,4},{4,6},{6,0},{1,3},{3,5},{5,7},{7,1},{8,10},{10,12},{12... | collective-permute-start | bytes 3538952 | tf_op jit(solution)/shard_map/ppermute | solution.py:16
  39.0 46.2 %collective-permute-start.10 = (bf16[96,6144]{1,0:T(8,128)(2,1)S(1)}, bf16[96,6144]{1,0:T(8,128)(2,1)S(1)}, u32[]{:S(2)}, u32[]{:S(2)}) collective-permute-start(bf16[96,6144]{1,0:T(8,128)(2,1)S(1)} %pad_maximum_fusion.refs_0_), channel_id=1, source_target_pairs={{0,6},{2,0},{4,2},{6,4},{1,7},{3,1},{5,3},{7,5},{8,14},{10,8},{12,... | collective-permute-start | bytes 3538952 | tf_op jit(solution)/shard_map/ppermute | solution.py:16
  65.0 34.5 %collective-permute-start.17 = (bf16[96,6144]{1,0:T(8,128)(2,1)S(1)}, bf16[96,6144]{1,0:T(8,128)(2,1)S(1)}, u32[]{:S(2)}, u32[]{:S(2)}) collective-permute-start(bf16[96,6144]{1,0:T(8,128)(2,1)S(1)} %constant_dynamic-update-slice_fusion.refs_2_), channel_id=1, source_target_pairs={{0,6},{2,0},{4,2},{6,4},{1,7},{3,1},{5,3},{7,5},{8,14},{10,8},{12,... | collective-permute-start | bytes 3538952 | tf_op jit(solution)/shard_map/ppermute | solution.py:16
  68.1 31.9 %collective-permute-start.16 = (bf16[96,6144]{1,0:T(8,128)(2,1)S(1)}, bf16[96,6144]{1,0:T(8,128)(2,1)S(1)}, u32[]{:S(2)}, u32[]{:S(2)}) collective-permute-start(bf16[96,6144]{1,0:T(8,128)(2,1)S(1)} %constant_dynamic-update-slice_fusion.refs_2_), channel_id=1, source_target_pairs={{0,2},{2,4},{4,6},{6,0},{1,3},{3,5},{5,7},{7,1},{8,10},{10,12},{12... | collective-permute-start | bytes 3538952 | tf_op jit(solution)/shard_map/ppermute | solution.py:16
  68.1 31.9 %collective-permute-start.19 = (bf16[96,6144]{1,0:T(8,128)(2,1)S(1)}, bf16[96,6144]{1,0:T(8,128)(2,1)S(1)}, u32[]{:S(2)}, u32[]{:S(2)}) collective-permute-start(bf16[96,6144]{1,0:T(8,128)(2,1)S(1)} %pad_maximum_fusion.2.refs_2_), channel_id=1, source_target_pairs={{0,1},{1,0},{2,3},{3,2},{4,5},{5,4},{6,7},{7,6},{8,9},{9,8},{10,11... | collective-permute-start | bytes 3538952 | tf_op jit(solution)/shard_map/ppermute | solution.py:16
  69.9 30.1 %collective-permute-start.18 = (bf16[96,6144]{1,0:T(8,128)(2,1)S(1)}, bf16[96,6144]{1,0:T(8,128)(2,1)S(1)}, u32[]{:S(2)}, u32[]{:S(2)}) collective-permute-start(bf16[96,6144]{1,0:T(8,128)(2,1)S(1)} %pad_maximum_fusion.2.refs_2_), channel_id=1, source_target_pairs={{0,8},{8,0},{1,9},{9,1},{2,10},{10,2},{3,11},{11,3},{4,12},{12,4},... | collective-permute-start | bytes 3538952 | tf_op jit(solution)/shard_map/ppermute | solution.py:16
  85.2 31.5 %collective-permute-start.15 = (bf16[96,6144]{1,0:T(8,128)(2,1)S(1)}, bf16[96,6144]{1,0:T(8,128)(2,1)S(1)}, u32[]{:S(2)}, u32[]{:S(2)}) collective-permute-start(bf16[96,6144]{1,0:T(8,128)(2,1)S(1)} %collective-permute-done.10.refs_1_), channel_id=1, source_target_pairs={{0,6},{2,0},{4,2},{6,4},{1,7},{3,1},{5,3},{7,5},{8,14},{10,8},{12,... | collective-permute-start | bytes 3538952 | tf_op jit(solution)/shard_map/ppermute | solution.py:16
  99.6 29.0 %collective-permute-start.21 = (bf16[96,6144]{1,0:T(8,128)(2,1)S(1)}, bf16[96,6144]{1,0:T(8,128)(2,1)S(1)}, u32[]{:S(2)}, u32[]{:S(2)}) collective-permute-start(bf16[96,6144]{1,0:T(8,128)(2,1)S(1)} %collective-permute-done.13.refs_3_), channel_id=1, source_target_pairs={{0,1},{1,0},{2,3},{3,2},{4,5},{5,4},{6,7},{7,6},{8,9},{9,8},{10,11... | collective-permute-start | bytes 3538952 | tf_op jit(solution)/shard_map/ppermute | solution.py:16
  100.0 29.1 %collective-permute-start.20 = (bf16[96,6144]{1,0:T(8,128)(2,1)S(1)}, bf16[96,6144]{1,0:T(8,128)(2,1)S(1)}, u32[]{:S(2)}, u32[]{:S(2)}) collective-permute-start(bf16[96,6144]{1,0:T(8,128)(2,1)S(1)} %collective-permute-done.16.refs_0_), channel_id=1, source_target_pairs={{0,2},{2,4},{4,6},{6,0},{1,3},{3,5},{5,7},{7,1},{8,10},{10,12},{12... | collective-permute-start | bytes 3538952 | tf_op jit(solution)/shard_map/ppermute | solution.py:16
  100.0 29.0 %collective-permute-start.22 = (bf16[96,6144]{1,0:T(8,128)(2,1)S(1)}, bf16[96,6144]{1,0:T(8,128)(2,1)S(1)}, u32[]{:S(2)}, u32[]{:S(2)}) collective-permute-start(bf16[96,6144]{1,0:T(8,128)(2,1)S(1)} %collective-permute-done.19.refs_3_), channel_id=1, source_target_pairs={{0,8},{8,0},{1,9},{9,1},{2,10},{10,2},{3,11},{11,3},{4,12},{12,4},... | collective-permute-start | bytes 3538952 | tf_op jit(solution)/shard_map/ppermute | solution.py:16
  100.6 48.6 %collective-permute-start.26 = (bf16[96,6144]{1,0:T(8,128)(2,1)S(1)}, bf16[96,6144]{1,0:T(8,128)(2,1)S(1)}, u32[]{:S(2)}, u32[]{:S(2)}) collective-permute-start(bf16[96,6144]{1,0:T(8,128)(2,1)S(1)} %get-tuple-element.127), channel_id=1, source_target_pairs={{0,1},{1,0},{2,3},{3,2},{4,5},{5,4},{6,7},{7,6},{8,9},{9,8},{10,11... | collective-permute-start | bytes 3538952 | tf_op jit(solution)/shard_map/ppermute | solution.py:16
  116.8 32.4 %collective-permute-start.23 = (bf16[96,6144]{1,0:T(8,128)(2,1)S(1)}, bf16[96,6144]{1,0:T(8,128)(2,1)S(1)}, u32[]{:S(2)}, u32[]{:S(2)}) collective-permute-start(bf16[96,6144]{1,0:T(8,128)(2,1)S(1)} %get-tuple-element.124), channel_id=1, source_target_pairs={{0,6},{2,0},{4,2},{6,4},{1,7},{3,1},{5,3},{7,5},{8,14},{10,8},{12,... | collective-permute-start | bytes 3538952 | tf_op jit(solution)/shard_map/ppermute | solution.py:16
  128.6 22.1 %collective-permute-start.25 = (bf16[96,6144]{1,0:T(8,128)(2,1)S(1)}, bf16[96,6144]{1,0:T(8,128)(2,1)S(1)}, u32[]{:S(2)}, u32[]{:S(2)}) collective-permute-start(bf16[96,6144]{1,0:T(8,128)(2,1)S(1)} %get-tuple-element.126), channel_id=1, source_target_pairs={{0,8},{8,0},{1,9},{9,1},{2,10},{10,2},{3,11},{11,3},{4,12},{12,4},... | collective-permute-start | bytes 3538952 | tf_op jit(solution)/shard_map/ppermute | solution.py:16
  130.0 21.7 %collective-permute-start.24 = (bf16[96,6144]{1,0:T(8,128)(2,1)S(1)}, bf16[96,6144]{1,0:T(8,128)(2,1)S(1)}, u32[]{:S(2)}, u32[]{:S(2)}) collective-permute-start(bf16[96,6144]{1,0:T(8,128)(2,1)S(1)} %get-tuple-element.125), channel_id=1, source_target_pairs={{0,2},{2,4},{4,6},{6,0},{1,3},{3,5},{5,7},{7,1},{8,10},{10,12},{12... | collective-permute-start | bytes 3538952 | tf_op jit(solution)/shard_map/ppermute | solution.py:16
  151.8 26.3 %collective-permute-start.27 = (bf16[96,6144]{1,0:T(8,128)(2,1)S(1)}, bf16[96,6144]{1,0:T(8,128)(2,1)S(1)}, u32[]{:S(2)}, u32[]{:S(2)}) collective-permute-start(bf16[96,6144]{1,0:T(8,128)(2,1)S(1)} %get-tuple-element.128), channel_id=1, source_target_pairs={{0,8},{8,0},{1,9},{9,1},{2,10},{10,2},{3,11},{11,3},{4,12},{12,4},... | collective-permute-start | bytes 3538952 | tf_op jit(solution)/shard_map/ppermute | solution.py:16
  151.8 25.3 %collective-permute-start.28 = (bf16[96,6144]{1,0:T(8,128)(2,1)S(1)}, bf16[96,6144]{1,0:T(8,128)(2,1)S(1)}, u32[]{:S(2)}, u32[]{:S(2)}) collective-permute-start(bf16[96,6144]{1,0:T(8,128)(2,1)S(1)} %get-tuple-element.130), channel_id=1, source_target_pairs={{0,2},{2,4},{4,6},{6,0},{1,3},{3,5},{5,7},{7,1},{8,10},{10,12},{12... | collective-permute-start | bytes 3538952 | tf_op jit(solution)/shard_map/ppermute | solution.py:16
  151.8 25.5 %collective-permute-start.29 = (bf16[96,6144]{1,0:T(8,128)(2,1)S(1)}, bf16[96,6144]{1,0:T(8,128)(2,1)S(1)}, u32[]{:S(2)}, u32[]{:S(2)}) collective-permute-start(bf16[96,6144]{1,0:T(8,128)(2,1)S(1)} %get-tuple-element.132), channel_id=1, source_target_pairs={{0,6},{2,0},{4,2},{6,4},{1,7},{3,1},{5,3},{7,5},{8,14},{10,8},{12,... | collective-permute-start | bytes 3538952 | tf_op jit(solution)/shard_map/ppermute | solution.py:16
  155.2 22.5 %collective-permute-start.30 = (bf16[96,6144]{1,0:T(8,128)(2,1)S(1)}, bf16[96,6144]{1,0:T(8,128)(2,1)S(1)}, u32[]{:S(2)}, u32[]{:S(2)}) collective-permute-start(bf16[96,6144]{1,0:T(8,128)(2,1)S(1)} %get-tuple-element.136), channel_id=1, source_target_pairs={{0,1},{1,0},{2,3},{3,2},{4,5},{5,4},{6,7},{7,6},{8,9},{9,8},{10,11... | collective-permute-start | bytes 3538952 | tf_op jit(solution)/shard_map/ppermute | solution.py:16
  178.0 23.7 %collective-permute-start.31 = (bf16[96,6144]{1,0:T(8,128)(2,1)S(1)}, bf16[96,6144]{1,0:T(8,128)(2,1)S(1)}, u32[]{:S(2)}, u32[]{:S(2)}) collective-permute-start(bf16[96,6144]{1,0:T(8,128)(2,1)S(1)} %add_convert_fusion.3), channel_id=1, source_target_pairs={{0,2},{2,4},{4,6},{6,0},{1,3},{3,5},{5,7},{7,1},{8,10},{10,12},{12... | collective-permute-start | bytes 3538952 | tf_op jit(solution)/shard_map/ppermute | solution.py:16
  178.1 23.7 %collective-permute-start.32 = (bf16[96,6144]{1,0:T(8,128)(2,1)S(1)}, bf16[96,6144]{1,0:T(8,128)(2,1)S(1)}, u32[]{:S(2)}, u32[]{:S(2)}) collective-permute-start(bf16[96,6144]{1,0:T(8,128)(2,1)S(1)} %add_convert_fusion.2), channel_id=1, source_target_pairs={{0,6},{2,0},{4,2},{6,4},{1,7},{3,1},{5,3},{7,5},{8,14},{10,8},{12,... | collective-permute-start | bytes 3538952 | tf_op jit(solution)/shard_map/ppermute | solution.py:16
  181.3 21.5 %collective-permute-start.33 = (bf16[96,6144]{1,0:T(8,128)(2,1)S(1)}, bf16[96,6144]{1,0:T(8,128)(2,1)S(1)}, u32[]{:S(2)}, u32[]{:S(2)}) collective-permute-start(bf16[96,6144]{1,0:T(8,128)(2,1)S(1)} %add_convert_fusion.1), channel_id=1, source_target_pairs={{0,1},{1,0},{2,3},{3,2},{4,5},{5,4},{6,7},{7,6},{8,9},{9,8},{10,11... | collective-permute-start | bytes 3538952 | tf_op jit(solution)/shard_map/ppermute | solution.py:16
  183.3 19.8 %collective-permute-start.34 = (bf16[96,6144]{1,0:T(8,128)(2,1)S(1)}, bf16[96,6144]{1,0:T(8,128)(2,1)S(1)}, u32[]{:S(2)}, u32[]{:S(2)}) collective-permute-start(bf16[96,6144]{1,0:T(8,128)(2,1)S(1)} %add_convert_fusion), channel_id=1, source_target_pairs={{0,8},{8,0},{1,9},{9,1},{2,10},{10,2},{3,11},{11,3},{4,12},{12,4},... | collective-permute-start | bytes 3538952 | tf_op jit(solution)/shard_map/ppermute | solution.py:16
  185.2 8.5 %collective-permute-start.35 = (f32[4,128]{1,0:T(4,128)S(1)}, f32[4,128]{1,0:T(4,128)S(1)}, u32[]{:S(2)}, u32[]{:S(2)}) collective-permute-start(f32[4,128]{1,0:T(4,128)S(1)} %pad_maximum_fusion.10), channel_id=1, source_target_pairs={{0,32},{32,64},{64,96},{96,0},{1,33},{33,65},{65,97},{97,1},{2,34}... | collective-permute-start | bytes 6152 | tf_op jit(solution)/shard_map/ppermute | solution.py:40
  204.9 12.6 %collective-permute-start.36 = (bf16[48,6144]{1,0:T(8,128)(2,1)S(1)}, bf16[48,6144]{1,0:T(8,128)(2,1)S(1)}, u32[]{:S(2)}, u32[]{:S(2)}) collective-permute-start(bf16[48,6144]{1,0:T(8,128)(2,1)S(1)} %pad_maximum_fusion.5), channel_id=1, source_target_pairs={{0,6},{2,0},{4,2},{6,4},{1,7},{3,1},{5,3},{7,5},{8,14},{10,8},{12,... | collective-permute-start | bytes 1769480 | tf_op jit(solution)/shard_map/ppermute | solution.py:16
  207.5 14.3 %collective-permute-start.37 = (bf16[48,6144]{1,0:T(8,128)(2,1)S(1)}, bf16[48,6144]{1,0:T(8,128)(2,1)S(1)}, u32[]{:S(2)}, u32[]{:S(2)}) collective-permute-start(bf16[48,6144]{1,0:T(8,128)(2,1)S(1)} %pad_maximum_fusion.6), channel_id=1, source_target_pairs={{0,2},{2,4},{4,6},{6,0},{1,3},{3,5},{5,7},{7,1},{8,10},{10,12},{12... | collective-permute-start | bytes 1769480 | tf_op jit(solution)/shard_map/ppermute | solution.py:16
  207.6 14.2 %collective-permute-start.38 = (bf16[48,6144]{1,0:T(8,128)(2,1)S(1)}, bf16[48,6144]{1,0:T(8,128)(2,1)S(1)}, u32[]{:S(2)}, u32[]{:S(2)}) collective-permute-start(bf16[48,6144]{1,0:T(8,128)(2,1)S(1)} %add_convert_fusion.4), channel_id=1, source_target_pairs={{0,1},{1,0},{2,3},{3,2},{4,5},{5,4},{6,7},{7,6},{8,9},{9,8},{10,11... | collective-permute-start | bytes 1769480 | tf_op jit(solution)/shard_map/ppermute | solution.py:16
  208.5 13.9 %collective-permute-start.39 = (bf16[48,6144]{1,0:T(8,128)(2,1)S(1)}, bf16[48,6144]{1,0:T(8,128)(2,1)S(1)}, u32[]{:S(2)}, u32[]{:S(2)}) collective-permute-start(bf16[48,6144]{1,0:T(8,128)(2,1)S(1)} %pad_maximum_fusion.7), channel_id=1, source_target_pairs={{0,8},{8,0},{1,9},{9,1},{2,10},{10,2},{3,11},{11,3},{4,12},{12,4},... | collective-permute-start | bytes 1769480 | tf_op jit(solution)/shard_map/ppermute | solution.py:16
  222.9 8.0 %collective-permute-start.41 = (bf16[24,6144]{1,0:T(8,128)(2,1)S(1)}, bf16[24,6144]{1,0:T(8,128)(2,1)S(1)}, u32[]{:S(2)}, u32[]{:S(2)}) collective-permute-start(bf16[24,6144]{1,0:T(8,128)(2,1)S(1)} %add_convert_fusion.11), channel_id=1, source_target_pairs={{0,2},{2,4},{4,6},{6,0},{1,3},{3,5},{5,7},{7,1},{8,10},{10,12},{12... | collective-permute-start | bytes 884744 | tf_op jit(solution)/shard_map/ppermute | solution.py:16
  223.1 7.8 %collective-permute-start.40 = (bf16[24,6144]{1,0:T(8,128)(2,1)S(1)}, bf16[24,6144]{1,0:T(8,128)(2,1)S(1)}, u32[]{:S(2)}, u32[]{:S(2)}) collective-permute-start(bf16[24,6144]{1,0:T(8,128)(2,1)S(1)} %add_convert_fusion.12), channel_id=1, source_target_pairs={{0,6},{2,0},{4,2},{6,4},{1,7},{3,1},{5,3},{7,5},{8,14},{10,8},{12,... | collective-permute-start | bytes 884744 | tf_op jit(solution)/shard_map/ppermute | solution.py:16
  226.3 6.7 %collective-permute-start.42 = (bf16[24,6144]{1,0:T(8,128)(2,1)S(1)}, bf16[24,6144]{1,0:T(8,128)(2,1)S(1)}, u32[]{:S(2)}, u32[]{:S(2)}) collective-permute-start(bf16[24,6144]{1,0:T(8,128)(2,1)S(1)} %add_convert_fusion.10), channel_id=1, source_target_pairs={{0,8},{8,0},{1,9},{9,1},{2,10},{10,2},{3,11},{11,3},{4,12},{12,4},... | collective-permute-start | bytes 884744 | tf_op jit(solution)/shard_map/ppermute | solution.py:16
  228.3 6.7 %collective-permute-start.43 = (bf16[24,6144]{1,0:T(8,128)(2,1)S(1)}, bf16[24,6144]{1,0:T(8,128)(2,1)S(1)}, u32[]{:S(2)}, u32[]{:S(2)}) collective-permute-start(bf16[24,6144]{1,0:T(8,128)(2,1)S(1)} %add_convert_fusion.9), channel_id=1, source_target_pairs={{0,1},{1,0},{2,3},{3,2},{4,5},{5,4},{6,7},{7,6},{8,9},{9,8},{10,11... | collective-permute-start | bytes 884744 | tf_op jit(solution)/shard_map/ppermute | solution.py:16
  235.8 18.2 %collective-permute-start.45 = (bf16[48,6144]{1,0:T(8,128)(2,1)S(1)}, bf16[48,6144]{1,0:T(8,128)(2,1)S(1)}, u32[]{:S(2)}, u32[]{:S(2)}) collective-permute-start(bf16[48,6144]{1,0:T(8,128)(2,1)S(1)} %pad_maximum_fusion.9), channel_id=1, source_target_pairs={{0,57},{1,56},{8,49},{9,48},{16,41},{17,40},{24,33},{25,32},{32,89... | collective-permute-start | bytes 1769480 | tf_op jit(solution)/shard_map/ppermute | solution.py:55
  235.9 18.7 %collective-permute-start.44 = (bf16[48,6144]{1,0:T(8,128)(2,1)S(1)}, bf16[48,6144]{1,0:T(8,128)(2,1)S(1)}, u32[]{:S(2)}, u32[]{:S(2)}) collective-permute-start(bf16[48,6144]{1,0:T(8,128)(2,1)S(1)} %pad_maximum_fusion.8), channel_id=1, source_target_pairs={{0,33},{1,32},{32,65},{33,64},{64,97},{65,96},{96,1},{97,0},{2,35}... | collective-permute-start | bytes 1769480 | tf_op jit(solution)/shard_map/ppermute | solution.py:45
  (12 other events, 160.5 us)

commit v8 on v6

--- a/solution.py
+++ b/solution.py
@@ -150,7 +150,7 @@
             pltpu.VMEM((total, units), BF16),
         ],
         compiler_params=pltpu.CompilerParams(
-            dimension_semantics=("arbitrary",), vmem_limit_bytes=18 << 20
+            dimension_semantics=("arbitrary",), vmem_limit_bytes=20 << 20
         ),
         cost_estimate=pl.CostEstimate(
             flops=6 * total * width * units,
@@ -188,39 +188,39 @@
     a1, b = split(own, 2)
     a1_y, b_behind, b_ahead = over_y(a1), right(b), left(b)
     a1_near = join(a1, a1_y)
-    b_opposite = right(b_behind)
+    a1_far, b_opposite = over_z(a1_near), right(b_behind)
+    partner, b_ahead, b_opposite = together(partner, b_ahead, b_opposite)
     b_ring = join(b, b_behind, b_ahead, b_opposite)
     b_y = over_y(b_ring)
 
     a2, g = split(partner, 2)
     a2_z, g_behind, g_ahead = over_z(a2), left(g), right(g)
-    g_behind, g_ahead, b_ring_late, a1_near_late = together(g_behind, g_ahead, b_ring, a1_near)
+    g_behind, g_ahead, b_ring_late = together(g_behind, g_ahead, b_ring)
     g_opposite = left(g_behind)
-    a1_far = over_z(a1_near_late)
     a2_near = join(a2, a2_z)
     near = join(a1_near, a2_near)
-    a1_far, b_ring_late = together(a1_far, b_ring_late)
     a2_far, b_z = over_y(a2_near), over_z(b_ring_late)
     near_late, g_opposite = together(near, g_opposite)
     near_left, near_right = right(near), left(near_late)
     g_ring = join(g, g_behind, g_ahead, g_opposite)
 
-    b_y, g_ring_out = together(b_y, g_ring)
-    g_y, g_z = over_y(g_ring_out), over_z(g_ring_out)
+    g_ring_sent = g_ring
+    near, b_ring, g_ring = experts([near, b_ring, g_ring], *matrices)
+    b_y, near, g_ring_y = together(b_y, near, g_ring_sent)
+    b_z, g_ring_z = together(b_z, g_ring_sent)
+    g_y, g_z = over_y(g_ring_y), over_z(g_ring_z)
+    a2_far, near_left, b_z = together(a2_far, near_left, b_z)
     far = join(a1_far, a2_far)
-    near, b_ring, g_ring, b_y = experts([near, b_ring, g_ring, b_y], *matrices)
     far_left, far_right = right(far), left(far)
 
-    near_left, near_right, far, b_z, near, b_ring, g_ring, b_y = together(
-        near_left, near_right, far, b_z, near, b_ring, g_ring, b_y
-    )
-    near_opposite, b_yz = left(near_right), over_y(b_z)
-    near_left, near_right, far, b_z = experts([near_left, near_right, far, b_z], *matrices)
-
-    far_left, far_right, g_y, g_z, near_left, near_right, far, b_z = together(
-        far_left, far_right, g_y, g_z, near_left, near_right, far, b_z
-    )
-    far_opposite, g_zy = right(far_left), over_z(g_y)
+    near_right_sent, b_y_sent = near_right, b_y
+    near_left, near_right, far, b_y, b_z = experts(
+        [near_left, near_right, far, b_y, b_z], *matrices
+    )
+    near_right_sent, b_y_sent, far = together(near_right_sent, b_y_sent, far)
+    near_opposite, b_yz = left(near_right_sent), over_z(b_y_sent)
+    far_opposite, g_zy = right(far_left), over_y(g_z)
+    far_left, far_right, g_y, g_z, far = together(far_left, far_right, g_y, g_z, far)
     far_left, far_right, g_y, g_z = experts([far_left, far_right, g_y, g_z], *matrices)
 
     near_opposite, far_opposite, b_yz, g_zy, far_left, far_right, g_y, g_z = together(

time: 253 us -> 254 us (level)
  waiting for transfers between devices: 128 us -> 122 us
    ppermute x42, waiting for transfers between devices: 93.5 us -> 104 us  [shift(): return lax.ppermute(value, axis, [(i, (i + by) % n) for i in range(n)])]
    ppermute x1, waiting for transfers between devices: 9.96 us -> 1.52 us  [to_partner(): return lax.ppermute(value, ('yh', 'yl'), [(y, 3 - y) for y in range(4)])]
    ppermute x1, waiting for transfers between devices: 10.8 us -> 4.51 us  [to_next_section(): lax.ppermute(value, ('zh', 'core'), [(s, (s + 1) % 4) for s in range(4)])]
    unnamed x21 -> x29, local copies, waits for them, and re-layouts: 5.14 us -> 7.42 us
  transfers between devices with their start and end apart: 46 -> 46, of which waited for: 25 -> 24; matrix products, arithmetic and copies ran while one was open for 2% -> 1% of each run, Pallas kernels for 17% -> 18%
where the time goes in v8:
time: 254 us; the launch traced here: 252 us
  waiting for transfers between devices  122 us (48%)
  starting transfers between devices  64.6 us (25%)
  Pallas kernels  45.6 us (18%)
  other arithmetic  8.26 us (3%)
  local copies, waits for them, and re-layouts  7.77 us (3%)
  matrix products  3.07 us (1%)
    ppermute x42, waiting for transfers between devices, shift(): return lax.ppermute(value, axis, [(i, (i + by) % n) for i in range(n)])  104 us
    ppermute x42, starting transfers between devices, shift(): return lax.ppermute(value, axis, [(i, (i + by) % n) for i in range(n)])  56.8 us
    pallas_call x4, Pallas kernels, experts(): pl.pallas_call(experts_kernel, grid=(2 * half,), in_specs=rows_in + [into...  45.6 us
    ppermute x1, waiting for transfers between devices, to_owner_across(): return lax.ppermute(value, ('zh', 'core', 'yh', 'yl', 'zl'), pairs)  12.5 us
    unnamed x29, local copies, waits for them, and re-layouts  7.42 us
    convert_element_type x16, other arithmetic, add(): return total.astype(BF16)  6.35 us
    ppermute x1, starting transfers between devices, to_owner(): return lax.ppermute(value, ('zh', 'core', 'zl'), pairs)  5.49 us
  transfers between devices with their start and end apart: 46, of which 24 were waited for; matrix products, arithmetic and copies ran while one was open for 1% of the time, Pallas kernels for 18%

profile of v8, /device:TPU:0, one launch (start us, length us, event | category | flops | bytes accessed | tf_op | source)
XLA Modules:
  0.0 252.2 jit_solution(12254966368645524411)
XLA Ops:
  2.4 1.6 collective-permute-start.3
  4.1 1.6 collective-permute-start
  5.7 1.7 collective-permute-start.2
  7.4 2.2 collective-permute-start.1
  9.6 2.8 %collective-permute-done.3 = bf16[24,6144]{1,0:T(8,128)(2,1)S(1)} collective-permute-done((bf16[24,6144]{1,0:T(8,128)(2,1)S(1)}, bf16[24,6144]{1,0:T(8,128)(2,1)S(1)}, u32[]{:S(2)}, u32[]{:S(2)}) %collective-permute-start.3) | collective-permute-done | bytes 294944 | tf_op jit(solution)/shard_map/ppermute | solution.py:16
  12.9 2.0 collective-permute-start.14
  14.9 6.4 %collective-permute-done.4 = bf16[24,6144]{1,0:T(8,128)(2,1)S(1)} collective-permute-done((bf16[24,6144]{1,0:T(8,128)(2,1)S(1)}, bf16[24,6144]{1,0:T(8,128)(2,1)S(1)}, u32[]{:S(2)}, u32[]{:S(2)}) %collective-permute-start.4) | collective-permute-done | bytes 294944 | tf_op jit(solution)/shard_map/ppermute | solution.py:16
  23.2 3.0 %collective-permute-start.6 = (bf16[24,6144]{1,0:T(8,128)(2,1)S(1)}, bf16[24,6144]{1,0:T(8,128)(2,1)S(1)}, u32[]{:S(2)}, u32[]{:S(2)}) collective-permute-start(bf16[24,6144]{1,0:T(8,128)(2,1)S(1)} %get-tuple-element.169), channel_id=1, source_target_pairs={{0,6},{2,0},{4,2},{6,4},{1,7},{3,1},{5,3},{7,5},{8,14},{10,8},{12,... | collective-permute-start | bytes 884744 | tf_op jit(solution)/shard_map/ppermute | solution.py:16
  26.2 1.9 collective-permute-start.5
  28.7 2.5 collective-permute-done.7
  31.2 3.0 %collective-permute-start.8 = (bf16[24,6144]{1,0:T(8,128)(2,1)S(1)}, bf16[24,6144]{1,0:T(8,128)(2,1)S(1)}, u32[]{:S(2)}, u32[]{:S(2)}) collective-permute-start(bf16[24,6144]{1,0:T(8,128)(2,1)S(1)} %collective-permute-done.6), channel_id=1, source_target_pairs={{0,6},{2,0},{4,2},{6,4},{1,7},{3,1},{5,3},{7,5},{8,14},{10,8},{12,... | collective-permute-start | bytes 884744 | tf_op jit(solution)/shard_map/ppermute | solution.py:16
  35.1 1.7 collective-permute-start.13
  38.7 3.7 %collective-permute-start.9 = (bf16[96,6144]{1,0:T(8,128)(2,1)S(1)}, bf16[96,6144]{1,0:T(8,128)(2,1)S(1)}, u32[]{:S(2)}, u32[]{:S(2)}) collective-permute-start(bf16[96,6144]{1,0:T(8,128)(2,1)S(1)} %pad_maximum_fusion.refs_0_), channel_id=1, source_target_pairs={{0,6},{2,0},{4,2},{6,4},{1,7},{3,1},{5,3},{7,5},{8,14},{10,8},{12,... | collective-permute-start | bytes 3538952 | tf_op jit(solution)/shard_map/ppermute | solution.py:16
  42.5 2.8 %copy-done.3 = bf16[1,512,6144]{2,1,0:T(8,128)(2,1)S(1)} copy-done((bf16[1,512,6144]{2,1,0:T(8,128)(2,1)S(1)}, bf16[1,512,6144]{2,1,0:T(8,128)(2,1)}, u32[]{:S(2)}) %copy-start.3) | copy-done | bytes 6291480
  45.3 8.7 %experts.4 = (bf16[96,6144]{1,0:T(8,128)(2,1)S(1)}, bf16[96,6144]{1,0:T(8,128)(2,1)S(1)}, bf16[96,6144]{1,0:T(8,128)(2,1)S(1)}) custom-call(bf16[96,6144]{1,0:T(8,128)(2,1)S(1)} %pad_maximum_fusion.refs_0_, bf16[96,6144]{1,0:T(8,128)(2,1)S(1)} %pad_maximum_fusion.1.refs_1_, bf16[96,6144]{1,0:T(8,128)(2,1)S(1)} %pad_maximum_fusion.2.refs_2_, ...), custom_call_target="tpu_custom_call" | custom-call | flops 5435817984 | bytes 25952256 | tf_op jit(solution)/shard_map/experts/pallas_call | solution.py:141
  54.0 3.2 %collective-permute-done.10.refs_3_ = bf16[96,6144]{1,0:T(8,128)(2,1)S(1)} collective-permute-done((bf16[96,6144]{1,0:T(8,128)(2,1)S(1)}, bf16[96,6144]{1,0:T(8,128)(2,1)S(1)}, u32[]{:S(2)}, u32[]{:S(2)}) %collective-permute-start.10) | collective-permute-done | bytes 1179680 | tf_op jit(solution)/shard_map/ppermute | solution.py:16
  57.6 3.6 %collective-permute-done.13.refs_4_ = bf16[96,6144]{1,0:T(8,128)(2,1)S(1)} collective-permute-done((bf16[96,6144]{1,0:T(8,128)(2,1)S(1)}, bf16[96,6144]{1,0:T(8,128)(2,1)S(1)}, u32[]{:S(2)}, u32[]{:S(2)}) %collective-permute-start.13) | collective-permute-done | bytes 1179680 | tf_op jit(solution)/shard_map/ppermute | solution.py:16
  61.2 1.7 collective-permute-start.19
  63.0 6.9 %collective-permute-done.11 = bf16[48,6144]{1,0:T(8,128)(2,1)S(1)} collective-permute-done((bf16[48,6144]{1,0:T(8,128)(2,1)S(1)}, bf16[48,6144]{1,0:T(8,128)(2,1)S(1)}, u32[]{:S(2)}, u32[]{:S(2)}) %collective-permute-start.11) | collective-permute-done | bytes 589856 | tf_op jit(solution)/shard_map/ppermute | solution.py:16
  70.0 3.2 %collective-permute-start.21 = (bf16[96,6144]{1,0:T(8,128)(2,1)S(1)}, bf16[96,6144]{1,0:T(8,128)(2,1)S(1)}, u32[]{:S(2)}, u32[]{:S(2)}) collective-permute-start(bf16[96,6144]{1,0:T(8,128)(2,1)S(1)} %constant_dynamic-update-slice_fusion.refs_2_), channel_id=1, source_target_pairs={{0,6},{2,0},{4,2},{6,4},{1,7},{3,1},{5,3},{7,5},{8,14},{10,8},{12,... | collective-permute-start | bytes 3538952 | tf_op jit(solution)/shard_map/ppermute | solution.py:16
  73.2 13.2 %experts.5 = (bf16[96,6144]{1,0:T(8,128)(2,1)S(1)}, bf16[96,6144]{1,0:T(8,128)(2,1)S(1)}, bf16[96,6144]{1,0:T(8,128)(2,1)S(1)}, bf16[96,6144]{1,0:T(8,128)(2,1)S(1)}, bf16[96,6144]{1,0:T(8,128)(2,1)S(1)}) custom-call(bf16[96,6144]{1,0:T(8,128)(2,1)S(1)} %collective-permute-done.12.refs_0_, bf16[96,6144]{1,0:T(8,128)(2,1)S(1)} %collective-permute-done.9.refs_1_, ...), custom_call_target="tpu_custom_call" | custom-call | flops 9059696640 | bytes 30670848 | tf_op jit(solution)/shard_map/experts/pallas_call | solution.py:141
  86.7 4.7 %collective-permute-done.22.refs_2_ = bf16[96,6144]{1,0:T(8,128)(2,1)S(1)} collective-permute-done((bf16[96,6144]{1,0:T(8,128)(2,1)S(1)}, bf16[96,6144]{1,0:T(8,128)(2,1)S(1)}, u32[]{:S(2)}, u32[]{:S(2)}) %collective-permute-start.22) | collective-permute-done | bytes 1179680 | tf_op jit(solution)/shard_map/ppermute | solution.py:16
  93.0 6.6 %collective-permute-done.21.refs_1_ = bf16[96,6144]{1,0:T(8,128)(2,1)S(1)} collective-permute-done((bf16[96,6144]{1,0:T(8,128)(2,1)S(1)}, bf16[96,6144]{1,0:T(8,128)(2,1)S(1)}, u32[]{:S(2)}, u32[]{:S(2)}) %collective-permute-start.21) | collective-permute-done | bytes 1179680 | tf_op jit(solution)/shard_map/ppermute | solution.py:16
  103.3 12.2 %experts.6 = (bf16[96,6144]{1,0:T(8,128)(2,1)S(1)}, bf16[96,6144]{1,0:T(8,128)(2,1)}, bf16[96,6144]{1,0:T(8,128)(2,1)S(1)}, bf16[96,6144]{1,0:T(8,128)(2,1)S(1)}) custom-call(bf16[96,6144]{1,0:T(8,128)(2,1)} %collective-permute-done.16.refs_0_, bf16[96,6144]{1,0:T(8,128)(2,1)S(1)} %copy-done.8, bf16[96,6144]{1,0:T(8,128)(2,1)S(1)} %copy-done.6, ...), custom_call_target="tpu_custom_call" | custom-call | flops 7247757312 | bytes 28311552 | tf_op jit(solution)/shard_map/experts/pallas_call | solution.py:141
  115.4 5.9 %collective-permute-done.15.refs_0_ = bf16[96,6144]{1,0:T(8,128)(2,1)S(1)} collective-permute-done((bf16[96,6144]{1,0:T(8,128)(2,1)S(1)}, bf16[96,6144]{1,0:T(8,128)(2,1)S(1)}, u32[]{:S(2)}, u32[]{:S(2)}) %collective-permute-start.15) | collective-permute-done | bytes 1179680 | tf_op jit(solution)/shard_map/ppermute | solution.py:16
  121.3 3.3 %collective-permute-start.23 = (bf16[96,6144]{1,0:T(8,128)(2,1)S(1)}, bf16[96,6144]{1,0:T(8,128)(2,1)S(1)}, u32[]{:S(2)}, u32[]{:S(2)}) collective-permute-start(bf16[96,6144]{1,0:T(8,128)(2,1)S(1)} %get-tuple-element.120), channel_id=1, source_target_pairs={{0,6},{2,0},{4,2},{6,4},{1,7},{3,1},{5,3},{7,5},{8,14},{10,8},{12,... | collective-permute-start | bytes 3538952 | tf_op jit(solution)/shard_map/ppermute | solution.py:16
  125.0 11.6 %experts.7 = (bf16[96,6144]{1,0:T(8,128)(2,1)S(1)}, bf16[96,6144]{1,0:T(8,128)(2,1)S(1)}, bf16[96,6144]{1,0:T(8,128)(2,1)S(1)}, bf16[96,6144]{1,0:T(8,128)(2,1)S(1)}) custom-call(bf16[96,6144]{1,0:T(8,128)(2,1)S(1)} %collective-permute-done.15.refs_0_, bf16[96,6144]{1,0:T(8,128)(2,1)} %collective-permute-done.17.refs_1_, ...), custom_call_target="tpu_custom_call" | custom-call | flops 7247757312 | bytes 28311552 | tf_op jit(solution)/shard_map/experts/pallas_call | solution.py:141
  136.7 5.3 %collective-permute-done.26 = bf16[96,6144]{1,0:T(8,128)(2,1)} collective-permute-done((bf16[96,6144]{1,0:T(8,128)(2,1)S(1)}, bf16[96,6144]{1,0:T(8,128)(2,1)}, u32[]{:S(2)}, u32[]{:S(2)}) %collective-permute-start.26) | collective-permute-done | bytes 1179680 | tf_op jit(solution)/shard_map/ppermute | solution.py:16
  142.0 1.9 collective-permute-done.25
  143.9 1.7 collective-permute-done.24
  145.6 1.7 collective-permute-start.27
  147.3 3.2 %collective-permute-start.29 = (bf16[96,6144]{1,0:T(8,128)(2,1)S(1)}, bf16[96,6144]{1,0:T(8,128)(2,1)S(1)}, u32[]{:S(2)}, u32[]{:S(2)}) collective-permute-start(bf16[96,6144]{1,0:T(8,128)(2,1)S(1)} %get-tuple-element.128), channel_id=1, source_target_pairs={{0,6},{2,0},{4,2},{6,4},{1,7},{3,1},{5,3},{7,5},{8,14},{10,8},{12,... | collective-permute-start | bytes 3538952 | tf_op jit(solution)/shard_map/ppermute | solution.py:16
  150.5 2.5 collective-permute-start.30
  153.3 19.1 %collective-permute-done.28 = bf16[96,6144]{1,0:T(8,128)(2,1)S(1)} collective-permute-done((bf16[96,6144]{1,0:T(8,128)(2,1)S(1)}, bf16[96,6144]{1,0:T(8,128)(2,1)S(1)}, u32[]{:S(2)}, u32[]{:S(2)}) %collective-permute-start.28) | collective-permute-done | bytes 1179680 | tf_op jit(solution)/shard_map/ppermute | solution.py:16
  173.4 3.2 %collective-permute-start.32 = (bf16[96,6144]{1,0:T(8,128)(2,1)S(1)}, bf16[96,6144]{1,0:T(8,128)(2,1)S(1)}, u32[]{:S(2)}, u32[]{:S(2)}) collective-permute-start(bf16[96,6144]{1,0:T(8,128)(2,1)S(1)} %add_convert_fusion.2), channel_id=1, source_target_pairs={{0,6},{2,0},{4,2},{6,4},{1,7},{3,1},{5,3},{7,5},{8,14},{10,8},{12,... | collective-permute-start | bytes 3538952 | tf_op jit(solution)/shard_map/ppermute | solution.py:16
  176.6 2.5 collective-permute-start.33
  179.5 4.5 %collective-permute-done.35 = f32[4,128]{1,0:T(4,128)S(1)} collective-permute-done((f32[4,128]{1,0:T(4,128)S(1)}, f32[4,128]{1,0:T(4,128)S(1)}, u32[]{:S(2)}, u32[]{:S(2)}) %collective-permute-start.35) | collective-permute-done | bytes 2080 | tf_op jit(solution)/shard_map/ppermute | solution.py:40
  184.0 13.6 %collective-permute-done.31 = bf16[96,6144]{1,0:T(8,128)(2,1)S(1)} collective-permute-done((bf16[96,6144]{1,0:T(8,128)(2,1)S(1)}, bf16[96,6144]{1,0:T(8,128)(2,1)S(1)}, u32[]{:S(2)}, u32[]{:S(2)}) %collective-permute-start.31) | collective-permute-done | bytes 1179680 | tf_op jit(solution)/shard_map/ppermute | solution.py:16
  199.1 3.1 %collective-permute-start.36 = (bf16[48,6144]{1,0:T(8,128)(2,1)S(1)}, bf16[48,6144]{1,0:T(8,128)(2,1)S(1)}, u32[]{:S(2)}, u32[]{:S(2)}) collective-permute-start(bf16[48,6144]{1,0:T(8,128)(2,1)S(1)} %pad_maximum_fusion.5), channel_id=1, source_target_pairs={{0,6},{2,0},{4,2},{6,4},{1,7},{3,1},{5,3},{7,5},{8,14},{10,8},{12,... | collective-permute-start | bytes 1769480 | tf_op jit(solution)/shard_map/ppermute | solution.py:16
  205.0 7.8 %collective-permute-done.36 = bf16[48,6144]{1,0:T(8,128)(2,1)S(1)} collective-permute-done((bf16[48,6144]{1,0:T(8,128)(2,1)S(1)}, bf16[48,6144]{1,0:T(8,128)(2,1)S(1)}, u32[]{:S(2)}, u32[]{:S(2)}) %collective-permute-start.36) | collective-permute-done | bytes 589856 | tf_op jit(solution)/shard_map/ppermute | solution.py:16
  212.8 3.7 %collective-permute-done.37 = bf16[48,6144]{1,0:T(8,128)(2,1)S(1)} collective-permute-done((bf16[48,6144]{1,0:T(8,128)(2,1)S(1)}, bf16[48,6144]{1,0:T(8,128)(2,1)S(1)}, u32[]{:S(2)}, u32[]{:S(2)}) %collective-permute-start.37) | collective-permute-done | bytes 589856 | tf_op jit(solution)/shard_map/ppermute | solution.py:16
  220.0 3.1 %collective-permute-start.40 = (bf16[24,6144]{1,0:T(8,128)(2,1)S(1)}, bf16[24,6144]{1,0:T(8,128)(2,1)S(1)}, u32[]{:S(2)}, u32[]{:S(2)}) collective-permute-start(bf16[24,6144]{1,0:T(8,128)(2,1)S(1)} %add_convert_fusion.13), channel_id=1, source_target_pairs={{0,6},{2,0},{4,2},{6,4},{1,7},{3,1},{5,3},{7,5},{8,14},{10,8},{12,... | collective-permute-start | bytes 884744 | tf_op jit(solution)/shard_map/ppermute | solution.py:16
  223.2 2.9 %collective-permute-done.43 = bf16[24,6144]{1,0:T(8,128)(2,1)S(1)} collective-permute-done((bf16[24,6144]{1,0:T(8,128)(2,1)S(1)}, bf16[24,6144]{1,0:T(8,128)(2,1)S(1)}, u32[]{:S(2)}, u32[]{:S(2)}) %collective-permute-start.43) | collective-permute-done | bytes 294944 | tf_op jit(solution)/shard_map/ppermute | solution.py:16
  226.1 1.8 collective-permute-done.41
  227.8 2.0 collective-permute-done.42
  231.8 5.5 %collective-permute-start.44 = (bf16[48,6144]{1,0:T(8,128)(2,1)S(1)}, bf16[48,6144]{1,0:T(8,128)(2,1)S(1)}, u32[]{:S(2)}, u32[]{:S(2)}) collective-permute-start(bf16[48,6144]{1,0:T(8,128)(2,1)S(1)} %pad_maximum_fusion.7), channel_id=1, source_target_pairs={{0,33},{1,32},{32,65},{33,64},{64,97},{65,96},{96,1},{97,0},{2,35}... | collective-permute-start | bytes 1769480 | tf_op jit(solution)/shard_map/ppermute | solution.py:45
  237.3 12.5 %collective-permute-done.45 = bf16[48,6144]{1,0:T(8,128)(2,1)S(1)} collective-permute-done((bf16[48,6144]{1,0:T(8,128)(2,1)S(1)}, bf16[48,6144]{1,0:T(8,128)(2,1)S(1)}, u32[]{:S(2)}, u32[]{:S(2)}) %collective-permute-start.45) | collective-permute-done | bytes 589856 | tf_op jit(solution)/shard_map/ppermute | solution.py:55
  250.4 1.8 fusion.2
  (124 shorter events, 26.6 us)
Async XLA Ops:
  2.0 40.4 %slice-start = ((s8[6291456]{0:T(1024)(128)(4,1)}), s8[4194304]{0:T(1024)(128)(4,1)S(1)}, s32[]{:S(2)}) async-start(s8[6291456]{0:T(1024)(128)(4,1)} %bitcast.38), calls=%async_computation | async-start | bytes 8388608
  2.4 9.9 %collective-permute-start.3 = (bf16[24,6144]{1,0:T(8,128)(2,1)S(1)}, bf16[24,6144]{1,0:T(8,128)(2,1)S(1)}, u32[]{:S(2)}, u32[]{:S(2)}) collective-permute-start(bf16[24,6144]{1,0:T(8,128)(2,1)S(1)} %get-tuple-element.172), channel_id=1, source_target_pairs={{0,2},{2,4},{4,6},{6,0},{1,3},{3,5},{5,7},{7,1},{8,10},{10,12},{12... | collective-permute-start | bytes 884744 | tf_op jit(solution)/shard_map/ppermute | solution.py:16
  4.1 8.8 %collective-permute-start = (bf16[24,6144]{1,0:T(8,128)(2,1)S(1)}, bf16[24,6144]{1,0:T(8,128)(2,1)S(1)}, u32[]{:S(2)}, u32[]{:S(2)}) collective-permute-start(bf16[24,6144]{1,0:T(8,128)(2,1)S(1)} %get-tuple-element.171), channel_id=1, source_target_pairs={{0,8},{8,0},{1,9},{9,1},{2,10},{10,2},{3,11},{11,3},{4,12},{12,4},... | collective-permute-start | bytes 884744 | tf_op jit(solution)/shard_map/ppermute | solution.py:16
  5.7 9.2 %collective-permute-start.2 = (bf16[24,6144]{1,0:T(8,128)(2,1)S(1)}, bf16[24,6144]{1,0:T(8,128)(2,1)S(1)}, u32[]{:S(2)}, u32[]{:S(2)}) collective-permute-start(bf16[24,6144]{1,0:T(8,128)(2,1)S(1)} %get-tuple-element.172), channel_id=1, source_target_pairs={{0,6},{2,0},{4,2},{6,4},{1,7},{3,1},{5,3},{7,5},{8,14},{10,8},{12,... | collective-permute-start | bytes 884744 | tf_op jit(solution)/shard_map/ppermute | solution.py:16
  7.4 15.4 %collective-permute-start.1 = (bf16[48,6144]{1,0:T(8,128)(2,1)S(1)}, bf16[48,6144]{1,0:T(8,128)(2,1)S(1)}, u32[]{:S(2)}, u32[]{:S(2)}) collective-permute-start(bf16[48,6144]{1,0:T(8,128)(2,1)S(1)} %convolution_convert_fusion.1), channel_id=1, source_target_pairs={{0,24},{8,16},{16,8},{24,0},{1,25},{9,17},{17,9},{25,1},{2,26},{10... | collective-permute-start | bytes 1769480 | tf_op jit(solution)/shard_map/ppermute | solution.py:36
  12.4 9.0 %collective-permute-start.4 = (bf16[24,6144]{1,0:T(8,128)(2,1)S(1)}, bf16[24,6144]{1,0:T(8,128)(2,1)S(1)}, u32[]{:S(2)}, u32[]{:S(2)}) collective-permute-start(bf16[24,6144]{1,0:T(8,128)(2,1)S(1)} %collective-permute-done.3), channel_id=1, source_target_pairs={{0,2},{2,4},{4,6},{6,0},{1,3},{3,5},{5,7},{7,1},{8,10},{10,12},{12... | collective-permute-start | bytes 884744 | tf_op jit(solution)/shard_map/ppermute | solution.py:16
  12.9 24.0 %collective-permute-start.14 = (bf16[48,6144]{1,0:T(8,128)(2,1)S(1)}, bf16[48,6144]{1,0:T(8,128)(2,1)S(1)}, u32[]{:S(2)}, u32[]{:S(2)}) collective-permute-start(bf16[48,6144]{1,0:T(8,128)(2,1)S(1)} %pad_maximum_fusion.4), channel_id=1, source_target_pairs={{0,1},{1,0},{2,3},{3,2},{4,5},{5,4},{6,7},{7,6},{8,9},{9,8},{10,11... | collective-permute-start | bytes 1769480 | tf_op jit(solution)/shard_map/ppermute | solution.py:16
  22.9 8.3 %collective-permute-start.7 = (bf16[24,6144]{1,0:T(8,128)(2,1)S(1)}, bf16[24,6144]{1,0:T(8,128)(2,1)S(1)}, u32[]{:S(2)}, u32[]{:S(2)}) collective-permute-start(bf16[24,6144]{1,0:T(8,128)(2,1)S(1)} %get-tuple-element.169), channel_id=1, source_target_pairs={{0,2},{2,4},{4,6},{6,0},{1,3},{3,5},{5,7},{7,1},{8,10},{10,12},{12... | collective-permute-start | bytes 884744 | tf_op jit(solution)/shard_map/ppermute | solution.py:16
  23.2 7.9 %collective-permute-start.6 = (bf16[24,6144]{1,0:T(8,128)(2,1)S(1)}, bf16[24,6144]{1,0:T(8,128)(2,1)S(1)}, u32[]{:S(2)}, u32[]{:S(2)}) collective-permute-start(bf16[24,6144]{1,0:T(8,128)(2,1)S(1)} %get-tuple-element.169), channel_id=1, source_target_pairs={{0,6},{2,0},{4,2},{6,4},{1,7},{3,1},{5,3},{7,5},{8,14},{10,8},{12,... | collective-permute-start | bytes 884744 | tf_op jit(solution)/shard_map/ppermute | solution.py:16
  26.2 7.9 %collective-permute-start.5 = (bf16[24,6144]{1,0:T(8,128)(2,1)S(1)}, bf16[24,6144]{1,0:T(8,128)(2,1)S(1)}, u32[]{:S(2)}, u32[]{:S(2)}) collective-permute-start(bf16[24,6144]{1,0:T(8,128)(2,1)S(1)} %get-tuple-element.170), channel_id=1, source_target_pairs={{0,1},{1,0},{2,3},{3,2},{4,5},{5,4},{6,7},{7,6},{8,9},{9,8},{10,11... | collective-permute-start | bytes 884744 | tf_op jit(solution)/shard_map/ppermute | solution.py:16
  28.2 29.0 %collective-permute-start.10 = (bf16[96,6144]{1,0:T(8,128)(2,1)S(1)}, bf16[96,6144]{1,0:T(8,128)(2,1)S(1)}, u32[]{:S(2)}, u32[]{:S(2)}) collective-permute-start(bf16[96,6144]{1,0:T(8,128)(2,1)S(1)} %pad_maximum_fusion.1.refs_1_), channel_id=1, source_target_pairs={{0,8},{8,0},{1,9},{9,1},{2,10},{10,2},{3,11},{11,3},{4,12},{12,4},... | collective-permute-start | bytes 3538952 | tf_op jit(solution)/shard_map/ppermute | solution.py:16
  31.2 7.5 %collective-permute-start.8 = (bf16[24,6144]{1,0:T(8,128)(2,1)S(1)}, bf16[24,6144]{1,0:T(8,128)(2,1)S(1)}, u32[]{:S(2)}, u32[]{:S(2)}) collective-permute-start(bf16[24,6144]{1,0:T(8,128)(2,1)S(1)} %collective-permute-done.6), channel_id=1, source_target_pairs={{0,6},{2,0},{4,2},{6,4},{1,7},{3,1},{5,3},{7,5},{8,14},{10,8},{12,... | collective-permute-start | bytes 884744 | tf_op jit(solution)/shard_map/ppermute | solution.py:16
  34.2 35.6 %collective-permute-start.11 = (bf16[48,6144]{1,0:T(8,128)(2,1)S(1)}, bf16[48,6144]{1,0:T(8,128)(2,1)S(1)}, u32[]{:S(2)}, u32[]{:S(2)}) collective-permute-start(bf16[48,6144]{1,0:T(8,128)(2,1)S(1)} %pad_maximum_fusion.3), channel_id=1, source_target_pairs={{0,8},{8,0},{1,9},{9,1},{2,10},{10,2},{3,11},{11,3},{4,12},{12,4},... | collective-permute-start | bytes 1769480 | tf_op jit(solution)/shard_map/ppermute | solution.py:16
  35.1 26.1 %collective-permute-start.13 = (bf16[96,6144]{1,0:T(8,128)(2,1)S(1)}, bf16[96,6144]{1,0:T(8,128)(2,1)S(1)}, u32[]{:S(2)}, u32[]{:S(2)}) collective-permute-start(bf16[96,6144]{1,0:T(8,128)(2,1)S(1)} %pad_maximum_fusion.1.refs_1_), channel_id=1, source_target_pairs={{0,1},{1,0},{2,3},{3,2},{4,5},{5,4},{6,7},{7,6},{8,9},{9,8},{10,11... | collective-permute-start | bytes 3538952 | tf_op jit(solution)/shard_map/ppermute | solution.py:16
  36.9 32.9 %collective-permute-start.12 = (bf16[96,6144]{1,0:T(8,128)(2,1)S(1)}, bf16[96,6144]{1,0:T(8,128)(2,1)S(1)}, u32[]{:S(2)}, u32[]{:S(2)}) collective-permute-start(bf16[96,6144]{1,0:T(8,128)(2,1)S(1)} %pad_maximum_fusion.refs_0_), channel_id=1, source_target_pairs={{0,2},{2,4},{4,6},{6,0},{1,3},{3,5},{5,7},{7,1},{8,10},{10,12},{12... | collective-permute-start | bytes 3538952 | tf_op jit(solution)/shard_map/ppermute | solution.py:16
  38.7 34.5 %collective-permute-start.9 = (bf16[96,6144]{1,0:T(8,128)(2,1)S(1)}, bf16[96,6144]{1,0:T(8,128)(2,1)S(1)}, u32[]{:S(2)}, u32[]{:S(2)}) collective-permute-start(bf16[96,6144]{1,0:T(8,128)(2,1)S(1)} %pad_maximum_fusion.refs_0_), channel_id=1, source_target_pairs={{0,6},{2,0},{4,2},{6,4},{1,7},{3,1},{5,3},{7,5},{8,14},{10,8},{12,... | collective-permute-start | bytes 3538952 | tf_op jit(solution)/shard_map/ppermute | solution.py:16
  45.3 27.9 %copy-start.4 = (bf16[1,512,6144]{2,1,0:T(8,128)(2,1)S(1)}, bf16[1,512,6144]{2,1,0:T(8,128)(2,1)}, u32[]{:S(2)}) copy-start(bf16[1,512,6144]{2,1,0:T(8,128)(2,1)} %param.13) | copy-start | bytes 18874372
  57.2 34.1 %collective-permute-start.22 = (bf16[96,6144]{1,0:T(8,128)(2,1)S(1)}, bf16[96,6144]{1,0:T(8,128)(2,1)S(1)}, u32[]{:S(2)}, u32[]{:S(2)}) collective-permute-start(bf16[96,6144]{1,0:T(8,128)(2,1)S(1)} %pad_maximum_fusion.2.refs_2_), channel_id=1, source_target_pairs={{0,8},{8,0},{1,9},{9,1},{2,10},{10,2},{3,11},{11,3},{4,12},{12,4},... | collective-permute-start | bytes 3538952 | tf_op jit(solution)/shard_map/ppermute | solution.py:16
  61.2 31.4 %collective-permute-start.19 = (bf16[96,6144]{1,0:T(8,128)(2,1)S(1)}, bf16[96,6144]{1,0:T(8,128)(2,1)S(1)}, u32[]{:S(2)}, u32[]{:S(2)}) collective-permute-start(bf16[96,6144]{1,0:T(8,128)(2,1)S(1)} %pad_maximum_fusion.2.refs_2_), channel_id=1, source_target_pairs={{0,1},{1,0},{2,3},{3,2},{4,5},{5,4},{6,7},{7,6},{8,9},{9,8},{10,11... | collective-permute-start | bytes 3538952 | tf_op jit(solution)/shard_map/ppermute | solution.py:16
  69.9 23.1 %collective-permute-start.16 = (bf16[96,6144]{1,0:T(8,128)(2,1)S(1)}, bf16[96,6144]{1,0:T(8,128)(2,1)}, u32[]{:S(2)}, u32[]{:S(2)}) collective-permute-start(bf16[96,6144]{1,0:T(8,128)(2,1)S(1)} %constant_dynamic-update-slice_fusion.refs_2_), channel_id=1, source_target_pairs={{0,2},{2,4},{4,6},{6,0},{1,3},{3,5},{5,7},{7,1},{8,10},{10,12},{12... | collective-permute-start | bytes 3538952 | tf_op jit(solution)/shard_map/ppermute | solution.py:16
  70.0 29.6 %collective-permute-start.21 = (bf16[96,6144]{1,0:T(8,128)(2,1)S(1)}, bf16[96,6144]{1,0:T(8,128)(2,1)S(1)}, u32[]{:S(2)}, u32[]{:S(2)}) collective-permute-start(bf16[96,6144]{1,0:T(8,128)(2,1)S(1)} %constant_dynamic-update-slice_fusion.refs_2_), channel_id=1, source_target_pairs={{0,6},{2,0},{4,2},{6,4},{1,7},{3,1},{5,3},{7,5},{8,14},{10,8},{12,... | collective-permute-start | bytes 3538952 | tf_op jit(solution)/shard_map/ppermute | solution.py:16
  86.4 34.9 %collective-permute-start.15 = (bf16[96,6144]{1,0:T(8,128)(2,1)S(1)}, bf16[96,6144]{1,0:T(8,128)(2,1)S(1)}, u32[]{:S(2)}, u32[]{:S(2)}) collective-permute-start(bf16[96,6144]{1,0:T(8,128)(2,1)S(1)} %collective-permute-done.9.refs_1_), channel_id=1, source_target_pairs={{0,6},{2,0},{4,2},{6,4},{1,7},{3,1},{5,3},{7,5},{8,14},{10,8},{12,... | collective-permute-start | bytes 3538952 | tf_op jit(solution)/shard_map/ppermute | solution.py:16
  92.3 32.3 %collective-permute-start.18 = (bf16[96,6144]{1,0:T(8,128)(2,1)S(1)}, bf16[96,6144]{1,0:T(8,128)(2,1)S(1)}, u32[]{:S(2)}, u32[]{:S(2)}) collective-permute-start(bf16[96,6144]{1,0:T(8,128)(2,1)S(1)} %collective-permute-done.10.refs_3_), channel_id=1, source_target_pairs={{0,1},{1,0},{2,3},{3,2},{4,5},{5,4},{6,7},{7,6},{8,9},{9,8},{10,11... | collective-permute-start | bytes 3538952 | tf_op jit(solution)/shard_map/ppermute | solution.py:16
  92.6 32.4 %collective-permute-start.20 = (bf16[96,6144]{1,0:T(8,128)(2,1)S(1)}, bf16[96,6144]{1,0:T(8,128)(2,1)S(1)}, u32[]{:S(2)}, u32[]{:S(2)}) collective-permute-start(bf16[96,6144]{1,0:T(8,128)(2,1)S(1)} %collective-permute-done.19.refs_3_), channel_id=1, source_target_pairs={{0,8},{8,0},{1,9},{9,1},{2,10},{10,2},{3,11},{11,3},{4,12},{12,4},... | collective-permute-start | bytes 3538952 | tf_op jit(solution)/shard_map/ppermute | solution.py:16
  93.0 32.0 %collective-permute-start.17 = (bf16[96,6144]{1,0:T(8,128)(2,1)}, bf16[96,6144]{1,0:T(8,128)(2,1)}, u32[]{:S(2)}, u32[]{:S(2)}) collective-permute-start(bf16[96,6144]{1,0:T(8,128)(2,1)} %collective-permute-done.16.refs_0_), channel_id=1, source_target_pairs={{0,2},{2,4},{4,6},{6,0},{1,3},{3,5},{5,7},{7,1},{8,10},{10,12},{12... | collective-permute-start | bytes 3538952 | tf_op jit(solution)/shard_map/ppermute | solution.py:16
  100.6 41.4 %collective-permute-start.26 = (bf16[96,6144]{1,0:T(8,128)(2,1)S(1)}, bf16[96,6144]{1,0:T(8,128)(2,1)}, u32[]{:S(2)}, u32[]{:S(2)}) collective-permute-start(bf16[96,6144]{1,0:T(8,128)(2,1)S(1)} %get-tuple-element.123), channel_id=1, source_target_pairs={{0,1},{1,0},{2,3},{3,2},{4,5},{5,4},{6,7},{7,6},{8,9},{9,8},{10,11... | collective-permute-start | bytes 3538952 | tf_op jit(solution)/shard_map/ppermute | solution.py:16
  121.3 20.7 %collective-permute-start.23 = (bf16[96,6144]{1,0:T(8,128)(2,1)S(1)}, bf16[96,6144]{1,0:T(8,128)(2,1)S(1)}, u32[]{:S(2)}, u32[]{:S(2)}) collective-permute-start(bf16[96,6144]{1,0:T(8,128)(2,1)S(1)} %get-tuple-element.120), channel_id=1, source_target_pairs={{0,6},{2,0},{4,2},{6,4},{1,7},{3,1},{5,3},{7,5},{8,14},{10,8},{12,... | collective-permute-start | bytes 3538952 | tf_op jit(solution)/shard_map/ppermute | solution.py:16
  124.6 19.3 %collective-permute-start.25 = (bf16[96,6144]{1,0:T(8,128)(2,1)S(1)}, bf16[96,6144]{1,0:T(8,128)(2,1)S(1)}, u32[]{:S(2)}, u32[]{:S(2)}) collective-permute-start(bf16[96,6144]{1,0:T(8,128)(2,1)S(1)} %get-tuple-element.122), channel_id=1, source_target_pairs={{0,8},{8,0},{1,9},{9,1},{2,10},{10,2},{3,11},{11,3},{4,12},{12,4},... | collective-permute-start | bytes 3538952 | tf_op jit(solution)/shard_map/ppermute | solution.py:16
  125.0 20.6 %collective-permute-start.24 = (bf16[96,6144]{1,0:T(8,128)(2,1)}, bf16[96,6144]{1,0:T(8,128)(2,1)S(1)}, u32[]{:S(2)}, u32[]{:S(2)}) collective-permute-start(bf16[96,6144]{1,0:T(8,128)(2,1)} %get-tuple-element.121), channel_id=1, source_target_pairs={{0,2},{2,4},{4,6},{6,0},{1,3},{3,5},{5,7},{7,1},{8,10},{10,12},{12... | collective-permute-start | bytes 3538952 | tf_op jit(solution)/shard_map/ppermute | solution.py:16
  145.6 27.7 %collective-permute-start.27 = (bf16[96,6144]{1,0:T(8,128)(2,1)S(1)}, bf16[96,6144]{1,0:T(8,128)(2,1)S(1)}, u32[]{:S(2)}, u32[]{:S(2)}) collective-permute-start(bf16[96,6144]{1,0:T(8,128)(2,1)S(1)} %get-tuple-element.124), channel_id=1, source_target_pairs={{0,8},{8,0},{1,9},{9,1},{2,10},{10,2},{3,11},{11,3},{4,12},{12,4},... | collective-permute-start | bytes 3538952 | tf_op jit(solution)/shard_map/ppermute | solution.py:16
  147.3 25.1 %collective-permute-start.28 = (bf16[96,6144]{1,0:T(8,128)(2,1)S(1)}, bf16[96,6144]{1,0:T(8,128)(2,1)S(1)}, u32[]{:S(2)}, u32[]{:S(2)}) collective-permute-start(bf16[96,6144]{1,0:T(8,128)(2,1)S(1)} %get-tuple-element.126), channel_id=1, source_target_pairs={{0,2},{2,4},{4,6},{6,0},{1,3},{3,5},{5,7},{7,1},{8,10},{10,12},{12... | collective-permute-start | bytes 3538952 | tf_op jit(solution)/shard_map/ppermute | solution.py:16
  147.3 25.4 %collective-permute-start.29 = (bf16[96,6144]{1,0:T(8,128)(2,1)S(1)}, bf16[96,6144]{1,0:T(8,128)(2,1)S(1)}, u32[]{:S(2)}, u32[]{:S(2)}) collective-permute-start(bf16[96,6144]{1,0:T(8,128)(2,1)S(1)} %get-tuple-element.128), channel_id=1, source_target_pairs={{0,6},{2,0},{4,2},{6,4},{1,7},{3,1},{5,3},{7,5},{8,14},{10,8},{12,... | collective-permute-start | bytes 3538952 | tf_op jit(solution)/shard_map/ppermute | solution.py:16
  150.5 22.5 %collective-permute-start.30 = (bf16[96,6144]{1,0:T(8,128)(2,1)S(1)}, bf16[96,6144]{1,0:T(8,128)(2,1)S(1)}, u32[]{:S(2)}, u32[]{:S(2)}) collective-permute-start(bf16[96,6144]{1,0:T(8,128)(2,1)S(1)} %get-tuple-element.132), channel_id=1, source_target_pairs={{0,1},{1,0},{2,3},{3,2},{4,5},{5,4},{6,7},{7,6},{8,9},{9,8},{10,11... | collective-permute-start | bytes 3538952 | tf_op jit(solution)/shard_map/ppermute | solution.py:16
  173.3 24.2 %collective-permute-start.31 = (bf16[96,6144]{1,0:T(8,128)(2,1)S(1)}, bf16[96,6144]{1,0:T(8,128)(2,1)S(1)}, u32[]{:S(2)}, u32[]{:S(2)}) collective-permute-start(bf16[96,6144]{1,0:T(8,128)(2,1)S(1)} %add_convert_fusion.3), channel_id=1, source_target_pairs={{0,2},{2,4},{4,6},{6,0},{1,3},{3,5},{5,7},{7,1},{8,10},{10,12},{12... | collective-permute-start | bytes 3538952 | tf_op jit(solution)/shard_map/ppermute | solution.py:16
  173.4 24.1 %collective-permute-start.32 = (bf16[96,6144]{1,0:T(8,128)(2,1)S(1)}, bf16[96,6144]{1,0:T(8,128)(2,1)S(1)}, u32[]{:S(2)}, u32[]{:S(2)}) collective-permute-start(bf16[96,6144]{1,0:T(8,128)(2,1)S(1)} %add_convert_fusion.2), channel_id=1, source_target_pairs={{0,6},{2,0},{4,2},{6,4},{1,7},{3,1},{5,3},{7,5},{8,14},{10,8},{12,... | collective-permute-start | bytes 3538952 | tf_op jit(solution)/shard_map/ppermute | solution.py:16
  176.6 20.9 %collective-permute-start.33 = (bf16[96,6144]{1,0:T(8,128)(2,1)S(1)}, bf16[96,6144]{1,0:T(8,128)(2,1)S(1)}, u32[]{:S(2)}, u32[]{:S(2)}) collective-permute-start(bf16[96,6144]{1,0:T(8,128)(2,1)S(1)} %add_convert_fusion.1), channel_id=1, source_target_pairs={{0,1},{1,0},{2,3},{3,2},{4,5},{5,4},{6,7},{7,6},{8,9},{9,8},{10,11... | collective-permute-start | bytes 3538952 | tf_op jit(solution)/shard_map/ppermute | solution.py:16
  179.1 18.4 %collective-permute-start.34 = (bf16[96,6144]{1,0:T(8,128)(2,1)S(1)}, bf16[96,6144]{1,0:T(8,128)(2,1)S(1)}, u32[]{:S(2)}, u32[]{:S(2)}) collective-permute-start(bf16[96,6144]{1,0:T(8,128)(2,1)S(1)} %add_convert_fusion), channel_id=1, source_target_pairs={{0,8},{8,0},{1,9},{9,1},{2,10},{10,2},{3,11},{11,3},{4,12},{12,4},... | collective-permute-start | bytes 3538952 | tf_op jit(solution)/shard_map/ppermute | solution.py:16
  179.5 4.5 %collective-permute-start.35 = (f32[4,128]{1,0:T(4,128)S(1)}, f32[4,128]{1,0:T(4,128)S(1)}, u32[]{:S(2)}, u32[]{:S(2)}) collective-permute-start(f32[4,128]{1,0:T(4,128)S(1)} %pad_maximum_fusion.9), channel_id=1, source_target_pairs={{0,32},{32,64},{64,96},{96,0},{1,33},{33,65},{65,97},{97,1},{2,34}... | collective-permute-start | bytes 6152 | tf_op jit(solution)/shard_map/ppermute | solution.py:40
  199.1 13.7 %collective-permute-start.36 = (bf16[48,6144]{1,0:T(8,128)(2,1)S(1)}, bf16[48,6144]{1,0:T(8,128)(2,1)S(1)}, u32[]{:S(2)}, u32[]{:S(2)}) collective-permute-start(bf16[48,6144]{1,0:T(8,128)(2,1)S(1)} %pad_maximum_fusion.5), channel_id=1, source_target_pairs={{0,6},{2,0},{4,2},{6,4},{1,7},{3,1},{5,3},{7,5},{8,14},{10,8},{12,... | collective-permute-start | bytes 1769480 | tf_op jit(solution)/shard_map/ppermute | solution.py:16
  202.3 14.2 %collective-permute-start.37 = (bf16[48,6144]{1,0:T(8,128)(2,1)S(1)}, bf16[48,6144]{1,0:T(8,128)(2,1)S(1)}, u32[]{:S(2)}, u32[]{:S(2)}) collective-permute-start(bf16[48,6144]{1,0:T(8,128)(2,1)S(1)} %pad_maximum_fusion.6), channel_id=1, source_target_pairs={{0,2},{2,4},{4,6},{6,0},{1,3},{3,5},{5,7},{7,1},{8,10},{10,12},{12... | collective-permute-start | bytes 1769480 | tf_op jit(solution)/shard_map/ppermute | solution.py:16
  202.8 13.7 %collective-permute-start.38 = (bf16[48,6144]{1,0:T(8,128)(2,1)S(1)}, bf16[48,6144]{1,0:T(8,128)(2,1)S(1)}, u32[]{:S(2)}, u32[]{:S(2)}) collective-permute-start(bf16[48,6144]{1,0:T(8,128)(2,1)S(1)} %add_convert_fusion.5), channel_id=1, source_target_pairs={{0,1},{1,0},{2,3},{3,2},{4,5},{5,4},{6,7},{7,6},{8,9},{9,8},{10,11... | collective-permute-start | bytes 1769480 | tf_op jit(solution)/shard_map/ppermute | solution.py:16
  204.6 13.1 %collective-permute-start.39 = (bf16[48,6144]{1,0:T(8,128)(2,1)S(1)}, bf16[48,6144]{1,0:T(8,128)(2,1)S(1)}, u32[]{:S(2)}, u32[]{:S(2)}) collective-permute-start(bf16[48,6144]{1,0:T(8,128)(2,1)S(1)} %add_convert_fusion.4), channel_id=1, source_target_pairs={{0,8},{8,0},{1,9},{9,1},{2,10},{10,2},{3,11},{11,3},{4,12},{12,4},... | collective-permute-start | bytes 1769480 | tf_op jit(solution)/shard_map/ppermute | solution.py:16
  219.3 6.8 %collective-permute-start.43 = (bf16[24,6144]{1,0:T(8,128)(2,1)S(1)}, bf16[24,6144]{1,0:T(8,128)(2,1)S(1)}, u32[]{:S(2)}, u32[]{:S(2)}) collective-permute-start(bf16[24,6144]{1,0:T(8,128)(2,1)S(1)} %add_convert_fusion.10), channel_id=1, source_target_pairs={{0,1},{1,0},{2,3},{3,2},{4,5},{5,4},{6,7},{7,6},{8,9},{9,8},{10,11... | collective-permute-start | bytes 884744 | tf_op jit(solution)/shard_map/ppermute | solution.py:16
  219.9 7.9 %collective-permute-start.41 = (bf16[24,6144]{1,0:T(8,128)(2,1)S(1)}, bf16[24,6144]{1,0:T(8,128)(2,1)S(1)}, u32[]{:S(2)}, u32[]{:S(2)}) collective-permute-start(bf16[24,6144]{1,0:T(8,128)(2,1)S(1)} %add_convert_fusion.12), channel_id=1, source_target_pairs={{0,2},{2,4},{4,6},{6,0},{1,3},{3,5},{5,7},{7,1},{8,10},{10,12},{12... | collective-permute-start | bytes 884744 | tf_op jit(solution)/shard_map/ppermute | solution.py:16
  220.0 7.8 %collective-permute-start.40 = (bf16[24,6144]{1,0:T(8,128)(2,1)S(1)}, bf16[24,6144]{1,0:T(8,128)(2,1)S(1)}, u32[]{:S(2)}, u32[]{:S(2)}) collective-permute-start(bf16[24,6144]{1,0:T(8,128)(2,1)S(1)} %add_convert_fusion.13), channel_id=1, source_target_pairs={{0,6},{2,0},{4,2},{6,4},{1,7},{3,1},{5,3},{7,5},{8,14},{10,8},{12,... | collective-permute-start | bytes 884744 | tf_op jit(solution)/shard_map/ppermute | solution.py:16
  223.1 6.7 %collective-permute-start.42 = (bf16[24,6144]{1,0:T(8,128)(2,1)S(1)}, bf16[24,6144]{1,0:T(8,128)(2,1)S(1)}, u32[]{:S(2)}, u32[]{:S(2)}) collective-permute-start(bf16[24,6144]{1,0:T(8,128)(2,1)S(1)} %add_convert_fusion.11), channel_id=1, source_target_pairs={{0,8},{8,0},{1,9},{9,1},{2,10},{10,2},{3,11},{11,3},{4,12},{12,4},... | collective-permute-start | bytes 884744 | tf_op jit(solution)/shard_map/ppermute | solution.py:16
  231.7 18.1 %collective-permute-start.45 = (bf16[48,6144]{1,0:T(8,128)(2,1)S(1)}, bf16[48,6144]{1,0:T(8,128)(2,1)S(1)}, u32[]{:S(2)}, u32[]{:S(2)}) collective-permute-start(bf16[48,6144]{1,0:T(8,128)(2,1)S(1)} %pad_maximum_fusion.8), channel_id=1, source_target_pairs={{0,57},{1,56},{8,49},{9,48},{16,41},{17,40},{24,33},{25,32},{32,89... | collective-permute-start | bytes 1769480 | tf_op jit(solution)/shard_map/ppermute | solution.py:55
  231.8 18.6 %collective-permute-start.44 = (bf16[48,6144]{1,0:T(8,128)(2,1)S(1)}, bf16[48,6144]{1,0:T(8,128)(2,1)S(1)}, u32[]{:S(2)}, u32[]{:S(2)}) collective-permute-start(bf16[48,6144]{1,0:T(8,128)(2,1)S(1)} %pad_maximum_fusion.7), channel_id=1, source_target_pairs={{0,33},{1,32},{32,65},{33,64},{64,97},{65,96},{96,1},{97,0},{2,35}... | collective-permute-start | bytes 1769480 | tf_op jit(solution)/shard_map/ppermute | solution.py:45
  (12 other events, 60.9 us)

commit v9 on v8

--- a/solution.py
+++ b/solution.py
@@ -186,30 +186,32 @@
     own = compact(mine_at, tokens)
 
     a1, b = split(own, 2)
-    a1_y, b_behind, b_ahead = over_y(a1), right(b), left(b)
+    partner, a1_y, b_behind, b_ahead = together(partner, over_y(a1), right(b), left(b))
+
+    a2, g = split(partner, 2)
+    b_opposite, a2_z, g_behind, g_ahead = right(b_behind), over_z(a2), left(g), right(g)
+    b_opposite, a1, a1_y = together(b_opposite, a1, a1_y)
     a1_near = join(a1, a1_y)
-    a1_far, b_opposite = over_z(a1_near), right(b_behind)
-    partner, b_ahead, b_opposite = together(partner, b_ahead, b_opposite)
+    a1_far = over_z(a1_near)
     b_ring = join(b, b_behind, b_ahead, b_opposite)
-    b_y = over_y(b_ring)
-
-    a2, g = split(partner, 2)
-    a2_z, g_behind, g_ahead = over_z(a2), left(g), right(g)
-    g_behind, g_ahead, b_ring_late = together(g_behind, g_ahead, b_ring)
+    g_behind, g_ahead = together(g_behind, g_ahead)
     g_opposite = left(g_behind)
     a2_near = join(a2, a2_z)
+    a2_far = over_y(a2_near)
     near = join(a1_near, a2_near)
-    a2_far, b_z = over_y(a2_near), over_z(b_ring_late)
-    near_late, g_opposite = together(near, g_opposite)
+    near_late, g_opposite, b_ring = together(near, g_opposite, b_ring)
     near_left, near_right = right(near), left(near_late)
+    b_y = over_y(b_ring)
+    a1_far, b_ring = together(a1_far, b_ring)
+    b_z = over_z(b_ring)
     g_ring = join(g, g_behind, g_ahead, g_opposite)
 
     g_ring_sent = g_ring
     near, b_ring, g_ring = experts([near, b_ring, g_ring], *matrices)
-    b_y, near, g_ring_y = together(b_y, near, g_ring_sent)
+    b_y, g_ring_y = together(b_y, g_ring_sent)
     b_z, g_ring_z = together(b_z, g_ring_sent)
     g_y, g_z = over_y(g_ring_y), over_z(g_ring_z)
-    a2_far, near_left, b_z = together(a2_far, near_left, b_z)
+    a2_far, near_left, b_ring = together(a2_far, near_left, b_ring)
     far = join(a1_far, a2_far)
     far_left, far_right = right(far), left(far)
 
@@ -262,7 +264,7 @@
         [a1_terms[1] + take(got[2:3], 1, 2)],
         [a2_terms[0] + take(got[3:], 0, 2)],
     )
-    ends = together(left(ends[0]), right(ends[1]), over_y(ends[2]), over_z(ends[3]))
+    ends = left(ends[0]), right(ends[1]), over_y(ends[2]), over_z(ends[3])
     own, partner = sums(
         [
             a1_terms[0] + take(got[2:3], 0, 2) + take(ends[2:3], 0, 1),

time: 254 us -> 264 us (1.039)
  local copies, waits for them, and re-layouts: 7.77 us -> 14.8 us
  waiting for transfers between devices: 122 us -> 125 us
    unnamed x29 -> x47, local copies, waits for them, and re-layouts: 7.42 us -> 14.4 us
    ppermute x42, waiting for transfers between devices: 104 us -> 107 us  [shift(): return lax.ppermute(value, axis, [(i, (i + by) % n) for i in range(n)])]
    convert_element_type x16 -> x15, other arithmetic: 6.35 us -> 6.36 us  [add(): return total.astype(BF16)]
  transfers between devices with their start and end apart: 46 -> 46, of which waited for: 24 -> 23; matrix products, arithmetic and copies ran while one was open for 1% -> 2% of each run, Pallas kernels for 18% -> 17%
where the time goes in v9:
time: 264 us; the launch traced here: 263 us
  waiting for transfers between devices  125 us (47%)
  starting transfers between devices  66.4 us (25%)
  Pallas kernels  45.6 us (17%)
  local copies, waits for them, and re-layouts  14.8 us (6%)
  other arithmetic  8.27 us (3%)
  matrix products  3.07 us (1%)
    ppermute x42, waiting for transfers between devices, shift(): return lax.ppermute(value, axis, [(i, (i + by) % n) for i in range(n)])  107 us
    ppermute x42, starting transfers between devices, shift(): return lax.ppermute(value, axis, [(i, (i + by) % n) for i in range(n)])  57.7 us
    pallas_call x4, Pallas kernels, experts(): pl.pallas_call(experts_kernel, grid=(2 * half,), in_specs=rows_in + [into...  45.6 us
    unnamed x47, local copies, waits for them, and re-layouts  14.4 us
    ppermute x1, waiting for transfers between devices, to_owner_across(): return lax.ppermute(value, ('zh', 'core', 'yh', 'yl', 'zl'), pairs)  13.1 us
    convert_element_type x15, other arithmetic, add(): return total.astype(BF16)  6.36 us
    ppermute x1, starting transfers between devices, to_owner(): return lax.ppermute(value, ('zh', 'core', 'zl'), pairs)  5.48 us
  transfers between devices with their start and end apart: 46, of which 23 were waited for; matrix products, arithmetic and copies ran while one was open for 2% of the time, Pallas kernels for 17%

profile of v9, /device:TPU:0, one launch (start us, length us, event | category | flops | bytes accessed | tf_op | source)
XLA Modules:
  0.0 263.4 jit_solution(16013227027057755693)
XLA Ops:
  2.0 3.2 %collective-permute-start = (bf16[48,6144]{1,0:T(8,128)(2,1)S(1)}, bf16[48,6144]{1,0:T(8,128)(2,1)S(1)}, u32[]{:S(2)}, u32[]{:S(2)}) collective-permute-start(bf16[48,6144]{1,0:T(8,128)(2,1)S(1)} %convolution_convert_fusion.1), channel_id=1, source_target_pairs={{0,24},{8,16},{16,8},{24,0},{1,25},{9,17},{17,9},{25,1},{2,26},{10... | collective-permute-start | bytes 1769480 | tf_op jit(solution)/shard_map/ppermute | solution.py:36
  5.8 2.8 %collective-permute-start.3 = (bf16[24,6144]{1,0:T(8,128)(2,1)S(1)}, bf16[24,6144]{1,0:T(8,128)(2,1)S(1)}, u32[]{:S(2)}, u32[]{:S(2)}) collective-permute-start(bf16[24,6144]{1,0:T(8,128)(2,1)S(1)} %get-tuple-element.175), channel_id=1, source_target_pairs={{0,6},{2,0},{4,2},{6,4},{1,7},{3,1},{5,3},{7,5},{8,14},{10,8},{12,... | collective-permute-start | bytes 884744 | tf_op jit(solution)/shard_map/ppermute | solution.py:16
  8.6 5.6 %collective-permute-done.1 = bf16[24,6144]{1,0:T(8,128)(2,1)S(1)} collective-permute-done((bf16[24,6144]{1,0:T(8,128)(2,1)S(1)}, bf16[24,6144]{1,0:T(8,128)(2,1)S(1)}, u32[]{:S(2)}, u32[]{:S(2)}) %collective-permute-start.1) | collective-permute-done | bytes 294944 | tf_op jit(solution)/shard_map/ppermute | solution.py:16
  14.5 3.4 %collective-permute-done.2 = bf16[24,6144]{1,0:T(8,128)(2,1)S(1)} collective-permute-done((bf16[24,6144]{1,0:T(8,128)(2,1)S(1)}, bf16[24,6144]{1,0:T(8,128)(2,1)S(1)}, u32[]{:S(2)}, u32[]{:S(2)}) %collective-permute-start.2) | collective-permute-done | bytes 294944 | tf_op jit(solution)/shard_map/ppermute | solution.py:16
  21.6 1.8 collective-permute-start.6
  23.4 1.9 collective-permute-start.5
  25.3 4.4 %collective-permute-done.4 = bf16[24,6144]{1,0:T(8,128)(2,1)S(1)} collective-permute-done((bf16[24,6144]{1,0:T(8,128)(2,1)S(1)}, bf16[24,6144]{1,0:T(8,128)(2,1)S(1)}, u32[]{:S(2)}, u32[]{:S(2)}) %collective-permute-start.4) | collective-permute-done | bytes 294944 | tf_op jit(solution)/shard_map/ppermute | solution.py:16
  29.7 4.4 %collective-permute-done.7 = bf16[24,6144]{1,0:T(8,128)(2,1)S(1)} collective-permute-done((bf16[24,6144]{1,0:T(8,128)(2,1)S(1)}, bf16[24,6144]{1,0:T(8,128)(2,1)S(1)}, u32[]{:S(2)}, u32[]{:S(2)}) %collective-permute-start.7) | collective-permute-done | bytes 294944 | tf_op jit(solution)/shard_map/ppermute | solution.py:16
  36.0 2.0 collective-permute-start.13
  38.7 2.6 collective-permute-done.8
  41.3 2.5 collective-permute-start.9
  44.0 5.4 %collective-permute-done.13 = bf16[48,6144]{1,0:T(8,128)(2,1)S(1)} collective-permute-done((bf16[48,6144]{1,0:T(8,128)(2,1)S(1)}, bf16[48,6144]{1,0:T(8,128)(2,1)S(1)}, u32[]{:S(2)}, u32[]{:S(2)}) %collective-permute-start.13) | collective-permute-done | bytes 589856 | tf_op jit(solution)/shard_map/ppermute | solution.py:16
  49.5 2.0 collective-permute-start.14
  51.5 2.8 %copy-done.3 = bf16[1,512,6144]{2,1,0:T(8,128)(2,1)S(1)} copy-done((bf16[1,512,6144]{2,1,0:T(8,128)(2,1)S(1)}, bf16[1,512,6144]{2,1,0:T(8,128)(2,1)}, u32[]{:S(2)}) %copy-start.3) | copy-done | bytes 6291480
  54.3 8.7 %experts.4 = (bf16[96,6144]{1,0:T(8,128)(2,1)S(1)}, bf16[96,6144]{1,0:T(8,128)(2,1)S(1)}, bf16[96,6144]{1,0:T(8,128)(2,1)S(1)}) custom-call(bf16[96,6144]{1,0:T(8,128)(2,1)S(1)} %pad_maximum_fusion.refs_0_, bf16[96,6144]{1,0:T(8,128)(2,1)S(1)} %pad_maximum_fusion.1.refs_1_, bf16[96,6144]{1,0:T(8,128)(2,1)S(1)} %pad_maximum_fusion.2.refs_2_, ...), custom_call_target="tpu_custom_call" | custom-call | flops 5435817984 | bytes 25952256 | tf_op jit(solution)/shard_map/experts/pallas_call | solution.py:141
  63.0 1.6 collective-permute-done.12.refs_0_
  64.8 1.9 collective-permute-start.16
  66.7 9.0 %collective-permute-done.14.refs_4_ = bf16[96,6144]{1,0:T(8,128)(2,1)S(1)} collective-permute-done((bf16[96,6144]{1,0:T(8,128)(2,1)S(1)}, bf16[96,6144]{1,0:T(8,128)(2,1)S(1)}, u32[]{:S(2)}, u32[]{:S(2)}) %collective-permute-start.14) | collective-permute-done | bytes 1179680 | tf_op jit(solution)/shard_map/ppermute | solution.py:16
  75.7 1.9 collective-permute-start.19
  77.6 1.8 collective-permute-start.22
  80.7 13.7 %experts.5 = (bf16[96,6144]{1,0:T(8,128)(2,1)}, bf16[96,6144]{1,0:T(8,128)(2,1)S(1)}, bf16[96,6144]{1,0:T(8,128)(2,1)S(1)}, bf16[96,6144]{1,0:T(8,128)(2,1)S(1)}, bf16[96,6144]{1,0:T(8,128)(2,1)S(1)}) custom-call(bf16[96,6144]{1,0:T(8,128)(2,1)S(1)} %copy-done.11, bf16[96,6144]{1,0:T(8,128)(2,1)S(1)} %collective-permute-done.9.refs_1_, ...), custom_call_target="tpu_custom_call" | custom-call | flops 9059696640 | bytes 30670848 | tf_op jit(solution)/shard_map/experts/pallas_call | solution.py:141
  95.3 2.2 collective-permute-start.18
  97.4 7.3 %collective-permute-done.19.refs_3_ = bf16[96,6144]{1,0:T(8,128)(2,1)} collective-permute-done((bf16[96,6144]{1,0:T(8,128)(2,1)S(1)}, bf16[96,6144]{1,0:T(8,128)(2,1)}, u32[]{:S(2)}, u32[]{:S(2)}) %collective-permute-start.19) | collective-permute-done | bytes 1179680 | tf_op jit(solution)/shard_map/ppermute | solution.py:16
  104.7 1.8 collective-permute-start.20
  106.5 1.9 collective-permute-start.26
  108.4 12.3 %experts.6 = (bf16[96,6144]{1,0:T(8,128)(2,1)S(1)}, bf16[96,6144]{1,0:T(8,128)(2,1)}, bf16[96,6144]{1,0:T(8,128)(2,1)S(1)}, bf16[96,6144]{1,0:T(8,128)(2,1)S(1)}) custom-call(bf16[96,6144]{1,0:T(8,128)(2,1)S(1)} %collective-permute-done.16.refs_0_, bf16[96,6144]{1,0:T(8,128)(2,1)S(1)} %collective-permute-done.21.refs_1_, ...), custom_call_target="tpu_custom_call" | custom-call | flops 7247757312 | bytes 28311552 | tf_op jit(solution)/shard_map/experts/pallas_call | solution.py:141
  123.6 6.3 %collective-permute-done.18.refs_2_ = bf16[96,6144]{1,0:T(8,128)(2,1)S(1)} collective-permute-done((bf16[96,6144]{1,0:T(8,128)(2,1)S(1)}, bf16[96,6144]{1,0:T(8,128)(2,1)S(1)}, u32[]{:S(2)}, u32[]{:S(2)}) %collective-permute-start.18) | collective-permute-done | bytes 1179680 | tf_op jit(solution)/shard_map/ppermute | solution.py:16
  130.9 1.8 collective-permute-start.25
  140.5 10.9 %experts.7 = (bf16[96,6144]{1,0:T(8,128)(2,1)S(1)}, bf16[96,6144]{1,0:T(8,128)(2,1)S(1)}, bf16[96,6144]{1,0:T(8,128)(2,1)S(1)}, bf16[96,6144]{1,0:T(8,128)(2,1)S(1)}) custom-call(bf16[96,6144]{1,0:T(8,128)(2,1)S(1)} %copy-done.7, bf16[96,6144]{1,0:T(8,128)(2,1)S(1)} %copy-done.13, bf16[96,6144]{1,0:T(8,128)(2,1)S(1)} %copy-done.9, ...), custom_call_target="tpu_custom_call" | custom-call | flops 7247757312 | bytes 28311552 | tf_op jit(solution)/shard_map/experts/pallas_call | solution.py:141
  152.0 5.0 %collective-permute-done.24 = bf16[96,6144]{1,0:T(8,128)(2,1)S(1)} collective-permute-done((bf16[96,6144]{1,0:T(8,128)(2,1)}, bf16[96,6144]{1,0:T(8,128)(2,1)S(1)}, u32[]{:S(2)}, u32[]{:S(2)}) %collective-permute-start.24) | collective-permute-done | bytes 1179680 | tf_op jit(solution)/shard_map/ppermute | solution.py:16
  157.4 3.2 %collective-permute-start.29 = (bf16[96,6144]{1,0:T(8,128)(2,1)S(1)}, bf16[96,6144]{1,0:T(8,128)(2,1)S(1)}, u32[]{:S(2)}, u32[]{:S(2)}) collective-permute-start(bf16[96,6144]{1,0:T(8,128)(2,1)S(1)} %get-tuple-element.134), channel_id=1, source_target_pairs={{0,6},{2,0},{4,2},{6,4},{1,7},{3,1},{5,3},{7,5},{8,14},{10,8},{12,... | collective-permute-start | bytes 3538952 | tf_op jit(solution)/shard_map/ppermute | solution.py:16
  162.5 20.0 %collective-permute-done.28 = bf16[96,6144]{1,0:T(8,128)(2,1)S(1)} collective-permute-done((bf16[96,6144]{1,0:T(8,128)(2,1)S(1)}, bf16[96,6144]{1,0:T(8,128)(2,1)S(1)}, u32[]{:S(2)}, u32[]{:S(2)}) %collective-permute-start.28) | collective-permute-done | bytes 1179680 | tf_op jit(solution)/shard_map/ppermute | solution.py:16
  183.6 3.2 %collective-permute-start.32 = (bf16[96,6144]{1,0:T(8,128)(2,1)S(1)}, bf16[96,6144]{1,0:T(8,128)(2,1)S(1)}, u32[]{:S(2)}, u32[]{:S(2)}) collective-permute-start(bf16[96,6144]{1,0:T(8,128)(2,1)S(1)} %add_convert_fusion.2), channel_id=1, source_target_pairs={{0,6},{2,0},{4,2},{6,4},{1,7},{3,1},{5,3},{7,5},{8,14},{10,8},{12,... | collective-permute-start | bytes 3538952 | tf_op jit(solution)/shard_map/ppermute | solution.py:16
  188.3 1.6 collective-permute-start.34
  190.0 4.5 %collective-permute-done.35 = f32[4,128]{1,0:T(4,128)S(1)} collective-permute-done((f32[4,128]{1,0:T(4,128)S(1)}, f32[4,128]{1,0:T(4,128)S(1)}, u32[]{:S(2)}, u32[]{:S(2)}) %collective-permute-start.35) | collective-permute-done | bytes 2080 | tf_op jit(solution)/shard_map/ppermute | solution.py:40
  194.5 12.7 %collective-permute-done.31 = bf16[96,6144]{1,0:T(8,128)(2,1)S(1)} collective-permute-done((bf16[96,6144]{1,0:T(8,128)(2,1)S(1)}, bf16[96,6144]{1,0:T(8,128)(2,1)S(1)}, u32[]{:S(2)}, u32[]{:S(2)}) %collective-permute-start.31) | collective-permute-done | bytes 1179680 | tf_op jit(solution)/shard_map/ppermute | solution.py:16
  208.9 2.3 collective-permute-start.37
  211.4 1.6 collective-permute-start.38
  213.3 1.7 collective-permute-start.39
  215.0 6.9 %collective-permute-done.36 = bf16[48,6144]{1,0:T(8,128)(2,1)S(1)} collective-permute-done((bf16[48,6144]{1,0:T(8,128)(2,1)S(1)}, bf16[48,6144]{1,0:T(8,128)(2,1)S(1)}, u32[]{:S(2)}, u32[]{:S(2)}) %collective-permute-start.36) | collective-permute-done | bytes 589856 | tf_op jit(solution)/shard_map/ppermute | solution.py:16
  221.9 2.0 collective-permute-done.38
  227.1 2.0 collective-permute-start.40
  229.2 2.6 collective-permute-done.41
  233.0 1.8 collective-permute-start.44
  235.2 5.8 %collective-permute-done.44 = bf16[24,6144]{1,0:T(8,128)(2,1)S(1)} collective-permute-done((bf16[24,6144]{1,0:T(8,128)(2,1)S(1)}, bf16[24,6144]{1,0:T(8,128)(2,1)S(1)}, u32[]{:S(2)}, u32[]{:S(2)}) %collective-permute-start.44) | collective-permute-done | bytes 294944 | tf_op jit(solution)/shard_map/ppermute | solution.py:16
  242.4 5.5 %collective-permute-start.42 = (bf16[48,6144]{1,0:T(8,128)(2,1)S(1)}, bf16[48,6144]{1,0:T(8,128)(2,1)S(1)}, u32[]{:S(2)}, u32[]{:S(2)}) collective-permute-start(bf16[48,6144]{1,0:T(8,128)(2,1)S(1)} %pad_maximum_fusion.7), channel_id=1, source_target_pairs={{0,33},{1,32},{32,65},{33,64},{64,97},{65,96},{96,1},{97,0},{2,35}... | collective-permute-start | bytes 1769480 | tf_op jit(solution)/shard_map/ppermute | solution.py:45
  247.8 13.1 %collective-permute-done.45 = bf16[48,6144]{1,0:T(8,128)(2,1)S(1)} collective-permute-done((bf16[48,6144]{1,0:T(8,128)(2,1)S(1)}, bf16[48,6144]{1,0:T(8,128)(2,1)S(1)}, u32[]{:S(2)}, u32[]{:S(2)}) %collective-permute-start.45) | collective-permute-done | bytes 589856 | tf_op jit(solution)/shard_map/ppermute | solution.py:55
  261.6 1.8 fusion.2
  (142 shorter events, 37.8 us)
Async XLA Ops:
  2.0 16.5 %collective-permute-start = (bf16[48,6144]{1,0:T(8,128)(2,1)S(1)}, bf16[48,6144]{1,0:T(8,128)(2,1)S(1)}, u32[]{:S(2)}, u32[]{:S(2)}) collective-permute-start(bf16[48,6144]{1,0:T(8,128)(2,1)S(1)} %convolution_convert_fusion.1), channel_id=1, source_target_pairs={{0,24},{8,16},{16,8},{24,0},{1,25},{9,17},{17,9},{25,1},{2,26},{10... | collective-permute-start | bytes 1769480 | tf_op jit(solution)/shard_map/ppermute | solution.py:36
  5.6 45.9 %slice-start = ((s8[6291456]{0:T(1024)(128)(4,1)}), s8[4194304]{0:T(1024)(128)(4,1)S(1)}, s32[]{:S(2)}) async-start(s8[6291456]{0:T(1024)(128)(4,1)} %bitcast.38), calls=%async_computation | async-start | bytes 8388608
  5.6 8.5 %collective-permute-start.1 = (bf16[24,6144]{1,0:T(8,128)(2,1)S(1)}, bf16[24,6144]{1,0:T(8,128)(2,1)S(1)}, u32[]{:S(2)}, u32[]{:S(2)}) collective-permute-start(bf16[24,6144]{1,0:T(8,128)(2,1)S(1)} %get-tuple-element.87), channel_id=1, source_target_pairs={{0,8},{8,0},{1,9},{9,1},{2,10},{10,2},{3,11},{11,3},{4,12},{12,4},... | collective-permute-start | bytes 884744 | tf_op jit(solution)/shard_map/ppermute | solution.py:16
  5.8 8.7 %collective-permute-start.3 = (bf16[24,6144]{1,0:T(8,128)(2,1)S(1)}, bf16[24,6144]{1,0:T(8,128)(2,1)S(1)}, u32[]{:S(2)}, u32[]{:S(2)}) collective-permute-start(bf16[24,6144]{1,0:T(8,128)(2,1)S(1)} %get-tuple-element.175), channel_id=1, source_target_pairs={{0,6},{2,0},{4,2},{6,4},{1,7},{3,1},{5,3},{7,5},{8,14},{10,8},{12,... | collective-permute-start | bytes 884744 | tf_op jit(solution)/shard_map/ppermute | solution.py:16
  8.6 9.3 %collective-permute-start.2 = (bf16[24,6144]{1,0:T(8,128)(2,1)S(1)}, bf16[24,6144]{1,0:T(8,128)(2,1)S(1)}, u32[]{:S(2)}, u32[]{:S(2)}) collective-permute-start(bf16[24,6144]{1,0:T(8,128)(2,1)S(1)} %get-tuple-element.175), channel_id=1, source_target_pairs={{0,2},{2,4},{4,6},{6,0},{1,3},{3,5},{5,7},{7,1},{8,10},{10,12},{12... | collective-permute-start | bytes 884744 | tf_op jit(solution)/shard_map/ppermute | solution.py:16
  18.5 11.2 %collective-permute-start.4 = (bf16[24,6144]{1,0:T(8,128)(2,1)S(1)}, bf16[24,6144]{1,0:T(8,128)(2,1)S(1)}, u32[]{:S(2)}, u32[]{:S(2)}) collective-permute-start(bf16[24,6144]{1,0:T(8,128)(2,1)S(1)} %collective-permute-done.2), channel_id=1, source_target_pairs={{0,2},{2,4},{4,6},{6,0},{1,3},{3,5},{5,7},{7,1},{8,10},{10,12},{12... | collective-permute-start | bytes 884744 | tf_op jit(solution)/shard_map/ppermute | solution.py:16
  20.1 14.0 %collective-permute-start.7 = (bf16[24,6144]{1,0:T(8,128)(2,1)S(1)}, bf16[24,6144]{1,0:T(8,128)(2,1)S(1)}, u32[]{:S(2)}, u32[]{:S(2)}) collective-permute-start(bf16[24,6144]{1,0:T(8,128)(2,1)S(1)} %get-tuple-element.173), channel_id=1, source_target_pairs={{0,2},{2,4},{4,6},{6,0},{1,3},{3,5},{5,7},{7,1},{8,10},{10,12},{12... | collective-permute-start | bytes 884744 | tf_op jit(solution)/shard_map/ppermute | solution.py:16
  21.6 12.5 %collective-permute-start.6 = (bf16[24,6144]{1,0:T(8,128)(2,1)S(1)}, bf16[24,6144]{1,0:T(8,128)(2,1)S(1)}, u32[]{:S(2)}, u32[]{:S(2)}) collective-permute-start(bf16[24,6144]{1,0:T(8,128)(2,1)S(1)} %get-tuple-element.173), channel_id=1, source_target_pairs={{0,6},{2,0},{4,2},{6,4},{1,7},{3,1},{5,3},{7,5},{8,14},{10,8},{12,... | collective-permute-start | bytes 884744 | tf_op jit(solution)/shard_map/ppermute | solution.py:16
  23.4 12.2 %collective-permute-start.5 = (bf16[24,6144]{1,0:T(8,128)(2,1)S(1)}, bf16[24,6144]{1,0:T(8,128)(2,1)S(1)}, u32[]{:S(2)}, u32[]{:S(2)}) collective-permute-start(bf16[24,6144]{1,0:T(8,128)(2,1)S(1)} %get-tuple-element.174), channel_id=1, source_target_pairs={{0,1},{1,0},{2,3},{3,2},{4,5},{5,4},{6,7},{7,6},{8,9},{9,8},{10,11... | collective-permute-start | bytes 884744 | tf_op jit(solution)/shard_map/ppermute | solution.py:16
  34.1 7.2 %collective-permute-start.8 = (bf16[24,6144]{1,0:T(8,128)(2,1)S(1)}, bf16[24,6144]{1,0:T(8,128)(2,1)S(1)}, u32[]{:S(2)}, u32[]{:S(2)}) collective-permute-start(bf16[24,6144]{1,0:T(8,128)(2,1)S(1)} %collective-permute-done.6), channel_id=1, source_target_pairs={{0,6},{2,0},{4,2},{6,4},{1,7},{3,1},{5,3},{7,5},{8,14},{10,8},{12,... | collective-permute-start | bytes 884744 | tf_op jit(solution)/shard_map/ppermute | solution.py:16
  35.6 27.3 %collective-permute-start.11 = (bf16[48,6144]{1,0:T(8,128)(2,1)S(1)}, bf16[48,6144]{1,0:T(8,128)(2,1)S(1)}, u32[]{:S(2)}, u32[]{:S(2)}) collective-permute-start(bf16[48,6144]{1,0:T(8,128)(2,1)S(1)} %pad_maximum_fusion.3), channel_id=1, source_target_pairs={{0,8},{8,0},{1,9},{9,1},{2,10},{10,2},{3,11},{11,3},{4,12},{12,4},... | collective-permute-start | bytes 1769480 | tf_op jit(solution)/shard_map/ppermute | solution.py:16
  36.0 13.5 %collective-permute-start.13 = (bf16[48,6144]{1,0:T(8,128)(2,1)S(1)}, bf16[48,6144]{1,0:T(8,128)(2,1)S(1)}, u32[]{:S(2)}, u32[]{:S(2)}) collective-permute-start(bf16[48,6144]{1,0:T(8,128)(2,1)S(1)} %pad_maximum_fusion.4), channel_id=1, source_target_pairs={{0,1},{1,0},{2,3},{3,2},{4,5},{5,4},{6,7},{7,6},{8,9},{9,8},{10,11... | collective-permute-start | bytes 1769480 | tf_op jit(solution)/shard_map/ppermute | solution.py:16
  38.1 26.5 %collective-permute-start.12 = (bf16[96,6144]{1,0:T(8,128)(2,1)S(1)}, bf16[96,6144]{1,0:T(8,128)(2,1)S(1)}, u32[]{:S(2)}, u32[]{:S(2)}) collective-permute-start(bf16[96,6144]{1,0:T(8,128)(2,1)S(1)} %pad_maximum_fusion.refs_0_), channel_id=1, source_target_pairs={{0,2},{2,4},{4,6},{6,0},{1,3},{3,5},{5,7},{7,1},{8,10},{10,12},{12... | collective-permute-start | bytes 3538952 | tf_op jit(solution)/shard_map/ppermute | solution.py:16
  41.3 38.1 %collective-permute-start.9 = (bf16[96,6144]{1,0:T(8,128)(2,1)S(1)}, bf16[96,6144]{1,0:T(8,128)(2,1)S(1)}, u32[]{:S(2)}, u32[]{:S(2)}) collective-permute-start(bf16[96,6144]{1,0:T(8,128)(2,1)S(1)} %pad_maximum_fusion.refs_0_), channel_id=1, source_target_pairs={{0,6},{2,0},{4,2},{6,4},{1,7},{3,1},{5,3},{7,5},{8,14},{10,8},{12,... | collective-permute-start | bytes 3538952 | tf_op jit(solution)/shard_map/ppermute | solution.py:16
  43.8 33.8 %collective-permute-start.10 = (bf16[96,6144]{1,0:T(8,128)(2,1)S(1)}, bf16[96,6144]{1,0:T(8,128)(2,1)S(1)}, u32[]{:S(2)}, u32[]{:S(2)}) collective-permute-start(bf16[96,6144]{1,0:T(8,128)(2,1)S(1)} %pad_maximum_fusion.1.refs_1_), channel_id=1, source_target_pairs={{0,8},{8,0},{1,9},{9,1},{2,10},{10,2},{3,11},{11,3},{4,12},{12,4},... | collective-permute-start | bytes 3538952 | tf_op jit(solution)/shard_map/ppermute | solution.py:16
  49.5 26.2 %collective-permute-start.14 = (bf16[96,6144]{1,0:T(8,128)(2,1)S(1)}, bf16[96,6144]{1,0:T(8,128)(2,1)S(1)}, u32[]{:S(2)}, u32[]{:S(2)}) collective-permute-start(bf16[96,6144]{1,0:T(8,128)(2,1)S(1)} %pad_maximum_fusion.1.refs_1_), channel_id=1, source_target_pairs={{0,1},{1,0},{2,3},{3,2},{4,5},{5,4},{6,7},{7,6},{8,9},{9,8},{10,11... | collective-permute-start | bytes 3538952 | tf_op jit(solution)/shard_map/ppermute | solution.py:16
  64.6 43.8 %slice-start.2 = ((s8[6291456]{0:T(1024)(128)(4,1)}), s8[4194304]{0:T(1024)(128)(4,1)S(1)}, s32[]{:S(2)}) async-start(s8[6291456]{0:T(1024)(128)(4,1)} %bitcast.50), calls=%async_computation.2 | async-start | bytes 8388608
  64.6 30.6 %collective-permute-start.21 = (bf16[96,6144]{1,0:T(8,128)(2,1)S(1)}, bf16[96,6144]{1,0:T(8,128)(2,1)S(1)}, u32[]{:S(2)}, u32[]{:S(2)}) collective-permute-start(bf16[96,6144]{1,0:T(8,128)(2,1)S(1)} %constant_dynamic-update-slice_fusion.refs_2_), channel_id=1, source_target_pairs={{0,6},{2,0},{4,2},{6,4},{1,7},{3,1},{5,3},{7,5},{8,14},{10,8},{12,... | collective-permute-start | bytes 3538952 | tf_op jit(solution)/shard_map/ppermute | solution.py:16
  64.8 32.6 %collective-permute-start.16 = (bf16[96,6144]{1,0:T(8,128)(2,1)S(1)}, bf16[96,6144]{1,0:T(8,128)(2,1)S(1)}, u32[]{:S(2)}, u32[]{:S(2)}) collective-permute-start(bf16[96,6144]{1,0:T(8,128)(2,1)S(1)} %constant_dynamic-update-slice_fusion.refs_2_), channel_id=1, source_target_pairs={{0,2},{2,4},{4,6},{6,0},{1,3},{3,5},{5,7},{7,1},{8,10},{10,12},{12... | collective-permute-start | bytes 3538952 | tf_op jit(solution)/shard_map/ppermute | solution.py:16
  75.7 29.0 %collective-permute-start.19 = (bf16[96,6144]{1,0:T(8,128)(2,1)S(1)}, bf16[96,6144]{1,0:T(8,128)(2,1)}, u32[]{:S(2)}, u32[]{:S(2)}) collective-permute-start(bf16[96,6144]{1,0:T(8,128)(2,1)S(1)} %pad_maximum_fusion.2.refs_2_), channel_id=1, source_target_pairs={{0,1},{1,0},{2,3},{3,2},{4,5},{5,4},{6,7},{7,6},{8,9},{9,8},{10,11... | collective-permute-start | bytes 3538952 | tf_op jit(solution)/shard_map/ppermute | solution.py:16
  77.6 28.9 %collective-permute-start.22 = (bf16[96,6144]{1,0:T(8,128)(2,1)S(1)}, bf16[96,6144]{1,0:T(8,128)(2,1)}, u32[]{:S(2)}, u32[]{:S(2)}) collective-permute-start(bf16[96,6144]{1,0:T(8,128)(2,1)S(1)} %pad_maximum_fusion.2.refs_2_), channel_id=1, source_target_pairs={{0,8},{8,0},{1,9},{9,1},{2,10},{10,2},{3,11},{11,3},{4,12},{12,4},... | collective-permute-start | bytes 3538952 | tf_op jit(solution)/shard_map/ppermute | solution.py:16
  94.4 27.3 %collective-permute-start.15 = (bf16[96,6144]{1,0:T(8,128)(2,1)S(1)}, bf16[96,6144]{1,0:T(8,128)(2,1)S(1)}, u32[]{:S(2)}, u32[]{:S(2)}) collective-permute-start(bf16[96,6144]{1,0:T(8,128)(2,1)S(1)} %collective-permute-done.9.refs_1_), channel_id=1, source_target_pairs={{0,6},{2,0},{4,2},{6,4},{1,7},{3,1},{5,3},{7,5},{8,14},{10,8},{12,... | collective-permute-start | bytes 3538952 | tf_op jit(solution)/shard_map/ppermute | solution.py:16
  95.3 34.6 %collective-permute-start.18 = (bf16[96,6144]{1,0:T(8,128)(2,1)S(1)}, bf16[96,6144]{1,0:T(8,128)(2,1)S(1)}, u32[]{:S(2)}, u32[]{:S(2)}) collective-permute-start(bf16[96,6144]{1,0:T(8,128)(2,1)S(1)} %collective-permute-done.10.refs_3_), channel_id=1, source_target_pairs={{0,1},{1,0},{2,3},{3,2},{4,5},{5,4},{6,7},{7,6},{8,9},{9,8},{10,11... | collective-permute-start | bytes 3538952 | tf_op jit(solution)/shard_map/ppermute | solution.py:16
  97.4 35.3 %collective-permute-start.17 = (bf16[96,6144]{1,0:T(8,128)(2,1)S(1)}, bf16[96,6144]{1,0:T(8,128)(2,1)S(1)}, u32[]{:S(2)}, u32[]{:S(2)}) collective-permute-start(bf16[96,6144]{1,0:T(8,128)(2,1)S(1)} %collective-permute-done.16.refs_0_), channel_id=1, source_target_pairs={{0,2},{2,4},{4,6},{6,0},{1,3},{3,5},{5,7},{7,1},{8,10},{10,12},{12... | collective-permute-start | bytes 3538952 | tf_op jit(solution)/shard_map/ppermute | solution.py:16
  104.7 29.1 %collective-permute-start.20 = (bf16[96,6144]{1,0:T(8,128)(2,1)}, bf16[96,6144]{1,0:T(8,128)(2,1)S(1)}, u32[]{:S(2)}, u32[]{:S(2)}) collective-permute-start(bf16[96,6144]{1,0:T(8,128)(2,1)} %collective-permute-done.19.refs_3_), channel_id=1, source_target_pairs={{0,8},{8,0},{1,9},{9,1},{2,10},{10,2},{3,11},{11,3},{4,12},{12,4},... | collective-permute-start | bytes 3538952 | tf_op jit(solution)/shard_map/ppermute | solution.py:16
  106.5 45.0 %collective-permute-start.26 = (bf16[96,6144]{1,0:T(8,128)(2,1)S(1)}, bf16[96,6144]{1,0:T(8,128)(2,1)}, u32[]{:S(2)}, u32[]{:S(2)}) collective-permute-start(bf16[96,6144]{1,0:T(8,128)(2,1)S(1)} %get-tuple-element.129), channel_id=1, source_target_pairs={{0,1},{1,0},{2,3},{3,2},{4,5},{5,4},{6,7},{7,6},{8,9},{9,8},{10,11... | collective-permute-start | bytes 3538952 | tf_op jit(solution)/shard_map/ppermute | solution.py:16
  122.7 28.7 %collective-permute-start.23 = (bf16[96,6144]{1,0:T(8,128)(2,1)}, bf16[96,6144]{1,0:T(8,128)(2,1)S(1)}, u32[]{:S(2)}, u32[]{:S(2)}) collective-permute-start(bf16[96,6144]{1,0:T(8,128)(2,1)} %get-tuple-element.126), channel_id=1, source_target_pairs={{0,6},{2,0},{4,2},{6,4},{1,7},{3,1},{5,3},{7,5},{8,14},{10,8},{12,... | collective-permute-start | bytes 3538952 | tf_op jit(solution)/shard_map/ppermute | solution.py:16
  130.9 21.1 %collective-permute-start.25 = (bf16[96,6144]{1,0:T(8,128)(2,1)S(1)}, bf16[96,6144]{1,0:T(8,128)(2,1)S(1)}, u32[]{:S(2)}, u32[]{:S(2)}) collective-permute-start(bf16[96,6144]{1,0:T(8,128)(2,1)S(1)} %get-tuple-element.128), channel_id=1, source_target_pairs={{0,8},{8,0},{1,9},{9,1},{2,10},{10,2},{3,11},{11,3},{4,12},{12,4},... | collective-permute-start | bytes 3538952 | tf_op jit(solution)/shard_map/ppermute | solution.py:16
  134.8 22.2 %collective-permute-start.24 = (bf16[96,6144]{1,0:T(8,128)(2,1)}, bf16[96,6144]{1,0:T(8,128)(2,1)S(1)}, u32[]{:S(2)}, u32[]{:S(2)}) collective-permute-start(bf16[96,6144]{1,0:T(8,128)(2,1)} %get-tuple-element.127), channel_id=1, source_target_pairs={{0,2},{2,4},{4,6},{6,0},{1,3},{3,5},{5,7},{7,1},{8,10},{10,12},{12... | collective-permute-start | bytes 3538952 | tf_op jit(solution)/shard_map/ppermute | solution.py:16
  157.0 26.4 %collective-permute-start.27 = (bf16[96,6144]{1,0:T(8,128)(2,1)S(1)}, bf16[96,6144]{1,0:T(8,128)(2,1)S(1)}, u32[]{:S(2)}, u32[]{:S(2)}) collective-permute-start(bf16[96,6144]{1,0:T(8,128)(2,1)S(1)} %get-tuple-element.130), channel_id=1, source_target_pairs={{0,8},{8,0},{1,9},{9,1},{2,10},{10,2},{3,11},{11,3},{4,12},{12,4},... | collective-permute-start | bytes 3538952 | tf_op jit(solution)/shard_map/ppermute | solution.py:16
  157.4 25.1 %collective-permute-start.28 = (bf16[96,6144]{1,0:T(8,128)(2,1)S(1)}, bf16[96,6144]{1,0:T(8,128)(2,1)S(1)}, u32[]{:S(2)}, u32[]{:S(2)}) collective-permute-start(bf16[96,6144]{1,0:T(8,128)(2,1)S(1)} %get-tuple-element.132), channel_id=1, source_target_pairs={{0,2},{2,4},{4,6},{6,0},{1,3},{3,5},{5,7},{7,1},{8,10},{10,12},{12... | collective-permute-start | bytes 3538952 | tf_op jit(solution)/shard_map/ppermute | solution.py:16
  157.4 25.4 %collective-permute-start.29 = (bf16[96,6144]{1,0:T(8,128)(2,1)S(1)}, bf16[96,6144]{1,0:T(8,128)(2,1)S(1)}, u32[]{:S(2)}, u32[]{:S(2)}) collective-permute-start(bf16[96,6144]{1,0:T(8,128)(2,1)S(1)} %get-tuple-element.134), channel_id=1, source_target_pairs={{0,6},{2,0},{4,2},{6,4},{1,7},{3,1},{5,3},{7,5},{8,14},{10,8},{12,... | collective-permute-start | bytes 3538952 | tf_op jit(solution)/shard_map/ppermute | solution.py:16
  160.7 22.5 %collective-permute-start.30 = (bf16[96,6144]{1,0:T(8,128)(2,1)S(1)}, bf16[96,6144]{1,0:T(8,128)(2,1)S(1)}, u32[]{:S(2)}, u32[]{:S(2)}) collective-permute-start(bf16[96,6144]{1,0:T(8,128)(2,1)S(1)} %copy-done.5), channel_id=1, source_target_pairs={{0,1},{1,0},{2,3},{3,2},{4,5},{5,4},{6,7},{7,6},{8,9},{9,8},{10,11... | collective-permute-start | bytes 3538952 | tf_op jit(solution)/shard_map/ppermute | solution.py:16
  183.5 23.7 %collective-permute-start.31 = (bf16[96,6144]{1,0:T(8,128)(2,1)S(1)}, bf16[96,6144]{1,0:T(8,128)(2,1)S(1)}, u32[]{:S(2)}, u32[]{:S(2)}) collective-permute-start(bf16[96,6144]{1,0:T(8,128)(2,1)S(1)} %add_convert_fusion.3), channel_id=1, source_target_pairs={{0,2},{2,4},{4,6},{6,0},{1,3},{3,5},{5,7},{7,1},{8,10},{10,12},{12... | collective-permute-start | bytes 3538952 | tf_op jit(solution)/shard_map/ppermute | solution.py:16
  183.6 23.6 %collective-permute-start.32 = (bf16[96,6144]{1,0:T(8,128)(2,1)S(1)}, bf16[96,6144]{1,0:T(8,128)(2,1)S(1)}, u32[]{:S(2)}, u32[]{:S(2)}) collective-permute-start(bf16[96,6144]{1,0:T(8,128)(2,1)S(1)} %add_convert_fusion.2), channel_id=1, source_target_pairs={{0,6},{2,0},{4,2},{6,4},{1,7},{3,1},{5,3},{7,5},{8,14},{10,8},{12,... | collective-permute-start | bytes 3538952 | tf_op jit(solution)/shard_map/ppermute | solution.py:16
  186.8 20.4 %collective-permute-start.33 = (bf16[96,6144]{1,0:T(8,128)(2,1)S(1)}, bf16[96,6144]{1,0:T(8,128)(2,1)S(1)}, u32[]{:S(2)}, u32[]{:S(2)}) collective-permute-start(bf16[96,6144]{1,0:T(8,128)(2,1)S(1)} %add_convert_fusion.1), channel_id=1, source_target_pairs={{0,1},{1,0},{2,3},{3,2},{4,5},{5,4},{6,7},{7,6},{8,9},{9,8},{10,11... | collective-permute-start | bytes 3538952 | tf_op jit(solution)/shard_map/ppermute | solution.py:16
  188.3 18.9 %collective-permute-start.34 = (bf16[96,6144]{1,0:T(8,128)(2,1)S(1)}, bf16[96,6144]{1,0:T(8,128)(2,1)S(1)}, u32[]{:S(2)}, u32[]{:S(2)}) collective-permute-start(bf16[96,6144]{1,0:T(8,128)(2,1)S(1)} %add_convert_fusion), channel_id=1, source_target_pairs={{0,8},{8,0},{1,9},{9,1},{2,10},{10,2},{3,11},{11,3},{4,12},{12,4},... | collective-permute-start | bytes 3538952 | tf_op jit(solution)/shard_map/ppermute | solution.py:16
  190.0 4.5 %collective-permute-start.35 = (f32[4,128]{1,0:T(4,128)S(1)}, f32[4,128]{1,0:T(4,128)S(1)}, u32[]{:S(2)}, u32[]{:S(2)}) collective-permute-start(f32[4,128]{1,0:T(4,128)S(1)} %pad_maximum_fusion.9), channel_id=1, source_target_pairs={{0,32},{32,64},{64,96},{96,0},{1,33},{33,65},{65,97},{97,1},{2,34}... | collective-permute-start | bytes 6152 | tf_op jit(solution)/shard_map/ppermute | solution.py:40
  208.8 13.1 %collective-permute-start.36 = (bf16[48,6144]{1,0:T(8,128)(2,1)S(1)}, bf16[48,6144]{1,0:T(8,128)(2,1)S(1)}, u32[]{:S(2)}, u32[]{:S(2)}) collective-permute-start(bf16[48,6144]{1,0:T(8,128)(2,1)S(1)} %pad_maximum_fusion.5), channel_id=1, source_target_pairs={{0,6},{2,0},{4,2},{6,4},{1,7},{3,1},{5,3},{7,5},{8,14},{10,8},{12,... | collective-permute-start | bytes 1769480 | tf_op jit(solution)/shard_map/ppermute | solution.py:16
  208.9 13.0 %collective-permute-start.37 = (bf16[48,6144]{1,0:T(8,128)(2,1)S(1)}, bf16[48,6144]{1,0:T(8,128)(2,1)S(1)}, u32[]{:S(2)}, u32[]{:S(2)}) collective-permute-start(bf16[48,6144]{1,0:T(8,128)(2,1)S(1)} %pad_maximum_fusion.6), channel_id=1, source_target_pairs={{0,2},{2,4},{4,6},{6,0},{1,3},{3,5},{5,7},{7,1},{8,10},{10,12},{12... | collective-permute-start | bytes 1769480 | tf_op jit(solution)/shard_map/ppermute | solution.py:16
  211.4 12.5 %collective-permute-start.38 = (bf16[48,6144]{1,0:T(8,128)(2,1)S(1)}, bf16[48,6144]{1,0:T(8,128)(2,1)S(1)}, u32[]{:S(2)}, u32[]{:S(2)}) collective-permute-start(bf16[48,6144]{1,0:T(8,128)(2,1)S(1)} %add_convert_fusion.5), channel_id=1, source_target_pairs={{0,1},{1,0},{2,3},{3,2},{4,5},{5,4},{6,7},{7,6},{8,9},{9,8},{10,11... | collective-permute-start | bytes 1769480 | tf_op jit(solution)/shard_map/ppermute | solution.py:16
  213.3 11.3 %collective-permute-start.39 = (bf16[48,6144]{1,0:T(8,128)(2,1)S(1)}, bf16[48,6144]{1,0:T(8,128)(2,1)S(1)}, u32[]{:S(2)}, u32[]{:S(2)}) collective-permute-start(bf16[48,6144]{1,0:T(8,128)(2,1)S(1)} %add_convert_fusion.4), channel_id=1, source_target_pairs={{0,8},{8,0},{1,9},{9,1},{2,10},{10,2},{3,11},{11,3},{4,12},{12,4},... | collective-permute-start | bytes 1769480 | tf_op jit(solution)/shard_map/ppermute | solution.py:16
  224.9 6.8 %collective-permute-start.41 = (bf16[24,6144]{1,0:T(8,128)(2,1)S(1)}, bf16[24,6144]{1,0:T(8,128)(2,1)S(1)}, u32[]{:S(2)}, u32[]{:S(2)}) collective-permute-start(bf16[24,6144]{1,0:T(8,128)(2,1)S(1)} %add_convert_fusion.11), channel_id=1, source_target_pairs={{0,6},{2,0},{4,2},{6,4},{1,7},{3,1},{5,3},{7,5},{8,14},{10,8},{12,... | collective-permute-start | bytes 884744 | tf_op jit(solution)/shard_map/ppermute | solution.py:16
  226.6 8.3 %collective-permute-start.43 = (bf16[24,6144]{1,0:T(8,128)(2,1)S(1)}, bf16[24,6144]{1,0:T(8,128)(2,1)S(1)}, u32[]{:S(2)}, u32[]{:S(2)}) collective-permute-start(bf16[24,6144]{1,0:T(8,128)(2,1)S(1)} %add_convert_fusion.9), channel_id=1, source_target_pairs={{0,1},{1,0},{2,3},{3,2},{4,5},{5,4},{6,7},{7,6},{8,9},{9,8},{10,11... | collective-permute-start | bytes 884744 | tf_op jit(solution)/shard_map/ppermute | solution.py:16
  227.1 7.9 %collective-permute-start.40 = (bf16[24,6144]{1,0:T(8,128)(2,1)S(1)}, bf16[24,6144]{1,0:T(8,128)(2,1)S(1)}, u32[]{:S(2)}, u32[]{:S(2)}) collective-permute-start(bf16[24,6144]{1,0:T(8,128)(2,1)S(1)} %add_convert_fusion.13), channel_id=1, source_target_pairs={{0,8},{8,0},{1,9},{9,1},{2,10},{10,2},{3,11},{11,3},{4,12},{12,4},... | collective-permute-start | bytes 884744 | tf_op jit(solution)/shard_map/ppermute | solution.py:16
  233.0 8.0 %collective-permute-start.44 = (bf16[24,6144]{1,0:T(8,128)(2,1)S(1)}, bf16[24,6144]{1,0:T(8,128)(2,1)S(1)}, u32[]{:S(2)}, u32[]{:S(2)}) collective-permute-start(bf16[24,6144]{1,0:T(8,128)(2,1)S(1)} %get-tuple-element.172), channel_id=1, source_target_pairs={{0,2},{2,4},{4,6},{6,0},{1,3},{3,5},{5,7},{7,1},{8,10},{10,12},{12... | collective-permute-start | bytes 884744 | tf_op jit(solution)/shard_map/ppermute | solution.py:16
  242.2 18.7 %collective-permute-start.45 = (bf16[48,6144]{1,0:T(8,128)(2,1)S(1)}, bf16[48,6144]{1,0:T(8,128)(2,1)S(1)}, u32[]{:S(2)}, u32[]{:S(2)}) collective-permute-start(bf16[48,6144]{1,0:T(8,128)(2,1)S(1)} %pad_maximum_fusion.8), channel_id=1, source_target_pairs={{0,57},{1,56},{8,49},{9,48},{16,41},{17,40},{24,33},{25,32},{32,89... | collective-permute-start | bytes 1769480 | tf_op jit(solution)/shard_map/ppermute | solution.py:55
  242.4 19.2 %collective-permute-start.42 = (bf16[48,6144]{1,0:T(8,128)(2,1)S(1)}, bf16[48,6144]{1,0:T(8,128)(2,1)S(1)}, u32[]{:S(2)}, u32[]{:S(2)}) collective-permute-start(bf16[48,6144]{1,0:T(8,128)(2,1)S(1)} %pad_maximum_fusion.7), channel_id=1, source_target_pairs={{0,33},{1,32},{32,65},{33,64},{64,97},{65,96},{96,1},{97,0},{2,35}... | collective-permute-start | bytes 1769480 | tf_op jit(solution)/shard_map/ppermute | solution.py:45
  (21 other events, 165.0 us)

commit v10 on v8

--- a/solution.py
+++ b/solution.py
@@ -187,29 +187,31 @@
 
     a1, b = split(own, 2)
     a1_y, b_behind, b_ahead = over_y(a1), right(b), left(b)
-    a1_near = join(a1, a1_y)
-    a1_far, b_opposite = over_z(a1_near), right(b_behind)
-    partner, b_ahead, b_opposite = together(partner, b_ahead, b_opposite)
+    b_opposite = right(b_behind)
     b_ring = join(b, b_behind, b_ahead, b_opposite)
     b_y = over_y(b_ring)
+    partner, a1_y = together(partner, a1_y)
+    a1_near = join(a1, a1_y)
+    a1_far = over_z(a1_near)
 
     a2, g = split(partner, 2)
     a2_z, g_behind, g_ahead = over_z(a2), left(g), right(g)
-    g_behind, g_ahead, b_ring_late = together(g_behind, g_ahead, b_ring)
+    a2_z, g_behind = together(a2_z, g_behind)
     g_opposite = left(g_behind)
+    a1_far, b_ring_late = together(a1_far, b_ring)
     a2_near = join(a2, a2_z)
     near = join(a1_near, a2_near)
     a2_far, b_z = over_y(a2_near), over_z(b_ring_late)
-    near_late, g_opposite = together(near, g_opposite)
-    near_left, near_right = right(near), left(near_late)
+    near, g_opposite, g_ahead = together(near, g_opposite, g_ahead)
+    near_left, near_right = right(near), left(near)
     g_ring = join(g, g_behind, g_ahead, g_opposite)
 
     g_ring_sent = g_ring
     near, b_ring, g_ring = experts([near, b_ring, g_ring], *matrices)
-    b_y, near, g_ring_y = together(b_y, near, g_ring_sent)
+    b_y, g_ring_y = together(b_y, g_ring_sent)
     b_z, g_ring_z = together(b_z, g_ring_sent)
     g_y, g_z = over_y(g_ring_y), over_z(g_ring_z)
-    a2_far, near_left, b_z = together(a2_far, near_left, b_z)
+    a2_far, near_left, b_ring = together(a2_far, near_left, b_ring)
     far = join(a1_far, a2_far)
     far_left, far_right = right(far), left(far)
 

time: 254 us -> 259 us (1.020)
  starting transfers between devices: 64.6 us -> 55.5 us
  waiting for transfers between devices: 122 us -> 129 us
  local copies, waits for them, and re-layouts: 7.77 us -> 11.1 us
  other arithmetic: 8.26 us -> 11.3 us
    ppermute x42, starting transfers between devices: 56.8 us -> 45.4 us  [shift(): return lax.ppermute(value, axis, [(i, (i + by) % n) for i in range(n)])]
    ppermute x1, waiting for transfers between devices: 4.51 us -> 8.96 us  [to_next_section(): lax.ppermute(value, ('zh', 'core'), [(s, (s + 1) % 4) for s in range(4)])]
    unnamed x29 -> x33, local copies, waits for them, and re-layouts: 7.42 us -> 10.7 us
    ppermute x1, waiting for transfers between devices: 12.5 us -> 9.4 us  [to_owner_across(): return lax.ppermute(value, ('zh', 'core', 'yh', 'yl', 'zl'), pairs)]
    convert_element_type x16, other arithmetic: 6.35 us -> 9.43 us  [add(): return total.astype(BF16)]
  transfers between devices with their start and end apart: 46 -> 46, of which waited for: 24 -> 25; matrix products, arithmetic and copies ran while one was open for 1% -> 2% of each run, Pallas kernels for 18% -> 17%
where the time goes in v10:
time: 259 us; the launch traced here: 255 us
  waiting for transfers between devices  129 us (50%)
  starting transfers between devices  55.5 us (21%)
  Pallas kernels  44.3 us (17%)
  other arithmetic  11.3 us (4%)
  local copies, waits for them, and re-layouts  11.1 us (4%)
  matrix products  3.07 us (1%)
    ppermute x42, waiting for transfers between devices, shift(): return lax.ppermute(value, axis, [(i, (i + by) % n) for i in range(n)])  106 us
    ppermute x42, starting transfers between devices, shift(): return lax.ppermute(value, axis, [(i, (i + by) % n) for i in range(n)])  45.4 us
    pallas_call x4, Pallas kernels, experts(): pl.pallas_call(experts_kernel, grid=(2 * half,), in_specs=rows_in + [into...  44.3 us
    unnamed x33, local copies, waits for them, and re-layouts  10.7 us
    convert_element_type x16, other arithmetic, add(): return total.astype(BF16)  9.43 us
    ppermute x1, waiting for transfers between devices, to_owner_across(): return lax.ppermute(value, ('zh', 'core', 'yh', 'yl', 'zl'), pairs)  9.4 us
    ppermute x1, waiting for transfers between devices, to_next_section(): lax.ppermute(value, ('zh', 'core'), [(s, (s + 1) % 4) for s in range(4)])  8.96 us
    ppermute x1, starting transfers between devices, to_owner(): return lax.ppermute(value, ('zh', 'core', 'zl'), pairs)  6.87 us
  transfers between devices with their start and end apart: 46, of which 25 were waited for; matrix products, arithmetic and copies ran while one was open for 2% of the time, Pallas kernels for 17%

profile of v10, /device:TPU:0, one launch (start us, length us, event | category | flops | bytes accessed | tf_op | source)
XLA Modules:
  0.0 255.2 jit_solution(16711803965612831057)
XLA Ops:
  2.0 3.2 %collective-permute-start = (bf16[48,6144]{1,0:T(8,128)(2,1)S(1)}, bf16[48,6144]{1,0:T(8,128)(2,1)S(1)}, u32[]{:S(2)}, u32[]{:S(2)}) collective-permute-start(bf16[48,6144]{1,0:T(8,128)(2,1)S(1)} %convolution_convert_fusion.1), channel_id=1, source_target_pairs={{0,24},{8,16},{16,8},{24,0},{1,25},{9,17},{17,9},{25,1},{2,26},{10... | collective-permute-start | bytes 1769480 | tf_op jit(solution)/shard_map/ppermute | solution.py:36
  5.6 1.6 collective-permute-start.7
  7.3 1.7 collective-permute-start.8
  9.1 6.3 %collective-permute-done.7 = bf16[24,6144]{1,0:T(8,128)(2,1)S(1)} collective-permute-done((bf16[24,6144]{1,0:T(8,128)(2,1)S(1)}, bf16[24,6144]{1,0:T(8,128)(2,1)S(1)}, u32[]{:S(2)}, u32[]{:S(2)}) %collective-permute-start.7) | collective-permute-done | bytes 294944 | tf_op jit(solution)/shard_map/ppermute | solution.py:16
  15.6 2.9 %collective-permute-done = bf16[48,6144]{1,0:T(8,128)(2,1)S(1)} collective-permute-done((bf16[48,6144]{1,0:T(8,128)(2,1)S(1)}, bf16[48,6144]{1,0:T(8,128)(2,1)S(1)}, u32[]{:S(2)}, u32[]{:S(2)}) %collective-permute-start) | collective-permute-done | bytes 589856 | tf_op jit(solution)/shard_map/ppermute | solution.py:36
  18.6 1.6 collective-permute-start.5
  20.1 1.7 collective-permute-start.3
  21.9 1.9 collective-permute-start.2
  24.1 2.5 collective-permute-done.9
  27.8 4.0 %collective-permute-done.2 = bf16[24,6144]{1,0:T(8,128)(2,1)S(1)} collective-permute-done((bf16[24,6144]{1,0:T(8,128)(2,1)S(1)}, bf16[24,6144]{1,0:T(8,128)(2,1)S(1)}, u32[]{:S(2)}, u32[]{:S(2)}) %collective-permute-start.2) | collective-permute-done | bytes 294944 | tf_op jit(solution)/shard_map/ppermute | solution.py:16
  31.8 1.5 collective-permute-start.4
  33.9 7.6 %collective-permute-done.4 = bf16[24,6144]{1,0:T(8,128)(2,1)S(1)} collective-permute-done((bf16[24,6144]{1,0:T(8,128)(2,1)S(1)}, bf16[24,6144]{1,0:T(8,128)(2,1)S(1)}, u32[]{:S(2)}, u32[]{:S(2)}) %collective-permute-start.4) | collective-permute-done | bytes 294944 | tf_op jit(solution)/shard_map/ppermute | solution.py:16
  41.5 3.2 %collective-permute-start.6 = (bf16[96,6144]{1,0:T(8,128)(2,1)S(1)}, bf16[96,6144]{1,0:T(8,128)(2,1)}, u32[]{:S(2)}, u32[]{:S(2)}) collective-permute-start(bf16[96,6144]{1,0:T(8,128)(2,1)S(1)} %pad_maximum_fusion.refs_0_), channel_id=1, source_target_pairs={{0,6},{2,0},{4,2},{6,4},{1,7},{3,1},{5,3},{7,5},{8,14},{10,8},{12,... | collective-permute-start | bytes 3538952 | tf_op jit(solution)/shard_map/ppermute | solution.py:16
  44.7 2.2 collective-permute-start.14
  47.0 2.8 %copy-done.3 = bf16[1,512,6144]{2,1,0:T(8,128)(2,1)S(1)} copy-done((bf16[1,512,6144]{2,1,0:T(8,128)(2,1)S(1)}, bf16[1,512,6144]{2,1,0:T(8,128)(2,1)}, u32[]{:S(2)}) %copy-start.3) | copy-done | bytes 6291480
  49.8 8.7 %experts.4 = (bf16[96,6144]{1,0:T(8,128)(2,1)S(1)}, bf16[96,6144]{1,0:T(8,128)(2,1)S(1)}, bf16[96,6144]{1,0:T(8,128)(2,1)S(1)}) custom-call(bf16[96,6144]{1,0:T(8,128)(2,1)S(1)} %pad_maximum_fusion.refs_0_, bf16[96,6144]{1,0:T(8,128)(2,1)S(1)} %pad_maximum_fusion.1.refs_1_, bf16[96,6144]{1,0:T(8,128)(2,1)S(1)} %pad_maximum_fusion.2.refs_2_, ...), custom_call_target="tpu_custom_call" | custom-call | flops 5435817984 | bytes 25952256 | tf_op jit(solution)/shard_map/experts/pallas_call | solution.py:141
  58.9 12.0 %collective-permute-done.14.refs_4_ = bf16[96,6144]{1,0:T(8,128)(2,1)S(1)} collective-permute-done((bf16[96,6144]{1,0:T(8,128)(2,1)S(1)}, bf16[96,6144]{1,0:T(8,128)(2,1)S(1)}, u32[]{:S(2)}, u32[]{:S(2)}) %collective-permute-start.14) | collective-permute-done | bytes 1179680 | tf_op jit(solution)/shard_map/ppermute | solution.py:16
  70.9 2.0 collective-permute-start.19
  73.0 3.2 %collective-permute-start.21 = (bf16[96,6144]{1,0:T(8,128)(2,1)S(1)}, bf16[96,6144]{1,0:T(8,128)(2,1)S(1)}, u32[]{:S(2)}, u32[]{:S(2)}) collective-permute-start(bf16[96,6144]{1,0:T(8,128)(2,1)S(1)} %constant_dynamic-update-slice_fusion.refs_2_), channel_id=1, source_target_pairs={{0,6},{2,0},{4,2},{6,4},{1,7},{3,1},{5,3},{7,5},{8,14},{10,8},{12,... | collective-permute-start | bytes 3538952 | tf_op jit(solution)/shard_map/ppermute | solution.py:16
  76.3 13.8 %experts.5 = (bf16[96,6144]{1,0:T(8,128)(2,1)S(1)}, bf16[96,6144]{1,0:T(8,128)(2,1)S(1)}, bf16[96,6144]{1,0:T(8,128)(2,1)S(1)}, bf16[96,6144]{1,0:T(8,128)(2,1)S(1)}, bf16[96,6144]{1,0:T(8,128)(2,1)S(1)}) custom-call(bf16[96,6144]{1,0:T(8,128)(2,1)S(1)} %collective-permute-done.12.refs_0_, bf16[96,6144]{1,0:T(8,128)(2,1)} %collective-permute-done.6.refs_1_, ...), custom_call_target="tpu_custom_call" | custom-call | flops 9059696640 | bytes 30670848 | tf_op jit(solution)/shard_map/experts/pallas_call | solution.py:141
  91.4 8.0 %collective-permute-done.19.refs_3_ = bf16[96,6144]{1,0:T(8,128)(2,1)S(1)} collective-permute-done((bf16[96,6144]{1,0:T(8,128)(2,1)S(1)}, bf16[96,6144]{1,0:T(8,128)(2,1)S(1)}, u32[]{:S(2)}, u32[]{:S(2)}) %collective-permute-start.19) | collective-permute-done | bytes 1179680 | tf_op jit(solution)/shard_map/ppermute | solution.py:16
  99.4 2.6 %collective-permute-done.21.refs_1_ = bf16[96,6144]{1,0:T(8,128)(2,1)S(1)} collective-permute-done((bf16[96,6144]{1,0:T(8,128)(2,1)S(1)}, bf16[96,6144]{1,0:T(8,128)(2,1)S(1)}, u32[]{:S(2)}, u32[]{:S(2)}) %collective-permute-start.21) | collective-permute-done | bytes 1179680 | tf_op jit(solution)/shard_map/ppermute | solution.py:16
  103.0 1.3 copy-done.6
  105.6 10.9 %experts.6 = (bf16[96,6144]{1,0:T(8,128)(2,1)S(1)}, bf16[96,6144]{1,0:T(8,128)(2,1)S(1)}, bf16[96,6144]{1,0:T(8,128)(2,1)S(1)}, bf16[96,6144]{1,0:T(8,128)(2,1)S(1)}) custom-call(bf16[96,6144]{1,0:T(8,128)(2,1)S(1)} %collective-permute-done.16.refs_0_, bf16[96,6144]{1,0:T(8,128)(2,1)S(1)} %copy-done.10, bf16[96,6144]{1,0:T(8,128)(2,1)S(1)} %copy-done.6, ...), custom_call_target="tpu_custom_call" | custom-call | flops 7247757312 | bytes 28311552 | tf_op jit(solution)/shard_map/experts/pallas_call | solution.py:141
  116.5 5.8 %collective-permute-done.15.refs_0_ = bf16[96,6144]{1,0:T(8,128)(2,1)S(1)} collective-permute-done((bf16[96,6144]{1,0:T(8,128)(2,1)}, bf16[96,6144]{1,0:T(8,128)(2,1)S(1)}, u32[]{:S(2)}, u32[]{:S(2)}) %collective-permute-start.15) | collective-permute-done | bytes 1179680 | tf_op jit(solution)/shard_map/ppermute | solution.py:16
  122.3 3.4 %collective-permute-start.23 = (bf16[96,6144]{1,0:T(8,128)(2,1)S(1)}, bf16[96,6144]{1,0:T(8,128)(2,1)}, u32[]{:S(2)}, u32[]{:S(2)}) collective-permute-start(bf16[96,6144]{1,0:T(8,128)(2,1)S(1)} %get-tuple-element.120), channel_id=1, source_target_pairs={{0,6},{2,0},{4,2},{6,4},{1,7},{3,1},{5,3},{7,5},{8,14},{10,8},{12,... | collective-permute-start | bytes 3538952 | tf_op jit(solution)/shard_map/ppermute | solution.py:16
  128.2 10.9 %experts.7 = (bf16[96,6144]{1,0:T(8,128)(2,1)S(1)}, bf16[96,6144]{1,0:T(8,128)(2,1)S(1)}, bf16[96,6144]{1,0:T(8,128)(2,1)S(1)}, bf16[96,6144]{1,0:T(8,128)(2,1)S(1)}) custom-call(bf16[96,6144]{1,0:T(8,128)(2,1)S(1)} %collective-permute-done.15.refs_0_, bf16[96,6144]{1,0:T(8,128)(2,1)S(1)} %copy-done.8, bf16[96,6144]{1,0:T(8,128)(2,1)S(1)} %collective-permute-done.18.refs_2_, ...), custom_call_target="tpu_custom_call" | custom-call | flops 7247757312 | bytes 28311552 | tf_op jit(solution)/shard_map/experts/pallas_call | solution.py:141
  139.1 4.5 %collective-permute-done.26 = bf16[96,6144]{1,0:T(8,128)(2,1)} collective-permute-done((bf16[96,6144]{1,0:T(8,128)(2,1)S(1)}, bf16[96,6144]{1,0:T(8,128)(2,1)}, u32[]{:S(2)}, u32[]{:S(2)}) %collective-permute-start.26) | collective-permute-done | bytes 1179680 | tf_op jit(solution)/shard_map/ppermute | solution.py:16
  143.6 2.0 collective-permute-done.24
  146.6 2.2 collective-permute-start.27
  148.8 3.2 %collective-permute-start.29 = (bf16[96,6144]{1,0:T(8,128)(2,1)S(1)}, bf16[96,6144]{1,0:T(8,128)(2,1)S(1)}, u32[]{:S(2)}, u32[]{:S(2)}) collective-permute-start(bf16[96,6144]{1,0:T(8,128)(2,1)S(1)} %get-tuple-element.128), channel_id=1, source_target_pairs={{0,6},{2,0},{4,2},{6,4},{1,7},{3,1},{5,3},{7,5},{8,14},{10,8},{12,... | collective-permute-start | bytes 3538952 | tf_op jit(solution)/shard_map/ppermute | solution.py:16
  152.6 21.3 %collective-permute-done.28 = bf16[96,6144]{1,0:T(8,128)(2,1)S(1)} collective-permute-done((bf16[96,6144]{1,0:T(8,128)(2,1)S(1)}, bf16[96,6144]{1,0:T(8,128)(2,1)S(1)}, u32[]{:S(2)}, u32[]{:S(2)}) %collective-permute-start.28) | collective-permute-done | bytes 1179680 | tf_op jit(solution)/shard_map/ppermute | solution.py:16
  174.9 3.2 %collective-permute-start.32 = (bf16[96,6144]{1,0:T(8,128)(2,1)S(1)}, bf16[96,6144]{1,0:T(8,128)(2,1)S(1)}, u32[]{:S(2)}, u32[]{:S(2)}) collective-permute-start(bf16[96,6144]{1,0:T(8,128)(2,1)S(1)} %add_convert_fusion.2), channel_id=1, source_target_pairs={{0,6},{2,0},{4,2},{6,4},{1,7},{3,1},{5,3},{7,5},{8,14},{10,8},{12,... | collective-permute-start | bytes 3538952 | tf_op jit(solution)/shard_map/ppermute | solution.py:16
  178.4 9.0 %collective-permute-done.35 = f32[4,128]{1,0:T(4,128)S(1)} collective-permute-done((f32[4,128]{1,0:T(4,128)S(1)}, f32[4,128]{1,0:T(4,128)S(1)}, u32[]{:S(2)}, u32[]{:S(2)}) %collective-permute-start.35) | collective-permute-done | bytes 2080 | tf_op jit(solution)/shard_map/ppermute | solution.py:40
  187.4 9.7 %collective-permute-done.31 = bf16[96,6144]{1,0:T(8,128)(2,1)S(1)} collective-permute-done((bf16[96,6144]{1,0:T(8,128)(2,1)S(1)}, bf16[96,6144]{1,0:T(8,128)(2,1)S(1)}, u32[]{:S(2)}, u32[]{:S(2)}) %collective-permute-start.31) | collective-permute-done | bytes 1179680 | tf_op jit(solution)/shard_map/ppermute | solution.py:16
  199.1 2.8 %collective-permute-start.36 = (bf16[48,6144]{1,0:T(8,128)(2,1)S(1)}, bf16[48,6144]{1,0:T(8,128)(2,1)S(1)}, u32[]{:S(2)}, u32[]{:S(2)}) collective-permute-start(bf16[48,6144]{1,0:T(8,128)(2,1)S(1)} %pad_maximum_fusion.5), channel_id=1, source_target_pairs={{0,6},{2,0},{4,2},{6,4},{1,7},{3,1},{5,3},{7,5},{8,14},{10,8},{12,... | collective-permute-start | bytes 1769480 | tf_op jit(solution)/shard_map/ppermute | solution.py:16
  202.3 1.4 add_convert_fusion.5
  205.4 5.1 %collective-permute-done.36 = bf16[48,6144]{1,0:T(8,128)(2,1)S(1)} collective-permute-done((bf16[48,6144]{1,0:T(8,128)(2,1)S(1)}, bf16[48,6144]{1,0:T(8,128)(2,1)S(1)}, u32[]{:S(2)}, u32[]{:S(2)}) %collective-permute-start.36) | collective-permute-done | bytes 589856 | tf_op jit(solution)/shard_map/ppermute | solution.py:16
  210.5 6.0 %collective-permute-done.37 = bf16[48,6144]{1,0:T(8,128)(2,1)S(1)} collective-permute-done((bf16[48,6144]{1,0:T(8,128)(2,1)S(1)}, bf16[48,6144]{1,0:T(8,128)(2,1)S(1)}, u32[]{:S(2)}, u32[]{:S(2)}) %collective-permute-start.37) | collective-permute-done | bytes 589856 | tf_op jit(solution)/shard_map/ppermute | solution.py:16
  220.4 1.3 collective-permute-start.43
  222.4 2.6 %collective-permute-start.40 = (bf16[24,6144]{1,0:T(8,128)(2,1)S(1)}, bf16[24,6144]{1,0:T(8,128)(2,1)S(1)}, u32[]{:S(2)}, u32[]{:S(2)}) collective-permute-start(bf16[24,6144]{1,0:T(8,128)(2,1)S(1)} %add_convert_fusion.13), channel_id=1, source_target_pairs={{0,6},{2,0},{4,2},{6,4},{1,7},{3,1},{5,3},{7,5},{8,14},{10,8},{12,... | collective-permute-start | bytes 884744 | tf_op jit(solution)/shard_map/ppermute | solution.py:16
  225.6 1.6 collective-permute-done.43
  227.2 2.4 collective-permute-done.41
  229.6 2.0 collective-permute-done.42
  234.5 6.9 %collective-permute-start.44 = (bf16[48,6144]{1,0:T(8,128)(2,1)S(1)}, bf16[48,6144]{1,0:T(8,128)(2,1)S(1)}, u32[]{:S(2)}, u32[]{:S(2)}) collective-permute-start(bf16[48,6144]{1,0:T(8,128)(2,1)S(1)} %pad_maximum_fusion.7), channel_id=1, source_target_pairs={{0,33},{1,32},{32,65},{33,64},{64,97},{65,96},{96,1},{97,0},{2,35}... | collective-permute-start | bytes 1769480 | tf_op jit(solution)/shard_map/ppermute | solution.py:45
  241.4 9.4 %collective-permute-done.45 = bf16[48,6144]{1,0:T(8,128)(2,1)S(1)} collective-permute-done((bf16[48,6144]{1,0:T(8,128)(2,1)S(1)}, bf16[48,6144]{1,0:T(8,128)(2,1)S(1)}, u32[]{:S(2)}, u32[]{:S(2)}) %collective-permute-start.45) | collective-permute-done | bytes 589856 | tf_op jit(solution)/shard_map/ppermute | solution.py:55
  251.4 2.0 collective-permute-done.44
  253.4 1.8 fusion.2
  (128 shorter events, 27.2 us)
Async XLA Ops:
  2.0 16.5 %collective-permute-start = (bf16[48,6144]{1,0:T(8,128)(2,1)S(1)}, bf16[48,6144]{1,0:T(8,128)(2,1)S(1)}, u32[]{:S(2)}, u32[]{:S(2)}) collective-permute-start(bf16[48,6144]{1,0:T(8,128)(2,1)S(1)} %convolution_convert_fusion.1), channel_id=1, source_target_pairs={{0,24},{8,16},{16,8},{24,0},{1,25},{9,17},{17,9},{25,1},{2,26},{10... | collective-permute-start | bytes 1769480 | tf_op jit(solution)/shard_map/ppermute | solution.py:36
  5.2 41.8 %slice-start = ((s8[6291456]{0:T(1024)(128)(4,1)}), s8[4194304]{0:T(1024)(128)(4,1)S(1)}, s32[]{:S(2)}) async-start(s8[6291456]{0:T(1024)(128)(4,1)} %bitcast.38), calls=%async_computation | async-start | bytes 8388608
  5.6 9.7 %collective-permute-start.7 = (bf16[24,6144]{1,0:T(8,128)(2,1)S(1)}, bf16[24,6144]{1,0:T(8,128)(2,1)S(1)}, u32[]{:S(2)}, u32[]{:S(2)}) collective-permute-start(bf16[24,6144]{1,0:T(8,128)(2,1)S(1)} %get-tuple-element.169), channel_id=1, source_target_pairs={{0,2},{2,4},{4,6},{6,0},{1,3},{3,5},{5,7},{7,1},{8,10},{10,12},{12... | collective-permute-start | bytes 884744 | tf_op jit(solution)/shard_map/ppermute | solution.py:16
  7.2 8.5 %collective-permute-start.1 = (bf16[24,6144]{1,0:T(8,128)(2,1)S(1)}, bf16[24,6144]{1,0:T(8,128)(2,1)S(1)}, u32[]{:S(2)}, u32[]{:S(2)}) collective-permute-start(bf16[24,6144]{1,0:T(8,128)(2,1)S(1)} %get-tuple-element.170), channel_id=1, source_target_pairs={{0,8},{8,0},{1,9},{9,1},{2,10},{10,2},{3,11},{11,3},{4,12},{12,4},... | collective-permute-start | bytes 884744 | tf_op jit(solution)/shard_map/ppermute | solution.py:16
  7.3 16.6 %collective-permute-start.8 = (bf16[24,6144]{1,0:T(8,128)(2,1)S(1)}, bf16[24,6144]{1,0:T(8,128)(2,1)S(1)}, u32[]{:S(2)}, u32[]{:S(2)}) collective-permute-start(bf16[24,6144]{1,0:T(8,128)(2,1)S(1)} %get-tuple-element.169), channel_id=1, source_target_pairs={{0,6},{2,0},{4,2},{6,4},{1,7},{3,1},{5,3},{7,5},{8,14},{10,8},{12,... | collective-permute-start | bytes 884744 | tf_op jit(solution)/shard_map/ppermute | solution.py:16
  15.4 11.2 %collective-permute-start.9 = (bf16[24,6144]{1,0:T(8,128)(2,1)S(1)}, bf16[24,6144]{1,0:T(8,128)(2,1)S(1)}, u32[]{:S(2)}, u32[]{:S(2)}) collective-permute-start(bf16[24,6144]{1,0:T(8,128)(2,1)S(1)} %collective-permute-done.7), channel_id=1, source_target_pairs={{0,2},{2,4},{4,6},{6,0},{1,3},{3,5},{5,7},{7,1},{8,10},{10,12},{12... | collective-permute-start | bytes 884744 | tf_op jit(solution)/shard_map/ppermute | solution.py:16
  18.6 15.3 %collective-permute-start.5 = (bf16[24,6144]{1,0:T(8,128)(2,1)S(1)}, bf16[24,6144]{1,0:T(8,128)(2,1)S(1)}, u32[]{:S(2)}, u32[]{:S(2)}) collective-permute-start(bf16[24,6144]{1,0:T(8,128)(2,1)S(1)} %get-tuple-element.171), channel_id=1, source_target_pairs={{0,2},{2,4},{4,6},{6,0},{1,3},{3,5},{5,7},{7,1},{8,10},{10,12},{12... | collective-permute-start | bytes 884744 | tf_op jit(solution)/shard_map/ppermute | solution.py:16
  20.1 7.7 %collective-permute-start.3 = (bf16[24,6144]{1,0:T(8,128)(2,1)S(1)}, bf16[24,6144]{1,0:T(8,128)(2,1)S(1)}, u32[]{:S(2)}, u32[]{:S(2)}) collective-permute-start(bf16[24,6144]{1,0:T(8,128)(2,1)S(1)} %get-tuple-element.171), channel_id=1, source_target_pairs={{0,6},{2,0},{4,2},{6,4},{1,7},{3,1},{5,3},{7,5},{8,14},{10,8},{12,... | collective-permute-start | bytes 884744 | tf_op jit(solution)/shard_map/ppermute | solution.py:16
  21.9 9.9 %collective-permute-start.2 = (bf16[24,6144]{1,0:T(8,128)(2,1)S(1)}, bf16[24,6144]{1,0:T(8,128)(2,1)S(1)}, u32[]{:S(2)}, u32[]{:S(2)}) collective-permute-start(bf16[24,6144]{1,0:T(8,128)(2,1)S(1)} %get-tuple-element.172), channel_id=1, source_target_pairs={{0,1},{1,0},{2,3},{3,2},{4,5},{5,4},{6,7},{7,6},{8,9},{9,8},{10,11... | collective-permute-start | bytes 884744 | tf_op jit(solution)/shard_map/ppermute | solution.py:16
  23.9 20.8 %collective-permute-start.13 = (bf16[48,6144]{1,0:T(8,128)(2,1)S(1)}, bf16[48,6144]{1,0:T(8,128)(2,1)S(1)}, u32[]{:S(2)}, u32[]{:S(2)}) collective-permute-start(bf16[48,6144]{1,0:T(8,128)(2,1)S(1)} %pad_maximum_fusion.4), channel_id=1, source_target_pairs={{0,1},{1,0},{2,3},{3,2},{4,5},{5,4},{6,7},{7,6},{8,9},{9,8},{10,11... | collective-permute-start | bytes 1769480 | tf_op jit(solution)/shard_map/ppermute | solution.py:16
  26.6 31.9 %collective-permute-start.10 = (bf16[96,6144]{1,0:T(8,128)(2,1)S(1)}, bf16[96,6144]{1,0:T(8,128)(2,1)S(1)}, u32[]{:S(2)}, u32[]{:S(2)}) collective-permute-start(bf16[96,6144]{1,0:T(8,128)(2,1)S(1)} %pad_maximum_fusion.1.refs_1_), channel_id=1, source_target_pairs={{0,8},{8,0},{1,9},{9,1},{2,10},{10,2},{3,11},{11,3},{4,12},{12,4},... | collective-permute-start | bytes 3538952 | tf_op jit(solution)/shard_map/ppermute | solution.py:16
  31.8 9.6 %collective-permute-start.4 = (bf16[24,6144]{1,0:T(8,128)(2,1)S(1)}, bf16[24,6144]{1,0:T(8,128)(2,1)S(1)}, u32[]{:S(2)}, u32[]{:S(2)}) collective-permute-start(bf16[24,6144]{1,0:T(8,128)(2,1)S(1)} %collective-permute-done.3), channel_id=1, source_target_pairs={{0,6},{2,0},{4,2},{6,4},{1,7},{3,1},{5,3},{7,5},{8,14},{10,8},{12,... | collective-permute-start | bytes 884744 | tf_op jit(solution)/shard_map/ppermute | solution.py:16
  33.5 39.4 %collective-permute-start.11 = (bf16[48,6144]{1,0:T(8,128)(2,1)S(1)}, bf16[48,6144]{1,0:T(8,128)(2,1)S(1)}, u32[]{:S(2)}, u32[]{:S(2)}) collective-permute-start(bf16[48,6144]{1,0:T(8,128)(2,1)S(1)} %pad_maximum_fusion.3), channel_id=1, source_target_pairs={{0,8},{8,0},{1,9},{9,1},{2,10},{10,2},{3,11},{11,3},{4,12},{12,4},... | collective-permute-start | bytes 1769480 | tf_op jit(solution)/shard_map/ppermute | solution.py:16
  41.5 31.4 %collective-permute-start.12 = (bf16[96,6144]{1,0:T(8,128)(2,1)S(1)}, bf16[96,6144]{1,0:T(8,128)(2,1)S(1)}, u32[]{:S(2)}, u32[]{:S(2)}) collective-permute-start(bf16[96,6144]{1,0:T(8,128)(2,1)S(1)} %pad_maximum_fusion.refs_0_), channel_id=1, source_target_pairs={{0,2},{2,4},{4,6},{6,0},{1,3},{3,5},{5,7},{7,1},{8,10},{10,12},{12... | collective-permute-start | bytes 3538952 | tf_op jit(solution)/shard_map/ppermute | solution.py:16
  41.5 34.8 %collective-permute-start.6 = (bf16[96,6144]{1,0:T(8,128)(2,1)S(1)}, bf16[96,6144]{1,0:T(8,128)(2,1)}, u32[]{:S(2)}, u32[]{:S(2)}) collective-permute-start(bf16[96,6144]{1,0:T(8,128)(2,1)S(1)} %pad_maximum_fusion.refs_0_), channel_id=1, source_target_pairs={{0,6},{2,0},{4,2},{6,4},{1,7},{3,1},{5,3},{7,5},{8,14},{10,8},{12,... | collective-permute-start | bytes 3538952 | tf_op jit(solution)/shard_map/ppermute | solution.py:16
  44.7 26.2 %collective-permute-start.14 = (bf16[96,6144]{1,0:T(8,128)(2,1)S(1)}, bf16[96,6144]{1,0:T(8,128)(2,1)S(1)}, u32[]{:S(2)}, u32[]{:S(2)}) collective-permute-start(bf16[96,6144]{1,0:T(8,128)(2,1)S(1)} %pad_maximum_fusion.1.refs_1_), channel_id=1, source_target_pairs={{0,1},{1,0},{2,3},{3,2},{4,5},{5,4},{6,7},{7,6},{8,9},{9,8},{10,11... | collective-permute-start | bytes 3538952 | tf_op jit(solution)/shard_map/ppermute | solution.py:16
  49.8 26.4 %copy-start.4 = (bf16[1,512,6144]{2,1,0:T(8,128)(2,1)S(1)}, bf16[1,512,6144]{2,1,0:T(8,128)(2,1)}, u32[]{:S(2)}) copy-start(bf16[1,512,6144]{2,1,0:T(8,128)(2,1)} %param.13) | copy-start | bytes 18874372
  58.5 31.8 %collective-permute-start.22 = (bf16[96,6144]{1,0:T(8,128)(2,1)S(1)}, bf16[96,6144]{1,0:T(8,128)(2,1)S(1)}, u32[]{:S(2)}, u32[]{:S(2)}) collective-permute-start(bf16[96,6144]{1,0:T(8,128)(2,1)S(1)} %pad_maximum_fusion.2.refs_2_), channel_id=1, source_target_pairs={{0,8},{8,0},{1,9},{9,1},{2,10},{10,2},{3,11},{11,3},{4,12},{12,4},... | collective-permute-start | bytes 3538952 | tf_op jit(solution)/shard_map/ppermute | solution.py:16
  70.9 28.5 %collective-permute-start.19 = (bf16[96,6144]{1,0:T(8,128)(2,1)S(1)}, bf16[96,6144]{1,0:T(8,128)(2,1)S(1)}, u32[]{:S(2)}, u32[]{:S(2)}) collective-permute-start(bf16[96,6144]{1,0:T(8,128)(2,1)S(1)} %pad_maximum_fusion.2.refs_2_), channel_id=1, source_target_pairs={{0,1},{1,0},{2,3},{3,2},{4,5},{5,4},{6,7},{7,6},{8,9},{9,8},{10,11... | collective-permute-start | bytes 3538952 | tf_op jit(solution)/shard_map/ppermute | solution.py:16
  72.9 26.4 %collective-permute-start.16 = (bf16[96,6144]{1,0:T(8,128)(2,1)S(1)}, bf16[96,6144]{1,0:T(8,128)(2,1)S(1)}, u32[]{:S(2)}, u32[]{:S(2)}) collective-permute-start(bf16[96,6144]{1,0:T(8,128)(2,1)S(1)} %constant_dynamic-update-slice_fusion.refs_2_), channel_id=1, source_target_pairs={{0,2},{2,4},{4,6},{6,0},{1,3},{3,5},{5,7},{7,1},{8,10},{10,12},{12... | collective-permute-start | bytes 3538952 | tf_op jit(solution)/shard_map/ppermute | solution.py:16
  73.0 29.0 %collective-permute-start.21 = (bf16[96,6144]{1,0:T(8,128)(2,1)S(1)}, bf16[96,6144]{1,0:T(8,128)(2,1)S(1)}, u32[]{:S(2)}, u32[]{:S(2)}) collective-permute-start(bf16[96,6144]{1,0:T(8,128)(2,1)S(1)} %constant_dynamic-update-slice_fusion.refs_2_), channel_id=1, source_target_pairs={{0,6},{2,0},{4,2},{6,4},{1,7},{3,1},{5,3},{7,5},{8,14},{10,8},{12,... | collective-permute-start | bytes 3538952 | tf_op jit(solution)/shard_map/ppermute | solution.py:16
  90.1 32.2 %collective-permute-start.15 = (bf16[96,6144]{1,0:T(8,128)(2,1)}, bf16[96,6144]{1,0:T(8,128)(2,1)S(1)}, u32[]{:S(2)}, u32[]{:S(2)}) collective-permute-start(bf16[96,6144]{1,0:T(8,128)(2,1)} %collective-permute-done.6.refs_1_), channel_id=1, source_target_pairs={{0,6},{2,0},{4,2},{6,4},{1,7},{3,1},{5,3},{7,5},{8,14},{10,8},{12,... | collective-permute-start | bytes 3538952 | tf_op jit(solution)/shard_map/ppermute | solution.py:16
  91.4 34.3 %collective-permute-start.18 = (bf16[96,6144]{1,0:T(8,128)(2,1)S(1)}, bf16[96,6144]{1,0:T(8,128)(2,1)S(1)}, u32[]{:S(2)}, u32[]{:S(2)}) collective-permute-start(bf16[96,6144]{1,0:T(8,128)(2,1)S(1)} %collective-permute-done.10.refs_3_), channel_id=1, source_target_pairs={{0,1},{1,0},{2,3},{3,2},{4,5},{5,4},{6,7},{7,6},{8,9},{9,8},{10,11... | collective-permute-start | bytes 3538952 | tf_op jit(solution)/shard_map/ppermute | solution.py:16
  99.4 26.5 %collective-permute-start.20 = (bf16[96,6144]{1,0:T(8,128)(2,1)S(1)}, bf16[96,6144]{1,0:T(8,128)(2,1)S(1)}, u32[]{:S(2)}, u32[]{:S(2)}) collective-permute-start(bf16[96,6144]{1,0:T(8,128)(2,1)S(1)} %collective-permute-done.19.refs_3_), channel_id=1, source_target_pairs={{0,8},{8,0},{1,9},{9,1},{2,10},{10,2},{3,11},{11,3},{4,12},{12,4},... | collective-permute-start | bytes 3538952 | tf_op jit(solution)/shard_map/ppermute | solution.py:16
  99.4 26.5 %collective-permute-start.17 = (bf16[96,6144]{1,0:T(8,128)(2,1)S(1)}, bf16[96,6144]{1,0:T(8,128)(2,1)S(1)}, u32[]{:S(2)}, u32[]{:S(2)}) collective-permute-start(bf16[96,6144]{1,0:T(8,128)(2,1)S(1)} %collective-permute-done.16.refs_0_), channel_id=1, source_target_pairs={{0,2},{2,4},{4,6},{6,0},{1,3},{3,5},{5,7},{7,1},{8,10},{10,12},{12... | collective-permute-start | bytes 3538952 | tf_op jit(solution)/shard_map/ppermute | solution.py:16
  103.0 40.6 %collective-permute-start.26 = (bf16[96,6144]{1,0:T(8,128)(2,1)S(1)}, bf16[96,6144]{1,0:T(8,128)(2,1)}, u32[]{:S(2)}, u32[]{:S(2)}) collective-permute-start(bf16[96,6144]{1,0:T(8,128)(2,1)S(1)} %get-tuple-element.123), channel_id=1, source_target_pairs={{0,1},{1,0},{2,3},{3,2},{4,5},{5,4},{6,7},{7,6},{8,9},{9,8},{10,11... | collective-permute-start | bytes 3538952 | tf_op jit(solution)/shard_map/ppermute | solution.py:16
  122.3 21.3 %collective-permute-start.23 = (bf16[96,6144]{1,0:T(8,128)(2,1)S(1)}, bf16[96,6144]{1,0:T(8,128)(2,1)}, u32[]{:S(2)}, u32[]{:S(2)}) collective-permute-start(bf16[96,6144]{1,0:T(8,128)(2,1)S(1)} %get-tuple-element.120), channel_id=1, source_target_pairs={{0,6},{2,0},{4,2},{6,4},{1,7},{3,1},{5,3},{7,5},{8,14},{10,8},{12,... | collective-permute-start | bytes 3538952 | tf_op jit(solution)/shard_map/ppermute | solution.py:16
  125.7 17.9 %collective-permute-start.25 = (bf16[96,6144]{1,0:T(8,128)(2,1)S(1)}, bf16[96,6144]{1,0:T(8,128)(2,1)S(1)}, u32[]{:S(2)}, u32[]{:S(2)}) collective-permute-start(bf16[96,6144]{1,0:T(8,128)(2,1)S(1)} %get-tuple-element.122), channel_id=1, source_target_pairs={{0,8},{8,0},{1,9},{9,1},{2,10},{10,2},{3,11},{11,3},{4,12},{12,4},... | collective-permute-start | bytes 3538952 | tf_op jit(solution)/shard_map/ppermute | solution.py:16
  126.9 18.7 %collective-permute-start.24 = (bf16[96,6144]{1,0:T(8,128)(2,1)S(1)}, bf16[96,6144]{1,0:T(8,128)(2,1)S(1)}, u32[]{:S(2)}, u32[]{:S(2)}) collective-permute-start(bf16[96,6144]{1,0:T(8,128)(2,1)S(1)} %get-tuple-element.121), channel_id=1, source_target_pairs={{0,2},{2,4},{4,6},{6,0},{1,3},{3,5},{5,7},{7,1},{8,10},{10,12},{12... | collective-permute-start | bytes 3538952 | tf_op jit(solution)/shard_map/ppermute | solution.py:16
  146.6 28.2 %collective-permute-start.27 = (bf16[96,6144]{1,0:T(8,128)(2,1)S(1)}, bf16[96,6144]{1,0:T(8,128)(2,1)S(1)}, u32[]{:S(2)}, u32[]{:S(2)}) collective-permute-start(bf16[96,6144]{1,0:T(8,128)(2,1)S(1)} %get-tuple-element.124), channel_id=1, source_target_pairs={{0,8},{8,0},{1,9},{9,1},{2,10},{10,2},{3,11},{11,3},{4,12},{12,4},... | collective-permute-start | bytes 3538952 | tf_op jit(solution)/shard_map/ppermute | solution.py:16
  148.8 25.1 %collective-permute-start.28 = (bf16[96,6144]{1,0:T(8,128)(2,1)S(1)}, bf16[96,6144]{1,0:T(8,128)(2,1)S(1)}, u32[]{:S(2)}, u32[]{:S(2)}) collective-permute-start(bf16[96,6144]{1,0:T(8,128)(2,1)S(1)} %get-tuple-element.126), channel_id=1, source_target_pairs={{0,2},{2,4},{4,6},{6,0},{1,3},{3,5},{5,7},{7,1},{8,10},{10,12},{12... | collective-permute-start | bytes 3538952 | tf_op jit(solution)/shard_map/ppermute | solution.py:16
  148.8 25.4 %collective-permute-start.29 = (bf16[96,6144]{1,0:T(8,128)(2,1)S(1)}, bf16[96,6144]{1,0:T(8,128)(2,1)S(1)}, u32[]{:S(2)}, u32[]{:S(2)}) collective-permute-start(bf16[96,6144]{1,0:T(8,128)(2,1)S(1)} %get-tuple-element.128), channel_id=1, source_target_pairs={{0,6},{2,0},{4,2},{6,4},{1,7},{3,1},{5,3},{7,5},{8,14},{10,8},{12,... | collective-permute-start | bytes 3538952 | tf_op jit(solution)/shard_map/ppermute | solution.py:16
  152.0 22.5 %collective-permute-start.30 = (bf16[96,6144]{1,0:T(8,128)(2,1)S(1)}, bf16[96,6144]{1,0:T(8,128)(2,1)S(1)}, u32[]{:S(2)}, u32[]{:S(2)}) collective-permute-start(bf16[96,6144]{1,0:T(8,128)(2,1)S(1)} %get-tuple-element.132), channel_id=1, source_target_pairs={{0,1},{1,0},{2,3},{3,2},{4,5},{5,4},{6,7},{7,6},{8,9},{9,8},{10,11... | collective-permute-start | bytes 3538952 | tf_op jit(solution)/shard_map/ppermute | solution.py:16
  174.8 22.3 %collective-permute-start.31 = (bf16[96,6144]{1,0:T(8,128)(2,1)S(1)}, bf16[96,6144]{1,0:T(8,128)(2,1)S(1)}, u32[]{:S(2)}, u32[]{:S(2)}) collective-permute-start(bf16[96,6144]{1,0:T(8,128)(2,1)S(1)} %add_convert_fusion.3), channel_id=1, source_target_pairs={{0,2},{2,4},{4,6},{6,0},{1,3},{3,5},{5,7},{7,1},{8,10},{10,12},{12... | collective-permute-start | bytes 3538952 | tf_op jit(solution)/shard_map/ppermute | solution.py:16
  174.9 22.6 %collective-permute-start.32 = (bf16[96,6144]{1,0:T(8,128)(2,1)S(1)}, bf16[96,6144]{1,0:T(8,128)(2,1)S(1)}, u32[]{:S(2)}, u32[]{:S(2)}) collective-permute-start(bf16[96,6144]{1,0:T(8,128)(2,1)S(1)} %add_convert_fusion.2), channel_id=1, source_target_pairs={{0,6},{2,0},{4,2},{6,4},{1,7},{3,1},{5,3},{7,5},{8,14},{10,8},{12,... | collective-permute-start | bytes 3538952 | tf_op jit(solution)/shard_map/ppermute | solution.py:16
  178.1 19.4 %collective-permute-start.33 = (bf16[96,6144]{1,0:T(8,128)(2,1)S(1)}, bf16[96,6144]{1,0:T(8,128)(2,1)S(1)}, u32[]{:S(2)}, u32[]{:S(2)}) collective-permute-start(bf16[96,6144]{1,0:T(8,128)(2,1)S(1)} %add_convert_fusion.1), channel_id=1, source_target_pairs={{0,1},{1,0},{2,3},{3,2},{4,5},{5,4},{6,7},{7,6},{8,9},{9,8},{10,11... | collective-permute-start | bytes 3538952 | tf_op jit(solution)/shard_map/ppermute | solution.py:16
  178.1 19.4 %collective-permute-start.34 = (bf16[96,6144]{1,0:T(8,128)(2,1)S(1)}, bf16[96,6144]{1,0:T(8,128)(2,1)S(1)}, u32[]{:S(2)}, u32[]{:S(2)}) collective-permute-start(bf16[96,6144]{1,0:T(8,128)(2,1)S(1)} %add_convert_fusion), channel_id=1, source_target_pairs={{0,8},{8,0},{1,9},{9,1},{2,10},{10,2},{3,11},{11,3},{4,12},{12,4},... | collective-permute-start | bytes 3538952 | tf_op jit(solution)/shard_map/ppermute | solution.py:16
  178.4 9.0 %collective-permute-start.35 = (f32[4,128]{1,0:T(4,128)S(1)}, f32[4,128]{1,0:T(4,128)S(1)}, u32[]{:S(2)}, u32[]{:S(2)}) collective-permute-start(f32[4,128]{1,0:T(4,128)S(1)} %pad_maximum_fusion.9), channel_id=1, source_target_pairs={{0,32},{32,64},{64,96},{96,0},{1,33},{33,65},{65,97},{97,1},{2,34}... | collective-permute-start | bytes 6152 | tf_op jit(solution)/shard_map/ppermute | solution.py:40
  199.1 11.4 %collective-permute-start.36 = (bf16[48,6144]{1,0:T(8,128)(2,1)S(1)}, bf16[48,6144]{1,0:T(8,128)(2,1)S(1)}, u32[]{:S(2)}, u32[]{:S(2)}) collective-permute-start(bf16[48,6144]{1,0:T(8,128)(2,1)S(1)} %pad_maximum_fusion.5), channel_id=1, source_target_pairs={{0,6},{2,0},{4,2},{6,4},{1,7},{3,1},{5,3},{7,5},{8,14},{10,8},{12,... | collective-permute-start | bytes 1769480 | tf_op jit(solution)/shard_map/ppermute | solution.py:16
  201.9 14.5 %collective-permute-start.37 = (bf16[48,6144]{1,0:T(8,128)(2,1)S(1)}, bf16[48,6144]{1,0:T(8,128)(2,1)S(1)}, u32[]{:S(2)}, u32[]{:S(2)}) collective-permute-start(bf16[48,6144]{1,0:T(8,128)(2,1)S(1)} %pad_maximum_fusion.6), channel_id=1, source_target_pairs={{0,2},{2,4},{4,6},{6,0},{1,3},{3,5},{5,7},{7,1},{8,10},{10,12},{12... | collective-permute-start | bytes 1769480 | tf_op jit(solution)/shard_map/ppermute | solution.py:16
  203.6 13.1 %collective-permute-start.38 = (bf16[48,6144]{1,0:T(8,128)(2,1)S(1)}, bf16[48,6144]{1,0:T(8,128)(2,1)S(1)}, u32[]{:S(2)}, u32[]{:S(2)}) collective-permute-start(bf16[48,6144]{1,0:T(8,128)(2,1)S(1)} %add_convert_fusion.5), channel_id=1, source_target_pairs={{0,1},{1,0},{2,3},{3,2},{4,5},{5,4},{6,7},{7,6},{8,9},{9,8},{10,11... | collective-permute-start | bytes 1769480 | tf_op jit(solution)/shard_map/ppermute | solution.py:16
  204.8 13.1 %collective-permute-start.39 = (bf16[48,6144]{1,0:T(8,128)(2,1)S(1)}, bf16[48,6144]{1,0:T(8,128)(2,1)S(1)}, u32[]{:S(2)}, u32[]{:S(2)}) collective-permute-start(bf16[48,6144]{1,0:T(8,128)(2,1)S(1)} %add_convert_fusion.4), channel_id=1, source_target_pairs={{0,8},{8,0},{1,9},{9,1},{2,10},{10,2},{3,11},{11,3},{4,12},{12,4},... | collective-permute-start | bytes 1769480 | tf_op jit(solution)/shard_map/ppermute | solution.py:16
  220.4 6.8 %collective-permute-start.43 = (bf16[24,6144]{1,0:T(8,128)(2,1)S(1)}, bf16[24,6144]{1,0:T(8,128)(2,1)S(1)}, u32[]{:S(2)}, u32[]{:S(2)}) collective-permute-start(bf16[24,6144]{1,0:T(8,128)(2,1)S(1)} %add_convert_fusion.10), channel_id=1, source_target_pairs={{0,1},{1,0},{2,3},{3,2},{4,5},{5,4},{6,7},{7,6},{8,9},{9,8},{10,11... | collective-permute-start | bytes 884744 | tf_op jit(solution)/shard_map/ppermute | solution.py:16
  221.7 7.9 %collective-permute-start.41 = (bf16[24,6144]{1,0:T(8,128)(2,1)S(1)}, bf16[24,6144]{1,0:T(8,128)(2,1)S(1)}, u32[]{:S(2)}, u32[]{:S(2)}) collective-permute-start(bf16[24,6144]{1,0:T(8,128)(2,1)S(1)} %add_convert_fusion.12), channel_id=1, source_target_pairs={{0,2},{2,4},{4,6},{6,0},{1,3},{3,5},{5,7},{7,1},{8,10},{10,12},{12... | collective-permute-start | bytes 884744 | tf_op jit(solution)/shard_map/ppermute | solution.py:16
  222.4 7.3 %collective-permute-start.40 = (bf16[24,6144]{1,0:T(8,128)(2,1)S(1)}, bf16[24,6144]{1,0:T(8,128)(2,1)S(1)}, u32[]{:S(2)}, u32[]{:S(2)}) collective-permute-start(bf16[24,6144]{1,0:T(8,128)(2,1)S(1)} %add_convert_fusion.13), channel_id=1, source_target_pairs={{0,6},{2,0},{4,2},{6,4},{1,7},{3,1},{5,3},{7,5},{8,14},{10,8},{12,... | collective-permute-start | bytes 884744 | tf_op jit(solution)/shard_map/ppermute | solution.py:16
  224.9 6.7 %collective-permute-start.42 = (bf16[24,6144]{1,0:T(8,128)(2,1)S(1)}, bf16[24,6144]{1,0:T(8,128)(2,1)S(1)}, u32[]{:S(2)}, u32[]{:S(2)}) collective-permute-start(bf16[24,6144]{1,0:T(8,128)(2,1)S(1)} %add_convert_fusion.11), channel_id=1, source_target_pairs={{0,8},{8,0},{1,9},{9,1},{2,10},{10,2},{3,11},{11,3},{4,12},{12,4},... | collective-permute-start | bytes 884744 | tf_op jit(solution)/shard_map/ppermute | solution.py:16
  234.4 16.4 %collective-permute-start.45 = (bf16[48,6144]{1,0:T(8,128)(2,1)S(1)}, bf16[48,6144]{1,0:T(8,128)(2,1)S(1)}, u32[]{:S(2)}, u32[]{:S(2)}) collective-permute-start(bf16[48,6144]{1,0:T(8,128)(2,1)S(1)} %pad_maximum_fusion.8), channel_id=1, source_target_pairs={{0,57},{1,56},{8,49},{9,48},{16,41},{17,40},{24,33},{25,32},{32,89... | collective-permute-start | bytes 1769480 | tf_op jit(solution)/shard_map/ppermute | solution.py:55
  234.5 18.9 %collective-permute-start.44 = (bf16[48,6144]{1,0:T(8,128)(2,1)S(1)}, bf16[48,6144]{1,0:T(8,128)(2,1)S(1)}, u32[]{:S(2)}, u32[]{:S(2)}) collective-permute-start(bf16[48,6144]{1,0:T(8,128)(2,1)S(1)} %pad_maximum_fusion.7), channel_id=1, source_target_pairs={{0,33},{1,32},{32,65},{33,64},{64,97},{65,96},{96,1},{97,0},{2,35}... | collective-permute-start | bytes 1769480 | tf_op jit(solution)/shard_map/ppermute | solution.py:45
  (14 other events, 74.5 us)

commit v11 on v6

--- a/solution.py
+++ b/solution.py
@@ -208,19 +208,20 @@
     b_y, g_ring_out = together(b_y, g_ring)
     g_y, g_z = over_y(g_ring_out), over_z(g_ring_out)
     far = join(a1_far, a2_far)
+    b_y_sent = b_y
     near, b_ring, g_ring, b_y = experts([near, b_ring, g_ring, b_y], *matrices)
     far_left, far_right = right(far), left(far)
 
-    near_left, near_right, far, b_z, near, b_ring, g_ring, b_y = together(
-        near_left, near_right, far, b_z, near, b_ring, g_ring, b_y
-    )
-    near_opposite, b_yz = left(near_right), over_y(b_z)
+    near_left, near_right, far, b_z, near, b_ring, g_ring, b_y, b_y_sent = together(
+        near_left, near_right, far, b_z, near, b_ring, g_ring, b_y, b_y_sent
+    )
+    near_opposite, b_yz = left(near_right), over_z(b_y_sent)
     near_left, near_right, far, b_z = experts([near_left, near_right, far, b_z], *matrices)
 
     far_left, far_right, g_y, g_z, near_left, near_right, far, b_z = together(
         far_left, far_right, g_y, g_z, near_left, near_right, far, b_z
     )
-    far_opposite, g_zy = right(far_left), over_z(g_y)
+    far_opposite, g_zy = right(far_left), over_y(g_z)
     far_left, far_right, g_y, g_z = experts([far_left, far_right, g_y, g_z], *matrices)
 
     near_opposite, far_opposite, b_yz, g_zy, far_left, far_right, g_y, g_z = together(

time: 253 us -> 260 us (1.028)
  waiting for transfers between devices: 128 us -> 139 us
  starting transfers between devices: 65.1 us -> 59.5 us
    ppermute x42, waiting for transfers between devices: 93.5 us -> 105 us  [shift(): return lax.ppermute(value, axis, [(i, (i + by) % n) for i in range(n)])]
    ppermute x42, starting transfers between devices: 57.8 us -> 52.4 us  [shift(): return lax.ppermute(value, axis, [(i, (i + by) % n) for i in range(n)])]
  transfers between devices with their start and end apart: 46 -> 46, of which waited for: 25 -> 24; matrix products, arithmetic and copies ran while one was open for 2% -> 1% of each run, Pallas kernels for 17% -> 17%
where the time goes in v11:
time: 260 us; the launch traced here: 259 us
  waiting for transfers between devices  139 us (53%)
  starting transfers between devices  59.5 us (23%)
  Pallas kernels  43.7 us (17%)
  other arithmetic  8.31 us (3%)
  local copies, waits for them, and re-layouts  5.49 us (2%)
  matrix products  3.07 us (1%)
    ppermute x42, waiting for transfers between devices, shift(): return lax.ppermute(value, axis, [(i, (i + by) % n) for i in range(n)])  105 us
    ppermute x42, starting transfers between devices, shift(): return lax.ppermute(value, axis, [(i, (i + by) % n) for i in range(n)])  52.4 us
    pallas_call x4, Pallas kernels, experts(): pl.pallas_call(experts_kernel, grid=(2 * half,), in_specs=rows_in + [into...  43.7 us
    ppermute x1, waiting for transfers between devices, to_owner_across(): return lax.ppermute(value, ('zh', 'core', 'yh', 'yl', 'zl'), pairs)  13.6 us
    ppermute x1, waiting for transfers between devices, to_next_section(): lax.ppermute(value, ('zh', 'core'), [(s, (s + 1) % 4) for s in range(4)])  10.1 us
    ppermute x1, waiting for transfers between devices, to_partner(): return lax.ppermute(value, ('yh', 'yl'), [(y, 3 - y) for y in range(4)])  9.96 us
    convert_element_type x16, other arithmetic, add(): return total.astype(BF16)  6.38 us
  transfers between devices with their start and end apart: 46, of which 24 were waited for; matrix products, arithmetic and copies ran while one was open for 1% of the time, Pallas kernels for 17%

profile of v11, /device:TPU:0, one launch (start us, length us, event | category | flops | bytes accessed | tf_op | source)
XLA Modules:
  0.0 259.1 jit_solution(13959593981099740804)
XLA Ops:
  2.5 1.6 collective-permute-start.6
  4.1 1.6 collective-permute-start
  5.7 1.7 collective-permute-start.7
  7.4 2.2 collective-permute-start.1
  9.6 2.8 %collective-permute-done.6 = bf16[24,6144]{1,0:T(8,128)(2,1)S(1)} collective-permute-done((bf16[24,6144]{1,0:T(8,128)(2,1)S(1)}, bf16[24,6144]{1,0:T(8,128)(2,1)S(1)}, u32[]{:S(2)}, u32[]{:S(2)}) %collective-permute-start.6) | collective-permute-done | bytes 294944 | tf_op jit(solution)/shard_map/ppermute | solution.py:16
  12.9 10.0 %collective-permute-done.1 = bf16[48,6144]{1,0:T(8,128)(2,1)S(1)} collective-permute-done((bf16[48,6144]{1,0:T(8,128)(2,1)S(1)}, bf16[48,6144]{1,0:T(8,128)(2,1)S(1)}, u32[]{:S(2)}, u32[]{:S(2)}) %collective-permute-start.1) | collective-permute-done | bytes 589856 | tf_op jit(solution)/shard_map/ppermute | solution.py:36
  23.3 3.0 %collective-permute-start.4 = (bf16[24,6144]{1,0:T(8,128)(2,1)S(1)}, bf16[24,6144]{1,0:T(8,128)(2,1)S(1)}, u32[]{:S(2)}, u32[]{:S(2)}) collective-permute-start(bf16[24,6144]{1,0:T(8,128)(2,1)S(1)} %get-tuple-element.177), channel_id=1, source_target_pairs={{0,6},{2,0},{4,2},{6,4},{1,7},{3,1},{5,3},{7,5},{8,14},{10,8},{12,... | collective-permute-start | bytes 884744 | tf_op jit(solution)/shard_map/ppermute | solution.py:16
  26.2 1.9 collective-permute-start.2
  28.3 2.8 %collective-permute-done.5 = bf16[24,6144]{1,0:T(8,128)(2,1)S(1)} collective-permute-done((bf16[24,6144]{1,0:T(8,128)(2,1)S(1)}, bf16[24,6144]{1,0:T(8,128)(2,1)S(1)}, u32[]{:S(2)}, u32[]{:S(2)}) %collective-permute-start.5) | collective-permute-done | bytes 294944 | tf_op jit(solution)/shard_map/ppermute | solution.py:16
  31.2 3.0 %collective-permute-start.9 = (bf16[24,6144]{1,0:T(8,128)(2,1)S(1)}, bf16[24,6144]{1,0:T(8,128)(2,1)S(1)}, u32[]{:S(2)}, u32[]{:S(2)}) collective-permute-start(bf16[24,6144]{1,0:T(8,128)(2,1)S(1)} %collective-permute-done.4), channel_id=1, source_target_pairs={{0,6},{2,0},{4,2},{6,4},{1,7},{3,1},{5,3},{7,5},{8,14},{10,8},{12,... | collective-permute-start | bytes 884744 | tf_op jit(solution)/shard_map/ppermute | solution.py:16
  34.4 1.9 collective-permute-start.11
  36.5 2.5 collective-permute-done.9
  39.0 3.7 %collective-permute-start.10 = (bf16[96,6144]{1,0:T(8,128)(2,1)S(1)}, bf16[96,6144]{1,0:T(8,128)(2,1)S(1)}, u32[]{:S(2)}, u32[]{:S(2)}) collective-permute-start(bf16[96,6144]{1,0:T(8,128)(2,1)S(1)} %pad_maximum_fusion.refs_0_), channel_id=1, source_target_pairs={{0,6},{2,0},{4,2},{6,4},{1,7},{3,1},{5,3},{7,5},{8,14},{10,8},{12,... | collective-permute-start | bytes 3538952 | tf_op jit(solution)/shard_map/ppermute | solution.py:16
  42.8 5.1 %collective-permute-done.11 = bf16[48,6144]{1,0:T(8,128)(2,1)S(1)} collective-permute-done((bf16[48,6144]{1,0:T(8,128)(2,1)S(1)}, bf16[48,6144]{1,0:T(8,128)(2,1)S(1)}, u32[]{:S(2)}, u32[]{:S(2)}) %collective-permute-start.11) | collective-permute-done | bytes 589856 | tf_op jit(solution)/shard_map/ppermute | solution.py:16
  47.9 1.9 collective-permute-start.13
  49.9 16.2 %collective-permute-done.12 = bf16[48,6144]{1,0:T(8,128)(2,1)S(1)} collective-permute-done((bf16[48,6144]{1,0:T(8,128)(2,1)S(1)}, bf16[48,6144]{1,0:T(8,128)(2,1)S(1)}, u32[]{:S(2)}, u32[]{:S(2)}) %collective-permute-start.12) | collective-permute-done | bytes 589856 | tf_op jit(solution)/shard_map/ppermute | solution.py:16
  66.5 1.7 collective-permute-start.16
  68.8 2.8 %copy-done.2 = bf16[1,512,6144]{2,1,0:T(8,128)(2,1)S(1)} copy-done((bf16[1,512,6144]{2,1,0:T(8,128)(2,1)S(1)}, bf16[1,512,6144]{2,1,0:T(8,128)(2,1)}, u32[]{:S(2)}) %copy-start.2) | copy-done | bytes 6291480
  71.6 10.9 %experts.4 = (bf16[96,6144]{1,0:T(8,128)(2,1)S(1)}, bf16[96,6144]{1,0:T(8,128)(2,1)S(1)}, bf16[96,6144]{1,0:T(8,128)(2,1)S(1)}, bf16[96,6144]{1,0:T(8,128)(2,1)S(1)}) custom-call(bf16[96,6144]{1,0:T(8,128)(2,1)S(1)} %pad_maximum_fusion.refs_0_, bf16[96,6144]{1,0:T(8,128)(2,1)S(1)} %pad_maximum_fusion.1.refs_1_, ...), custom_call_target="tpu_custom_call" | custom-call | flops 7247757312 | bytes 28311552 | tf_op jit(solution)/shard_map/experts/pallas_call | solution.py:141
  82.6 1.8 collective-permute-start.15
  84.3 10.9 %experts.5 = (bf16[96,6144]{1,0:T(8,128)(2,1)S(1)}, bf16[96,6144]{1,0:T(8,128)(2,1)S(1)}, bf16[96,6144]{1,0:T(8,128)(2,1)S(1)}, bf16[96,6144]{1,0:T(8,128)(2,1)S(1)}) custom-call(bf16[96,6144]{1,0:T(8,128)(2,1)S(1)} %collective-permute-done.3.refs_0_, bf16[96,6144]{1,0:T(8,128)(2,1)S(1)} %collective-permute-done.10.refs_1_, ...), custom_call_target="tpu_custom_call" | custom-call | flops 7247757312 | bytes 28311552 | tf_op jit(solution)/shard_map/experts/pallas_call | solution.py:141
  95.3 1.8 collective-permute-start.21
  97.1 3.4 %collective-permute-done.19.refs_3_ = bf16[96,6144]{1,0:T(8,128)(2,1)S(1)} collective-permute-done((bf16[96,6144]{1,0:T(8,128)(2,1)S(1)}, bf16[96,6144]{1,0:T(8,128)(2,1)S(1)}, u32[]{:S(2)}, u32[]{:S(2)}) %collective-permute-start.19) | collective-permute-done | bytes 1179680 | tf_op jit(solution)/shard_map/ppermute | solution.py:16
  104.8 10.9 %experts.6 = (bf16[96,6144]{1,0:T(8,128)(2,1)S(1)}, bf16[96,6144]{1,0:T(8,128)(2,1)S(1)}, bf16[96,6144]{1,0:T(8,128)(2,1)S(1)}, bf16[96,6144]{1,0:T(8,128)(2,1)S(1)}) custom-call(bf16[96,6144]{1,0:T(8,128)(2,1)S(1)} %collective-permute-done.16.refs_0_, bf16[96,6144]{1,0:T(8,128)(2,1)S(1)} %collective-permute-done.17.refs_1_, bf16[96,6144]{1,0:T(8,128)(2,1)S(1)} %copy-done.4, ...), custom_call_target="tpu_custom_call" | custom-call | flops 7247757312 | bytes 28311552 | tf_op jit(solution)/shard_map/experts/pallas_call | solution.py:141
  115.8 7.2 %collective-permute-done.21.refs_2_ = bf16[96,6144]{1,0:T(8,128)(2,1)S(1)} collective-permute-done((bf16[96,6144]{1,0:T(8,128)(2,1)S(1)}, bf16[96,6144]{1,0:T(8,128)(2,1)S(1)}, u32[]{:S(2)}, u32[]{:S(2)}) %collective-permute-start.21) | collective-permute-done | bytes 1179680 | tf_op jit(solution)/shard_map/ppermute | solution.py:16
  123.0 1.9 collective-permute-start.26
  125.2 5.2 %collective-permute-done.22.refs_3_ = bf16[96,6144]{1,0:T(8,128)(2,1)S(1)} collective-permute-done((bf16[96,6144]{1,0:T(8,128)(2,1)S(1)}, bf16[96,6144]{1,0:T(8,128)(2,1)S(1)}, u32[]{:S(2)}, u32[]{:S(2)}) %collective-permute-start.22) | collective-permute-done | bytes 1179680 | tf_op jit(solution)/shard_map/ppermute | solution.py:16
  130.5 11.0 %experts.7 = (bf16[96,6144]{1,0:T(8,128)(2,1)S(1)}, bf16[96,6144]{1,0:T(8,128)(2,1)S(1)}, bf16[96,6144]{1,0:T(8,128)(2,1)S(1)}, bf16[96,6144]{1,0:T(8,128)(2,1)S(1)}) custom-call(bf16[96,6144]{1,0:T(8,128)(2,1)S(1)} %collective-permute-done.15.refs_0_, bf16[96,6144]{1,0:T(8,128)(2,1)S(1)} %collective-permute-done.20.refs_1_, ...), custom_call_target="tpu_custom_call" | custom-call | flops 7247757312 | bytes 28311552 | tf_op jit(solution)/shard_map/experts/pallas_call | solution.py:141
  141.5 5.3 %collective-permute-done.25 = bf16[96,6144]{1,0:T(8,128)(2,1)S(1)} collective-permute-done((bf16[96,6144]{1,0:T(8,128)(2,1)S(1)}, bf16[96,6144]{1,0:T(8,128)(2,1)S(1)}, u32[]{:S(2)}, u32[]{:S(2)}) %collective-permute-start.25) | collective-permute-done | bytes 1179680 | tf_op jit(solution)/shard_map/ppermute | solution.py:16
  150.1 2.4 collective-permute-start.27
  152.5 1.8 collective-permute-start.28
  154.3 1.4 collective-permute-start.29
  156.8 20.8 %collective-permute-done.28 = bf16[96,6144]{1,0:T(8,128)(2,1)S(1)} collective-permute-done((bf16[96,6144]{1,0:T(8,128)(2,1)S(1)}, bf16[96,6144]{1,0:T(8,128)(2,1)S(1)}, u32[]{:S(2)}, u32[]{:S(2)}) %collective-permute-start.28) | collective-permute-done | bytes 1179680 | tf_op jit(solution)/shard_map/ppermute | solution.py:16
  178.6 1.9 collective-permute-start.31
  180.5 1.4 collective-permute-start.32
  183.2 10.1 %collective-permute-done.35 = f32[4,128]{1,0:T(4,128)S(1)} collective-permute-done((f32[4,128]{1,0:T(4,128)S(1)}, f32[4,128]{1,0:T(4,128)S(1)}, u32[]{:S(2)}, u32[]{:S(2)}) %collective-permute-start.35) | collective-permute-done | bytes 2080 | tf_op jit(solution)/shard_map/ppermute | solution.py:40
  193.3 10.1 %collective-permute-done.31 = bf16[96,6144]{1,0:T(8,128)(2,1)S(1)} collective-permute-done((bf16[96,6144]{1,0:T(8,128)(2,1)S(1)}, bf16[96,6144]{1,0:T(8,128)(2,1)S(1)}, u32[]{:S(2)}, u32[]{:S(2)}) %collective-permute-start.31) | collective-permute-done | bytes 1179680 | tf_op jit(solution)/shard_map/ppermute | solution.py:16
  204.1 3.8 %collective-permute-start.36 = (bf16[48,6144]{1,0:T(8,128)(2,1)S(1)}, bf16[48,6144]{1,0:T(8,128)(2,1)S(1)}, u32[]{:S(2)}, u32[]{:S(2)}) collective-permute-start(bf16[48,6144]{1,0:T(8,128)(2,1)S(1)} %pad_maximum_fusion.5), channel_id=1, source_target_pairs={{0,6},{2,0},{4,2},{6,4},{1,7},{3,1},{5,3},{7,5},{8,14},{10,8},{12,... | collective-permute-start | bytes 1769480 | tf_op jit(solution)/shard_map/ppermute | solution.py:16
  210.9 7.1 %collective-permute-done.36 = bf16[48,6144]{1,0:T(8,128)(2,1)S(1)} collective-permute-done((bf16[48,6144]{1,0:T(8,128)(2,1)S(1)}, bf16[48,6144]{1,0:T(8,128)(2,1)S(1)}, u32[]{:S(2)}, u32[]{:S(2)}) %collective-permute-start.36) | collective-permute-done | bytes 589856 | tf_op jit(solution)/shard_map/ppermute | solution.py:16
  217.9 4.3 %collective-permute-done.37 = bf16[48,6144]{1,0:T(8,128)(2,1)S(1)} collective-permute-done((bf16[48,6144]{1,0:T(8,128)(2,1)S(1)}, bf16[48,6144]{1,0:T(8,128)(2,1)S(1)}, u32[]{:S(2)}, u32[]{:S(2)}) %collective-permute-start.37) | collective-permute-done | bytes 589856 | tf_op jit(solution)/shard_map/ppermute | solution.py:16
  222.3 1.7 collective-permute-done.39
  226.4 3.2 %collective-permute-start.40 = (bf16[24,6144]{1,0:T(8,128)(2,1)S(1)}, bf16[24,6144]{1,0:T(8,128)(2,1)S(1)}, u32[]{:S(2)}, u32[]{:S(2)}) collective-permute-start(bf16[24,6144]{1,0:T(8,128)(2,1)S(1)} %add_convert_fusion.13), channel_id=1, source_target_pairs={{0,6},{2,0},{4,2},{6,4},{1,7},{3,1},{5,3},{7,5},{8,14},{10,8},{12,... | collective-permute-start | bytes 884744 | tf_op jit(solution)/shard_map/ppermute | solution.py:16
  229.6 2.7 %collective-permute-done.43 = bf16[24,6144]{1,0:T(8,128)(2,1)S(1)} collective-permute-done((bf16[24,6144]{1,0:T(8,128)(2,1)S(1)}, bf16[24,6144]{1,0:T(8,128)(2,1)S(1)}, u32[]{:S(2)}, u32[]{:S(2)}) %collective-permute-start.43) | collective-permute-done | bytes 294944 | tf_op jit(solution)/shard_map/ppermute | solution.py:16
  232.3 2.0 collective-permute-done.41
  234.3 2.0 collective-permute-done.42
  238.3 4.8 %collective-permute-start.44 = (bf16[48,6144]{1,0:T(8,128)(2,1)S(1)}, bf16[48,6144]{1,0:T(8,128)(2,1)S(1)}, u32[]{:S(2)}, u32[]{:S(2)}) collective-permute-start(bf16[48,6144]{1,0:T(8,128)(2,1)S(1)} %pad_maximum_fusion.7), channel_id=1, source_target_pairs={{0,33},{1,32},{32,65},{33,64},{64,97},{65,96},{96,1},{97,0},{2,35}... | collective-permute-start | bytes 1769480 | tf_op jit(solution)/shard_map/ppermute | solution.py:45
  243.1 13.6 %collective-permute-done.45 = bf16[48,6144]{1,0:T(8,128)(2,1)S(1)} collective-permute-done((bf16[48,6144]{1,0:T(8,128)(2,1)S(1)}, bf16[48,6144]{1,0:T(8,128)(2,1)S(1)}, u32[]{:S(2)}, u32[]{:S(2)}) %collective-permute-start.45) | collective-permute-done | bytes 589856 | tf_op jit(solution)/shard_map/ppermute | solution.py:55
  257.4 1.8 fusion.2
  (117 shorter events, 25.0 us)
Async XLA Ops:
  1.7 67.1 %slice-start.2 = ((s8[6291456]{0:T(1024)(128)(4,1)}), s8[4194304]{0:T(1024)(128)(4,1)S(1)}, s32[]{:S(2)}) async-start(s8[6291456]{0:T(1024)(128)(4,1)} %bitcast.44), calls=%async_computation.2 | async-start | bytes 8388608
  2.4 66.4 %slice-start = ((s8[6291456]{0:T(1024)(128)(4,1)}), s8[4194304]{0:T(1024)(128)(4,1)S(1)}, s32[]{:S(2)}) async-start(s8[6291456]{0:T(1024)(128)(4,1)} %bitcast.38), calls=%async_computation | async-start | bytes 8388608
  2.5 9.9 %collective-permute-start.6 = (bf16[24,6144]{1,0:T(8,128)(2,1)S(1)}, bf16[24,6144]{1,0:T(8,128)(2,1)S(1)}, u32[]{:S(2)}, u32[]{:S(2)}) collective-permute-start(bf16[24,6144]{1,0:T(8,128)(2,1)S(1)} %get-tuple-element.175), channel_id=1, source_target_pairs={{0,2},{2,4},{4,6},{6,0},{1,3},{3,5},{5,7},{7,1},{8,10},{10,12},{12... | collective-permute-start | bytes 884744 | tf_op jit(solution)/shard_map/ppermute | solution.py:16
  4.1 8.8 %collective-permute-start = (bf16[24,6144]{1,0:T(8,128)(2,1)S(1)}, bf16[24,6144]{1,0:T(8,128)(2,1)S(1)}, u32[]{:S(2)}, u32[]{:S(2)}) collective-permute-start(bf16[24,6144]{1,0:T(8,128)(2,1)S(1)} %get-tuple-element.176), channel_id=1, source_target_pairs={{0,8},{8,0},{1,9},{9,1},{2,10},{10,2},{3,11},{11,3},{4,12},{12,4},... | collective-permute-start | bytes 884744 | tf_op jit(solution)/shard_map/ppermute | solution.py:16
  5.7 22.5 %collective-permute-start.7 = (bf16[24,6144]{1,0:T(8,128)(2,1)S(1)}, bf16[24,6144]{1,0:T(8,128)(2,1)S(1)}, u32[]{:S(2)}, u32[]{:S(2)}) collective-permute-start(bf16[24,6144]{1,0:T(8,128)(2,1)S(1)} %get-tuple-element.175), channel_id=1, source_target_pairs={{0,6},{2,0},{4,2},{6,4},{1,7},{3,1},{5,3},{7,5},{8,14},{10,8},{12,... | collective-permute-start | bytes 884744 | tf_op jit(solution)/shard_map/ppermute | solution.py:16
  7.4 15.4 %collective-permute-start.1 = (bf16[48,6144]{1,0:T(8,128)(2,1)S(1)}, bf16[48,6144]{1,0:T(8,128)(2,1)S(1)}, u32[]{:S(2)}, u32[]{:S(2)}) collective-permute-start(bf16[48,6144]{1,0:T(8,128)(2,1)S(1)} %convolution_convert_fusion.1), channel_id=1, source_target_pairs={{0,24},{8,16},{16,8},{24,0},{1,25},{9,17},{17,9},{25,1},{2,26},{10... | collective-permute-start | bytes 1769480 | tf_op jit(solution)/shard_map/ppermute | solution.py:36
  12.4 15.8 %collective-permute-start.8 = (bf16[24,6144]{1,0:T(8,128)(2,1)S(1)}, bf16[24,6144]{1,0:T(8,128)(2,1)S(1)}, u32[]{:S(2)}, u32[]{:S(2)}) collective-permute-start(bf16[24,6144]{1,0:T(8,128)(2,1)S(1)} %collective-permute-done.6), channel_id=1, source_target_pairs={{0,2},{2,4},{4,6},{6,0},{1,3},{3,5},{5,7},{7,1},{8,10},{10,12},{12... | collective-permute-start | bytes 884744 | tf_op jit(solution)/shard_map/ppermute | solution.py:16
  22.9 8.3 %collective-permute-start.5 = (bf16[24,6144]{1,0:T(8,128)(2,1)S(1)}, bf16[24,6144]{1,0:T(8,128)(2,1)S(1)}, u32[]{:S(2)}, u32[]{:S(2)}) collective-permute-start(bf16[24,6144]{1,0:T(8,128)(2,1)S(1)} %get-tuple-element.177), channel_id=1, source_target_pairs={{0,2},{2,4},{4,6},{6,0},{1,3},{3,5},{5,7},{7,1},{8,10},{10,12},{12... | collective-permute-start | bytes 884744 | tf_op jit(solution)/shard_map/ppermute | solution.py:16
  23.3 7.9 %collective-permute-start.4 = (bf16[24,6144]{1,0:T(8,128)(2,1)S(1)}, bf16[24,6144]{1,0:T(8,128)(2,1)S(1)}, u32[]{:S(2)}, u32[]{:S(2)}) collective-permute-start(bf16[24,6144]{1,0:T(8,128)(2,1)S(1)} %get-tuple-element.177), channel_id=1, source_target_pairs={{0,6},{2,0},{4,2},{6,4},{1,7},{3,1},{5,3},{7,5},{8,14},{10,8},{12,... | collective-permute-start | bytes 884744 | tf_op jit(solution)/shard_map/ppermute | solution.py:16
  26.2 7.9 %collective-permute-start.2 = (bf16[24,6144]{1,0:T(8,128)(2,1)S(1)}, bf16[24,6144]{1,0:T(8,128)(2,1)S(1)}, u32[]{:S(2)}, u32[]{:S(2)}) collective-permute-start(bf16[24,6144]{1,0:T(8,128)(2,1)S(1)} %get-tuple-element.178), channel_id=1, source_target_pairs={{0,1},{1,0},{2,3},{3,2},{4,5},{5,4},{6,7},{7,6},{8,9},{9,8},{10,11... | collective-permute-start | bytes 884744 | tf_op jit(solution)/shard_map/ppermute | solution.py:16
  28.2 38.3 %collective-permute-start.14 = (bf16[96,6144]{1,0:T(8,128)(2,1)S(1)}, bf16[96,6144]{1,0:T(8,128)(2,1)S(1)}, u32[]{:S(2)}, u32[]{:S(2)}) collective-permute-start(bf16[96,6144]{1,0:T(8,128)(2,1)S(1)} %pad_maximum_fusion.1.refs_1_), channel_id=1, source_target_pairs={{0,8},{8,0},{1,9},{9,1},{2,10},{10,2},{3,11},{11,3},{4,12},{12,4},... | collective-permute-start | bytes 3538952 | tf_op jit(solution)/shard_map/ppermute | solution.py:16
  31.2 7.8 %collective-permute-start.9 = (bf16[24,6144]{1,0:T(8,128)(2,1)S(1)}, bf16[24,6144]{1,0:T(8,128)(2,1)S(1)}, u32[]{:S(2)}, u32[]{:S(2)}) collective-permute-start(bf16[24,6144]{1,0:T(8,128)(2,1)S(1)} %collective-permute-done.4), channel_id=1, source_target_pairs={{0,6},{2,0},{4,2},{6,4},{1,7},{3,1},{5,3},{7,5},{8,14},{10,8},{12,... | collective-permute-start | bytes 884744 | tf_op jit(solution)/shard_map/ppermute | solution.py:16
  34.2 31.9 %collective-permute-start.12 = (bf16[48,6144]{1,0:T(8,128)(2,1)S(1)}, bf16[48,6144]{1,0:T(8,128)(2,1)S(1)}, u32[]{:S(2)}, u32[]{:S(2)}) collective-permute-start(bf16[48,6144]{1,0:T(8,128)(2,1)S(1)} %pad_maximum_fusion.4), channel_id=1, source_target_pairs={{0,8},{8,0},{1,9},{9,1},{2,10},{10,2},{3,11},{11,3},{4,12},{12,4},... | collective-permute-start | bytes 1769480 | tf_op jit(solution)/shard_map/ppermute | solution.py:16
  34.4 13.5 %collective-permute-start.11 = (bf16[48,6144]{1,0:T(8,128)(2,1)S(1)}, bf16[48,6144]{1,0:T(8,128)(2,1)S(1)}, u32[]{:S(2)}, u32[]{:S(2)}) collective-permute-start(bf16[48,6144]{1,0:T(8,128)(2,1)S(1)} %pad_maximum_fusion.3), channel_id=1, source_target_pairs={{0,1},{1,0},{2,3},{3,2},{4,5},{5,4},{6,7},{7,6},{8,9},{9,8},{10,11... | collective-permute-start | bytes 1769480 | tf_op jit(solution)/shard_map/ppermute | solution.py:16
  36.4 31.8 %collective-permute-start.3 = (bf16[96,6144]{1,0:T(8,128)(2,1)S(1)}, bf16[96,6144]{1,0:T(8,128)(2,1)S(1)}, u32[]{:S(2)}, u32[]{:S(2)}) collective-permute-start(bf16[96,6144]{1,0:T(8,128)(2,1)S(1)} %pad_maximum_fusion.refs_0_), channel_id=1, source_target_pairs={{0,2},{2,4},{4,6},{6,0},{1,3},{3,5},{5,7},{7,1},{8,10},{10,12},{12... | collective-permute-start | bytes 3538952 | tf_op jit(solution)/shard_map/ppermute | solution.py:16
  39.0 29.5 %collective-permute-start.10 = (bf16[96,6144]{1,0:T(8,128)(2,1)S(1)}, bf16[96,6144]{1,0:T(8,128)(2,1)S(1)}, u32[]{:S(2)}, u32[]{:S(2)}) collective-permute-start(bf16[96,6144]{1,0:T(8,128)(2,1)S(1)} %pad_maximum_fusion.refs_0_), channel_id=1, source_target_pairs={{0,6},{2,0},{4,2},{6,4},{1,7},{3,1},{5,3},{7,5},{8,14},{10,8},{12,... | collective-permute-start | bytes 3538952 | tf_op jit(solution)/shard_map/ppermute | solution.py:16
  47.9 34.6 %collective-permute-start.13 = (bf16[96,6144]{1,0:T(8,128)(2,1)S(1)}, bf16[96,6144]{1,0:T(8,128)(2,1)S(1)}, u32[]{:S(2)}, u32[]{:S(2)}) collective-permute-start(bf16[96,6144]{1,0:T(8,128)(2,1)S(1)} %pad_maximum_fusion.1.refs_1_), channel_id=1, source_target_pairs={{0,1},{1,0},{2,3},{3,2},{4,5},{5,4},{6,7},{7,6},{8,9},{9,8},{10,11... | collective-permute-start | bytes 3538952 | tf_op jit(solution)/shard_map/ppermute | solution.py:16
  66.1 29.2 %collective-permute-start.17 = (bf16[96,6144]{1,0:T(8,128)(2,1)S(1)}, bf16[96,6144]{1,0:T(8,128)(2,1)S(1)}, u32[]{:S(2)}, u32[]{:S(2)}) collective-permute-start(bf16[96,6144]{1,0:T(8,128)(2,1)S(1)} %constant_dynamic-update-slice_fusion.refs_2_), channel_id=1, source_target_pairs={{0,6},{2,0},{4,2},{6,4},{1,7},{3,1},{5,3},{7,5},{8,14},{10,8},{12,... | collective-permute-start | bytes 3538952 | tf_op jit(solution)/shard_map/ppermute | solution.py:16
  66.5 30.6 %collective-permute-start.16 = (bf16[96,6144]{1,0:T(8,128)(2,1)S(1)}, bf16[96,6144]{1,0:T(8,128)(2,1)S(1)}, u32[]{:S(2)}, u32[]{:S(2)}) collective-permute-start(bf16[96,6144]{1,0:T(8,128)(2,1)S(1)} %constant_dynamic-update-slice_fusion.refs_2_), channel_id=1, source_target_pairs={{0,2},{2,4},{4,6},{6,0},{1,3},{3,5},{5,7},{7,1},{8,10},{10,12},{12... | collective-permute-start | bytes 3538952 | tf_op jit(solution)/shard_map/ppermute | solution.py:16
  68.2 32.3 %collective-permute-start.19 = (bf16[96,6144]{1,0:T(8,128)(2,1)S(1)}, bf16[96,6144]{1,0:T(8,128)(2,1)S(1)}, u32[]{:S(2)}, u32[]{:S(2)}) collective-permute-start(bf16[96,6144]{1,0:T(8,128)(2,1)S(1)} %pad_maximum_fusion.2.refs_2_), channel_id=1, source_target_pairs={{0,1},{1,0},{2,3},{3,2},{4,5},{5,4},{6,7},{7,6},{8,9},{9,8},{10,11... | collective-permute-start | bytes 3538952 | tf_op jit(solution)/shard_map/ppermute | solution.py:16
  68.5 32.0 %collective-permute-start.18 = (bf16[96,6144]{1,0:T(8,128)(2,1)S(1)}, bf16[96,6144]{1,0:T(8,128)(2,1)S(1)}, u32[]{:S(2)}, u32[]{:S(2)}) collective-permute-start(bf16[96,6144]{1,0:T(8,128)(2,1)S(1)} %pad_maximum_fusion.2.refs_2_), channel_id=1, source_target_pairs={{0,8},{8,0},{1,9},{9,1},{2,10},{10,2},{3,11},{11,3},{4,12},{12,4},... | collective-permute-start | bytes 3538952 | tf_op jit(solution)/shard_map/ppermute | solution.py:16
  82.6 42.4 %collective-permute-start.15 = (bf16[96,6144]{1,0:T(8,128)(2,1)S(1)}, bf16[96,6144]{1,0:T(8,128)(2,1)S(1)}, u32[]{:S(2)}, u32[]{:S(2)}) collective-permute-start(bf16[96,6144]{1,0:T(8,128)(2,1)S(1)} %collective-permute-done.10.refs_1_), channel_id=1, source_target_pairs={{0,6},{2,0},{4,2},{6,4},{1,7},{3,1},{5,3},{7,5},{8,14},{10,8},{12,... | collective-permute-start | bytes 3538952 | tf_op jit(solution)/shard_map/ppermute | solution.py:16
  95.3 27.7 %collective-permute-start.21 = (bf16[96,6144]{1,0:T(8,128)(2,1)S(1)}, bf16[96,6144]{1,0:T(8,128)(2,1)S(1)}, u32[]{:S(2)}, u32[]{:S(2)}) collective-permute-start(bf16[96,6144]{1,0:T(8,128)(2,1)S(1)} %collective-permute-done.14.refs_3_), channel_id=1, source_target_pairs={{0,1},{1,0},{2,3},{3,2},{4,5},{5,4},{6,7},{7,6},{8,9},{9,8},{10,11... | collective-permute-start | bytes 3538952 | tf_op jit(solution)/shard_map/ppermute | solution.py:16
  101.5 23.7 %collective-permute-start.20 = (bf16[96,6144]{1,0:T(8,128)(2,1)S(1)}, bf16[96,6144]{1,0:T(8,128)(2,1)S(1)}, u32[]{:S(2)}, u32[]{:S(2)}) collective-permute-start(bf16[96,6144]{1,0:T(8,128)(2,1)S(1)} %collective-permute-done.16.refs_0_), channel_id=1, source_target_pairs={{0,2},{2,4},{4,6},{6,0},{1,3},{3,5},{5,7},{7,1},{8,10},{10,12},{12... | collective-permute-start | bytes 3538952 | tf_op jit(solution)/shard_map/ppermute | solution.py:16
  101.5 28.9 %collective-permute-start.22 = (bf16[96,6144]{1,0:T(8,128)(2,1)S(1)}, bf16[96,6144]{1,0:T(8,128)(2,1)S(1)}, u32[]{:S(2)}, u32[]{:S(2)}) collective-permute-start(bf16[96,6144]{1,0:T(8,128)(2,1)S(1)} %collective-permute-done.19.refs_3_), channel_id=1, source_target_pairs={{0,8},{8,0},{1,9},{9,1},{2,10},{10,2},{3,11},{11,3},{4,12},{12,4},... | collective-permute-start | bytes 3538952 | tf_op jit(solution)/shard_map/ppermute | solution.py:16
  102.8 44.0 %collective-permute-start.25 = (bf16[96,6144]{1,0:T(8,128)(2,1)S(1)}, bf16[96,6144]{1,0:T(8,128)(2,1)S(1)}, u32[]{:S(2)}, u32[]{:S(2)}) collective-permute-start(bf16[96,6144]{1,0:T(8,128)(2,1)S(1)} %get-tuple-element.128), channel_id=1, source_target_pairs={{0,8},{8,0},{1,9},{9,1},{2,10},{10,2},{3,11},{11,3},{4,12},{12,4},... | collective-permute-start | bytes 3538952 | tf_op jit(solution)/shard_map/ppermute | solution.py:16
  123.0 24.5 %collective-permute-start.26 = (bf16[96,6144]{1,0:T(8,128)(2,1)S(1)}, bf16[96,6144]{1,0:T(8,128)(2,1)S(1)}, u32[]{:S(2)}, u32[]{:S(2)}) collective-permute-start(bf16[96,6144]{1,0:T(8,128)(2,1)S(1)} %get-tuple-element.129), channel_id=1, source_target_pairs={{0,1},{1,0},{2,3},{3,2},{4,5},{5,4},{6,7},{7,6},{8,9},{9,8},{10,11... | collective-permute-start | bytes 3538952 | tf_op jit(solution)/shard_map/ppermute | solution.py:16
  125.0 23.9 %collective-permute-start.23 = (bf16[96,6144]{1,0:T(8,128)(2,1)S(1)}, bf16[96,6144]{1,0:T(8,128)(2,1)}, u32[]{:S(2)}, u32[]{:S(2)}) collective-permute-start(bf16[96,6144]{1,0:T(8,128)(2,1)S(1)} %get-tuple-element.126), channel_id=1, source_target_pairs={{0,6},{2,0},{4,2},{6,4},{1,7},{3,1},{5,3},{7,5},{8,14},{10,8},{12,... | collective-permute-start | bytes 3538952 | tf_op jit(solution)/shard_map/ppermute | solution.py:16
  130.4 19.7 %collective-permute-start.24 = (bf16[96,6144]{1,0:T(8,128)(2,1)S(1)}, bf16[96,6144]{1,0:T(8,128)(2,1)S(1)}, u32[]{:S(2)}, u32[]{:S(2)}) collective-permute-start(bf16[96,6144]{1,0:T(8,128)(2,1)S(1)} %get-tuple-element.127), channel_id=1, source_target_pairs={{0,2},{2,4},{4,6},{6,0},{1,3},{3,5},{5,7},{7,1},{8,10},{10,12},{12... | collective-permute-start | bytes 3538952 | tf_op jit(solution)/shard_map/ppermute | solution.py:16
  150.1 28.4 %collective-permute-start.27 = (bf16[96,6144]{1,0:T(8,128)(2,1)S(1)}, bf16[96,6144]{1,0:T(8,128)(2,1)S(1)}, u32[]{:S(2)}, u32[]{:S(2)}) collective-permute-start(bf16[96,6144]{1,0:T(8,128)(2,1)S(1)} %get-tuple-element.130), channel_id=1, source_target_pairs={{0,8},{8,0},{1,9},{9,1},{2,10},{10,2},{3,11},{11,3},{4,12},{12,4},... | collective-permute-start | bytes 3538952 | tf_op jit(solution)/shard_map/ppermute | solution.py:16
  152.5 25.1 %collective-permute-start.28 = (bf16[96,6144]{1,0:T(8,128)(2,1)S(1)}, bf16[96,6144]{1,0:T(8,128)(2,1)S(1)}, u32[]{:S(2)}, u32[]{:S(2)}) collective-permute-start(bf16[96,6144]{1,0:T(8,128)(2,1)S(1)} %get-tuple-element.132), channel_id=1, source_target_pairs={{0,2},{2,4},{4,6},{6,0},{1,3},{3,5},{5,7},{7,1},{8,10},{10,12},{12... | collective-permute-start | bytes 3538952 | tf_op jit(solution)/shard_map/ppermute | solution.py:16
  154.3 23.6 %collective-permute-start.29 = (bf16[96,6144]{1,0:T(8,128)(2,1)S(1)}, bf16[96,6144]{1,0:T(8,128)(2,1)S(1)}, u32[]{:S(2)}, u32[]{:S(2)}) collective-permute-start(bf16[96,6144]{1,0:T(8,128)(2,1)S(1)} %get-tuple-element.134), channel_id=1, source_target_pairs={{0,6},{2,0},{4,2},{6,4},{1,7},{3,1},{5,3},{7,5},{8,14},{10,8},{12,... | collective-permute-start | bytes 3538952 | tf_op jit(solution)/shard_map/ppermute | solution.py:16
  155.7 22.5 %collective-permute-start.30 = (bf16[96,6144]{1,0:T(8,128)(2,1)S(1)}, bf16[96,6144]{1,0:T(8,128)(2,1)S(1)}, u32[]{:S(2)}, u32[]{:S(2)}) collective-permute-start(bf16[96,6144]{1,0:T(8,128)(2,1)S(1)} %get-tuple-element.138), channel_id=1, source_target_pairs={{0,1},{1,0},{2,3},{3,2},{4,5},{5,4},{6,7},{7,6},{8,9},{9,8},{10,11... | collective-permute-start | bytes 3538952 | tf_op jit(solution)/shard_map/ppermute | solution.py:16
  178.6 24.9 %collective-permute-start.31 = (bf16[96,6144]{1,0:T(8,128)(2,1)S(1)}, bf16[96,6144]{1,0:T(8,128)(2,1)S(1)}, u32[]{:S(2)}, u32[]{:S(2)}) collective-permute-start(bf16[96,6144]{1,0:T(8,128)(2,1)S(1)} %add_convert_fusion.3), channel_id=1, source_target_pairs={{0,2},{2,4},{4,6},{6,0},{1,3},{3,5},{5,7},{7,1},{8,10},{10,12},{12... | collective-permute-start | bytes 3538952 | tf_op jit(solution)/shard_map/ppermute | solution.py:16
  180.5 23.2 %collective-permute-start.32 = (bf16[96,6144]{1,0:T(8,128)(2,1)S(1)}, bf16[96,6144]{1,0:T(8,128)(2,1)S(1)}, u32[]{:S(2)}, u32[]{:S(2)}) collective-permute-start(bf16[96,6144]{1,0:T(8,128)(2,1)S(1)} %add_convert_fusion.2), channel_id=1, source_target_pairs={{0,6},{2,0},{4,2},{6,4},{1,7},{3,1},{5,3},{7,5},{8,14},{10,8},{12,... | collective-permute-start | bytes 3538952 | tf_op jit(solution)/shard_map/ppermute | solution.py:16
  181.9 21.8 %collective-permute-start.33 = (bf16[96,6144]{1,0:T(8,128)(2,1)S(1)}, bf16[96,6144]{1,0:T(8,128)(2,1)S(1)}, u32[]{:S(2)}, u32[]{:S(2)}) collective-permute-start(bf16[96,6144]{1,0:T(8,128)(2,1)S(1)} %add_convert_fusion.1), channel_id=1, source_target_pairs={{0,1},{1,0},{2,3},{3,2},{4,5},{5,4},{6,7},{7,6},{8,9},{9,8},{10,11... | collective-permute-start | bytes 3538952 | tf_op jit(solution)/shard_map/ppermute | solution.py:16
  183.2 20.4 %collective-permute-start.34 = (bf16[96,6144]{1,0:T(8,128)(2,1)S(1)}, bf16[96,6144]{1,0:T(8,128)(2,1)S(1)}, u32[]{:S(2)}, u32[]{:S(2)}) collective-permute-start(bf16[96,6144]{1,0:T(8,128)(2,1)S(1)} %add_convert_fusion), channel_id=1, source_target_pairs={{0,8},{8,0},{1,9},{9,1},{2,10},{10,2},{3,11},{11,3},{4,12},{12,4},... | collective-permute-start | bytes 3538952 | tf_op jit(solution)/shard_map/ppermute | solution.py:16
  183.2 10.1 %collective-permute-start.35 = (f32[4,128]{1,0:T(4,128)S(1)}, f32[4,128]{1,0:T(4,128)S(1)}, u32[]{:S(2)}, u32[]{:S(2)}) collective-permute-start(f32[4,128]{1,0:T(4,128)S(1)} %pad_maximum_fusion.9), channel_id=1, source_target_pairs={{0,32},{32,64},{64,96},{96,0},{1,33},{33,65},{65,97},{97,1},{2,34}... | collective-permute-start | bytes 6152 | tf_op jit(solution)/shard_map/ppermute | solution.py:40
  204.1 13.8 %collective-permute-start.36 = (bf16[48,6144]{1,0:T(8,128)(2,1)S(1)}, bf16[48,6144]{1,0:T(8,128)(2,1)S(1)}, u32[]{:S(2)}, u32[]{:S(2)}) collective-permute-start(bf16[48,6144]{1,0:T(8,128)(2,1)S(1)} %pad_maximum_fusion.5), channel_id=1, source_target_pairs={{0,6},{2,0},{4,2},{6,4},{1,7},{3,1},{5,3},{7,5},{8,14},{10,8},{12,... | collective-permute-start | bytes 1769480 | tf_op jit(solution)/shard_map/ppermute | solution.py:16
  207.9 14.3 %collective-permute-start.37 = (bf16[48,6144]{1,0:T(8,128)(2,1)S(1)}, bf16[48,6144]{1,0:T(8,128)(2,1)S(1)}, u32[]{:S(2)}, u32[]{:S(2)}) collective-permute-start(bf16[48,6144]{1,0:T(8,128)(2,1)S(1)} %pad_maximum_fusion.6), channel_id=1, source_target_pairs={{0,2},{2,4},{4,6},{6,0},{1,3},{3,5},{5,7},{7,1},{8,10},{10,12},{12... | collective-permute-start | bytes 1769480 | tf_op jit(solution)/shard_map/ppermute | solution.py:16
  209.3 13.0 %collective-permute-start.38 = (bf16[48,6144]{1,0:T(8,128)(2,1)S(1)}, bf16[48,6144]{1,0:T(8,128)(2,1)S(1)}, u32[]{:S(2)}, u32[]{:S(2)}) collective-permute-start(bf16[48,6144]{1,0:T(8,128)(2,1)S(1)} %add_convert_fusion.5), channel_id=1, source_target_pairs={{0,1},{1,0},{2,3},{3,2},{4,5},{5,4},{6,7},{7,6},{8,9},{9,8},{10,11... | collective-permute-start | bytes 1769480 | tf_op jit(solution)/shard_map/ppermute | solution.py:16
  210.8 13.1 %collective-permute-start.39 = (bf16[48,6144]{1,0:T(8,128)(2,1)S(1)}, bf16[48,6144]{1,0:T(8,128)(2,1)S(1)}, u32[]{:S(2)}, u32[]{:S(2)}) collective-permute-start(bf16[48,6144]{1,0:T(8,128)(2,1)S(1)} %add_convert_fusion.4), channel_id=1, source_target_pairs={{0,8},{8,0},{1,9},{9,1},{2,10},{10,2},{3,11},{11,3},{4,12},{12,4},... | collective-permute-start | bytes 1769480 | tf_op jit(solution)/shard_map/ppermute | solution.py:16
  225.5 6.8 %collective-permute-start.43 = (bf16[24,6144]{1,0:T(8,128)(2,1)S(1)}, bf16[24,6144]{1,0:T(8,128)(2,1)S(1)}, u32[]{:S(2)}, u32[]{:S(2)}) collective-permute-start(bf16[24,6144]{1,0:T(8,128)(2,1)S(1)} %add_convert_fusion.10), channel_id=1, source_target_pairs={{0,1},{1,0},{2,3},{3,2},{4,5},{5,4},{6,7},{7,6},{8,9},{9,8},{10,11... | collective-permute-start | bytes 884744 | tf_op jit(solution)/shard_map/ppermute | solution.py:16
  226.4 7.9 %collective-permute-start.41 = (bf16[24,6144]{1,0:T(8,128)(2,1)S(1)}, bf16[24,6144]{1,0:T(8,128)(2,1)S(1)}, u32[]{:S(2)}, u32[]{:S(2)}) collective-permute-start(bf16[24,6144]{1,0:T(8,128)(2,1)S(1)} %add_convert_fusion.12), channel_id=1, source_target_pairs={{0,2},{2,4},{4,6},{6,0},{1,3},{3,5},{5,7},{7,1},{8,10},{10,12},{12... | collective-permute-start | bytes 884744 | tf_op jit(solution)/shard_map/ppermute | solution.py:16
  226.4 7.9 %collective-permute-start.40 = (bf16[24,6144]{1,0:T(8,128)(2,1)S(1)}, bf16[24,6144]{1,0:T(8,128)(2,1)S(1)}, u32[]{:S(2)}, u32[]{:S(2)}) collective-permute-start(bf16[24,6144]{1,0:T(8,128)(2,1)S(1)} %add_convert_fusion.13), channel_id=1, source_target_pairs={{0,6},{2,0},{4,2},{6,4},{1,7},{3,1},{5,3},{7,5},{8,14},{10,8},{12,... | collective-permute-start | bytes 884744 | tf_op jit(solution)/shard_map/ppermute | solution.py:16
  229.6 6.7 %collective-permute-start.42 = (bf16[24,6144]{1,0:T(8,128)(2,1)S(1)}, bf16[24,6144]{1,0:T(8,128)(2,1)S(1)}, u32[]{:S(2)}, u32[]{:S(2)}) collective-permute-start(bf16[24,6144]{1,0:T(8,128)(2,1)S(1)} %add_convert_fusion.11), channel_id=1, source_target_pairs={{0,8},{8,0},{1,9},{9,1},{2,10},{10,2},{3,11},{11,3},{4,12},{12,4},... | collective-permute-start | bytes 884744 | tf_op jit(solution)/shard_map/ppermute | solution.py:16
  238.1 18.6 %collective-permute-start.45 = (bf16[48,6144]{1,0:T(8,128)(2,1)S(1)}, bf16[48,6144]{1,0:T(8,128)(2,1)S(1)}, u32[]{:S(2)}, u32[]{:S(2)}) collective-permute-start(bf16[48,6144]{1,0:T(8,128)(2,1)S(1)} %pad_maximum_fusion.8), channel_id=1, source_target_pairs={{0,57},{1,56},{8,49},{9,48},{16,41},{17,40},{24,33},{25,32},{32,89... | collective-permute-start | bytes 1769480 | tf_op jit(solution)/shard_map/ppermute | solution.py:55
  238.3 19.1 %collective-permute-start.44 = (bf16[48,6144]{1,0:T(8,128)(2,1)S(1)}, bf16[48,6144]{1,0:T(8,128)(2,1)S(1)}, u32[]{:S(2)}, u32[]{:S(2)}) collective-permute-start(bf16[48,6144]{1,0:T(8,128)(2,1)S(1)} %pad_maximum_fusion.7), channel_id=1, source_target_pairs={{0,33},{1,32},{32,65},{33,64},{64,97},{65,96},{96,1},{97,0},{2,35}... | collective-permute-start | bytes 1769480 | tf_op jit(solution)/shard_map/ppermute | solution.py:45
  (8 other events, 120.6 us)
